TPU v7x, 32 devices: a whole 2x2x4 slice. The times are simulated.
32 devices in a mesh: grp: 2 (over y), freq: 4 (over z), tm: 2 (over x), pol: 2 (over core).
Axes of the slice: x: 2, y: 2, z: 4, core: 2. Of those that a mesh axis runs over, the one named last changes fastest.
Arguments:
- voltages: bfloat16 [2, 8, 1024, 4, 2, 256], P('pol', ('grp', 'freq'), 'tm'), parts along dimension 1, may hold values from -6 to 6
- feed_gains: float32 [8, 2, 4, 2, 256], P(('grp', 'freq'), 'pol'), parts along dimension 0, may hold values from -5 to 5
- owner_table: int32 [64], replicated, may hold values from 0 to 3, as said below
- keep_flags: int32 [1024], replicated, may hold values 0 or 1
Outputs:
- owned: bfloat16 [128, 64, 2048], P(('grp', 'tm', 'pol'), None, 'freq'), parts along dimension 0
There are 2 independent parts, one for each index of `grp`. A program takes and returns all parts, laid end to end along the dimension named above; an argument that names none is the same for every part. Nothing has to cross between parts.
Inputs may be any that keep to these rules, and one draw needn't show every extreme that they name: `owner_table`: each index of freq owns from 0 to 32 beam sets; one owns exactly 32.
All inputs are finite; a program needn't handle non-finite values.
Results may differ from a plain program's by a relative error of at most 0.0058.
Values may be sent and summed in bfloat16 or wider, within the bound.
No kernel may reach another device: no remote copies, remote signals or barrier semaphores. Data moves between devices by JAX's collectives and lax.ppermute only.
A program may use at most 64 MiB of HBM per device.

v0:
```python
import jax
import jax.numpy as jnp
from jax import lax
from jax.sharding import PartitionSpec as P

NS = 256
CYL = 4
UPCH = 16
TAPS = 16
SET_BEAMS = 16


def shifted(block, axis, distance):
    devices = range(lax.axis_size(axis))
    route = [(i - distance, i) for i in devices if i - distance in devices]
    return lax.ppermute(block, axis, route)


def window_taps():
    span = TAPS * UPCH
    steps = jnp.arange(span, dtype=jnp.float32)
    weights = (
        jnp.sinc((steps - (span - 1) / 2.0) / UPCH) * jnp.sin(jnp.pi * (steps + 0.5) / span) ** 2
    )
    weights = weights / jnp.sqrt(jnp.sum(weights * weights))
    return weights.reshape(TAPS, UPCH)


def fine_tables():
    rows = jnp.arange(UPCH, dtype=jnp.int32)
    phase = rows[:, None] * rows[None, :] % UPCH
    angle = 2.0 * jnp.pi * phase.astype(jnp.float32) / UPCH
    return (jnp.cos(angle), jnp.sin(angle))


def beam_matrix():
    rows = jnp.arange(NS, dtype=jnp.int32)
    phase = rows[:, None] * rows[None, :] % NS
    angle = 2.0 * jnp.pi * phase.astype(jnp.float32) / NS
    scale = 1.0 / jnp.sqrt(jnp.float32(NS))
    cosine = jnp.cos(angle) * scale
    sine = jnp.sin(angle) * scale
    upper = jnp.concatenate([cosine, -sine], axis=1)
    lower = jnp.concatenate([sine, cosine], axis=1)
    return jnp.concatenate([upper, lower], axis=0).astype(jnp.bfloat16)


def cylinder_tables():
    rows = jnp.arange(CYL, dtype=jnp.int32)
    phase = rows[:, None] * rows[None, :] % CYL
    angle = 2.0 * jnp.pi * phase.astype(jnp.float32) / CYL
    return (0.5 * jnp.cos(angle), 0.5 * jnp.sin(angle))


def power_frames(frames, gain_pol, n_out):
    window = window_taps()
    fine_cos, fine_sin = fine_tables()
    beam_table = beam_matrix()
    cyl_cos, cyl_sin = cylinder_tables()
    highest = lax.Precision.HIGHEST
    chan_count = frames.shape[0]
    summed = jnp.zeros((chan_count, n_out) + frames.shape[2:], jnp.float32)
    for tap_index in range(TAPS):
        weights = window[tap_index].reshape(1, 1, UPCH, 1, 1, 1)
        summed = summed + weights * frames[:, tap_index : tap_index + n_out].astype(jnp.float32)
    real_part = summed[:, :, :, :, 0, :]
    imag_part = summed[:, :, :, :, 1, :]
    spec_real = jnp.einsum("qk,cmkxn->mcqxn", fine_cos, real_part, precision=highest) + jnp.einsum(
        "qk,cmkxn->mcqxn", fine_sin, imag_part, precision=highest
    )
    spec_imag = jnp.einsum("qk,cmkxn->mcqxn", fine_cos, imag_part, precision=highest) - jnp.einsum(
        "qk,cmkxn->mcqxn", fine_sin, real_part, precision=highest
    )
    gain_real = gain_pol[:, :, 0, :][None, :, None]
    gain_imag = gain_pol[:, :, 1, :][None, :, None]
    cal_real = spec_real * gain_real - spec_imag * gain_imag
    cal_imag = spec_real * gain_imag + spec_imag * gain_real
    calibrated = jnp.stack([cal_real, cal_imag], axis=4).astype(jnp.bfloat16)
    row_count = n_out * chan_count * UPCH
    flat = calibrated.reshape(row_count * CYL, 2 * NS)
    partial_value = jnp.dot(flat, beam_table, preferred_element_type=jnp.float32)
    partial_value = partial_value.reshape(row_count, CYL, 2, NS)
    beam_real = partial_value[:, :, 0, :]
    beam_imag = partial_value[:, :, 1, :]
    form_real = jnp.einsum("ec,rcn->ren", cyl_cos, beam_real, precision=highest) + jnp.einsum(
        "ec,rcn->ren", cyl_sin, beam_imag, precision=highest
    )
    form_imag = jnp.einsum("ec,rcn->ren", cyl_cos, beam_imag, precision=highest) - jnp.einsum(
        "ec,rcn->ren", cyl_sin, beam_real, precision=highest
    )
    powers = (form_real * form_real + form_imag * form_imag).astype(jnp.bfloat16)
    return powers.reshape(n_out, chan_count * UPCH, CYL * NS)


def slot_columns(owner_table, keep_flags, n_owner, most_sets):
    count = owner_table.shape[0]
    order = jnp.arange(count, dtype=jnp.int32)
    same_owner = owner_table[:, None] == owner_table[None, :]
    earlier = order[None, :] < order[:, None]
    set_rank = jnp.sum(jnp.logical_and(same_owner, earlier).astype(jnp.int32), axis=1)
    slot_index = owner_table * most_sets + set_rank
    places = jnp.arange(n_owner * most_sets, dtype=jnp.int32)
    matches = (slot_index[None, :] == places[:, None]).astype(jnp.int32)
    filled = jnp.sum(matches, axis=1)
    set_of = jnp.sum(matches * order[None, :], axis=1)
    within = jnp.arange(SET_BEAMS, dtype=jnp.int32)
    beam_index = (set_of[:, None] * SET_BEAMS + within[None, :]).reshape(-1)
    kept = jnp.take(keep_flags, beam_index).reshape(-1, SET_BEAMS)
    column_mask = (filled[:, None] * kept).reshape(-1)
    return (beam_index, column_mask)


def per_device(voltages, feed_gains, owner_table, keep_flags):
    samples = voltages[0]
    chan_count = samples.shape[0]
    frame_count = samples.shape[1] // UPCH
    frames = samples.reshape(chan_count, frame_count, UPCH, CYL, 2, NS)
    gain_pol = feed_gains[:, 0]
    history = TAPS - 1
    tail_frames = frames[:, frame_count - history :]
    before = shifted(tail_frames, "tm", 1)
    joined = jnp.concatenate([before, frames], axis=1)
    powers = power_frames(joined, gain_pol, frame_count)
    n_owner = lax.axis_size("freq")
    most_sets = 2 * owner_table.shape[0] // n_owner
    beam_index, column_mask = slot_columns(owner_table, keep_flags, n_owner, most_sets)
    mask_values = column_mask.astype(jnp.bfloat16)[None, None, :]
    summed = (
        lax.psum_scatter(powers, "pol", scatter_dimension=0, tiled=True)
        .astype(jnp.float32)
        .astype(jnp.bfloat16)
    )
    outgoing = jnp.take(summed, beam_index, axis=2) * mask_values
    return lax.all_to_all(outgoing, "freq", split_axis=2, concat_axis=1, tiled=True)


def solution(mesh):
    return jax.shard_map(
        per_device,
        mesh=mesh,
        in_specs=(
            P("pol", ("grp", "freq"), "tm", None, None, None),
            P(("grp", "freq"), "pol", None, None, None),
            P(),
            P(),
        ),
        out_specs=P(("grp", "tm", "pol"), None, "freq"),
        check_vma=False,
    )
```

profile of v0, /device:TPU:0, one launch (start us, length us, event | category | flops | bytes accessed | tf_op | source)
XLA Modules:
  0.0 210.3 jit_solution(8894756028634160894)
XLA Ops:
  6.5 0.0 copy-start
  6.5 2.0 copy.21
  8.6 0.0 copy-start.1
  8.6 0.1 slice.172
  8.7 1.1 copy.53
  9.7 5.8 %collective-permute-start = (bf16[1,15,16,4,2,256]{5,2,3,1,4,0:T(8,128)(2,1)}, bf16[1,15,16,4,2,256]{5,2,3,1,4,0:T(8,128)(2,1)}, u32[]{:S(2)}, u32[]{:S(2)}) collective-permute-start(bf16[1,15,16,4,2,256]{5,2,3,1,4,0:T(8,128)(2,1)} %copy.53), channel_id=1, source_target_pairs={{0,2},{1,3},{4,6},{5,7},{8,10},{9,11},{12,14},{13,15},{16,18},{17,... | collective-permute-start | bytes 2949128 | tf_op jit(solution)/shard_map/ppermute | solution.py:16
  15.6 0.6 multiply_reduce_fusion
  16.2 1.0 fusion.33
  17.8 0.1 broadcast_divide_fusion
  17.8 1.1 negate_convert_fusion
  19.0 0.1 fusion.116
  19.1 0.0 copy-done.1
  19.1 16.8 %collective-permute-done = bf16[1,15,16,4,2,256]{5,2,3,1,4,0:T(8,128)(2,1)} collective-permute-done((bf16[1,15,16,4,2,256]{5,2,3,1,4,0:T(8,128)(2,1)}, bf16[1,15,16,4,2,256]{5,2,3,1,4,0:T(8,128)(2,1)}, u32[]{:S(2)}, u32[]{:S(2)}) %collective-permute-start) | collective-permute-done | bytes 983072 | tf_op jit(solution)/shard_map/ppermute | solution.py:16
  35.9 1.3 constant_dynamic-update-slice_fusion.1
  37.2 0.3 constant_dynamic-update-slice_fusion
  37.5 8.6 %multiply_add_fusion = f32[1,32,16,4,2,256]{5,2,3,1,4,0:T(8,128)S(1)} fusion(bf16[1,47,16,4,2,256]{5,2,3,1,4,0:T(8,128)(2,1)S(1)} %constant_dynamic-update-slice_fusion, f32[16]{0:T(128)S(1)} %get-tuple-element.16, f32[16]{0:T(128)S(1)} %get-tuple-element.17, f32[16]{0:T(128)S(1)} %get-tuple-element.18, f32[16]{0:T(128)S(1)} %get-tuple-element.19, ...), kind=kLoop, calls=%fused_computation.3 | loop fusion | flops 49283072 | bytes 37749760 | tf_op jit(solution)/shard_map/add | solution.py:65
  46.1 2.0 fusion.6
  48.1 1.9 fusion.9
  50.0 2.0 fusion.21
  52.0 2.6 %fusion.26 = (bf16[32,1,16,4,1,256]{5,2,3,0,4,1:T(8,128)(2,1)S(1)}, bf16[32,1,16,4,1,256]{5,2,3,0,4,1:T(8,128)(2,1)S(1)}) fusion(f32[32,4,256,16]{2,3,1,0:T(8,128)S(1)} %fusion.21, f32[4,256]{1,0:T(4,128)S(1)} %get-tuple-element.33, f32[4,256]{1,0:T(4,128)S(1)} %get-tuple-element.34, f32[32,4,256,16]{2,3,1,0:T(8,128)S(1)} %fusion.6, ...), kind=kOutput, calls=%fused_computation.36 | convolution fusion | flops 105385472 | bytes 8396800 | tf_op jit(solution)/shard_map/qk,cmkxn->mcqxn/dot_general | solution.py:71
  54.7 0.2 pad_maximum_fusion
  54.9 4.8 %copy.25 = bf16[32,1,16,4,2,256]{5,4,2,0,3,1:T(2,128)(2,1)} copy(bf16[32,1,16,4,2,256]{5,2,3,0,4,1:T(8,128)(2,1)S(1)} %pad_maximum_fusion) | data formatting | bytes 4194304 | tf_op jit(solution)/shard_map/stack | solution.py:78
  59.7 3.2 %reshape.273 = bf16[512,4,512,1]{2,0,1,3:T(8,128)(2,1)S(1)} reshape(bf16[32,1,16,4,2,256]{5,4,2,0,3,1:T(2,128)(2,1)} %copy.25) | data formatting | bytes 4194304 | tf_op jit(solution)/shard_map/convert_element_type | solution.py:78
  62.8 1.3 fusion
  64.1 0.3 slice_bitcast_fusion.1
  64.4 4.4 %fusion.10 = f32[512,256,4]{1,2,0:T(4,128)S(1)} fusion(f32[512,4,256]{2,0,1:T(8,128)S(1)} %get-tuple-element.12), kind=kOutput, calls=%fused_computation.24 | convolution fusion | flops 25166064 | bytes 4194304 | tf_op jit(solution)/shard_map/ec,rcn->ren/dot_general | solution.py:88
  68.8 4.4 %fusion.12 = f32[512,256,4]{1,2,0:T(4,128)S(1)} fusion(f32[512,4,256]{2,0,1:T(8,128)S(1)} %get-tuple-element.12), kind=kOutput, calls=%fused_computation.26 | convolution fusion | flops 25166064 | bytes 4194304 | tf_op jit(solution)/shard_map/ec,rcn->ren/dot_general | solution.py:85
  73.2 4.4 %fusion.14 = f32[512,256,4]{1,2,0:T(4,128)S(1)} fusion(f32[512,4,256]{2,0,1:T(8,128)S(1)} %get-tuple-element.11), kind=kOutput, calls=%fused_computation.28 | convolution fusion | flops 25166064 | bytes 4194304 | tf_op jit(solution)/shard_map/ec,rcn->ren/dot_general | solution.py:88
  77.6 5.5 %fusion.22 = bf16[512,4,256]{2,1,0:T(4,128)(2,1)S(1)} fusion(f32[512,256,4]{1,2,0:T(4,128)S(1)} %fusion.10, f32[512,256,4]{1,2,0:T(4,128)S(1)} %fusion.14, f32[512,256,4]{1,2,0:T(4,128)S(1)} %fusion.12, f32[512,4,256]{2,0,1:T(8,128)S(1)} %get-tuple-element.11), kind=kOutput, calls=%fused_computation.34 | convolution fusion | flops 28311792 | bytes 9437184 | tf_op jit(solution)/shard_map/ec,rcn->ren/dot_general | solution.py:85
  83.1 0.8 reshape.254
  83.9 12.3 %copy.30 = bf16[32,16,1024]{1,0,2:T(8,128)(2,1)} copy(bf16[32,16,1024]{2,1,0:T(8,128)(2,1)S(1)} %reshape.254) | data formatting | bytes 2097152 | tf_op jit(solution)/shard_map/reshape | solution.py:92
  96.2 0.0 reduce-scatter.2.cloned.1.call-update
  96.2 0.6 copy-done.2
  96.8 0.2 convert_reduce_fusion.1
  97.0 0.1 convert_reduce_fusion
  97.1 0.1 iota_add_fusion
  97.2 0.1 add.291
  97.3 0.1 add.250
  97.4 0.1 mul.504
  97.5 0.1 mul.505
  97.6 8.6 %gather_fusion.1 = s32[2048]{0:T(1024)S(1)} fusion(s32[1024]{0:T(1024)S(1)} %copy-done, s32[2048]{0:T(1024)S(1)} %broadcast_clamp_fusion), kind=kCustom, calls=%fused_computation.1 | custom fusion | bytes 24576 | tf_op jit(solution)/shard_map/jit(_take)/gather | solution.py:108
  106.2 8.6 %reduce-scatter.2.cloned.1.call-done = bf16[16,16,1024]{1,0,2:T(8,128)(2,1)} async-done(((bf16[32,16,1024]{1,0,2:T(8,128)(2,1)}), bf16[16,16,1024]{1,0,2:T(8,128)(2,1)}) %reduce-scatter.2.cloned.1.call-update) | async-done | bytes 524304 | tf_op jit(solution)/shard_map/reduce_scatter | solution.py:129
  114.8 18.4 %gather_fusion = bf16[2048,16,16]{2,1,0:T(8,128)(2,1)} fusion(bf16[16,16,1024]{1,0,2:T(8,128)(2,1)} %reduce-scatter.2.cloned.1.call-done, s32[2048]{0:T(1024)S(1)} %broadcast_clamp_fusion), kind=kCustom, calls=%fused_computation | custom fusion | bytes 2105344 | tf_op jit(solution)/shard_map/jit(_take)/gather | solution.py:133
  133.2 13.1 %fusion.117 = bf16[2048,16,16]{2,1,0:T(8,128)(2,1)} fusion(bf16[2048]{0:T(1024)(128)(2,1)S(1)} %get-tuple-element.7, bf16[2048,16,16]{2,1,0:T(8,128)(2,1)} %gather_fusion, pred[2048]{0:T(1024)(128)(4,1)S(1)} %get-tuple-element.8), kind=kLoop, calls=%fused_computation.161 | loop fusion | flops 1048576 | bytes 2103296
  146.3 10.2 %reshape.278 = bf16[4,2,65536]{2,1,0:T(2,128)(2,1)S(1)} reshape(bf16[2048,16,16]{2,1,0:T(8,128)(2,1)} %fusion.117) | data formatting | bytes 2097152
  156.6 30.8 %all_to_all.18 = bf16[4,2,65536]{2,1,0:T(2,128)(2,1)S(1)} all-to-all(bf16[4,2,65536]{2,1,0:T(2,128)(2,1)S(1)} %reshape.278), channel_id=1, replica_groups=mesh['grp'=2,'freq'=4,'tm'=2,'pol'=2] {'freq'}, dimensions={0} | all-to-all | bytes 2097152 | tf_op jit(solution)/shard_map/all_to_all | solution.py:134
  187.4 6.9 %reshape.279 = bf16[2048,16,16]{2,1,0:T(8,128)(2,1)} reshape(bf16[4,2,65536]{2,1,0:T(2,128)(2,1)S(1)} %all_to_all.18) | data formatting | bytes 2097152
  194.3 9.1 %copy.31 = bf16[16,4,16,512]{3,2,1,0:T(8,128)(2,1)} copy(bf16[16,4,16,512]{2,0,3,1:T(8,128)(2,1)} %bitcast.109) | data formatting | bytes 2097152 | tf_op jit(solution)/shard_map/all_to_all | solution.py:134
  (11 shorter events, 0.1 us)
Async XLA Ops:
  6.5 91.0 %copy-start = (s32[1024]{0:T(1024)S(1)}, s32[1024]{0:T(1024)}, u32[]{:S(2)}) copy-start(s32[1024]{0:T(1024)} %param.7) | copy-start | bytes 12292
  6.5 108.3 %reduce-scatter.2.cloned.1.call-start = ((), (), s32[]{:S(2)}) async-start(), calls=%async_computation.2 | async-start | bytes 12582912 | tf_op jit(solution)/shard_map/reduce_scatter | solution.py:129
  8.6 10.5 %copy-start.1 = (f32[1,1,4,2,256]{4,3,2,1,0:T(2,128)S(1)}, f32[1,1,4,2,256]{4,3,2,1,0:T(2,128)}, u32[]{:S(2)}) copy-start(f32[1,1,4,2,256]{4,3,2,1,0:T(2,128)} %param.5) | copy-start | bytes 24580
  9.7 26.2 %collective-permute-start = (bf16[1,15,16,4,2,256]{5,2,3,1,4,0:T(8,128)(2,1)}, bf16[1,15,16,4,2,256]{5,2,3,1,4,0:T(8,128)(2,1)}, u32[]{:S(2)}, u32[]{:S(2)}) collective-permute-start(bf16[1,15,16,4,2,256]{5,2,3,1,4,0:T(8,128)(2,1)} %copy.53), channel_id=1, source_target_pairs={{0,2},{1,3},{4,6},{5,7},{8,10},{9,11},{12,14},{13,15},{16,18},{17,... | collective-permute-start | bytes 2949128 | tf_op jit(solution)/shard_map/ppermute | solution.py:16
  96.2 0.7 copy-start.2
Sparse Core Ops, SparseCore 0:
  96.3 18.4 reduce-scatter.1
where the time goes:
time: 211 us; the launch traced here: 210 us
  local copies, waits for them, and re-layouts  80.3 us (38%)
  blocking collectives  30.8 us (15%)
  matrix products  28.5 us (14%)
  waiting for transfers between devices  25.5 us (12%)
  other arithmetic  25.1 us (12%)
  between operations  14.3 us (7%)
  starting transfers between devices  5.82 us (3%)
    all_to_all x1, blocking collectives, per_device(): lax.all_to_all(outgoing, 'freq', split_axis=2, concat_axis=1, tiled=True)  30.8 us
    unnamed x12, local copies, waits for them, and re-layouts  22.2 us
    gather x1, local copies, waits for them, and re-layouts, per_device(): outgoing = jnp.take(summed, beam_index, axis=2) * mask_values  18.4 us
    ppermute x1, waiting for transfers between devices, shifted(): return lax.ppermute(block, axis, route)  16.8 us
    unnamed x1, other arithmetic  13.1 us
    reshape x2, local copies, waits for them, and re-layouts, power_frames(): return powers.reshape(n_out, chan_count * UPCH, CYL * NS)  13 us
    all_to_all x1, local copies, waits for them, and re-layouts, per_device(): lax.all_to_all(outgoing, 'freq', split_axis=2, concat_axis=1, tiled=True)  9.1 us
    reduce_scatter x1, waiting for transfers between devices, per_device(): lax.psum_scatter(powers, 'pol', scatter_dimension=0, tiled=True)  8.64 us
  transfers between devices with their start and end apart: 2, of which 2 were waited for; matrix products, arithmetic and copies ran while one was open for 6% of the time, Pallas kernels for 0%

commit v1 on v0

v1 whole, which is shorter than its diff:
```python
import functools

import jax
import jax.numpy as jnp
import numpy as np
from jax import lax
from jax.experimental import pallas as pl
from jax.experimental.pallas import tpu as pltpu
from jax.sharding import PartitionSpec as P

NS = 256
CYL = 4
UPCH = 16
TAPS = 16
SET_BEAMS = 16
BLOCK = 8
ROWS = 2 * UPCH


def window_taps():
    span = TAPS * UPCH
    steps = np.arange(span, dtype=np.float64)
    weights = np.sinc((steps - (span - 1) / 2.0) / UPCH) * np.sin(np.pi * (steps + 0.5) / span) ** 2
    return weights / np.sqrt(np.sum(weights * weights))


def filter_matrix():
    weights = window_taps()
    fine = np.arange(UPCH)
    sample = np.arange(TAPS * UPCH)
    phase = 2.0 * np.pi * ((fine[:, None] * sample[None, :]) % UPCH) / UPCH
    cosine = np.cos(phase) * weights
    sine = np.sin(phase) * weights
    table = np.zeros((2, BLOCK, UPCH, TAPS + BLOCK, UPCH, 2))
    for frame in range(BLOCK):
        taps = slice(frame + 1, frame + 1 + TAPS)
        cos_part = cosine.reshape(UPCH, TAPS, UPCH)
        sin_part = sine.reshape(UPCH, TAPS, UPCH)
        table[0, frame, :, taps, :, 0] = cos_part
        table[0, frame, :, taps, :, 1] = sin_part
        table[1, frame, :, taps, :, 0] = -sin_part
        table[1, frame, :, taps, :, 1] = cos_part
    table = table.reshape(2 * BLOCK * UPCH, (TAPS + BLOCK) * ROWS).astype(np.float32)
    high = table.astype(jnp.bfloat16)
    low = (table - high.astype(np.float32)).astype(jnp.bfloat16)
    return np.concatenate([high, low], axis=0)


def beam_matrix():
    rows = np.arange(NS)
    angle = 2.0 * np.pi * (rows[:, None] * rows[None, :] % NS) / NS
    scale = 1.0 / np.sqrt(NS)
    cosine = (np.cos(angle) * scale).astype(np.float32)
    sine = (np.sin(angle) * scale).astype(np.float32)
    upper = np.concatenate([cosine, -sine], axis=1)
    lower = np.concatenate([sine, cosine], axis=1)
    table = np.concatenate([upper, lower], axis=0).astype(jnp.bfloat16)
    return (table.astype(np.float32) * 0.5).astype(jnp.bfloat16)


def form_powers(parts, gain_ref, beam_ref, out_ref, out_start):
    half = BLOCK * UPCH
    beams = []
    for cyl in range(CYL):
        total = None
        for table, samples in parts(cyl):
            term = jnp.dot(table, samples, preferred_element_type=jnp.float32)
            total = term if total is None else total + term
        spec = total[: 2 * half] + total[2 * half :]
        real, imag = spec[:half], spec[half:]
        gain_real = gain_ref[cyl, 0:1, :]
        gain_imag = gain_ref[cyl, 1:2, :]
        cal_real = (real * gain_real - imag * gain_imag).astype(jnp.bfloat16)
        cal_imag = (real * gain_imag + imag * gain_real).astype(jnp.bfloat16)
        beam = jnp.dot(cal_real, beam_ref[:NS, :], preferred_element_type=jnp.float32)
        beam = beam + jnp.dot(cal_imag, beam_ref[NS:, :], preferred_element_type=jnp.float32)
        beams.append((beam[:, :NS], beam[:, NS:]))
    (r0, i0), (r1, i1), (r2, i2), (r3, i3) = beams
    pr, pi, mr, mi = r0 + r2, i0 + i2, r0 - r2, i0 - i2
    sr, si, dr, di = r1 + r3, i1 + i3, r1 - r3, i1 - i3
    formed = [(pr + sr, pi + si), (mr + di, mi - dr), (pr - sr, pi - si), (mr - di, mi + dr)]
    for element, (fr, fi) in enumerate(formed):
        power = (fr * fr + fi * fi).astype(jnp.bfloat16)
        out_ref[pl.ds(out_start, half), element * NS : (element + 1) * NS] = power


def columns(cyl):
    return slice(cyl * NS, (cyl + 1) * NS)


def local_kernel(blocks, first, filt_ref, x_ref, gain_ref, beam_ref, out_ref):
    depth = (TAPS + BLOCK) * ROWS

    def step(block, carry):
        start = pl.multiple_of((first - TAPS + block * BLOCK) * ROWS, 256)

        def parts(cyl):
            return [(filt_ref[...], x_ref[pl.ds(start, depth), columns(cyl)])]

        form_powers(parts, gain_ref, beam_ref, out_ref, pl.multiple_of(block * BLOCK * UPCH, 128))
        return carry

    lax.fori_loop(0, blocks, step, 0)


def near_kernel(filt_ref, near_ref, x_ref, gain_ref, beam_ref, out_ref):
    reach = BLOCK * ROWS

    def parts(cyl):
        return [
            (filt_ref[:, :reach], near_ref[:, columns(cyl)]),
            (filt_ref[:, reach:], x_ref[: 2 * reach, columns(cyl)]),
        ]

    form_powers(parts, gain_ref, beam_ref, out_ref, 0)


def far_kernel(filt_ref, edge_ref, far_ref, near_ref, x_ref, gain_ref, beam_ref, out_ref):
    reach = BLOCK * ROWS

    def parts(cyl):
        return [
            (filt_ref[:, reach : 2 * reach], near_ref[:, columns(cyl)]),
            (filt_ref[:, 2 * reach :], x_ref[:reach, columns(cyl)]),
            (edge_ref[...], far_ref[:, columns(cyl)]),
        ]

    form_powers(parts, gain_ref, beam_ref, out_ref, 0)


def place_table_kernel(most_sets, me_ref, owner_ref, out_ref):
    n_owner, beams, width = out_ref.shape
    sets = owner_ref.shape[1]
    owner = owner_ref[...].astype(jnp.float32)
    set_of = lax.broadcasted_iota(jnp.int32, (beams, sets), 0) // SET_BEAMS
    lane = lax.broadcasted_iota(jnp.int32, (beams, sets), 1)
    own = jnp.sum(jnp.where(set_of == lane, owner, 0.0), axis=1, keepdims=True)
    same = jnp.logical_and(owner == own, lane < set_of)
    rank = jnp.sum(jnp.where(same, 1.0, 0.0), axis=1, keepdims=True)
    within = lax.broadcasted_iota(jnp.int32, (beams, 1), 0) % SET_BEAMS
    column = (own * most_sets + rank).astype(jnp.int32) * SET_BEAMS + within
    place = lax.broadcasted_iota(jnp.int32, (beams, width), 1)
    for k in range(n_owner):
        owner_k = lax.rem(me_ref[0] + k, n_owner)
        hit = (column - owner_k * width) == place
        out_ref[k] = jnp.where(hit, 1.0, 0.0).astype(jnp.bfloat16)


def place_kernel(mine_ref, other_ref, keep_ref, table_ref, *out_refs):
    total = mine_ref[...].astype(jnp.float32) + other_ref[...].astype(jnp.float32)
    total = (total * keep_ref[...].astype(jnp.float32)).astype(jnp.bfloat16)
    for k, out_ref in enumerate(out_refs):
        placed = jnp.dot(total, table_ref[k], preferred_element_type=jnp.float32)
        out_ref[...] = placed.astype(jnp.bfloat16)


def gather_kernel(n_owner, where_ref, *refs):
    late, near, far, out_ref = refs[:n_owner], refs[n_owner : 2 * n_owner], refs[2 * n_owner : -1], refs[-1]
    me = where_ref[0]

    def copy(block, frame, k):
        source = lax.rem(me + n_owner - k, n_owner)
        rows = pl.ds(pl.multiple_of(source * UPCH, UPCH), UPCH)
        count = block.shape[0] // UPCH
        out_ref[frame : frame + count, rows, :] = block[...].reshape(count, UPCH, block.shape[1])

    @pl.when(where_ref[1] == 1)
    def _():
        for k in range(n_owner):
            copy(late[k], 0, k)

    @pl.when(where_ref[1] == 0)
    def _():
        for k in range(n_owner):
            copy(far[k], 0, k)
            copy(near[k], BLOCK, k)


VMEM = pl.BlockSpec(memory_space=pltpu.VMEM)
SMEM = pl.BlockSpec(memory_space=pltpu.SMEM)


def call(body, out_shape, n_in, flops, nbytes, scalars=0):
    many = isinstance(out_shape, (list, tuple))
    return pl.pallas_call(
        body,
        out_shape=out_shape,
        in_specs=[SMEM] * scalars + [VMEM] * n_in,
        out_specs=[VMEM] * len(out_shape) if many else VMEM,
        cost_estimate=pl.CostEstimate(flops=flops, bytes_accessed=nbytes, transcendentals=0),
        compiler_params=pltpu.CompilerParams(vmem_limit_bytes=40 << 20),
    )


def per_device(voltages, feed_gains, owner_table, keep_flags):
    samples = voltages[0, 0]
    gain = feed_gains[0, 0]
    frame_count = samples.shape[0] // UPCH
    kept = frame_count // 2
    assert voltages.shape[1] == 1 and kept == 2 * BLOCK and kept >= TAPS
    n_owner = lax.axis_size("freq")
    n_tm = lax.axis_size("tm")
    me = lax.axis_index("freq")
    pol = lax.axis_index("pol")
    most_sets = 2 * owner_table.shape[0] // n_owner
    beams = keep_flags.shape[0]
    width = most_sets * SET_BEAMS
    bf16 = jnp.bfloat16
    filt = jnp.asarray(filter_matrix())
    edge = jnp.asarray(filter_matrix()[:, ROWS : BLOCK * ROWS])
    beam_table = jnp.asarray(beam_matrix())

    def rows_of(part):
        return part.transpose(0, 2, 1, 3).reshape(part.shape[0] * 2, CYL * NS)

    def ahead(part):
        return lax.ppermute(part, "tm", [(i, i + 1) for i in range(n_tm - 1)])

    length = samples.shape[0]
    near_at = length - BLOCK * UPCH
    far_at = length - (TAPS - 1) * UPCH
    near = ahead(rows_of(samples[near_at:]))
    far = ahead(rows_of(samples[far_at:near_at]))
    x = rows_of(samples)

    def powers(body, frames, *args):
        rows = frames * UPCH
        flops = frames // BLOCK * 2 * 512 * 1024 * 1024
        return call(body, jax.ShapeDtypeStruct((rows, CYL * NS), bf16), len(args), flops, 3 << 20)(*args)

    def swap(block, source):
        return lax.ppermute(block, "pol", [(source, 1 - source)])

    where = jnp.stack([me, pol]).astype(jnp.int32)
    table = call(
        functools.partial(place_table_kernel, most_sets),
        jax.ShapeDtypeStruct((n_owner, beams, width), bf16),
        1,
        1 << 24,
        4 << 20,
        scalars=1,
    )(where, owner_table.reshape(1, -1))
    keep = keep_flags.reshape(1, -1)

    def regroup(mine, target):
        other = swap(mine, 1 - target)
        rows = mine.shape[0]
        shape = jax.ShapeDtypeStruct((rows, width), bf16)
        blocks = call(place_kernel, [shape] * n_owner, 4, 2 * rows * beams * beams * 2, 6 << 20)(
            mine, other, keep, table
        )
        got = [blocks[0]]
        for k in range(1, n_owner):
            route = [(i * 2 + target, (i + k) % n_owner * 2 + target) for i in range(n_owner)]
            got.append(lax.ppermute(blocks[k], ("freq", "pol"), route))
        return got

    late_powers = powers(functools.partial(local_kernel, kept // BLOCK, kept), kept, filt, x, gain, beam_table)
    late = regroup(late_powers, 1)
    near_powers = powers(near_kernel, BLOCK, filt, near, x, gain, beam_table)
    early_near = regroup(near_powers, 0)
    far_powers = powers(far_kernel, BLOCK, filt, edge, far, near, x, gain, beam_table)
    early_far = regroup(far_powers, 0)
    out_shape = jax.ShapeDtypeStruct((kept, n_owner * UPCH, width), bf16)
    return call(functools.partial(gather_kernel, n_owner), out_shape, 3 * n_owner, 0, 3 << 20, scalars=1)(
        where, *late, *early_near, *early_far
    )


def solution(mesh):
    return jax.shard_map(
        per_device,
        mesh=mesh,
        in_specs=(
            P("pol", ("grp", "freq"), "tm", None, None, None),
            P(("grp", "freq"), "pol", None, None, None),
            P(),
            P(),
        ),
        out_specs=P(("grp", "tm", "pol"), None, "freq"),
        check_vma=False,
    )
```

time: 211 us -> 73.1 us (0.35)
  local copies, waits for them, and re-layouts: 80.3 us -> 6.37 us
  blocking collectives: 30.8 us -> 0 us
  starting transfers between devices: 5.82 us -> 35.4 us
  matrix products: 28.5 us -> 0 us
  other arithmetic: 25.1 us -> 0.07 us
  Pallas kernels: 0 us -> 21.3 us
  waiting for transfers between devices: 25.5 us -> 8.37 us
  between operations: 14.3 us -> 0.32 us
    all_to_all x1 -> x0, blocking collectives: 30.8 us -> none  [per_device(): lax.all_to_all(outgoing, 'freq', split_axis=2, concat_axis=1, tiled=True)]
    ppermute x1 -> x14, starting transfers between devices: 5.82 us -> 35.4 us  [the longest x9 22.8 us: regroup(): got.append(lax.ppermute(blocks[k], ('freq', 'pol'), route))]
    dot_general x9 -> x0, matrix products: 28.5 us -> none  [the longest x1 5.49 us: power_frames(): jnp.einsum('ec,rcn->ren', cyl_cos, beam_real, precision=highest)]
    gather x2 -> x0, local copies, waits for them, and re-layouts: 26.9 us -> none  [the longest x1 18.4 us: per_device(): outgoing = jnp.take(summed, beam_index, axis=2) * mask_values]
    pallas_call x0 -> x8, Pallas kernels: none -> 21.3 us  [the longest x3 13.9 us: powers(): call(body, jax.ShapeDtypeStruct((rows, CYL * NS), bf16), len(args), flops...]
    unnamed x12 -> x17, local copies, waits for them, and re-layouts: 22.2 us -> 3.06 us
    unnamed x1 -> x0, other arithmetic: 13.1 us -> none
    reshape x2 -> x0, local copies, waits for them, and re-layouts: 13 us -> none  [power_frames(): return powers.reshape(n_out, chan_count * UPCH, CYL * NS)]
  transfers between devices with their start and end apart: 2 -> 14, of which waited for: 2 -> 3; matrix products, arithmetic and copies ran while one was open for 6% -> 4% of each run, Pallas kernels for 0% -> 27%
where the time goes in v1:
time: 73.1 us; the launch traced here: 71.9 us
  starting transfers between devices  35.4 us (48%)
  Pallas kernels  21.3 us (29%)
  waiting for transfers between devices  8.37 us (11%)
  local copies, waits for them, and re-layouts  6.37 us (9%)
    ppermute x9, starting transfers between devices, regroup(): got.append(lax.ppermute(blocks[k], ('freq', 'pol'), route))  22.8 us
    pallas_call x3, Pallas kernels, powers(): call(body, jax.ShapeDtypeStruct((rows, CYL * NS), bf16), len(args), flops...  13.9 us
    ppermute x2, starting transfers between devices, ahead(): return lax.ppermute(part, 'tm', [(i, i + 1) for i in range(n_tm - 1)])  7.73 us
    ppermute x3, starting transfers between devices, swap(): return lax.ppermute(block, 'pol', [(source, 1 - source)])  4.84 us
    ppermute x9, waiting for transfers between devices, regroup(): got.append(lax.ppermute(blocks[k], ('freq', 'pol'), route))  4.21 us
    ppermute x2, waiting for transfers between devices, ahead(): return lax.ppermute(part, 'tm', [(i, i + 1) for i in range(n_tm - 1)])  4.15 us
    pallas_call x3, Pallas kernels, regroup(): call(place_kernel, [shape] * n_owner, 4, 2 * rows * beams * beams * 2, 6...  4 us
    transpose x5, local copies, waits for them, and re-layouts, rows_of(): return part.transpose(0, 2, 1, 3).reshape(part.shape[0] * 2, CYL * NS)  3.31 us
  transfers between devices with their start and end apart: 14, of which 3 were waited for; matrix products, arithmetic and copies ran while one was open for 4% of the time, Pallas kernels for 27%

profile of v1, /device:TPU:0, one launch (start us, length us, event | category | flops | bytes accessed | tf_op | source)
XLA Modules:
  0.0 71.9 jit_solution(1396771966185489374)
XLA Ops:
  0.0 1.5 %slice_bitcast_fusion.1 = bf16[112,2,4,256]{3,1,2,0:T(2,128)(2,1)S(1)} fusion(bf16[1,1,512,4,2,256]{5,4,3,2,1,0:T(2,128)(2,1)} %param.7), kind=kLoop, calls=%fused_computation.1 | loop fusion | bytes 917504 | tf_op jit(solution)/shard_map/transpose | solution.py:214
  1.5 0.2 copy.10
  1.7 0.9 %copy.13 = bf16[28,8,4,256]{3,1,2,0:T(8,128)(2,1)} copy(bf16[28,8,4,256]{3,2,1,0:T(4,128)(2,1)S(1)} %bitcast.38) | data formatting | bytes 917504
  2.6 5.6 %collective-permute-start.9 = (bf16[224,1024]{1,0:T(8,128)(2,1)}, bf16[224,1024]{1,0:T(8,128)(2,1)}, u32[]{:S(2)}, u32[]{:S(2)}) collective-permute-start(bf16[224,1024]{1,0:T(8,128)(2,1)} %bitcast.22), channel_id=1, source_target_pairs={{0,2},{1,3},{4,6},{5,7},{8,10},{9,11},{12,14},{13,15},{16,18},{17,... | collective-permute-start | bytes 1376264 | tf_op jit(solution)/shard_map/ppermute | solution.py:217
  8.2 0.4 slice_bitcast_fusion
  8.6 0.2 copy.9
  8.8 0.9 %copy.12 = bf16[32,8,4,256]{3,1,2,0:T(8,128)(2,1)} copy(bf16[32,8,4,256]{3,2,1,0:T(4,128)(2,1)S(1)} %bitcast.37) | data formatting | bytes 1048576
  9.7 2.1 %collective-permute-start.4 = (bf16[256,1024]{1,0:T(8,128)(2,1)}, bf16[256,1024]{1,0:T(8,128)(2,1)}, u32[]{:S(2)}, u32[]{:S(2)}) collective-permute-start(bf16[256,1024]{1,0:T(8,128)(2,1)} %bitcast.19), channel_id=1, source_target_pairs={{0,2},{1,3},{4,6},{5,7},{8,10},{9,11},{12,14},{13,15},{16,18},{17,... | collective-permute-start | bytes 1572872 | tf_op jit(solution)/shard_map/ppermute | solution.py:217
  11.8 1.1 %copy.8 = bf16[512,2,4,256]{3,2,1,0:T(4,128)(2,1)S(1)} copy(bf16[512,2,4,256]{3,1,2,0:T(2,128)(2,1)S(1)} %bitcast.36) | data formatting | bytes 4194304 | tf_op jit(solution)/shard_map/transpose | solution.py:214
  12.9 0.0 copy-start
  12.9 0.0 copy-start.1
  12.9 0.0 copy-start.4
  12.9 0.5 copy.11
  13.4 0.6 copy-done
  14.0 0.1 copy-done.1
  14.1 6.2 %shard_map.73.mine_ref = bf16[256,1024]{1,0:T(8,128)(2,1)} custom-call(bf16[512,768]{1,0:T(8,128)(2,1)S(1)} %copy-done, bf16[1024,1024]{1,0:T(8,128)(2,1)S(1)} %bitcast.25, f32[4,2,256]{2,1,0:T(2,128)S(1)} %bitcast.31, bf16[512,512]{1,0:T(8,128)(2,1)S(1)} %copy-done.1), custom_call_target="tpu_custom_call" | custom-call | flops 2147483648 | bytes 3145728 | tf_op jit(solution)/shard_map/pallas_call | solution.py:229
  20.4 2.3 %collective-permute-start = (bf16[256,1024]{1,0:T(8,128)(2,1)}, bf16[256,1024]{1,0:T(8,128)(2,1)}, u32[]{:S(2)}, u32[]{:S(2)}) collective-permute-start(bf16[256,1024]{1,0:T(8,128)(2,1)} %shard_map.73.mine_ref), channel_id=1, source_target_pairs={{0,1},{2,3},{4,5},{6,7},{8,9},{10,11},{12,13},{14,15},{16,17},{18,... | collective-permute-start | bytes 1572872 | tf_op jit(solution)/shard_map/ppermute | solution.py:232
  22.6 0.1 pad_add_fusion.me_ref.where_ref
  22.7 1.8 %shard_map.74.table_ref = bf16[4,1024,512]{2,1,0:T(8,128)(2,1)S(1)} custom-call(s32[2]{0:T(128)S(1)} %pad_add_fusion.me_ref.where_ref, s32[1,64]{1,0:T(1,128)S(1)} %bitcast.34), custom_call_target="tpu_custom_call" | custom-call | flops 16777216 | bytes 4194304 | tf_op jit(solution)/shard_map/pallas_call | solution.py:235
  24.6 0.0 copy-start.2
  24.6 4.2 %collective-permute-done.4.near_ref = bf16[256,1024]{1,0:T(8,128)(2,1)} collective-permute-done((bf16[256,1024]{1,0:T(8,128)(2,1)}, bf16[256,1024]{1,0:T(8,128)(2,1)}, u32[]{:S(2)}, u32[]{:S(2)}) %collective-permute-start.4) | collective-permute-done | bytes 524320 | tf_op jit(solution)/shard_map/ppermute | solution.py:217
  28.7 3.8 %shard_map.76.mine_ref = bf16[128,1024]{1,0:T(8,128)(2,1)S(1)} custom-call(bf16[512,768]{1,0:T(8,128)(2,1)S(1)} %copy-done, bf16[256,1024]{1,0:T(8,128)(2,1)} %collective-permute-done.4.near_ref, bf16[1024,1024]{1,0:T(8,128)(2,1)S(1)} %bitcast.26, f32[4,2,256]{2,1,0:T(2,128)S(1)} %bitcast.32, bf16[512,512]{1,0:T(8,128)(2,1)S(1)} %copy-done.1), custom_call_target="tpu_custom_call" | custom-call | flops 1073741824 | bytes 3145728 | tf_op jit(solution)/shard_map/pallas_call | solution.py:229
  32.5 0.0 copy-start.3
  32.5 1.3 %collective-permute-start.5 = (bf16[128,1024]{1,0:T(8,128)(2,1)S(1)}, bf16[128,1024]{1,0:T(8,128)(2,1)S(1)}, u32[]{:S(2)}, u32[]{:S(2)}) collective-permute-start(bf16[128,1024]{1,0:T(8,128)(2,1)S(1)} %shard_map.76.mine_ref), channel_id=1, source_target_pairs={{1,0},{3,2},{5,4},{7,6},{9,8},{11,10},{13,12},{15,14},{17,16},{19,... | collective-permute-start | bytes 786440 | tf_op jit(solution)/shard_map/ppermute | solution.py:232
  33.8 0.0 collective-permute-done.9.far_ref
  33.8 3.9 %shard_map.78.mine_ref = bf16[128,1024]{1,0:T(8,128)(2,1)S(1)} custom-call(bf16[512,768]{1,0:T(8,128)(2,1)S(1)} %copy-done, bf16[512,224]{1,0:T(8,128)(2,1)S(1)} %copy-done.2, bf16[224,1024]{1,0:T(8,128)(2,1)} %collective-permute-done.9.far_ref, bf16[256,1024]{1,0:T(8,128)(2,1)} %collective-permute-done.4.near_ref, bf16[1024,1024]{1,0:T(8,128)(2,1)S(1)} %bitcast.27, ...), custom_call_target="tpu_custom_call" | custom-call | flops 1073741824 | bytes 3145728 | tf_op jit(solution)/shard_map/pallas_call | solution.py:229
  37.8 1.3 %collective-permute-start.10 = (bf16[128,1024]{1,0:T(8,128)(2,1)S(1)}, bf16[128,1024]{1,0:T(8,128)(2,1)S(1)}, u32[]{:S(2)}, u32[]{:S(2)}) collective-permute-start(bf16[128,1024]{1,0:T(8,128)(2,1)S(1)} %shard_map.78.mine_ref), channel_id=1, source_target_pairs={{1,0},{3,2},{5,4},{7,6},{9,8},{11,10},{13,12},{15,14},{17,16},{19,... | collective-permute-start | bytes 786440 | tf_op jit(solution)/shard_map/ppermute | solution.py:232
  39.1 0.0 collective-permute-done.other_ref
  39.1 2.5 %shard_map.75 = (bf16[256,512]{1,0:T(8,128)(2,1)S(1)}, bf16[256,512]{1,0:T(8,128)(2,1)S(1)}, bf16[256,512]{1,0:T(8,128)(2,1)S(1)}, bf16[256,512]{1,0:T(8,128)(2,1)S(1)}) custom-call(bf16[256,1024]{1,0:T(8,128)(2,1)} %shard_map.73.mine_ref, bf16[256,1024]{1,0:T(8,128)(2,1)} %collective-permute-done.other_ref, s32[1,1024]{1,0:T(1,128)S(1)} %bitcast.28, ...), custom_call_target="tpu_custom_call" | custom-call | flops 1073741824 | bytes 6291456 | tf_op jit(solution)/shard_map/pallas_call | solution.py:249
  41.6 0.7 collective-permute-start.1
  42.3 0.7 collective-permute-start.2
  43.0 0.7 collective-permute-start.3
  43.6 0.0 collective-permute-done.5.other_ref
  43.7 0.7 %shard_map.77 = (bf16[128,512]{1,0:T(8,128)(2,1)S(1)}, bf16[128,512]{1,0:T(8,128)(2,1)S(1)}, bf16[128,512]{1,0:T(8,128)(2,1)S(1)}, bf16[128,512]{1,0:T(8,128)(2,1)S(1)}) custom-call(bf16[128,1024]{1,0:T(8,128)(2,1)S(1)} %shard_map.76.mine_ref, bf16[128,1024]{1,0:T(8,128)(2,1)S(1)} %collective-permute-done.5.other_ref, s32[1,1024]{1,0:T(1,128)S(1)} %bitcast.29, ...), custom_call_target="tpu_custom_call" | custom-call | flops 536870912 | bytes 6291456 | tf_op jit(solution)/shard_map/pallas_call | solution.py:249
  44.4 3.5 %collective-permute-start.6 = (bf16[128,512]{1,0:T(8,128)(2,1)S(1)}, bf16[128,512]{1,0:T(8,128)(2,1)S(1)}, u32[]{:S(2)}, u32[]{:S(2)}) collective-permute-start(bf16[128,512]{1,0:T(8,128)(2,1)S(1)} %get-tuple-element.22), channel_id=1, source_target_pairs={{0,4},{4,8},{8,12},{12,0},{2,6},{6,10},{10,14},{14,2},{16,20},{20,... | collective-permute-start | bytes 393224 | tf_op jit(solution)/shard_map/ppermute | solution.py:255
  47.9 0.0 collective-permute-done.10.other_ref
  47.9 4.5 %collective-permute-start.7 = (bf16[128,512]{1,0:T(8,128)(2,1)S(1)}, bf16[128,512]{1,0:T(8,128)(2,1)S(1)}, u32[]{:S(2)}, u32[]{:S(2)}) collective-permute-start(bf16[128,512]{1,0:T(8,128)(2,1)S(1)} %get-tuple-element.23), channel_id=1, source_target_pairs={{0,8},{4,12},{8,0},{12,4},{2,10},{6,14},{10,2},{14,6},{16,24},{20,... | collective-permute-start | bytes 393224 | tf_op jit(solution)/shard_map/ppermute | solution.py:255
  52.4 0.7 %shard_map.79 = (bf16[128,512]{1,0:T(8,128)(2,1)S(1)}, bf16[128,512]{1,0:T(8,128)(2,1)S(1)}, bf16[128,512]{1,0:T(8,128)(2,1)S(1)}, bf16[128,512]{1,0:T(8,128)(2,1)S(1)}) custom-call(bf16[128,1024]{1,0:T(8,128)(2,1)S(1)} %shard_map.78.mine_ref, bf16[128,1024]{1,0:T(8,128)(2,1)S(1)} %collective-permute-done.10.other_ref, s32[1,1024]{1,0:T(1,128)S(1)} %bitcast.30, ...), custom_call_target="tpu_custom_call" | custom-call | flops 536870912 | bytes 6291456 | tf_op jit(solution)/shard_map/pallas_call | solution.py:249
  53.2 0.0 collective-permute-done.1.refs_1_
  53.2 3.3 %collective-permute-start.8 = (bf16[128,512]{1,0:T(8,128)(2,1)S(1)}, bf16[128,512]{1,0:T(8,128)(2,1)S(1)}, u32[]{:S(2)}, u32[]{:S(2)}) collective-permute-start(bf16[128,512]{1,0:T(8,128)(2,1)S(1)} %get-tuple-element.24), channel_id=1, source_target_pairs={{0,12},{4,0},{8,4},{12,8},{2,14},{6,2},{10,6},{14,10},{16,28},{20,... | collective-permute-start | bytes 393224 | tf_op jit(solution)/shard_map/ppermute | solution.py:255
  56.5 2.6 %collective-permute-start.11 = (bf16[128,512]{1,0:T(8,128)(2,1)S(1)}, bf16[128,512]{1,0:T(8,128)(2,1)S(1)}, u32[]{:S(2)}, u32[]{:S(2)}) collective-permute-start(bf16[128,512]{1,0:T(8,128)(2,1)S(1)} %get-tuple-element.26), channel_id=1, source_target_pairs={{0,4},{4,8},{8,12},{12,0},{2,6},{6,10},{10,14},{14,2},{16,20},{20,... | collective-permute-start | bytes 393224 | tf_op jit(solution)/shard_map/ppermute | solution.py:255
  59.0 0.0 collective-permute-done.3.refs_3_
  59.0 2.2 %collective-permute-start.12 = (bf16[128,512]{1,0:T(8,128)(2,1)S(1)}, bf16[128,512]{1,0:T(8,128)(2,1)S(1)}, u32[]{:S(2)}, u32[]{:S(2)}) collective-permute-start(bf16[128,512]{1,0:T(8,128)(2,1)S(1)} %get-tuple-element.27), channel_id=1, source_target_pairs={{0,8},{4,12},{8,0},{12,4},{2,10},{6,14},{10,2},{14,6},{16,24},{20,... | collective-permute-start | bytes 393224 | tf_op jit(solution)/shard_map/ppermute | solution.py:255
  61.3 4.7 %collective-permute-start.13 = (bf16[128,512]{1,0:T(8,128)(2,1)S(1)}, bf16[128,512]{1,0:T(8,128)(2,1)S(1)}, u32[]{:S(2)}, u32[]{:S(2)}) collective-permute-start(bf16[128,512]{1,0:T(8,128)(2,1)S(1)} %get-tuple-element.28), channel_id=1, source_target_pairs={{0,12},{4,0},{8,4},{12,8},{2,14},{6,2},{10,6},{14,10},{16,28},{20,... | collective-permute-start | bytes 393224 | tf_op jit(solution)/shard_map/ppermute | solution.py:255
  66.1 0.0 collective-permute-done.11.refs_9_
  66.1 3.5 %collective-permute-done.12.refs_10_ = bf16[128,512]{1,0:T(8,128)(2,1)S(1)} collective-permute-done((bf16[128,512]{1,0:T(8,128)(2,1)S(1)}, bf16[128,512]{1,0:T(8,128)(2,1)S(1)}, u32[]{:S(2)}, u32[]{:S(2)}) %collective-permute-start.12) | collective-permute-done | bytes 131104 | tf_op jit(solution)/shard_map/ppermute | solution.py:255
  69.6 0.7 collective-permute-done.13.refs_11_
  70.3 1.6 %shard_map.80 = bf16[16,64,512]{2,1,0:T(8,128)(2,1)} custom-call(s32[2]{0:T(128)S(1)} %pad_add_fusion.me_ref.where_ref, bf16[256,512]{1,0:T(8,128)(2,1)S(1)} %get-tuple-element.17.refs_0_, bf16[256,512]{1,0:T(8,128)(2,1)S(1)} %collective-permute-done.1.refs_1_, bf16[256,512]{1,0:T(8,128)(2,1)S(1)} %collective-permute-done.2.refs_2_, ...), custom_call_target="tpu_custom_call" | custom-call | bytes 3145728 | tf_op jit(solution)/shard_map/pallas_call | solution.py:265
  (11 shorter events, 0.0 us)
Async XLA Ops:
  0.0 8.2 %copy-start.6 = (bf16[1,1,512,4,2,256]{5,4,3,2,1,0:T(2,128)(2,1)S(1)}, bf16[1,1,512,4,2,256]{5,4,3,2,1,0:T(2,128)(2,1)}, u32[]{:S(2)}) copy-start(bf16[1,1,512,4,2,256]{5,4,3,2,1,0:T(2,128)(2,1)} %param.7) | copy-start | bytes 6291460
  2.6 31.3 %collective-permute-start.9 = (bf16[224,1024]{1,0:T(8,128)(2,1)}, bf16[224,1024]{1,0:T(8,128)(2,1)}, u32[]{:S(2)}, u32[]{:S(2)}) collective-permute-start(bf16[224,1024]{1,0:T(8,128)(2,1)} %bitcast.22), channel_id=1, source_target_pairs={{0,2},{1,3},{4,6},{5,7},{8,10},{9,11},{12,14},{13,15},{16,18},{17,... | collective-permute-start | bytes 1376264 | tf_op jit(solution)/shard_map/ppermute | solution.py:217
  9.7 19.0 %collective-permute-start.4 = (bf16[256,1024]{1,0:T(8,128)(2,1)}, bf16[256,1024]{1,0:T(8,128)(2,1)}, u32[]{:S(2)}, u32[]{:S(2)}) collective-permute-start(bf16[256,1024]{1,0:T(8,128)(2,1)} %bitcast.19), channel_id=1, source_target_pairs={{0,2},{1,3},{4,6},{5,7},{8,10},{9,11},{12,14},{13,15},{16,18},{17,... | collective-permute-start | bytes 1572872 | tf_op jit(solution)/shard_map/ppermute | solution.py:217
  12.9 1.1 %copy-start = (bf16[512,768]{1,0:T(8,128)(2,1)S(1)}, bf16[512,768]{1,0:T(8,128)(2,1)}, u32[]{:S(2)}) copy-start(bf16[512,768]{1,0:T(8,128)(2,1)} %constant.15.clone.filt_ref) | copy-start | bytes 2359300
  12.9 1.3 %copy-start.1 = (bf16[512,512]{1,0:T(8,128)(2,1)S(1)}, bf16[512,512]{1,0:T(8,128)(2,1)}, u32[]{:S(2)}) copy-start(bf16[512,512]{1,0:T(8,128)(2,1)} %constant.17.clone.beam_ref) | copy-start | bytes 1572868
  12.9 1.3 %copy-start.4 = (f32[1,1,4,2,256]{4,3,2,1,0:T(2,128)S(1)}, f32[1,1,4,2,256]{4,3,2,1,0:T(2,128)}, u32[]{:S(2)}) copy-start(f32[1,1,4,2,256]{4,3,2,1,0:T(2,128)} %param.8) | copy-start | bytes 24580
  14.1 8.6 %copy-start.5 = (s32[64]{0:T(128)S(1)}, s32[64]{0:T(128)}, u32[]{:S(2)}) copy-start(s32[64]{0:T(128)} %param.9) | copy-start | bytes 772
  20.4 18.7 %collective-permute-start = (bf16[256,1024]{1,0:T(8,128)(2,1)}, bf16[256,1024]{1,0:T(8,128)(2,1)}, u32[]{:S(2)}, u32[]{:S(2)}) collective-permute-start(bf16[256,1024]{1,0:T(8,128)(2,1)} %shard_map.73.mine_ref), channel_id=1, source_target_pairs={{0,1},{2,3},{4,5},{6,7},{8,9},{10,11},{12,13},{14,15},{16,17},{18,... | collective-permute-start | bytes 1572872 | tf_op jit(solution)/shard_map/ppermute | solution.py:232
  24.6 9.3 %copy-start.2 = (bf16[512,224]{1,0:T(8,128)(2,1)S(1)}, bf16[512,224]{1,0:T(8,128)(2,1)}, u32[]{:S(2)}) copy-start(bf16[512,224]{1,0:T(8,128)(2,1)} %constant.16.clone.edge_ref) | copy-start | bytes 688132
  32.5 6.6 %copy-start.3 = (s32[1024]{0:T(1024)S(1)}, s32[1024]{0:T(1024)}, u32[]{:S(2)}) copy-start(s32[1024]{0:T(1024)} %param.10) | copy-start | bytes 12292
  32.5 11.1 %collective-permute-start.5 = (bf16[128,1024]{1,0:T(8,128)(2,1)S(1)}, bf16[128,1024]{1,0:T(8,128)(2,1)S(1)}, u32[]{:S(2)}, u32[]{:S(2)}) collective-permute-start(bf16[128,1024]{1,0:T(8,128)(2,1)S(1)} %shard_map.76.mine_ref), channel_id=1, source_target_pairs={{1,0},{3,2},{5,4},{7,6},{9,8},{11,10},{13,12},{15,14},{17,16},{19,... | collective-permute-start | bytes 786440 | tf_op jit(solution)/shard_map/ppermute | solution.py:232
  37.8 10.1 %collective-permute-start.10 = (bf16[128,1024]{1,0:T(8,128)(2,1)S(1)}, bf16[128,1024]{1,0:T(8,128)(2,1)S(1)}, u32[]{:S(2)}, u32[]{:S(2)}) collective-permute-start(bf16[128,1024]{1,0:T(8,128)(2,1)S(1)} %shard_map.78.mine_ref), channel_id=1, source_target_pairs={{1,0},{3,2},{5,4},{7,6},{9,8},{11,10},{13,12},{15,14},{17,16},{19,... | collective-permute-start | bytes 786440 | tf_op jit(solution)/shard_map/ppermute | solution.py:232
  41.6 11.6 %collective-permute-start.1 = (bf16[256,512]{1,0:T(8,128)(2,1)S(1)}, bf16[256,512]{1,0:T(8,128)(2,1)S(1)}, u32[]{:S(2)}, u32[]{:S(2)}) collective-permute-start(bf16[256,512]{1,0:T(8,128)(2,1)S(1)} %get-tuple-element.18), channel_id=1, source_target_pairs={{1,5},{5,9},{9,13},{13,1},{3,7},{7,11},{11,15},{15,3},{17,21},{21,... | collective-permute-start | bytes 786440 | tf_op jit(solution)/shard_map/ppermute | solution.py:255
  42.3 14.2 %collective-permute-start.2 = (bf16[256,512]{1,0:T(8,128)(2,1)S(1)}, bf16[256,512]{1,0:T(8,128)(2,1)S(1)}, u32[]{:S(2)}, u32[]{:S(2)}) collective-permute-start(bf16[256,512]{1,0:T(8,128)(2,1)S(1)} %get-tuple-element.19), channel_id=1, source_target_pairs={{1,9},{5,13},{9,1},{13,5},{3,11},{7,15},{11,3},{15,7},{17,25},{21,... | collective-permute-start | bytes 786440 | tf_op jit(solution)/shard_map/ppermute | solution.py:255
  43.0 16.1 %collective-permute-start.3 = (bf16[256,512]{1,0:T(8,128)(2,1)S(1)}, bf16[256,512]{1,0:T(8,128)(2,1)S(1)}, u32[]{:S(2)}, u32[]{:S(2)}) collective-permute-start(bf16[256,512]{1,0:T(8,128)(2,1)S(1)} %get-tuple-element.20), channel_id=1, source_target_pairs={{1,13},{5,1},{9,5},{13,9},{3,15},{7,3},{11,7},{15,11},{17,29},{21,... | collective-permute-start | bytes 786440 | tf_op jit(solution)/shard_map/ppermute | solution.py:255
  44.4 16.9 %collective-permute-start.6 = (bf16[128,512]{1,0:T(8,128)(2,1)S(1)}, bf16[128,512]{1,0:T(8,128)(2,1)S(1)}, u32[]{:S(2)}, u32[]{:S(2)}) collective-permute-start(bf16[128,512]{1,0:T(8,128)(2,1)S(1)} %get-tuple-element.22), channel_id=1, source_target_pairs={{0,4},{4,8},{8,12},{12,0},{2,6},{6,10},{10,14},{14,2},{16,20},{20,... | collective-permute-start | bytes 393224 | tf_op jit(solution)/shard_map/ppermute | solution.py:255
  47.9 18.2 %collective-permute-start.7 = (bf16[128,512]{1,0:T(8,128)(2,1)S(1)}, bf16[128,512]{1,0:T(8,128)(2,1)S(1)}, u32[]{:S(2)}, u32[]{:S(2)}) collective-permute-start(bf16[128,512]{1,0:T(8,128)(2,1)S(1)} %get-tuple-element.23), channel_id=1, source_target_pairs={{0,8},{4,12},{8,0},{12,4},{2,10},{6,14},{10,2},{14,6},{16,24},{20,... | collective-permute-start | bytes 393224 | tf_op jit(solution)/shard_map/ppermute | solution.py:255
  53.2 12.9 %collective-permute-start.8 = (bf16[128,512]{1,0:T(8,128)(2,1)S(1)}, bf16[128,512]{1,0:T(8,128)(2,1)S(1)}, u32[]{:S(2)}, u32[]{:S(2)}) collective-permute-start(bf16[128,512]{1,0:T(8,128)(2,1)S(1)} %get-tuple-element.24), channel_id=1, source_target_pairs={{0,12},{4,0},{8,4},{12,8},{2,14},{6,2},{10,6},{14,10},{16,28},{20,... | collective-permute-start | bytes 393224 | tf_op jit(solution)/shard_map/ppermute | solution.py:255
  56.5 9.6 %collective-permute-start.11 = (bf16[128,512]{1,0:T(8,128)(2,1)S(1)}, bf16[128,512]{1,0:T(8,128)(2,1)S(1)}, u32[]{:S(2)}, u32[]{:S(2)}) collective-permute-start(bf16[128,512]{1,0:T(8,128)(2,1)S(1)} %get-tuple-element.26), channel_id=1, source_target_pairs={{0,4},{4,8},{8,12},{12,0},{2,6},{6,10},{10,14},{14,2},{16,20},{20,... | collective-permute-start | bytes 393224 | tf_op jit(solution)/shard_map/ppermute | solution.py:255
  59.0 10.6 %collective-permute-start.12 = (bf16[128,512]{1,0:T(8,128)(2,1)S(1)}, bf16[128,512]{1,0:T(8,128)(2,1)S(1)}, u32[]{:S(2)}, u32[]{:S(2)}) collective-permute-start(bf16[128,512]{1,0:T(8,128)(2,1)S(1)} %get-tuple-element.27), channel_id=1, source_target_pairs={{0,8},{4,12},{8,0},{12,4},{2,10},{6,14},{10,2},{14,6},{16,24},{20,... | collective-permute-start | bytes 393224 | tf_op jit(solution)/shard_map/ppermute | solution.py:255
  61.3 9.0 %collective-permute-start.13 = (bf16[128,512]{1,0:T(8,128)(2,1)S(1)}, bf16[128,512]{1,0:T(8,128)(2,1)S(1)}, u32[]{:S(2)}, u32[]{:S(2)}) collective-permute-start(bf16[128,512]{1,0:T(8,128)(2,1)S(1)} %get-tuple-element.28), channel_id=1, source_target_pairs={{0,12},{4,0},{8,4},{12,8},{2,14},{6,2},{10,6},{14,10},{16,28},{20,... | collective-permute-start | bytes 393224 | tf_op jit(solution)/shard_map/ppermute | solution.py:255

commit v2 on v1

--- a/solution.py
+++ b/solution.py
@@ -8,12 +8,14 @@
 from jax.experimental.pallas import tpu as pltpu
 from jax.sharding import PartitionSpec as P
 
+
 NS = 256
 CYL = 4
 UPCH = 16
 TAPS = 16
 SET_BEAMS = 16
 BLOCK = 8
+LANES = 128
 ROWS = 2 * UPCH
 
 
@@ -55,12 +57,12 @@
     upper = np.concatenate([cosine, -sine], axis=1)
     lower = np.concatenate([sine, cosine], axis=1)
     table = np.concatenate([upper, lower], axis=0).astype(jnp.bfloat16)
+    table = table.reshape(2 * NS, 2, NS // LANES, LANES).transpose(0, 2, 1, 3).reshape(2 * NS, 2 * NS)
     return (table.astype(np.float32) * 0.5).astype(jnp.bfloat16)
 
 
-def form_powers(parts, gain_ref, beam_ref, out_ref, out_start):
+def form_powers(parts, gain_ref, beam_ref, out_ref, cal_ref, out_start):
     half = BLOCK * UPCH
-    beams = []
     for cyl in range(CYL):
         total = None
         for table, samples in parts(cyl):
@@ -70,25 +72,31 @@
         real, imag = spec[:half], spec[half:]
         gain_real = gain_ref[cyl, 0:1, :]
         gain_imag = gain_ref[cyl, 1:2, :]
-        cal_real = (real * gain_real - imag * gain_imag).astype(jnp.bfloat16)
-        cal_imag = (real * gain_imag + imag * gain_real).astype(jnp.bfloat16)
-        beam = jnp.dot(cal_real, beam_ref[:NS, :], preferred_element_type=jnp.float32)
-        beam = beam + jnp.dot(cal_imag, beam_ref[NS:, :], preferred_element_type=jnp.float32)
-        beams.append((beam[:, :NS], beam[:, NS:]))
-    (r0, i0), (r1, i1), (r2, i2), (r3, i3) = beams
-    pr, pi, mr, mi = r0 + r2, i0 + i2, r0 - r2, i0 - i2
-    sr, si, dr, di = r1 + r3, i1 + i3, r1 - r3, i1 - i3
-    formed = [(pr + sr, pi + si), (mr + di, mi - dr), (pr - sr, pi - si), (mr - di, mi + dr)]
-    for element, (fr, fi) in enumerate(formed):
-        power = (fr * fr + fi * fi).astype(jnp.bfloat16)
-        out_ref[pl.ds(out_start, half), element * NS : (element + 1) * NS] = power
+        rows = slice(cyl * half, (cyl + 1) * half)
+        cal_ref[rows, :NS] = (real * gain_real - imag * gain_imag).astype(jnp.bfloat16)
+        cal_ref[rows, NS:] = (real * gain_imag + imag * gain_real).astype(jnp.bfloat16)
+    for strip in range(NS // LANES):
+        beam = jnp.dot(
+            cal_ref[...],
+            beam_ref[:, strip * 2 * LANES : (strip + 1) * 2 * LANES],
+            preferred_element_type=jnp.float32,
+        )
+        beams = [beam[cyl * half : (cyl + 1) * half] for cyl in range(CYL)]
+        (r0, i0), (r1, i1), (r2, i2), (r3, i3) = [(b[:, :LANES], b[:, LANES:]) for b in beams]
+        pr, pi, mr, mi = r0 + r2, i0 + i2, r0 - r2, i0 - i2
+        sr, si, dr, di = r1 + r3, i1 + i3, r1 - r3, i1 - i3
+        formed = [(pr + sr, pi + si), (mr + di, mi - dr), (pr - sr, pi - si), (mr - di, mi + dr)]
+        for element, (fr, fi) in enumerate(formed):
+            power = (fr * fr + fi * fi).astype(jnp.bfloat16)
+            at = element * NS + strip * LANES
+            out_ref[pl.ds(out_start, half), at : at + LANES] = power
 
 
 def columns(cyl):
     return slice(cyl * NS, (cyl + 1) * NS)
 
 
-def local_kernel(blocks, first, filt_ref, x_ref, gain_ref, beam_ref, out_ref):
+def local_kernel(blocks, first, filt_ref, x_ref, gain_ref, beam_ref, out_ref, cal_ref):
     depth = (TAPS + BLOCK) * ROWS
 
     def step(block, carry):
@@ -97,13 +105,13 @@
         def parts(cyl):
             return [(filt_ref[...], x_ref[pl.ds(start, depth), columns(cyl)])]
 
-        form_powers(parts, gain_ref, beam_ref, out_ref, pl.multiple_of(block * BLOCK * UPCH, 128))
+        form_powers(parts, gain_ref, beam_ref, out_ref, cal_ref, pl.multiple_of(block * BLOCK * UPCH, 128))
         return carry
 
     lax.fori_loop(0, blocks, step, 0)
 
 
-def near_kernel(filt_ref, near_ref, x_ref, gain_ref, beam_ref, out_ref):
+def near_kernel(filt_ref, near_ref, x_ref, gain_ref, beam_ref, out_ref, cal_ref):
     reach = BLOCK * ROWS
 
     def parts(cyl):
@@ -112,10 +120,10 @@
             (filt_ref[:, reach:], x_ref[: 2 * reach, columns(cyl)]),
         ]
 
-    form_powers(parts, gain_ref, beam_ref, out_ref, 0)
-
-
-def far_kernel(filt_ref, edge_ref, far_ref, near_ref, x_ref, gain_ref, beam_ref, out_ref):
+    form_powers(parts, gain_ref, beam_ref, out_ref, cal_ref, 0)
+
+
+def far_kernel(filt_ref, edge_ref, far_ref, near_ref, x_ref, gain_ref, beam_ref, out_ref, cal_ref):
     reach = BLOCK * ROWS
 
     def parts(cyl):
@@ -125,7 +133,7 @@
             (edge_ref[...], far_ref[:, columns(cyl)]),
         ]
 
-    form_powers(parts, gain_ref, beam_ref, out_ref, 0)
+    form_powers(parts, gain_ref, beam_ref, out_ref, cal_ref, 0)
 
 
 def place_table_kernel(most_sets, me_ref, owner_ref, out_ref):
@@ -141,7 +149,7 @@
     column = (own * most_sets + rank).astype(jnp.int32) * SET_BEAMS + within
     place = lax.broadcasted_iota(jnp.int32, (beams, width), 1)
     for k in range(n_owner):
-        owner_k = lax.rem(me_ref[0] + k, n_owner)
+        owner_k = me_ref[0] ^ k
         hit = (column - owner_k * width) == place
         out_ref[k] = jnp.where(hit, 1.0, 0.0).astype(jnp.bfloat16)
 
@@ -159,7 +167,7 @@
     me = where_ref[0]
 
     def copy(block, frame, k):
-        source = lax.rem(me + n_owner - k, n_owner)
+        source = me ^ k
         rows = pl.ds(pl.multiple_of(source * UPCH, UPCH), UPCH)
         count = block.shape[0] // UPCH
         out_ref[frame : frame + count, rows, :] = block[...].reshape(count, UPCH, block.shape[1])
@@ -178,15 +186,22 @@
 
 VMEM = pl.BlockSpec(memory_space=pltpu.VMEM)
 SMEM = pl.BlockSpec(memory_space=pltpu.SMEM)
-
-
-def call(body, out_shape, n_in, flops, nbytes, scalars=0):
+ANY = pl.BlockSpec(memory_space=pl.ANY)
+
+
+def call(body, out_shape, n_in, flops, nbytes, scalars=0, after=0, scratch=()):
     many = isinstance(out_shape, (list, tuple))
+
+    def kernel(*refs):
+        seen = scalars + n_in
+        body(*refs[:seen], *refs[seen + after :])
+
     return pl.pallas_call(
-        body,
+        kernel,
         out_shape=out_shape,
-        in_specs=[SMEM] * scalars + [VMEM] * n_in,
+        in_specs=[SMEM] * scalars + [VMEM] * n_in + [ANY] * after,
         out_specs=[VMEM] * len(out_shape) if many else VMEM,
+        scratch_shapes=list(scratch),
         cost_estimate=pl.CostEstimate(flops=flops, bytes_accessed=nbytes, transcendentals=0),
         compiler_params=pltpu.CompilerParams(vmem_limit_bytes=40 << 20),
     )
@@ -197,8 +212,9 @@
     gain = feed_gains[0, 0]
     frame_count = samples.shape[0] // UPCH
     kept = frame_count // 2
+    n_owner = lax.axis_size("freq")
     assert voltages.shape[1] == 1 and kept == 2 * BLOCK and kept >= TAPS
-    n_owner = lax.axis_size("freq")
+    assert n_owner & (n_owner - 1) == 0
     n_tm = lax.axis_size("tm")
     me = lax.axis_index("freq")
     pol = lax.axis_index("pol")
@@ -210,39 +226,20 @@
     edge = jnp.asarray(filter_matrix()[:, ROWS : BLOCK * ROWS])
     beam_table = jnp.asarray(beam_matrix())
 
-    def rows_of(part):
-        return part.transpose(0, 2, 1, 3).reshape(part.shape[0] * 2, CYL * NS)
-
     def ahead(part):
         return lax.ppermute(part, "tm", [(i, i + 1) for i in range(n_tm - 1)])
 
-    length = samples.shape[0]
-    near_at = length - BLOCK * UPCH
-    far_at = length - (TAPS - 1) * UPCH
-    near = ahead(rows_of(samples[near_at:]))
-    far = ahead(rows_of(samples[far_at:near_at]))
-    x = rows_of(samples)
-
-    def powers(body, frames, *args):
+    def powers(body, frames, *args, after=()):
         rows = frames * UPCH
         flops = frames // BLOCK * 2 * 512 * 1024 * 1024
-        return call(body, jax.ShapeDtypeStruct((rows, CYL * NS), bf16), len(args), flops, 3 << 20)(*args)
+        shape = jax.ShapeDtypeStruct((rows, CYL * NS), bf16)
+        scratch = [pltpu.VMEM((CYL * BLOCK * UPCH, 2 * NS), bf16)]
+        return call(body, shape, len(args), flops, 3 << 20, after=len(after), scratch=scratch)(*args, *after)
 
     def swap(block, source):
         return lax.ppermute(block, "pol", [(source, 1 - source)])
 
-    where = jnp.stack([me, pol]).astype(jnp.int32)
-    table = call(
-        functools.partial(place_table_kernel, most_sets),
-        jax.ShapeDtypeStruct((n_owner, beams, width), bf16),
-        1,
-        1 << 24,
-        4 << 20,
-        scalars=1,
-    )(where, owner_table.reshape(1, -1))
-    keep = keep_flags.reshape(1, -1)
-
-    def regroup(mine, target):
+    def regroup(mine, target, table):
         other = swap(mine, 1 - target)
         rows = mine.shape[0]
         shape = jax.ShapeDtypeStruct((rows, width), bf16)
@@ -251,16 +248,39 @@
         )
         got = [blocks[0]]
         for k in range(1, n_owner):
-            route = [(i * 2 + target, (i + k) % n_owner * 2 + target) for i in range(n_owner)]
+            route = [(i * 2 + target, (i ^ k) * 2 + target) for i in range(n_owner)]
             got.append(lax.ppermute(blocks[k], ("freq", "pol"), route))
         return got
 
-    late_powers = powers(functools.partial(local_kernel, kept // BLOCK, kept), kept, filt, x, gain, beam_table)
-    late = regroup(late_powers, 1)
-    near_powers = powers(near_kernel, BLOCK, filt, near, x, gain, beam_table)
-    early_near = regroup(near_powers, 0)
-    far_powers = powers(far_kernel, BLOCK, filt, edge, far, near, x, gain, beam_table)
-    early_far = regroup(far_powers, 0)
+    where = jnp.stack([me, pol]).astype(jnp.int32)
+    keep = keep_flags.reshape(1, -1)
+    x = samples.transpose(0, 2, 1, 3).reshape(samples.shape[0] * 2, CYL * NS)
+    x = lax.optimization_barrier(x)
+    length = x.shape[0]
+    near_at = length - BLOCK * ROWS
+    far_at = length - (TAPS - 1) * ROWS
+    near = ahead(x[near_at:])
+    far = ahead(x[far_at:near_at])
+
+    late_powers = powers(
+        functools.partial(local_kernel, kept // BLOCK, kept), kept, filt, x, gain, beam_table
+    )
+    table = call(
+        functools.partial(place_table_kernel, most_sets),
+        jax.ShapeDtypeStruct((n_owner, beams, width), bf16),
+        1,
+        1 << 24,
+        4 << 20,
+        scalars=1,
+        after=1,
+    )(where, owner_table.reshape(1, -1), late_powers)
+    late = regroup(late_powers, 1, table)
+    near_powers = powers(near_kernel, BLOCK, filt, near, x, gain, beam_table, after=late[:1])
+    early_near = regroup(near_powers, 0, table)
+    far_powers = powers(
+        far_kernel, BLOCK, filt, edge, far, near, x, gain, beam_table, after=early_near[:1]
+    )
+    early_far = regroup(far_powers, 0, table)
     out_shape = jax.ShapeDtypeStruct((kept, n_owner * UPCH, width), bf16)
     return call(functools.partial(gather_kernel, n_owner), out_shape, 3 * n_owner, 0, 3 << 20, scalars=1)(
         where, *late, *early_near, *early_far

time: 73.1 us -> 73.4 us (level)
  waiting for transfers between devices: 8.37 us -> 15 us
  Pallas kernels: 21.3 us -> 16.2 us
  local copies, waits for them, and re-layouts: 6.37 us -> 5.56 us
    pallas_call x3, Pallas kernels: 13.9 us -> 8.75 us  [powers(): call(body, shape, len(args), flops, 3 << 20, after=len(after), scratch=sc...]
    ppermute x9, waiting for transfers between devices: 4.21 us -> 7.76 us  [regroup(): got.append(lax.ppermute(blocks[k], ('freq', 'pol'), route))]
    ppermute x3, waiting for transfers between devices: 0.01 us -> 2.13 us  [swap(): return lax.ppermute(block, 'pol', [(source, 1 - source)])]
    unnamed x17 -> x13, local copies, waits for them, and re-layouts: 3.06 us -> 1.27 us
    slice x0 -> x2, local copies, waits for them, and re-layouts: none -> 1.62 us  [the longest x1 0.83 us: per_device(): near = ahead(x[near_at:])]
    ppermute x3, starting transfers between devices: 4.84 us -> 5.9 us  [swap(): return lax.ppermute(block, 'pol', [(source, 1 - source)])]
    ppermute x2, waiting for transfers between devices: 4.15 us -> 5.11 us  [ahead(): return lax.ppermute(part, 'tm', [(i, i + 1) for i in range(n_tm - 1)])]
    transpose x5 -> x1, local copies, waits for them, and re-layouts: 3.31 us -> 2.67 us  [per_device(): x = samples.transpose(0, 2, 1, 3).reshape(samples.shape[0] * 2, CYL * NS)]
  transfers between devices with their start and end apart: 14 -> 14, of which waited for: 3 -> 5; matrix products, arithmetic and copies ran while one was open for 4% -> 2% of each run, Pallas kernels for 27% -> 12%
where the time goes in v2:
time: 73.4 us; the launch traced here: 72.3 us
  starting transfers between devices  35.3 us (48%)
  Pallas kernels  16.2 us (22%)
  waiting for transfers between devices  15 us (20%)
  local copies, waits for them, and re-layouts  5.56 us (8%)
    ppermute x9, starting transfers between devices, regroup(): got.append(lax.ppermute(blocks[k], ('freq', 'pol'), route))  22.3 us
    pallas_call x3, Pallas kernels, powers(): call(body, shape, len(args), flops, 3 << 20, after=len(after), scratch=sc...  8.75 us
    ppermute x9, waiting for transfers between devices, regroup(): got.append(lax.ppermute(blocks[k], ('freq', 'pol'), route))  7.76 us
    ppermute x2, starting transfers between devices, ahead(): return lax.ppermute(part, 'tm', [(i, i + 1) for i in range(n_tm - 1)])  7.11 us
    ppermute x3, starting transfers between devices, swap(): return lax.ppermute(block, 'pol', [(source, 1 - source)])  5.9 us
    ppermute x2, waiting for transfers between devices, ahead(): return lax.ppermute(part, 'tm', [(i, i + 1) for i in range(n_tm - 1)])  5.11 us
    pallas_call x3, Pallas kernels, regroup(): call(place_kernel, [shape] * n_owner, 4, 2 * rows * beams * beams * 2, 6...  4 us
    transpose x1, local copies, waits for them, and re-layouts, per_device(): x = samples.transpose(0, 2, 1, 3).reshape(samples.shape[0] * 2, CYL * NS)  2.67 us
  transfers between devices with their start and end apart: 14, of which 5 were waited for; matrix products, arithmetic and copies ran while one was open for 2% of the time, Pallas kernels for 12%

profile of v2, /device:TPU:0, one launch (start us, length us, event | category | flops | bytes accessed | tf_op | source)
XLA Modules:
  0.0 72.3 jit_solution(18192568121114911279)
XLA Ops:
  0.0 2.7 %copy.8 = bf16[512,2,4,256]{3,2,1,0:T(4,128)(2,1)S(1)} copy(bf16[512,2,4,256]{3,1,2,0:T(2,128)(2,1)} %bitcast.24) | data formatting | bytes 4194304 | tf_op jit(solution)/shard_map/transpose | solution.py:257
  2.7 0.0 copy-start
  2.7 0.0 copy-start.1
  2.7 0.0 copy-start.4
  2.7 0.5 copy.9
  3.2 0.6 copy-done
  3.8 0.1 copy-done.1
  4.0 3.7 %shard_map.73.refs_2_.refs_0_ = bf16[256,1024]{1,0:T(8,128)(2,1)} custom-call(bf16[512,768]{1,0:T(8,128)(2,1)S(1)} %copy-done, bf16[1024,1024]{1,0:T(8,128)(2,1)S(1)} %bitcast.11, f32[4,2,256]{2,1,0:T(2,128)S(1)} %bitcast.19, bf16[512,512]{1,0:T(8,128)(2,1)S(1)} %copy-done.1), custom_call_target="tpu_custom_call" | custom-call | flops 2147483648 | bytes 3145728 | tf_op jit(solution)/shard_map/pallas_call | solution.py:237
  7.6 3.2 %collective-permute-start = (bf16[256,1024]{1,0:T(8,128)(2,1)}, bf16[256,1024]{1,0:T(8,128)(2,1)}, u32[]{:S(2)}, u32[]{:S(2)}) collective-permute-start(bf16[256,1024]{1,0:T(8,128)(2,1)} %shard_map.73.refs_2_.refs_0_), channel_id=1, source_target_pairs={{0,1},{2,3},{4,5},{6,7},{8,9},{10,11},{12,13},{14,15},{16,17},{18,... | collective-permute-start | bytes 1572872 | tf_op jit(solution)/shard_map/ppermute | solution.py:240
  10.8 0.8 %slice.8 = bf16[256,1024]{1,0:T(8,128)(2,1)} slice(bf16[1024,1024]{1,0:T(8,128)(2,1)S(1)} %bitcast.12), slice={[768:1024], [0:1024]} | slice | bytes 1048576 | tf_op jit(solution)/shard_map/slice | solution.py:262
  11.6 5.0 %collective-permute-start.4 = (bf16[256,1024]{1,0:T(8,128)(2,1)}, bf16[256,1024]{1,0:T(8,128)(2,1)}, u32[]{:S(2)}, u32[]{:S(2)}) collective-permute-start(bf16[256,1024]{1,0:T(8,128)(2,1)} %slice.8), channel_id=1, source_target_pairs={{0,2},{1,3},{4,6},{5,7},{8,10},{9,11},{12,14},{13,15},{16,18},{17,... | collective-permute-start | bytes 1572872 | tf_op jit(solution)/shard_map/ppermute | solution.py:230
  16.7 0.8 %slice.9 = bf16[224,1024]{1,0:T(8,128)(2,1)} slice(bf16[1024,1024]{1,0:T(8,128)(2,1)S(1)} %bitcast.13), slice={[544:768], [0:1024]} | slice | bytes 917504 | tf_op jit(solution)/shard_map/slice | solution.py:263
  17.5 2.1 %collective-permute-start.9 = (bf16[224,1024]{1,0:T(8,128)(2,1)}, bf16[224,1024]{1,0:T(8,128)(2,1)}, u32[]{:S(2)}, u32[]{:S(2)}) collective-permute-start(bf16[224,1024]{1,0:T(8,128)(2,1)} %slice.9), channel_id=1, source_target_pairs={{0,2},{1,3},{4,6},{5,7},{8,10},{9,11},{12,14},{13,15},{16,18},{17,... | collective-permute-start | bytes 1376264 | tf_op jit(solution)/shard_map/ppermute | solution.py:230
  19.5 0.1 pad_add_fusion.refs_0_
  19.6 0.0 copy-done.5
  19.6 1.8 %shard_map.74.refs_3_ = bf16[4,1024,512]{2,1,0:T(8,128)(2,1)S(1)} custom-call(s32[2]{0:T(128)S(1)} %pad_add_fusion.refs_0_, s32[1,64]{1,0:T(1,128)S(1)} %bitcast.22, bf16[256,1024]{1,0:T(8,128)(2,1)} %shard_map.73.refs_2_.refs_0_), custom_call_target="tpu_custom_call" | custom-call | flops 16777216 | bytes 4194304 | tf_op jit(solution)/shard_map/pallas_call | solution.py:268
  21.5 0.0 collective-permute-done.refs_1_
  21.5 2.5 %shard_map.75 = (bf16[256,512]{1,0:T(8,128)(2,1)S(1)}, bf16[256,512]{1,0:T(8,128)(2,1)S(1)}, bf16[256,512]{1,0:T(8,128)(2,1)S(1)}, bf16[256,512]{1,0:T(8,128)(2,1)S(1)}) custom-call(bf16[256,1024]{1,0:T(8,128)(2,1)} %shard_map.73.refs_2_.refs_0_, bf16[256,1024]{1,0:T(8,128)(2,1)} %collective-permute-done.refs_1_, s32[1,1024]{1,0:T(1,128)S(1)} %bitcast.16, ...), custom_call_target="tpu_custom_call" | custom-call | flops 1073741824 | bytes 6291456 | tf_op jit(solution)/shard_map/pallas_call | solution.py:246
  24.0 4.5 %collective-permute-done.4.refs_1_.refs_3_ = bf16[256,1024]{1,0:T(8,128)(2,1)} collective-permute-done((bf16[256,1024]{1,0:T(8,128)(2,1)}, bf16[256,1024]{1,0:T(8,128)(2,1)}, u32[]{:S(2)}, u32[]{:S(2)}) %collective-permute-start.4) | collective-permute-done | bytes 524320 | tf_op jit(solution)/shard_map/ppermute | solution.py:230
  28.5 2.5 %shard_map.76.refs_0_ = bf16[128,1024]{1,0:T(8,128)(2,1)S(1)} custom-call(bf16[512,768]{1,0:T(8,128)(2,1)S(1)} %copy-done, bf16[256,1024]{1,0:T(8,128)(2,1)} %collective-permute-done.4.refs_1_.refs_3_, bf16[1024,1024]{1,0:T(8,128)(2,1)S(1)} %bitcast.14, f32[4,2,256]{2,1,0:T(2,128)S(1)} %bitcast.20, bf16[512,512]{1,0:T(8,128)(2,1)S(1)} %copy-done.1, ...), custom_call_target="tpu_custom_call" | custom-call | flops 1073741824 | bytes 3145728 | tf_op jit(solution)/shard_map/pallas_call | solution.py:237
  31.0 0.0 copy-start.2
  31.0 1.4 %collective-permute-start.5 = (bf16[128,1024]{1,0:T(8,128)(2,1)S(1)}, bf16[128,1024]{1,0:T(8,128)(2,1)S(1)}, u32[]{:S(2)}, u32[]{:S(2)}) collective-permute-start(bf16[128,1024]{1,0:T(8,128)(2,1)S(1)} %shard_map.76.refs_0_), channel_id=1, source_target_pairs={{1,0},{3,2},{5,4},{7,6},{9,8},{11,10},{13,12},{15,14},{17,16},{19,... | collective-permute-start | bytes 786440 | tf_op jit(solution)/shard_map/ppermute | solution.py:240
  32.4 2.1 %collective-permute-done.5.refs_1_ = bf16[128,1024]{1,0:T(8,128)(2,1)S(1)} collective-permute-done((bf16[128,1024]{1,0:T(8,128)(2,1)S(1)}, bf16[128,1024]{1,0:T(8,128)(2,1)S(1)}, u32[]{:S(2)}, u32[]{:S(2)}) %collective-permute-start.5) | collective-permute-done | bytes 262176 | tf_op jit(solution)/shard_map/ppermute | solution.py:240
  34.5 0.7 %shard_map.77 = (bf16[128,512]{1,0:T(8,128)(2,1)S(1)}, bf16[128,512]{1,0:T(8,128)(2,1)S(1)}, bf16[128,512]{1,0:T(8,128)(2,1)S(1)}, bf16[128,512]{1,0:T(8,128)(2,1)S(1)}) custom-call(bf16[128,1024]{1,0:T(8,128)(2,1)S(1)} %shard_map.76.refs_0_, bf16[128,1024]{1,0:T(8,128)(2,1)S(1)} %collective-permute-done.5.refs_1_, s32[1,1024]{1,0:T(1,128)S(1)} %bitcast.17, ...), custom_call_target="tpu_custom_call" | custom-call | flops 536870912 | bytes 6291456 | tf_op jit(solution)/shard_map/pallas_call | solution.py:246
  35.3 0.7 collective-permute-done.9.refs_2_
  35.9 2.6 %shard_map.78.refs_0_ = bf16[128,1024]{1,0:T(8,128)(2,1)S(1)} custom-call(bf16[512,768]{1,0:T(8,128)(2,1)S(1)} %copy-done, bf16[512,224]{1,0:T(8,128)(2,1)S(1)} %copy-done.2, bf16[224,1024]{1,0:T(8,128)(2,1)} %collective-permute-done.9.refs_2_, bf16[256,1024]{1,0:T(8,128)(2,1)} %collective-permute-done.4.refs_1_.refs_3_, bf16[1024,1024]{1,0:T(8,128)(2,1)S(1)} %bitcast.15, ...), custom_call_target="tpu_custom_call" | custom-call | flops 1073741824 | bytes 3145728 | tf_op jit(solution)/shard_map/pallas_call | solution.py:237
  38.5 1.3 %collective-permute-start.10 = (bf16[128,1024]{1,0:T(8,128)(2,1)S(1)}, bf16[128,1024]{1,0:T(8,128)(2,1)S(1)}, u32[]{:S(2)}, u32[]{:S(2)}) collective-permute-start(bf16[128,1024]{1,0:T(8,128)(2,1)S(1)} %shard_map.78.refs_0_), channel_id=1, source_target_pairs={{1,0},{3,2},{5,4},{7,6},{9,8},{11,10},{13,12},{15,14},{17,16},{19,... | collective-permute-start | bytes 786440 | tf_op jit(solution)/shard_map/ppermute | solution.py:240
  39.8 0.7 collective-permute-start.1
  40.5 0.7 collective-permute-start.2
  41.2 0.7 collective-permute-start.3
  41.9 3.5 %collective-permute-start.6 = (bf16[128,512]{1,0:T(8,128)(2,1)S(1)}, bf16[128,512]{1,0:T(8,128)(2,1)S(1)}, u32[]{:S(2)}, u32[]{:S(2)}) collective-permute-start(bf16[128,512]{1,0:T(8,128)(2,1)S(1)} %get-tuple-element.22), channel_id=1, source_target_pairs={{0,4},{4,0},{8,12},{12,8},{2,6},{6,2},{10,14},{14,10},{16,20},{20,... | collective-permute-start | bytes 393224 | tf_op jit(solution)/shard_map/ppermute | solution.py:252
  45.4 0.0 collective-permute-done.10.refs_1_
  45.4 4.5 %collective-permute-start.7 = (bf16[128,512]{1,0:T(8,128)(2,1)S(1)}, bf16[128,512]{1,0:T(8,128)(2,1)S(1)}, u32[]{:S(2)}, u32[]{:S(2)}) collective-permute-start(bf16[128,512]{1,0:T(8,128)(2,1)S(1)} %get-tuple-element.23), channel_id=1, source_target_pairs={{0,8},{4,12},{8,0},{12,4},{2,10},{6,14},{10,2},{14,6},{16,24},{20,... | collective-permute-start | bytes 393224 | tf_op jit(solution)/shard_map/ppermute | solution.py:252
  49.9 0.8 %shard_map.79 = (bf16[128,512]{1,0:T(8,128)(2,1)S(1)}, bf16[128,512]{1,0:T(8,128)(2,1)S(1)}, bf16[128,512]{1,0:T(8,128)(2,1)S(1)}, bf16[128,512]{1,0:T(8,128)(2,1)S(1)}) custom-call(bf16[128,1024]{1,0:T(8,128)(2,1)S(1)} %shard_map.78.refs_0_, bf16[128,1024]{1,0:T(8,128)(2,1)S(1)} %collective-permute-done.10.refs_1_, s32[1,1024]{1,0:T(1,128)S(1)} %bitcast.18, ...), custom_call_target="tpu_custom_call" | custom-call | flops 536870912 | bytes 6291456 | tf_op jit(solution)/shard_map/pallas_call | solution.py:246
  50.7 0.0 collective-permute-done.1.refs_2_
  50.7 2.1 %collective-permute-start.8 = (bf16[128,512]{1,0:T(8,128)(2,1)S(1)}, bf16[128,512]{1,0:T(8,128)(2,1)S(1)}, u32[]{:S(2)}, u32[]{:S(2)}) collective-permute-start(bf16[128,512]{1,0:T(8,128)(2,1)S(1)} %get-tuple-element.24), channel_id=1, source_target_pairs={{0,12},{4,8},{8,4},{12,0},{2,14},{6,10},{10,6},{14,2},{16,28},{20,... | collective-permute-start | bytes 393224 | tf_op jit(solution)/shard_map/ppermute | solution.py:252
  52.8 0.0 collective-permute-done.2.refs_3_
  52.8 2.6 %collective-permute-start.11 = (bf16[128,512]{1,0:T(8,128)(2,1)S(1)}, bf16[128,512]{1,0:T(8,128)(2,1)S(1)}, u32[]{:S(2)}, u32[]{:S(2)}) collective-permute-start(bf16[128,512]{1,0:T(8,128)(2,1)S(1)} %get-tuple-element.26), channel_id=1, source_target_pairs={{0,4},{4,0},{8,12},{12,8},{2,6},{6,2},{10,14},{14,10},{16,20},{20,... | collective-permute-start | bytes 393224 | tf_op jit(solution)/shard_map/ppermute | solution.py:252
  55.4 0.0 collective-permute-done.3.refs_4_
  55.4 5.4 %collective-permute-start.12 = (bf16[128,512]{1,0:T(8,128)(2,1)S(1)}, bf16[128,512]{1,0:T(8,128)(2,1)S(1)}, u32[]{:S(2)}, u32[]{:S(2)}) collective-permute-start(bf16[128,512]{1,0:T(8,128)(2,1)S(1)} %get-tuple-element.27), channel_id=1, source_target_pairs={{0,8},{4,12},{8,0},{12,4},{2,10},{6,14},{10,2},{14,6},{16,24},{20,... | collective-permute-start | bytes 393224 | tf_op jit(solution)/shard_map/ppermute | solution.py:252
  60.8 0.0 collective-permute-done.6.refs_6_
  60.8 2.1 %collective-permute-start.13 = (bf16[128,512]{1,0:T(8,128)(2,1)S(1)}, bf16[128,512]{1,0:T(8,128)(2,1)S(1)}, u32[]{:S(2)}, u32[]{:S(2)}) collective-permute-start(bf16[128,512]{1,0:T(8,128)(2,1)S(1)} %get-tuple-element.28), channel_id=1, source_target_pairs={{0,12},{4,8},{8,4},{12,0},{2,14},{6,10},{10,6},{14,2},{16,28},{20,... | collective-permute-start | bytes 393224 | tf_op jit(solution)/shard_map/ppermute | solution.py:252
  63.0 1.2 %collective-permute-done.7.refs_7_ = bf16[128,512]{1,0:T(8,128)(2,1)S(1)} collective-permute-done((bf16[128,512]{1,0:T(8,128)(2,1)S(1)}, bf16[128,512]{1,0:T(8,128)(2,1)S(1)}, u32[]{:S(2)}, u32[]{:S(2)}) %collective-permute-start.7) | collective-permute-done | bytes 131104 | tf_op jit(solution)/shard_map/ppermute | solution.py:252
  64.2 0.0 collective-permute-done.8.refs_8_
  64.2 0.0 collective-permute-done.11.refs_10_
  64.2 6.5 %collective-permute-done.12.refs_11_ = bf16[128,512]{1,0:T(8,128)(2,1)S(1)} collective-permute-done((bf16[128,512]{1,0:T(8,128)(2,1)S(1)}, bf16[128,512]{1,0:T(8,128)(2,1)S(1)}, u32[]{:S(2)}, u32[]{:S(2)}) %collective-permute-start.12) | collective-permute-done | bytes 131104 | tf_op jit(solution)/shard_map/ppermute | solution.py:252
  70.7 0.0 collective-permute-done.13.refs_12_
  70.7 1.6 %shard_map.80 = bf16[16,64,512]{2,1,0:T(8,128)(2,1)} custom-call(s32[2]{0:T(128)S(1)} %pad_add_fusion.refs_0_, bf16[256,512]{1,0:T(8,128)(2,1)S(1)} %get-tuple-element.17.refs_5_.refs_1_, bf16[256,512]{1,0:T(8,128)(2,1)S(1)} %collective-permute-done.1.refs_2_, bf16[256,512]{1,0:T(8,128)(2,1)S(1)} %collective-permute-done.2.refs_3_, ...), custom_call_target="tpu_custom_call" | custom-call | bytes 3145728 | tf_op jit(solution)/shard_map/pallas_call | solution.py:285
  (5 shorter events, 0.0 us)
Async XLA Ops:
  2.7 1.1 %copy-start = (bf16[512,768]{1,0:T(8,128)(2,1)S(1)}, bf16[512,768]{1,0:T(8,128)(2,1)}, u32[]{:S(2)}) copy-start(bf16[512,768]{1,0:T(8,128)(2,1)} %constant.15.clone.refs_0_) | copy-start | bytes 2359300
  2.7 1.3 %copy-start.1 = (bf16[512,512]{1,0:T(8,128)(2,1)S(1)}, bf16[512,512]{1,0:T(8,128)(2,1)}, u32[]{:S(2)}) copy-start(bf16[512,512]{1,0:T(8,128)(2,1)} %constant.17.clone.refs_3_.refs_4_.refs_6_) | copy-start | bytes 1572868
  2.7 1.3 %copy-start.4 = (f32[1,1,4,2,256]{4,3,2,1,0:T(2,128)S(1)}, f32[1,1,4,2,256]{4,3,2,1,0:T(2,128)}, u32[]{:S(2)}) copy-start(f32[1,1,4,2,256]{4,3,2,1,0:T(2,128)} %param.8) | copy-start | bytes 24580
  4.0 15.7 %copy-start.5 = (s32[64]{0:T(128)S(1)}, s32[64]{0:T(128)}, u32[]{:S(2)}) copy-start(s32[64]{0:T(128)} %param.9) | copy-start | bytes 772
  7.6 13.9 %collective-permute-start = (bf16[256,1024]{1,0:T(8,128)(2,1)}, bf16[256,1024]{1,0:T(8,128)(2,1)}, u32[]{:S(2)}, u32[]{:S(2)}) collective-permute-start(bf16[256,1024]{1,0:T(8,128)(2,1)} %shard_map.73.refs_2_.refs_0_), channel_id=1, source_target_pairs={{0,1},{2,3},{4,5},{6,7},{8,9},{10,11},{12,13},{14,15},{16,17},{18,... | collective-permute-start | bytes 1572872 | tf_op jit(solution)/shard_map/ppermute | solution.py:240
  11.6 16.8 %collective-permute-start.4 = (bf16[256,1024]{1,0:T(8,128)(2,1)}, bf16[256,1024]{1,0:T(8,128)(2,1)}, u32[]{:S(2)}, u32[]{:S(2)}) collective-permute-start(bf16[256,1024]{1,0:T(8,128)(2,1)} %slice.8), channel_id=1, source_target_pairs={{0,2},{1,3},{4,6},{5,7},{8,10},{9,11},{12,14},{13,15},{16,18},{17,... | collective-permute-start | bytes 1572872 | tf_op jit(solution)/shard_map/ppermute | solution.py:230
  17.5 18.5 %collective-permute-start.9 = (bf16[224,1024]{1,0:T(8,128)(2,1)}, bf16[224,1024]{1,0:T(8,128)(2,1)}, u32[]{:S(2)}, u32[]{:S(2)}) collective-permute-start(bf16[224,1024]{1,0:T(8,128)(2,1)} %slice.9), channel_id=1, source_target_pairs={{0,2},{1,3},{4,6},{5,7},{8,10},{9,11},{12,14},{13,15},{16,18},{17,... | collective-permute-start | bytes 1376264 | tf_op jit(solution)/shard_map/ppermute | solution.py:230
  19.6 1.9 %copy-start.3 = (s32[1024]{0:T(1024)S(1)}, s32[1024]{0:T(1024)}, u32[]{:S(2)}) copy-start(s32[1024]{0:T(1024)} %param.10) | copy-start | bytes 12292
  31.0 5.0 %copy-start.2 = (bf16[512,224]{1,0:T(8,128)(2,1)S(1)}, bf16[512,224]{1,0:T(8,128)(2,1)}, u32[]{:S(2)}) copy-start(bf16[512,224]{1,0:T(8,128)(2,1)} %constant.16.clone.refs_1_) | copy-start | bytes 688132
  31.0 3.6 %collective-permute-start.5 = (bf16[128,1024]{1,0:T(8,128)(2,1)S(1)}, bf16[128,1024]{1,0:T(8,128)(2,1)S(1)}, u32[]{:S(2)}, u32[]{:S(2)}) collective-permute-start(bf16[128,1024]{1,0:T(8,128)(2,1)S(1)} %shard_map.76.refs_0_), channel_id=1, source_target_pairs={{1,0},{3,2},{5,4},{7,6},{9,8},{11,10},{13,12},{15,14},{17,16},{19,... | collective-permute-start | bytes 786440 | tf_op jit(solution)/shard_map/ppermute | solution.py:240
  38.5 6.9 %collective-permute-start.10 = (bf16[128,1024]{1,0:T(8,128)(2,1)S(1)}, bf16[128,1024]{1,0:T(8,128)(2,1)S(1)}, u32[]{:S(2)}, u32[]{:S(2)}) collective-permute-start(bf16[128,1024]{1,0:T(8,128)(2,1)S(1)} %shard_map.78.refs_0_), channel_id=1, source_target_pairs={{1,0},{3,2},{5,4},{7,6},{9,8},{11,10},{13,12},{15,14},{17,16},{19,... | collective-permute-start | bytes 786440 | tf_op jit(solution)/shard_map/ppermute | solution.py:240
  39.8 10.8 %collective-permute-start.1 = (bf16[256,512]{1,0:T(8,128)(2,1)S(1)}, bf16[256,512]{1,0:T(8,128)(2,1)S(1)}, u32[]{:S(2)}, u32[]{:S(2)}) collective-permute-start(bf16[256,512]{1,0:T(8,128)(2,1)S(1)} %get-tuple-element.18), channel_id=1, source_target_pairs={{1,5},{5,1},{9,13},{13,9},{3,7},{7,3},{11,15},{15,11},{17,21},{21,... | collective-permute-start | bytes 786440 | tf_op jit(solution)/shard_map/ppermute | solution.py:252
  40.5 12.3 %collective-permute-start.2 = (bf16[256,512]{1,0:T(8,128)(2,1)S(1)}, bf16[256,512]{1,0:T(8,128)(2,1)S(1)}, u32[]{:S(2)}, u32[]{:S(2)}) collective-permute-start(bf16[256,512]{1,0:T(8,128)(2,1)S(1)} %get-tuple-element.19), channel_id=1, source_target_pairs={{1,9},{5,13},{9,1},{13,5},{3,11},{7,15},{11,3},{15,7},{17,25},{21,... | collective-permute-start | bytes 786440 | tf_op jit(solution)/shard_map/ppermute | solution.py:252
  41.2 14.2 %collective-permute-start.3 = (bf16[256,512]{1,0:T(8,128)(2,1)S(1)}, bf16[256,512]{1,0:T(8,128)(2,1)S(1)}, u32[]{:S(2)}, u32[]{:S(2)}) collective-permute-start(bf16[256,512]{1,0:T(8,128)(2,1)S(1)} %get-tuple-element.20), channel_id=1, source_target_pairs={{1,13},{5,9},{9,5},{13,1},{3,15},{7,11},{11,7},{15,3},{17,29},{21,... | collective-permute-start | bytes 786440 | tf_op jit(solution)/shard_map/ppermute | solution.py:252
  41.9 18.9 %collective-permute-start.6 = (bf16[128,512]{1,0:T(8,128)(2,1)S(1)}, bf16[128,512]{1,0:T(8,128)(2,1)S(1)}, u32[]{:S(2)}, u32[]{:S(2)}) collective-permute-start(bf16[128,512]{1,0:T(8,128)(2,1)S(1)} %get-tuple-element.22), channel_id=1, source_target_pairs={{0,4},{4,0},{8,12},{12,8},{2,6},{6,2},{10,14},{14,10},{16,20},{20,... | collective-permute-start | bytes 393224 | tf_op jit(solution)/shard_map/ppermute | solution.py:252
  45.4 18.8 %collective-permute-start.7 = (bf16[128,512]{1,0:T(8,128)(2,1)S(1)}, bf16[128,512]{1,0:T(8,128)(2,1)S(1)}, u32[]{:S(2)}, u32[]{:S(2)}) collective-permute-start(bf16[128,512]{1,0:T(8,128)(2,1)S(1)} %get-tuple-element.23), channel_id=1, source_target_pairs={{0,8},{4,12},{8,0},{12,4},{2,10},{6,14},{10,2},{14,6},{16,24},{20,... | collective-permute-start | bytes 393224 | tf_op jit(solution)/shard_map/ppermute | solution.py:252
  50.7 13.5 %collective-permute-start.8 = (bf16[128,512]{1,0:T(8,128)(2,1)S(1)}, bf16[128,512]{1,0:T(8,128)(2,1)S(1)}, u32[]{:S(2)}, u32[]{:S(2)}) collective-permute-start(bf16[128,512]{1,0:T(8,128)(2,1)S(1)} %get-tuple-element.24), channel_id=1, source_target_pairs={{0,12},{4,8},{8,4},{12,0},{2,14},{6,10},{10,6},{14,2},{16,28},{20,... | collective-permute-start | bytes 393224 | tf_op jit(solution)/shard_map/ppermute | solution.py:252
  52.8 11.4 %collective-permute-start.11 = (bf16[128,512]{1,0:T(8,128)(2,1)S(1)}, bf16[128,512]{1,0:T(8,128)(2,1)S(1)}, u32[]{:S(2)}, u32[]{:S(2)}) collective-permute-start(bf16[128,512]{1,0:T(8,128)(2,1)S(1)} %get-tuple-element.26), channel_id=1, source_target_pairs={{0,4},{4,0},{8,12},{12,8},{2,6},{6,2},{10,14},{14,10},{16,20},{20,... | collective-permute-start | bytes 393224 | tf_op jit(solution)/shard_map/ppermute | solution.py:252
  55.4 15.3 %collective-permute-start.12 = (bf16[128,512]{1,0:T(8,128)(2,1)S(1)}, bf16[128,512]{1,0:T(8,128)(2,1)S(1)}, u32[]{:S(2)}, u32[]{:S(2)}) collective-permute-start(bf16[128,512]{1,0:T(8,128)(2,1)S(1)} %get-tuple-element.27), channel_id=1, source_target_pairs={{0,8},{4,12},{8,0},{12,4},{2,10},{6,14},{10,2},{14,6},{16,24},{20,... | collective-permute-start | bytes 393224 | tf_op jit(solution)/shard_map/ppermute | solution.py:252
  60.8 9.9 %collective-permute-start.13 = (bf16[128,512]{1,0:T(8,128)(2,1)S(1)}, bf16[128,512]{1,0:T(8,128)(2,1)S(1)}, u32[]{:S(2)}, u32[]{:S(2)}) collective-permute-start(bf16[128,512]{1,0:T(8,128)(2,1)S(1)} %get-tuple-element.28), channel_id=1, source_target_pairs={{0,12},{4,8},{8,4},{12,0},{2,14},{6,10},{10,6},{14,2},{16,28},{20,... | collective-permute-start | bytes 393224 | tf_op jit(solution)/shard_map/ppermute | solution.py:252

commit v3 on v2

--- a/solution.py
+++ b/solution.py
@@ -61,7 +61,11 @@
     return (table.astype(np.float32) * 0.5).astype(jnp.bfloat16)
 
 
-def form_powers(parts, gain_ref, beam_ref, out_ref, cal_ref, out_start):
+def columns(cyl):
+    return slice(cyl * NS, (cyl + 1) * NS)
+
+
+def form_powers(parts, gain_ref, beam_ref, cal_ref, emit):
     half = BLOCK * UPCH
     for cyl in range(CYL):
         total = None
@@ -87,56 +91,91 @@
         sr, si, dr, di = r1 + r3, i1 + i3, r1 - r3, i1 - i3
         formed = [(pr + sr, pi + si), (mr + di, mi - dr), (pr - sr, pi - si), (mr - di, mi + dr)]
         for element, (fr, fi) in enumerate(formed):
-            power = (fr * fr + fi * fi).astype(jnp.bfloat16)
-            at = element * NS + strip * LANES
-            out_ref[pl.ds(out_start, half), at : at + LANES] = power
-
-
-def columns(cyl):
-    return slice(cyl * NS, (cyl + 1) * NS)
-
-
-def local_kernel(blocks, first, filt_ref, x_ref, gain_ref, beam_ref, out_ref, cal_ref):
+            emit(element * NS + strip * LANES, fr * fr + fi * fi)
+
+
+def sum_block(parts_of, gains, beam_ref, keep_ref, cal_ref, sum_ref, at):
+    rows = pl.ds(at, BLOCK * UPCH)
+
+    def first(column, power):
+        sum_ref[rows, column : column + LANES] = power.astype(jnp.bfloat16)
+
+    def second(column, power):
+        lanes = slice(column, column + LANES)
+        total = sum_ref[rows, lanes].astype(jnp.float32) + power.astype(jnp.bfloat16).astype(jnp.float32)
+        sum_ref[rows, lanes] = (total * keep_ref[:, lanes].astype(jnp.float32)).astype(jnp.bfloat16)
+
+    form_powers(parts_of(0), gains[0], beam_ref, cal_ref, first)
+    form_powers(parts_of(1), gains[1], beam_ref, cal_ref, second)
+
+
+def place(sum_ref, table_ref, out_refs, rows):
+    for k, out_ref in enumerate(out_refs):
+        placed = jnp.dot(sum_ref[...], table_ref[k], preferred_element_type=jnp.float32)
+        out_ref[rows, :] = placed.astype(jnp.bfloat16)
+
+
+def late_kernel(blocks, n_owner, where_ref, filt_ref, x0, x1, g0, g1, beam_ref, keep_ref, table_ref, *refs):
+    out_refs, (cal_ref, sum_ref) = refs[:n_owner], refs[n_owner:]
     depth = (TAPS + BLOCK) * ROWS
 
-    def step(block, carry):
-        start = pl.multiple_of((first - TAPS + block * BLOCK) * ROWS, 256)
-
-        def parts(cyl):
-            return [(filt_ref[...], x_ref[pl.ds(start, depth), columns(cyl)])]
-
-        form_powers(parts, gain_ref, beam_ref, out_ref, cal_ref, pl.multiple_of(block * BLOCK * UPCH, 128))
-        return carry
-
-    lax.fori_loop(0, blocks, step, 0)
-
-
-def near_kernel(filt_ref, near_ref, x_ref, gain_ref, beam_ref, out_ref, cal_ref):
+    @pl.when(where_ref[1] == 1)
+    def _():
+        def step(block, carry):
+            start = pl.multiple_of(block * BLOCK * ROWS, BLOCK * ROWS)
+
+            def parts_of(pol):
+                return lambda cyl: [(filt_ref[...], (x0, x1)[pol][pl.ds(start, depth), columns(cyl)])]
+
+            at = pl.multiple_of(block * BLOCK * UPCH, BLOCK * UPCH)
+            sum_block(parts_of, (g0, g1), beam_ref, keep_ref, cal_ref, sum_ref, at)
+            return carry
+
+        lax.fori_loop(0, blocks, step, 0)
+        place(sum_ref, table_ref, out_refs, slice(None))
+
+
+def near_kernel(n_owner, where_ref, filt_ref, n0, n1, x0, x1, g0, g1, beam_ref, keep_ref, table_ref, *refs):
+    out_refs, (cal_ref, sum_ref) = refs[:n_owner], refs[n_owner:]
     reach = BLOCK * ROWS
 
-    def parts(cyl):
-        return [
-            (filt_ref[:, :reach], near_ref[:, columns(cyl)]),
-            (filt_ref[:, reach:], x_ref[: 2 * reach, columns(cyl)]),
-        ]
-
-    form_powers(parts, gain_ref, beam_ref, out_ref, cal_ref, 0)
-
-
-def far_kernel(filt_ref, edge_ref, far_ref, near_ref, x_ref, gain_ref, beam_ref, out_ref, cal_ref):
+    @pl.when(where_ref[1] == 0)
+    def _():
+        def parts_of(pol):
+            near, x = (n0, n1)[pol], (x0, x1)[pol]
+            return lambda cyl: [
+                (filt_ref[:, :reach], near[:, columns(cyl)]),
+                (filt_ref[:, reach:], x[: 2 * reach, columns(cyl)]),
+            ]
+
+        sum_block(parts_of, (g0, g1), beam_ref, keep_ref, cal_ref, sum_ref, 0)
+        place(sum_ref, table_ref, out_refs, slice(None))
+
+
+def far_kernel(
+    n_owner, where_ref, filt_ref, edge_ref, f0, f1, n0, n1, x0, x1, g0, g1, beam_ref, keep_ref, table_ref, *refs
+):
+    near_refs, out_refs, (cal_ref, sum_ref) = refs[:n_owner], refs[n_owner : 2 * n_owner], refs[2 * n_owner :]
     reach = BLOCK * ROWS
-
-    def parts(cyl):
-        return [
-            (filt_ref[:, reach : 2 * reach], near_ref[:, columns(cyl)]),
-            (filt_ref[:, 2 * reach :], x_ref[:reach, columns(cyl)]),
-            (edge_ref[...], far_ref[:, columns(cyl)]),
-        ]
-
-    form_powers(parts, gain_ref, beam_ref, out_ref, cal_ref, 0)
-
-
-def place_table_kernel(most_sets, me_ref, owner_ref, out_ref):
+    half = BLOCK * UPCH
+
+    @pl.when(where_ref[1] == 0)
+    def _():
+        def parts_of(pol):
+            far, near, x = (f0, f1)[pol], (n0, n1)[pol], (x0, x1)[pol]
+            return lambda cyl: [
+                (filt_ref[:, reach : 2 * reach], near[:, columns(cyl)]),
+                (filt_ref[:, 2 * reach :], x[:reach, columns(cyl)]),
+                (edge_ref[...], far[:, columns(cyl)]),
+            ]
+
+        sum_block(parts_of, (g0, g1), beam_ref, keep_ref, cal_ref, sum_ref, 0)
+        place(sum_ref, table_ref, out_refs, slice(0, half))
+        for near_ref, out_ref in zip(near_refs, out_refs):
+            out_ref[half:, :] = near_ref[...]
+
+
+def place_table_kernel(most_sets, where_ref, owner_ref, out_ref):
     n_owner, beams, width = out_ref.shape
     sets = owner_ref.shape[1]
     owner = owner_ref[...].astype(jnp.float32)
@@ -147,41 +186,24 @@
     rank = jnp.sum(jnp.where(same, 1.0, 0.0), axis=1, keepdims=True)
     within = lax.broadcasted_iota(jnp.int32, (beams, 1), 0) % SET_BEAMS
     column = (own * most_sets + rank).astype(jnp.int32) * SET_BEAMS + within
-    place = lax.broadcasted_iota(jnp.int32, (beams, width), 1)
+    lane_at = lax.broadcasted_iota(jnp.int32, (beams, width), 1)
     for k in range(n_owner):
-        owner_k = me_ref[0] ^ k
-        hit = (column - owner_k * width) == place
+        owner_k = where_ref[0] ^ k
+        hit = (column - owner_k * width) == lane_at
         out_ref[k] = jnp.where(hit, 1.0, 0.0).astype(jnp.bfloat16)
 
 
-def place_kernel(mine_ref, other_ref, keep_ref, table_ref, *out_refs):
-    total = mine_ref[...].astype(jnp.float32) + other_ref[...].astype(jnp.float32)
-    total = (total * keep_ref[...].astype(jnp.float32)).astype(jnp.bfloat16)
-    for k, out_ref in enumerate(out_refs):
-        placed = jnp.dot(total, table_ref[k], preferred_element_type=jnp.float32)
-        out_ref[...] = placed.astype(jnp.bfloat16)
-
-
 def gather_kernel(n_owner, where_ref, *refs):
-    late, near, far, out_ref = refs[:n_owner], refs[n_owner : 2 * n_owner], refs[2 * n_owner : -1], refs[-1]
-    me = where_ref[0]
-
-    def copy(block, frame, k):
-        source = me ^ k
-        rows = pl.ds(pl.multiple_of(source * UPCH, UPCH), UPCH)
-        count = block.shape[0] // UPCH
-        out_ref[frame : frame + count, rows, :] = block[...].reshape(count, UPCH, block.shape[1])
-
-    @pl.when(where_ref[1] == 1)
-    def _():
-        for k in range(n_owner):
-            copy(late[k], 0, k)
-
-    @pl.when(where_ref[1] == 0)
-    def _():
-        for k in range(n_owner):
-            copy(far[k], 0, k)
-            copy(near[k], BLOCK, k)
+    late, early, out_ref = refs[:n_owner], refs[n_owner : 2 * n_owner], refs[-1]
+    for pol, blocks in enumerate((early, late)):
+
+        @pl.when(where_ref[1] == pol)
+        def _(blocks=blocks):
+            for k, block in enumerate(blocks):
+                source = where_ref[0] ^ k
+                rows = pl.ds(pl.multiple_of(source * UPCH, UPCH), UPCH)
+                count = block.shape[0] // UPCH
+                out_ref[:, rows, :] = block[...].reshape(count, UPCH, block.shape[1])
 
 
 VMEM = pl.BlockSpec(memory_space=pltpu.VMEM)
@@ -226,45 +248,45 @@
     edge = jnp.asarray(filter_matrix()[:, ROWS : BLOCK * ROWS])
     beam_table = jnp.asarray(beam_matrix())
 
-    def ahead(part):
-        return lax.ppermute(part, "tm", [(i, i + 1) for i in range(n_tm - 1)])
-
-    def powers(body, frames, *args, after=()):
-        rows = frames * UPCH
-        flops = frames // BLOCK * 2 * 512 * 1024 * 1024
-        shape = jax.ShapeDtypeStruct((rows, CYL * NS), bf16)
-        scratch = [pltpu.VMEM((CYL * BLOCK * UPCH, 2 * NS), bf16)]
-        return call(body, shape, len(args), flops, 3 << 20, after=len(after), scratch=scratch)(*args, *after)
-
-    def swap(block, source):
-        return lax.ppermute(block, "pol", [(source, 1 - source)])
-
-    def regroup(mine, target, table):
-        other = swap(mine, 1 - target)
-        rows = mine.shape[0]
-        shape = jax.ShapeDtypeStruct((rows, width), bf16)
-        blocks = call(place_kernel, [shape] * n_owner, 4, 2 * rows * beams * beams * 2, 6 << 20)(
-            mine, other, keep, table
-        )
+    pairs = [(i, i + 1) for i in range(n_tm - 1)]
+
+    def ahead(part, source):
+        return lax.ppermute(part, ("tm", "pol"), [(i * 2 + source, j * 2) for i, j in pairs])
+
+    def swap(part):
+        return lax.ppermute(part, "pol", [(0, 1), (1, 0)])
+
+    def spread(blocks, target):
         got = [blocks[0]]
         for k in range(1, n_owner):
             route = [(i * 2 + target, (i ^ k) * 2 + target) for i in range(n_owner)]
             got.append(lax.ppermute(blocks[k], ("freq", "pol"), route))
         return got
 
+    def form(body, frames, rows_out, *args, after=()):
+        flops = frames // BLOCK * 4 * 512 * 1024 * 1024
+        shape = [jax.ShapeDtypeStruct((rows_out, width), bf16)] * n_owner
+        scratch = [
+            pltpu.VMEM((CYL * BLOCK * UPCH, 2 * NS), bf16),
+            pltpu.VMEM((frames * UPCH, beams), bf16),
+        ]
+        return call(
+            body, shape, len(args) - 1, flops, 4 << 20, scalars=1, after=len(after), scratch=scratch
+        )(*args, *after)
+
     where = jnp.stack([me, pol]).astype(jnp.int32)
     keep = keep_flags.reshape(1, -1)
+    gain_other = swap(gain)
     x = samples.transpose(0, 2, 1, 3).reshape(samples.shape[0] * 2, CYL * NS)
     x = lax.optimization_barrier(x)
     length = x.shape[0]
     near_at = length - BLOCK * ROWS
     far_at = length - (TAPS - 1) * ROWS
-    near = ahead(x[near_at:])
-    far = ahead(x[far_at:near_at])
-
-    late_powers = powers(
-        functools.partial(local_kernel, kept // BLOCK, kept), kept, filt, x, gain, beam_table
-    )
+    near0 = ahead(x[near_at:], 0)
+    near1 = ahead(x[near_at:], 1)
+    x_other = swap(x)
+    far0 = ahead(x[far_at:near_at], 0)
+    far1 = ahead(x[far_at:near_at], 1)
     table = call(
         functools.partial(place_table_kernel, most_sets),
         jax.ShapeDtypeStruct((n_owner, beams, width), bf16),
@@ -272,18 +294,19 @@
         1 << 24,
         4 << 20,
         scalars=1,
-        after=1,
-    )(where, owner_table.reshape(1, -1), late_powers)
-    late = regroup(late_powers, 1, table)
-    near_powers = powers(near_kernel, BLOCK, filt, near, x, gain, beam_table, after=late[:1])
-    early_near = regroup(near_powers, 0, table)
-    far_powers = powers(
-        far_kernel, BLOCK, filt, edge, far, near, x, gain, beam_table, after=early_near[:1]
-    )
-    early_far = regroup(far_powers, 0, table)
+    )(where, owner_table.reshape(1, -1))
+    common = (gain, gain_other, beam_table, keep, table)
+    body = functools.partial(late_kernel, kept // BLOCK, n_owner)
+    late = form(body, kept, kept * UPCH, where, filt, x, x_other, *common)
+    late_got = spread(late, 1)
+    body = functools.partial(near_kernel, n_owner)
+    near = form(body, BLOCK, BLOCK * UPCH, where, filt, near0, near1, x, x_other, *common, after=late[:1])
+    body = functools.partial(far_kernel, n_owner)
+    early = form(body, BLOCK, kept * UPCH, where, filt, edge, far0, far1, near0, near1, x, x_other, *common, *near)
+    early_got = spread(early, 0)
     out_shape = jax.ShapeDtypeStruct((kept, n_owner * UPCH, width), bf16)
-    return call(functools.partial(gather_kernel, n_owner), out_shape, 3 * n_owner, 0, 3 << 20, scalars=1)(
-        where, *late, *early_near, *early_far
+    return call(functools.partial(gather_kernel, n_owner), out_shape, 2 * n_owner, 0, 3 << 20, scalars=1)(
+        where, *late_got, *early_got
     )
 
 

time: 73.4 us -> 57.6 us (0.78)
  the two profiles are of different devices: /device:TPU:0 before, /device:TPU:14 now
where the time goes in v3:
time: 57.6 us; the launch traced here: 57.2 us
  waiting for transfers between devices  20.1 us (35%)
  starting transfers between devices  16.5 us (29%)
  Pallas kernels  15.4 us (27%)
  local copies, waits for them, and re-layouts  4.84 us (8%)
    pallas_call x3, Pallas kernels, form(): call(body, shape, len(args) - 1, flops, 4 << 20, scalars=1, after=len(aft...  11.9 us
    ppermute x6, starting transfers between devices, spread(): got.append(lax.ppermute(blocks[k], ('freq', 'pol'), route))  11.2 us
    ppermute x6, waiting for transfers between devices, spread(): got.append(lax.ppermute(blocks[k], ('freq', 'pol'), route))  10.8 us
    ppermute x4, waiting for transfers between devices, ahead(): lax.ppermute(part, ('tm', 'pol'), [(i * 2 + source, j * 2) for i, j in pa...  9.33 us
    ppermute x4, starting transfers between devices, ahead(): lax.ppermute(part, ('tm', 'pol'), [(i * 2 + source, j * 2) for i, j in pa...  5.14 us
    transpose x1, local copies, waits for them, and re-layouts, per_device(): x = samples.transpose(0, 2, 1, 3).reshape(samples.shape[0] * 2, CYL * NS)  2.67 us
    pallas_call x1, Pallas kernels, per_device(): call(functools.partial(place_table_kernel, most_sets), jax.ShapeDtypeStru...  1.85 us
    pallas_call x1, Pallas kernels, per_device(): call(functools.partial(gather_kernel, n_owner), out_shape, 2 * n_owner, 0...  1.6 us
  transfers between devices with their start and end apart: 12, of which 6 were waited for; matrix products, arithmetic and copies ran while one was open for 3% of the time, Pallas kernels for 24%

profile of v3, /device:TPU:14, one launch (start us, length us, event | category | flops | bytes accessed | tf_op | source)
XLA Modules:
  0.0 57.2 jit_solution(12956405090630662129)
XLA Ops:
  0.0 2.7 %copy.8 = bf16[512,2,4,256]{3,2,1,0:T(4,128)(2,1)S(1)} copy(bf16[512,2,4,256]{3,1,2,0:T(2,128)(2,1)} %bitcast.26) | data formatting | bytes 4194304 | tf_op jit(solution)/shard_map/transpose | solution.py:280
  2.7 0.0 copy-start.3
  2.7 0.0 copy-start.5
  2.7 0.5 copy.9
  3.2 0.1 collective-permute-start
  3.3 0.8 %slice.11 = bf16[256,1024]{1,0:T(8,128)(2,1)} slice(bf16[1024,1024]{1,0:T(8,128)(2,1)S(1)} %bitcast.12), slice={[768:1024], [0:1024]} | slice | bytes 1048576 | tf_op jit(solution)/shard_map/slice | solution.py:285
  4.1 1.3 %collective-permute-start.8 = (bf16[256,1024]{1,0:T(8,128)(2,1)}, bf16[256,1024]{1,0:T(8,128)(2,1)S(1)}, u32[]{:S(2)}, u32[]{:S(2)}) collective-permute-start(bf16[256,1024]{1,0:T(8,128)(2,1)} %slice.11), channel_id=1, source_target_pairs={{1,2},{5,6},{9,10},{13,14},{17,18},{21,22},{25,26},{29,30}} | collective-permute-start | bytes 1572872 | tf_op jit(solution)/shard_map/ppermute | solution.py:254
  5.4 1.3 %collective-permute-start.7 = (bf16[256,1024]{1,0:T(8,128)(2,1)}, bf16[256,1024]{1,0:T(8,128)(2,1)S(1)}, u32[]{:S(2)}, u32[]{:S(2)}) collective-permute-start(bf16[256,1024]{1,0:T(8,128)(2,1)} %slice.11), channel_id=1, source_target_pairs={{0,2},{4,6},{8,10},{12,14},{16,18},{20,22},{24,26},{28,30}} | collective-permute-start | bytes 1572872 | tf_op jit(solution)/shard_map/ppermute | solution.py:254
  6.7 0.0 copy-done.3
  6.7 0.1 collective-permute-start.1
  6.8 0.8 %slice.10 = bf16[224,1024]{1,0:T(8,128)(2,1)} slice(bf16[1024,1024]{1,0:T(8,128)(2,1)S(1)} %bitcast.13), slice={[544:768], [0:1024]} | slice | bytes 917504 | tf_op jit(solution)/shard_map/slice | solution.py:288
  7.6 1.3 %collective-permute-start.6 = (bf16[224,1024]{1,0:T(8,128)(2,1)}, bf16[224,1024]{1,0:T(8,128)(2,1)}, u32[]{:S(2)}, u32[]{:S(2)}) collective-permute-start(bf16[224,1024]{1,0:T(8,128)(2,1)} %slice.10), channel_id=1, source_target_pairs={{1,2},{5,6},{9,10},{13,14},{17,18},{21,22},{25,26},{29,30}} | collective-permute-start | bytes 1376264 | tf_op jit(solution)/shard_map/ppermute | solution.py:254
  8.9 0.1 pad_add_fusion.refs_0_
  9.0 0.0 copy-done.5
  9.0 0.0 copy-start
  9.0 0.0 copy-start.1
  9.0 0.0 copy-start.4
  9.0 1.8 %shard_map.73.refs_8_.refs_10_.refs_13_ = bf16[4,1024,512]{2,1,0:T(8,128)(2,1)S(1)} custom-call(s32[2]{0:T(128)S(1)} %pad_add_fusion.refs_0_, s32[1,64]{1,0:T(1,128)S(1)} %bitcast.24), custom_call_target="tpu_custom_call" | custom-call | flops 16777216 | bytes 4194304 | tf_op jit(solution)/shard_map/pallas_call | solution.py:290
  10.8 0.0 collective-permute-done.1.refs_5_.refs_7_.refs_10_
  10.8 1.3 %collective-permute-start.5 = (bf16[224,1024]{1,0:T(8,128)(2,1)}, bf16[224,1024]{1,0:T(8,128)(2,1)S(1)}, u32[]{:S(2)}, u32[]{:S(2)}) collective-permute-start(bf16[224,1024]{1,0:T(8,128)(2,1)} %slice.10), channel_id=1, source_target_pairs={{0,2},{4,6},{8,10},{12,14},{16,18},{20,22},{24,26},{28,30}} | collective-permute-start | bytes 1376264 | tf_op jit(solution)/shard_map/ppermute | solution.py:254
  12.1 0.0 collective-permute-done.refs_3_.refs_5_.refs_8_
  12.2 0.0 copy-done
  12.2 0.0 copy-done.1
  12.2 0.0 copy-done.4
  12.2 1.6 %shard_map.74 = (bf16[256,512]{1,0:T(8,128)(2,1)S(1)}, bf16[256,512]{1,0:T(8,128)(2,1)S(1)}, bf16[256,512]{1,0:T(8,128)(2,1)S(1)}, bf16[256,512]{1,0:T(8,128)(2,1)S(1)}) custom-call(s32[2]{0:T(128)S(1)} %pad_add_fusion.refs_0_, bf16[512,768]{1,0:T(8,128)(2,1)S(1)} %copy-done, bf16[1024,1024]{1,0:T(8,128)(2,1)S(1)} %bitcast.14, ...), custom_call_target="tpu_custom_call" | custom-call | flops 4294967296 | bytes 4194304 | tf_op jit(solution)/shard_map/pallas_call | solution.py:273
  13.8 0.7 %collective-permute-start.2 = (bf16[256,512]{1,0:T(8,128)(2,1)S(1)}, bf16[256,512]{1,0:T(8,128)(2,1)S(1)}, u32[]{:S(2)}, u32[]{:S(2)}) collective-permute-start(bf16[256,512]{1,0:T(8,128)(2,1)S(1)} %get-tuple-element.18), channel_id=1, source_target_pairs={{1,5},{5,1},{9,13},{13,9},{3,7},{7,3},{11,15},{15,11},{17,21},{21,... | collective-permute-start | bytes 786440 | tf_op jit(solution)/shard_map/ppermute | solution.py:263
  14.5 4.0 %collective-permute-done.8.refs_3_.refs_6_ = bf16[256,1024]{1,0:T(8,128)(2,1)S(1)} collective-permute-done((bf16[256,1024]{1,0:T(8,128)(2,1)}, bf16[256,1024]{1,0:T(8,128)(2,1)S(1)}, u32[]{:S(2)}, u32[]{:S(2)}) %collective-permute-start.8) | collective-permute-done | bytes 524320 | tf_op jit(solution)/shard_map/ppermute | solution.py:254
  18.5 0.7 %collective-permute-start.3 = (bf16[256,512]{1,0:T(8,128)(2,1)S(1)}, bf16[256,512]{1,0:T(8,128)(2,1)S(1)}, u32[]{:S(2)}, u32[]{:S(2)}) collective-permute-start(bf16[256,512]{1,0:T(8,128)(2,1)S(1)} %get-tuple-element.19), channel_id=1, source_target_pairs={{1,9},{5,13},{9,1},{13,5},{3,11},{7,15},{11,3},{15,7},{17,25},{21,... | collective-permute-start | bytes 786440 | tf_op jit(solution)/shard_map/ppermute | solution.py:263
  19.2 3.1 %collective-permute-done.7.refs_2_.refs_5_ = bf16[256,1024]{1,0:T(8,128)(2,1)S(1)} collective-permute-done((bf16[256,1024]{1,0:T(8,128)(2,1)}, bf16[256,1024]{1,0:T(8,128)(2,1)S(1)}, u32[]{:S(2)}, u32[]{:S(2)}) %collective-permute-start.7) | collective-permute-done | bytes 524320 | tf_op jit(solution)/shard_map/ppermute | solution.py:254
  22.3 0.7 %collective-permute-start.4 = (bf16[256,512]{1,0:T(8,128)(2,1)S(1)}, bf16[256,512]{1,0:T(8,128)(2,1)S(1)}, u32[]{:S(2)}, u32[]{:S(2)}) collective-permute-start(bf16[256,512]{1,0:T(8,128)(2,1)S(1)} %get-tuple-element.20), channel_id=1, source_target_pairs={{1,13},{5,9},{9,5},{13,1},{3,15},{7,11},{11,7},{15,3},{17,29},{21,... | collective-permute-start | bytes 786440 | tf_op jit(solution)/shard_map/ppermute | solution.py:263
  23.0 0.0 copy-start.2
  23.0 5.1 %shard_map.75 = (bf16[128,512]{1,0:T(8,128)(2,1)S(1)}, bf16[128,512]{1,0:T(8,128)(2,1)S(1)}, bf16[128,512]{1,0:T(8,128)(2,1)S(1)}, bf16[128,512]{1,0:T(8,128)(2,1)S(1)}) custom-call(s32[2]{0:T(128)S(1)} %pad_add_fusion.refs_0_, bf16[512,768]{1,0:T(8,128)(2,1)S(1)} %copy-done, bf16[256,1024]{1,0:T(8,128)(2,1)S(1)} %collective-permute-done.7.refs_2_.refs_5_, ...), custom_call_target="tpu_custom_call" | custom-call | flops 2147483648 | bytes 4194304 | tf_op jit(solution)/shard_map/pallas_call | solution.py:273
  28.0 0.4 collective-permute-done.6.refs_4_
  28.5 1.8 %collective-permute-done.5.refs_3_ = bf16[224,1024]{1,0:T(8,128)(2,1)S(1)} collective-permute-done((bf16[224,1024]{1,0:T(8,128)(2,1)}, bf16[224,1024]{1,0:T(8,128)(2,1)S(1)}, u32[]{:S(2)}, u32[]{:S(2)}) %collective-permute-start.5) | collective-permute-done | bytes 458784 | tf_op jit(solution)/shard_map/ppermute | solution.py:254
  30.2 0.0 copy-done.2
  30.3 5.3 %shard_map.76 = (bf16[256,512]{1,0:T(8,128)(2,1)S(1)}, bf16[256,512]{1,0:T(8,128)(2,1)S(1)}, bf16[256,512]{1,0:T(8,128)(2,1)S(1)}, bf16[256,512]{1,0:T(8,128)(2,1)S(1)}) custom-call(s32[2]{0:T(128)S(1)} %pad_add_fusion.refs_0_, bf16[512,768]{1,0:T(8,128)(2,1)S(1)} %copy-done, bf16[512,224]{1,0:T(8,128)(2,1)S(1)} %copy-done.2, ...), custom_call_target="tpu_custom_call" | custom-call | flops 2147483648 | bytes 4194304 | tf_op jit(solution)/shard_map/pallas_call | solution.py:273
  35.5 2.3 %collective-permute-start.9 = (bf16[256,512]{1,0:T(8,128)(2,1)S(1)}, bf16[256,512]{1,0:T(8,128)(2,1)S(1)}, u32[]{:S(2)}, u32[]{:S(2)}) collective-permute-start(bf16[256,512]{1,0:T(8,128)(2,1)S(1)} %get-tuple-element.26), channel_id=1, source_target_pairs={{0,4},{4,0},{8,12},{12,8},{2,6},{6,2},{10,14},{14,10},{16,20},{20,... | collective-permute-start | bytes 786440 | tf_op jit(solution)/shard_map/ppermute | solution.py:263
  37.9 4.5 %collective-permute-start.10 = (bf16[256,512]{1,0:T(8,128)(2,1)S(1)}, bf16[256,512]{1,0:T(8,128)(2,1)S(1)}, u32[]{:S(2)}, u32[]{:S(2)}) collective-permute-start(bf16[256,512]{1,0:T(8,128)(2,1)S(1)} %get-tuple-element.27), channel_id=1, source_target_pairs={{0,8},{4,12},{8,0},{12,4},{2,10},{6,14},{10,2},{14,6},{16,24},{20,... | collective-permute-start | bytes 786440 | tf_op jit(solution)/shard_map/ppermute | solution.py:263
  42.4 0.0 collective-permute-done.2.refs_2_
  42.4 2.4 %collective-permute-start.11 = (bf16[256,512]{1,0:T(8,128)(2,1)S(1)}, bf16[256,512]{1,0:T(8,128)(2,1)S(1)}, u32[]{:S(2)}, u32[]{:S(2)}) collective-permute-start(bf16[256,512]{1,0:T(8,128)(2,1)S(1)} %get-tuple-element.28), channel_id=1, source_target_pairs={{0,12},{4,8},{8,4},{12,0},{2,14},{6,10},{10,6},{14,2},{16,28},{20,... | collective-permute-start | bytes 786440 | tf_op jit(solution)/shard_map/ppermute | solution.py:263
  44.8 0.0 collective-permute-done.3.refs_3_
  44.8 0.0 collective-permute-done.4.refs_4_
  44.8 0.0 collective-permute-done.9.refs_6_
  44.8 7.1 %collective-permute-done.10.refs_7_ = bf16[256,512]{1,0:T(8,128)(2,1)S(1)} collective-permute-done((bf16[256,512]{1,0:T(8,128)(2,1)S(1)}, bf16[256,512]{1,0:T(8,128)(2,1)S(1)}, u32[]{:S(2)}, u32[]{:S(2)}) %collective-permute-start.10) | collective-permute-done | bytes 262176 | tf_op jit(solution)/shard_map/ppermute | solution.py:263
  51.9 3.7 %collective-permute-done.11.refs_8_ = bf16[256,512]{1,0:T(8,128)(2,1)S(1)} collective-permute-done((bf16[256,512]{1,0:T(8,128)(2,1)S(1)}, bf16[256,512]{1,0:T(8,128)(2,1)S(1)}, u32[]{:S(2)}, u32[]{:S(2)}) %collective-permute-start.11) | collective-permute-done | bytes 262176 | tf_op jit(solution)/shard_map/ppermute | solution.py:263
  55.6 1.6 %shard_map.77 = bf16[16,64,512]{2,1,0:T(8,128)(2,1)} custom-call(s32[2]{0:T(128)S(1)} %pad_add_fusion.refs_0_, bf16[256,512]{1,0:T(8,128)(2,1)S(1)} %get-tuple-element.17.refs_11_.refs_1_, bf16[256,512]{1,0:T(8,128)(2,1)S(1)} %collective-permute-done.2.refs_2_, bf16[256,512]{1,0:T(8,128)(2,1)S(1)} %collective-permute-done.3.refs_3_, ...), custom_call_target="tpu_custom_call" | custom-call | bytes 3145728 | tf_op jit(solution)/shard_map/pallas_call | solution.py:308
Async XLA Ops:
  2.7 4.0 %copy-start.3 = (f32[1,1,4,2,256]{4,3,2,1,0:T(2,128)S(1)}, f32[1,1,4,2,256]{4,3,2,1,0:T(2,128)}, u32[]{:S(2)}) copy-start(f32[1,1,4,2,256]{4,3,2,1,0:T(2,128)} %param.8) | copy-start | bytes 24580
  2.7 6.3 %copy-start.5 = (s32[64]{0:T(128)S(1)}, s32[64]{0:T(128)}, u32[]{:S(2)}) copy-start(s32[64]{0:T(128)} %param.9) | copy-start | bytes 772
  3.2 9.0 %collective-permute-start = (bf16[1024,1024]{1,0:T(8,128)(2,1)S(1)}, bf16[1024,1024]{1,0:T(8,128)(2,1)}, u32[]{:S(2)}, u32[]{:S(2)}) collective-permute-start(bf16[1024,1024]{1,0:T(8,128)(2,1)S(1)} %bitcast.11), channel_id=1, source_target_pairs={{0,1},{1,0},{2,3},{3,2},{4,5},{5,4},{6,7},{7,6},{8,9},{9,8},{10,11... | collective-permute-start | bytes 6291464 | tf_op jit(solution)/shard_map/ppermute | solution.py:257
  4.1 14.4 %collective-permute-start.8 = (bf16[256,1024]{1,0:T(8,128)(2,1)}, bf16[256,1024]{1,0:T(8,128)(2,1)S(1)}, u32[]{:S(2)}, u32[]{:S(2)}) collective-permute-start(bf16[256,1024]{1,0:T(8,128)(2,1)} %slice.11), channel_id=1, source_target_pairs={{1,2},{5,6},{9,10},{13,14},{17,18},{21,22},{25,26},{29,30}} | collective-permute-start | bytes 1572872 | tf_op jit(solution)/shard_map/ppermute | solution.py:254
  5.4 16.9 %collective-permute-start.7 = (bf16[256,1024]{1,0:T(8,128)(2,1)}, bf16[256,1024]{1,0:T(8,128)(2,1)S(1)}, u32[]{:S(2)}, u32[]{:S(2)}) collective-permute-start(bf16[256,1024]{1,0:T(8,128)(2,1)} %slice.11), channel_id=1, source_target_pairs={{0,2},{4,6},{8,10},{12,14},{16,18},{20,22},{24,26},{28,30}} | collective-permute-start | bytes 1572872 | tf_op jit(solution)/shard_map/ppermute | solution.py:254
  6.7 4.1 %collective-permute-start.1 = (f32[4,2,256]{2,1,0:T(2,128)S(1)}, f32[4,2,256]{2,1,0:T(2,128)S(1)}, u32[]{:S(2)}, u32[]{:S(2)}) collective-permute-start(f32[4,2,256]{2,1,0:T(2,128)S(1)} %bitcast.17), channel_id=1, source_target_pairs={{0,1},{1,0},{2,3},{3,2},{4,5},{5,4},{6,7},{7,6},{8,9},{9,8},{10,11... | collective-permute-start | bytes 24584 | tf_op jit(solution)/shard_map/ppermute | solution.py:257
  7.6 20.9 %collective-permute-start.6 = (bf16[224,1024]{1,0:T(8,128)(2,1)}, bf16[224,1024]{1,0:T(8,128)(2,1)}, u32[]{:S(2)}, u32[]{:S(2)}) collective-permute-start(bf16[224,1024]{1,0:T(8,128)(2,1)} %slice.10), channel_id=1, source_target_pairs={{1,2},{5,6},{9,10},{13,14},{17,18},{21,22},{25,26},{29,30}} | collective-permute-start | bytes 1376264 | tf_op jit(solution)/shard_map/ppermute | solution.py:254
  9.0 3.2 %copy-start = (bf16[512,768]{1,0:T(8,128)(2,1)S(1)}, bf16[512,768]{1,0:T(8,128)(2,1)}, u32[]{:S(2)}) copy-start(bf16[512,768]{1,0:T(8,128)(2,1)} %constant.15.clone.refs_1_) | copy-start | bytes 2359300
  9.0 3.2 %copy-start.1 = (bf16[512,512]{1,0:T(8,128)(2,1)S(1)}, bf16[512,512]{1,0:T(8,128)(2,1)}, u32[]{:S(2)}) copy-start(bf16[512,512]{1,0:T(8,128)(2,1)} %constant.17.clone.refs_6_.refs_8_.refs_11_) | copy-start | bytes 1572868
  9.0 3.2 %copy-start.4 = (s32[1024]{0:T(1024)S(1)}, s32[1024]{0:T(1024)}, u32[]{:S(2)}) copy-start(s32[1024]{0:T(1024)} %param.10) | copy-start | bytes 12292
  10.8 19.4 %collective-permute-start.5 = (bf16[224,1024]{1,0:T(8,128)(2,1)}, bf16[224,1024]{1,0:T(8,128)(2,1)S(1)}, u32[]{:S(2)}, u32[]{:S(2)}) collective-permute-start(bf16[224,1024]{1,0:T(8,128)(2,1)} %slice.10), channel_id=1, source_target_pairs={{0,2},{4,6},{8,10},{12,14},{16,18},{20,22},{24,26},{28,30}} | collective-permute-start | bytes 1376264 | tf_op jit(solution)/shard_map/ppermute | solution.py:254
  13.8 28.6 %collective-permute-start.2 = (bf16[256,512]{1,0:T(8,128)(2,1)S(1)}, bf16[256,512]{1,0:T(8,128)(2,1)S(1)}, u32[]{:S(2)}, u32[]{:S(2)}) collective-permute-start(bf16[256,512]{1,0:T(8,128)(2,1)S(1)} %get-tuple-element.18), channel_id=1, source_target_pairs={{1,5},{5,1},{9,13},{13,9},{3,7},{7,3},{11,15},{15,11},{17,21},{21,... | collective-permute-start | bytes 786440 | tf_op jit(solution)/shard_map/ppermute | solution.py:263
  18.5 26.2 %collective-permute-start.3 = (bf16[256,512]{1,0:T(8,128)(2,1)S(1)}, bf16[256,512]{1,0:T(8,128)(2,1)S(1)}, u32[]{:S(2)}, u32[]{:S(2)}) collective-permute-start(bf16[256,512]{1,0:T(8,128)(2,1)S(1)} %get-tuple-element.19), channel_id=1, source_target_pairs={{1,9},{5,13},{9,1},{13,5},{3,11},{7,15},{11,3},{15,7},{17,25},{21,... | collective-permute-start | bytes 786440 | tf_op jit(solution)/shard_map/ppermute | solution.py:263
  22.3 22.5 %collective-permute-start.4 = (bf16[256,512]{1,0:T(8,128)(2,1)S(1)}, bf16[256,512]{1,0:T(8,128)(2,1)S(1)}, u32[]{:S(2)}, u32[]{:S(2)}) collective-permute-start(bf16[256,512]{1,0:T(8,128)(2,1)S(1)} %get-tuple-element.20), channel_id=1, source_target_pairs={{1,13},{5,9},{9,5},{13,1},{3,15},{7,11},{11,7},{15,3},{17,29},{21,... | collective-permute-start | bytes 786440 | tf_op jit(solution)/shard_map/ppermute | solution.py:263
  23.0 7.3 %copy-start.2 = (bf16[512,224]{1,0:T(8,128)(2,1)S(1)}, bf16[512,224]{1,0:T(8,128)(2,1)}, u32[]{:S(2)}) copy-start(bf16[512,224]{1,0:T(8,128)(2,1)} %constant.16.clone.refs_2_) | copy-start | bytes 688132
  35.5 9.3 %collective-permute-start.9 = (bf16[256,512]{1,0:T(8,128)(2,1)S(1)}, bf16[256,512]{1,0:T(8,128)(2,1)S(1)}, u32[]{:S(2)}, u32[]{:S(2)}) collective-permute-start(bf16[256,512]{1,0:T(8,128)(2,1)S(1)} %get-tuple-element.26), channel_id=1, source_target_pairs={{0,4},{4,0},{8,12},{12,8},{2,6},{6,2},{10,14},{14,10},{16,20},{20,... | collective-permute-start | bytes 786440 | tf_op jit(solution)/shard_map/ppermute | solution.py:263
  37.9 14.0 %collective-permute-start.10 = (bf16[256,512]{1,0:T(8,128)(2,1)S(1)}, bf16[256,512]{1,0:T(8,128)(2,1)S(1)}, u32[]{:S(2)}, u32[]{:S(2)}) collective-permute-start(bf16[256,512]{1,0:T(8,128)(2,1)S(1)} %get-tuple-element.27), channel_id=1, source_target_pairs={{0,8},{4,12},{8,0},{12,4},{2,10},{6,14},{10,2},{14,6},{16,24},{20,... | collective-permute-start | bytes 786440 | tf_op jit(solution)/shard_map/ppermute | solution.py:263
  42.4 13.2 %collective-permute-start.11 = (bf16[256,512]{1,0:T(8,128)(2,1)S(1)}, bf16[256,512]{1,0:T(8,128)(2,1)S(1)}, u32[]{:S(2)}, u32[]{:S(2)}) collective-permute-start(bf16[256,512]{1,0:T(8,128)(2,1)S(1)} %get-tuple-element.28), channel_id=1, source_target_pairs={{0,12},{4,8},{8,4},{12,0},{2,14},{6,10},{10,6},{14,2},{16,28},{20,... | collective-permute-start | bytes 786440 | tf_op jit(solution)/shard_map/ppermute | solution.py:263

commit v4 on v3

--- a/solution.py
+++ b/solution.py
@@ -61,18 +61,10 @@
     return (table.astype(np.float32) * 0.5).astype(jnp.bfloat16)
 
 
-def columns(cyl):
-    return slice(cyl * NS, (cyl + 1) * NS)
-
-
-def form_powers(parts, gain_ref, beam_ref, cal_ref, emit):
+def form_powers(spectra, gain_ref, beam_ref, cal_ref, emit):
     half = BLOCK * UPCH
     for cyl in range(CYL):
-        total = None
-        for table, samples in parts(cyl):
-            term = jnp.dot(table, samples, preferred_element_type=jnp.float32)
-            total = term if total is None else total + term
-        spec = total[: 2 * half] + total[2 * half :]
+        spec = spectra(cyl)
         real, imag = spec[:half], spec[half:]
         gain_real = gain_ref[cyl, 0:1, :]
         gain_imag = gain_ref[cyl, 1:2, :]
@@ -94,7 +86,39 @@
             emit(element * NS + strip * LANES, fr * fr + fi * fi)
 
 
-def sum_block(parts_of, gains, beam_ref, keep_ref, cal_ref, sum_ref, at):
+def filtered(table, x_ref, cyl, start, count):
+    strips = NS // LANES
+    rows = [
+        x_ref[cyl * strips + strip, pl.ds(start, count)].reshape(2 * count, LANES) for strip in range(strips)
+    ]
+    both = jnp.dot(table, jnp.concatenate(rows, axis=1), preferred_element_type=jnp.float32)
+    return both[: both.shape[0] // 2] + both[both.shape[0] // 2 :]
+
+
+def fetches(source_ref, first, count, x_ref, at, sems):
+    strips = NS // LANES
+    return [
+        pltpu.make_async_copy(
+            source_ref.at[pl.ds(first, count), j // strips, :, pl.ds(j % strips * LANES, LANES)],
+            x_ref.at[j, pl.ds(at, count)],
+            sems.at[j],
+        )
+        for j in range(CYL * strips)
+    ]
+
+
+def start(copies):
+    for copy in copies:
+        copy.start()
+
+
+def wait_cylinder(copies, cyl):
+    strips = NS // LANES
+    for copy in copies[cyl * strips : (cyl + 1) * strips]:
+        copy.wait()
+
+
+def adder(pol, sum_ref, keep_ref, at):
     rows = pl.ds(at, BLOCK * UPCH)
 
     def first(column, power):
@@ -105,8 +129,7 @@
         total = sum_ref[rows, lanes].astype(jnp.float32) + power.astype(jnp.bfloat16).astype(jnp.float32)
         sum_ref[rows, lanes] = (total * keep_ref[:, lanes].astype(jnp.float32)).astype(jnp.bfloat16)
 
-    form_powers(parts_of(0), gains[0], beam_ref, cal_ref, first)
-    form_powers(parts_of(1), gains[1], beam_ref, cal_ref, second)
+    return (first, second)[pol]
 
 
 def place(sum_ref, table_ref, out_refs, rows):
@@ -115,64 +138,86 @@
         out_ref[rows, :] = placed.astype(jnp.bfloat16)
 
 
-def late_kernel(blocks, n_owner, where_ref, filt_ref, x0, x1, g0, g1, beam_ref, keep_ref, table_ref, *refs):
-    out_refs, (cal_ref, sum_ref) = refs[:n_owner], refs[n_owner:]
-    depth = (TAPS + BLOCK) * ROWS
+def late_kernel(blocks, n_owner, where_ref, filt_ref, g0, g1, beam_ref, keep_ref, table_ref, v0, v1, *refs):
+    out_refs, (cal_ref, sum_ref, x0, x1, sems) = refs[:n_owner], refs[n_owner:]
+    depth = (TAPS + BLOCK) * UPCH
+    length = x0.shape[1]
 
     @pl.when(where_ref[1] == 1)
     def _():
-        def step(block, carry):
-            start = pl.multiple_of(block * BLOCK * ROWS, BLOCK * ROWS)
-
-            def parts_of(pol):
-                return lambda cyl: [(filt_ref[...], (x0, x1)[pol][pl.ds(start, depth), columns(cyl)])]
-
-            at = pl.multiple_of(block * BLOCK * UPCH, BLOCK * UPCH)
-            sum_block(parts_of, (g0, g1), beam_ref, keep_ref, cal_ref, sum_ref, at)
-            return carry
-
-        lax.fori_loop(0, blocks, step, 0)
+        copies = [fetches(v, 0, length, x, 0, sems.at[pol]) for pol, (v, x) in enumerate(((v0, x0), (v1, x1)))]
+        start(copies[0])
+        start(copies[1])
+        for pol, (x, gain) in enumerate(((x0, g0), (x1, g1))):
+
+            def step(block, carry, pol=pol, x=x, gain=gain):
+                at = pl.multiple_of(block * BLOCK * UPCH, BLOCK * UPCH)
+
+                def spectra(cyl):
+                    @pl.when(block == 0)
+                    def _():
+                        wait_cylinder(copies[pol], cyl)
+
+                    return filtered(filt_ref[...], x, cyl, at, depth)
+
+                form_powers(spectra, gain, beam_ref, cal_ref, adder(pol, sum_ref, keep_ref, at))
+                return carry
+
+            lax.fori_loop(0, blocks, step, 0)
         place(sum_ref, table_ref, out_refs, slice(None))
 
 
-def near_kernel(n_owner, where_ref, filt_ref, n0, n1, x0, x1, g0, g1, beam_ref, keep_ref, table_ref, *refs):
-    out_refs, (cal_ref, sum_ref) = refs[:n_owner], refs[n_owner:]
-    reach = BLOCK * ROWS
+def near_kernel(n_owner, where_ref, filt_ref, g0, g1, beam_ref, keep_ref, table_ref, n0, n1, v0, v1, *refs):
+    out_refs, pre_ref, (cal_ref, sum_ref, x0, x1, sems) = refs[:n_owner], refs[n_owner], refs[n_owner + 1 :]
+    reach = BLOCK * UPCH
 
     @pl.when(where_ref[1] == 0)
     def _():
-        def parts_of(pol):
-            near, x = (n0, n1)[pol], (x0, x1)[pol]
-            return lambda cyl: [
-                (filt_ref[:, :reach], near[:, columns(cyl)]),
-                (filt_ref[:, reach:], x[: 2 * reach, columns(cyl)]),
-            ]
-
-        sum_block(parts_of, (g0, g1), beam_ref, keep_ref, cal_ref, sum_ref, 0)
+        copies = []
+        for pol, (v, n, x) in enumerate(((v0, n0, x0), (v1, n1, x1))):
+            here = fetches(v, 0, 2 * reach, x, reach, sems.at[pol, 0])
+            there = fetches(n, 0, reach, x, 0, sems.at[pol, 1])
+            for a, b in zip(here, there):
+                a.start()
+                b.start()
+            copies.append((here, there))
+        for pol, (x, gain) in enumerate(((x0, g0), (x1, g1))):
+
+            def spectra(cyl, pol=pol, x=x):
+                wait_cylinder(copies[pol][0], cyl)
+                wait_cylinder(copies[pol][1], cyl)
+                pre_ref[pol * CYL + cyl] = filtered(filt_ref[:, 2 * reach :], x, cyl, 0, 2 * reach)
+                return filtered(filt_ref[...], x, cyl, 0, 3 * reach)
+
+            form_powers(spectra, gain, beam_ref, cal_ref, adder(pol, sum_ref, keep_ref, 0))
         place(sum_ref, table_ref, out_refs, slice(None))
 
 
-def far_kernel(
-    n_owner, where_ref, filt_ref, edge_ref, f0, f1, n0, n1, x0, x1, g0, g1, beam_ref, keep_ref, table_ref, *refs
-):
-    near_refs, out_refs, (cal_ref, sum_ref) = refs[:n_owner], refs[n_owner : 2 * n_owner], refs[2 * n_owner :]
-    reach = BLOCK * ROWS
+def far_kernel(n_owner, where_ref, filt_ref, g0, g1, beam_ref, keep_ref, table_ref, pre_ref, *refs):
+    near_refs, (f0, f1), refs = refs[:n_owner], refs[n_owner : n_owner + 2], refs[n_owner + 2 :]
+    out_refs, (cal_ref, sum_ref, x0, x1, sems) = refs[:n_owner], refs[n_owner:]
     half = BLOCK * UPCH
+    reach = BLOCK * UPCH
+    length = f0.shape[0]
+    skip = reach - length
 
     @pl.when(where_ref[1] == 0)
     def _():
-        def parts_of(pol):
-            far, near, x = (f0, f1)[pol], (n0, n1)[pol], (x0, x1)[pol]
-            return lambda cyl: [
-                (filt_ref[:, reach : 2 * reach], near[:, columns(cyl)]),
-                (filt_ref[:, 2 * reach :], x[:reach, columns(cyl)]),
-                (edge_ref[...], far[:, columns(cyl)]),
-            ]
-
-        sum_block(parts_of, (g0, g1), beam_ref, keep_ref, cal_ref, sum_ref, 0)
-        place(sum_ref, table_ref, out_refs, slice(0, half))
+        for x in (x0, x1):
+            x[:, :skip] = jnp.zeros((x.shape[0], skip, *x.shape[2:]), x.dtype)
+        copies = [fetches(f, 0, length, x, skip, sems.at[pol]) for pol, (f, x) in enumerate(((f0, x0), (f1, x1)))]
+        start(copies[0])
+        start(copies[1])
         for near_ref, out_ref in zip(near_refs, out_refs):
             out_ref[half:, :] = near_ref[...]
+        for pol, (x, gain) in enumerate(((x0, g0), (x1, g1))):
+
+            def spectra(cyl, pol=pol, x=x):
+                wait_cylinder(copies[pol], cyl)
+                return pre_ref[pol * CYL + cyl] + filtered(filt_ref[:, : 2 * reach], x, cyl, 0, reach)
+
+            form_powers(spectra, gain, beam_ref, cal_ref, adder(pol, sum_ref, keep_ref, 0))
+        place(sum_ref, table_ref, out_refs, slice(0, half))
 
 
 def place_table_kernel(most_sets, where_ref, owner_ref, out_ref):
@@ -211,17 +256,17 @@
 ANY = pl.BlockSpec(memory_space=pl.ANY)
 
 
-def call(body, out_shape, n_in, flops, nbytes, scalars=0, after=0, scratch=()):
+def call(body, out_shape, n_in, flops, nbytes, scalars=0, whole=0, after=0, scratch=()):
     many = isinstance(out_shape, (list, tuple))
 
     def kernel(*refs):
-        seen = scalars + n_in
+        seen = scalars + n_in + whole
         body(*refs[:seen], *refs[seen + after :])
 
     return pl.pallas_call(
         kernel,
         out_shape=out_shape,
-        in_specs=[SMEM] * scalars + [VMEM] * n_in + [ANY] * after,
+        in_specs=[SMEM] * scalars + [VMEM] * n_in + [ANY] * (whole + after),
         out_specs=[VMEM] * len(out_shape) if many else VMEM,
         scratch_shapes=list(scratch),
         cost_estimate=pl.CostEstimate(flops=flops, bytes_accessed=nbytes, transcendentals=0),
@@ -245,7 +290,6 @@
     width = most_sets * SET_BEAMS
     bf16 = jnp.bfloat16
     filt = jnp.asarray(filter_matrix())
-    edge = jnp.asarray(filter_matrix()[:, ROWS : BLOCK * ROWS])
     beam_table = jnp.asarray(beam_matrix())
 
     pairs = [(i, i + 1) for i in range(n_tm - 1)]
@@ -263,30 +307,40 @@
             got.append(lax.ppermute(blocks[k], ("freq", "pol"), route))
         return got
 
-    def form(body, frames, rows_out, *args, after=()):
+    def form(body, frames, rows_out, held, sem_shape, arrays, raw, after=(), more=()):
         flops = frames // BLOCK * 4 * 512 * 1024 * 1024
         shape = [jax.ShapeDtypeStruct((rows_out, width), bf16)] * n_owner
+        strips = CYL * NS // LANES
         scratch = [
             pltpu.VMEM((CYL * BLOCK * UPCH, 2 * NS), bf16),
             pltpu.VMEM((frames * UPCH, beams), bf16),
+            pltpu.VMEM((strips, held, 2, LANES), bf16),
+            pltpu.VMEM((strips, held, 2, LANES), bf16),
+            pltpu.SemaphoreType.DMA(sem_shape + (strips,)),
         ]
         return call(
-            body, shape, len(args) - 1, flops, 4 << 20, scalars=1, after=len(after), scratch=scratch
-        )(*args, *after)
+            body,
+            shape + list(more),
+            len(arrays),
+            flops,
+            4 << 20,
+            scalars=1,
+            whole=len(raw),
+            after=len(after),
+            scratch=scratch,
+        )(where, *arrays, *raw, *after)
 
     where = jnp.stack([me, pol]).astype(jnp.int32)
     keep = keep_flags.reshape(1, -1)
+    length = samples.shape[0]
+    near_at = length - BLOCK * UPCH
+    far_at = length - (TAPS - 1) * UPCH
+    near0 = ahead(samples[near_at:], 0)
+    near1 = ahead(samples[near_at:], 1)
+    other = swap(samples)
     gain_other = swap(gain)
-    x = samples.transpose(0, 2, 1, 3).reshape(samples.shape[0] * 2, CYL * NS)
-    x = lax.optimization_barrier(x)
-    length = x.shape[0]
-    near_at = length - BLOCK * ROWS
-    far_at = length - (TAPS - 1) * ROWS
-    near0 = ahead(x[near_at:], 0)
-    near1 = ahead(x[near_at:], 1)
-    x_other = swap(x)
-    far0 = ahead(x[far_at:near_at], 0)
-    far1 = ahead(x[far_at:near_at], 1)
+    far0 = ahead(samples[far_at:near_at], 0)
+    far1 = ahead(samples[far_at:near_at], 1)
     table = call(
         functools.partial(place_table_kernel, most_sets),
         jax.ShapeDtypeStruct((n_owner, beams, width), bf16),
@@ -296,13 +350,37 @@
         scalars=1,
     )(where, owner_table.reshape(1, -1))
     common = (gain, gain_other, beam_table, keep, table)
-    body = functools.partial(late_kernel, kept // BLOCK, n_owner)
-    late = form(body, kept, kept * UPCH, where, filt, x, x_other, *common)
+    late = form(
+        functools.partial(late_kernel, kept // BLOCK, n_owner),
+        kept,
+        kept * UPCH,
+        length,
+        (2,),
+        (filt, *common),
+        (samples, other),
+    )
     late_got = spread(late, 1)
-    body = functools.partial(near_kernel, n_owner)
-    near = form(body, BLOCK, BLOCK * UPCH, where, filt, near0, near1, x, x_other, *common, after=late[:1])
-    body = functools.partial(far_kernel, n_owner)
-    early = form(body, BLOCK, kept * UPCH, where, filt, edge, far0, far1, near0, near1, x, x_other, *common, *near)
+    reach = BLOCK * UPCH
+    *near, pre = form(
+        functools.partial(near_kernel, n_owner),
+        BLOCK,
+        reach,
+        3 * reach,
+        (2, 2),
+        (filt, *common),
+        (near0, near1, samples, other),
+        after=late[:1],
+        more=[jax.ShapeDtypeStruct((2 * CYL, 2 * reach, NS), jnp.float32)],
+    )
+    early = form(
+        functools.partial(far_kernel, n_owner),
+        BLOCK,
+        kept * UPCH,
+        reach,
+        (2,),
+        (filt, *common, pre, *near),
+        (far0, far1),
+    )
     early_got = spread(early, 0)
     out_shape = jax.ShapeDtypeStruct((kept, n_owner * UPCH, width), bf16)
     return call(functools.partial(gather_kernel, n_owner), out_shape, 2 * n_owner, 0, 3 << 20, scalars=1)(

time: 57.6 us -> 62.8 us (1.090)
  the two profiles are of different devices: /device:TPU:14 before, /device:TPU:0 now
where the time goes in v4:
time: 62.8 us; the launch traced here: 62 us
  starting transfers between devices  21.3 us (34%)
  Pallas kernels  21.3 us (34%)
  waiting for transfers between devices  14.2 us (23%)
  local copies, waits for them, and re-layouts  4.97 us (8%)
    pallas_call x3, Pallas kernels, form(): call(body, shape + list(more), len(arrays), flops, 4 << 20, scalars=1, wh...  17.8 us
    ppermute x6, waiting for transfers between devices, spread(): got.append(lax.ppermute(blocks[k], ('freq', 'pol'), route))  12.8 us
    ppermute x6, starting transfers between devices, spread(): got.append(lax.ppermute(blocks[k], ('freq', 'pol'), route))  12.1 us
    ppermute x4, starting transfers between devices, ahead(): lax.ppermute(part, ('tm', 'pol'), [(i * 2 + source, j * 2) for i, j in pa...  7.85 us
    slice x1, local copies, waits for them, and re-layouts, per_device(): near0 = ahead(samples[near_at:], 0)  2.19 us
    slice x1, local copies, waits for them, and re-layouts, per_device(): far0 = ahead(samples[far_at:near_at], 0)  2.1 us
    pallas_call x1, Pallas kernels, per_device(): call(functools.partial(place_table_kernel, most_sets), jax.ShapeDtypeStru...  1.85 us
    pallas_call x1, Pallas kernels, per_device(): call(functools.partial(gather_kernel, n_owner), out_shape, 2 * n_owner, 0...  1.6 us
  transfers between devices with their start and end apart: 12, of which 3 were waited for; matrix products, arithmetic and copies ran while one was open for 7% of the time, Pallas kernels for 32%

profile of v4, /device:TPU:0, one launch (start us, length us, event | category | flops | bytes accessed | tf_op | source)
XLA Modules:
  0.0 62.0 jit_solution(2535971233427898410)
XLA Ops:
  0.0 0.5 collective-permute-start.1
  0.5 2.2 %slice_bitcast_fusion = bf16[128,4,2,256]{3,2,1,0:T(2,128)(2,1)} fusion(bf16[1,1,512,4,2,256]{5,4,3,2,1,0:T(2,128)(2,1)} %param.6), kind=kLoop, calls=%fused_computation | loop fusion | bytes 1048576 | tf_op jit(solution)/shard_map/slice | solution.py:338
  2.7 4.4 %collective-permute-start.5 = (bf16[128,4,2,256]{3,2,1,0:T(2,128)(2,1)}, bf16[128,4,2,256]{3,2,1,0:T(2,128)(2,1)S(1)}, u32[]{:S(2)}, u32[]{:S(2)}) collective-permute-start(bf16[128,4,2,256]{3,2,1,0:T(2,128)(2,1)} %slice_bitcast_fusion), channel_id=1, source_target_pairs={{0,2},{4,6},{8,10},{12,14},{16,18},{20,22},{24,26},{28,30}} | collective-permute-start | bytes 1572872 | tf_op jit(solution)/shard_map/ppermute | solution.py:298
  7.1 0.7 %collective-permute-start.6 = (bf16[128,4,2,256]{3,2,1,0:T(2,128)(2,1)}, bf16[128,4,2,256]{3,2,1,0:T(2,128)(2,1)S(1)}, u32[]{:S(2)}, u32[]{:S(2)}) collective-permute-start(bf16[128,4,2,256]{3,2,1,0:T(2,128)(2,1)} %slice_bitcast_fusion), channel_id=1, source_target_pairs={{1,2},{5,6},{9,10},{13,14},{17,18},{21,22},{25,26},{29,30}} | collective-permute-start | bytes 1572872 | tf_op jit(solution)/shard_map/ppermute | solution.py:298
  7.8 0.8 %collective-permute-start = (f32[4,2,256]{2,1,0:T(2,128)}, f32[4,2,256]{2,1,0:T(2,128)S(1)}, u32[]{:S(2)}, u32[]{:S(2)}) collective-permute-start(f32[4,2,256]{2,1,0:T(2,128)} %bitcast.13), channel_id=1, source_target_pairs={{0,1},{1,0},{2,3},{3,2},{4,5},{5,4},{6,7},{7,6},{8,9},{9,8},{10,11... | collective-permute-start | bytes 24584 | tf_op jit(solution)/shard_map/ppermute | solution.py:301
  8.6 2.1 %slice_bitcast_fusion.1 = bf16[112,4,2,256]{3,2,1,0:T(2,128)(2,1)} fusion(bf16[1,1,512,4,2,256]{5,4,3,2,1,0:T(2,128)(2,1)} %param.6), kind=kLoop, calls=%fused_computation.1 | loop fusion | bytes 917504 | tf_op jit(solution)/shard_map/slice | solution.py:342
  10.7 2.1 %collective-permute-start.7 = (bf16[112,4,2,256]{3,2,1,0:T(2,128)(2,1)}, bf16[112,4,2,256]{3,2,1,0:T(2,128)(2,1)}, u32[]{:S(2)}, u32[]{:S(2)}) collective-permute-start(bf16[112,4,2,256]{3,2,1,0:T(2,128)(2,1)} %slice_bitcast_fusion.1), channel_id=1, source_target_pairs={{0,2},{4,6},{8,10},{12,14},{16,18},{20,22},{24,26},{28,30}} | collective-permute-start | bytes 1376264 | tf_op jit(solution)/shard_map/ppermute | solution.py:298
  12.7 0.1 pad_add_fusion.refs_0_
  12.8 0.0 copy-start.5
  12.8 0.7 %copy-done.5 = s32[64]{0:T(128)S(1)} copy-done((s32[64]{0:T(128)S(1)}, s32[64]{0:T(128)}, u32[]{:S(2)}) %copy-start.5) | copy-done | bytes 280
  13.5 0.0 copy-start
  13.5 0.0 copy-start.1
  13.5 0.0 copy-start.2
  13.5 0.0 copy-start.3
  13.5 0.0 copy-start.4
  13.5 1.8 %shard_map.64.refs_6_ = bf16[4,1024,512]{2,1,0:T(8,128)(2,1)S(1)} custom-call(s32[2]{0:T(128)S(1)} %pad_add_fusion.refs_0_, s32[1,64]{1,0:T(1,128)S(1)} %bitcast.20), custom_call_target="tpu_custom_call" | custom-call | flops 16777216 | bytes 4194304 | tf_op jit(solution)/shard_map/pallas_call | solution.py:344
  15.4 0.0 collective-permute-done.refs_3_
  15.4 0.7 %collective-permute-start.8 = (bf16[112,4,2,256]{3,2,1,0:T(2,128)(2,1)}, bf16[112,4,2,256]{3,2,1,0:T(2,128)(2,1)S(1)}, u32[]{:S(2)}, u32[]{:S(2)}) collective-permute-start(bf16[112,4,2,256]{3,2,1,0:T(2,128)(2,1)} %slice_bitcast_fusion.1), channel_id=1, source_target_pairs={{1,2},{5,6},{9,10},{13,14},{17,18},{21,22},{25,26},{29,30}} | collective-permute-start | bytes 1376264 | tf_op jit(solution)/shard_map/ppermute | solution.py:298
  16.1 0.0 collective-permute-done.1.refs_8_.refs_10_
  16.1 0.0 copy-done
  16.1 0.0 copy-done.1
  16.1 0.0 copy-done.2
  16.1 0.0 copy-done.3
  16.1 0.0 copy-done.4
  16.1 0.7 %shard_map.65 = (bf16[256,512]{1,0:T(8,128)(2,1)S(1)}, bf16[256,512]{1,0:T(8,128)(2,1)S(1)}, bf16[256,512]{1,0:T(8,128)(2,1)S(1)}, bf16[256,512]{1,0:T(8,128)(2,1)S(1)}) custom-call(s32[2]{0:T(128)S(1)} %pad_add_fusion.refs_0_, bf16[512,768]{1,0:T(8,128)(2,1)S(1)} %copy-done.1, f32[4,2,256]{2,1,0:T(2,128)S(1)} %bitcast.14, ...), custom_call_target="tpu_custom_call" | custom-call | flops 4294967296 | bytes 4194304 | tf_op jit(solution)/shard_map/pallas_call | solution.py:321
  16.8 0.7 %collective-permute-start.2 = (bf16[256,512]{1,0:T(8,128)(2,1)S(1)}, bf16[256,512]{1,0:T(8,128)(2,1)S(1)}, u32[]{:S(2)}, u32[]{:S(2)}) collective-permute-start(bf16[256,512]{1,0:T(8,128)(2,1)S(1)} %get-tuple-element.19), channel_id=1, source_target_pairs={{1,5},{5,1},{9,13},{13,9},{3,7},{7,3},{11,15},{15,11},{17,21},{21,... | collective-permute-start | bytes 786440 | tf_op jit(solution)/shard_map/ppermute | solution.py:307
  17.5 1.4 %collective-permute-done.5.refs_7_ = bf16[128,4,2,256]{3,2,1,0:T(2,128)(2,1)S(1)} collective-permute-done((bf16[128,4,2,256]{3,2,1,0:T(2,128)(2,1)}, bf16[128,4,2,256]{3,2,1,0:T(2,128)(2,1)S(1)}, u32[]{:S(2)}, u32[]{:S(2)}) %collective-permute-start.5) | collective-permute-done | bytes 524320 | tf_op jit(solution)/shard_map/ppermute | solution.py:298
  19.0 0.7 %collective-permute-start.3 = (bf16[256,512]{1,0:T(8,128)(2,1)S(1)}, bf16[256,512]{1,0:T(8,128)(2,1)S(1)}, u32[]{:S(2)}, u32[]{:S(2)}) collective-permute-start(bf16[256,512]{1,0:T(8,128)(2,1)S(1)} %get-tuple-element.20), channel_id=1, source_target_pairs={{1,9},{5,13},{9,1},{13,5},{3,11},{7,15},{11,3},{15,7},{17,25},{21,... | collective-permute-start | bytes 786440 | tf_op jit(solution)/shard_map/ppermute | solution.py:307
  19.6 0.0 collective-permute-done.6.refs_8_
  19.6 0.7 %collective-permute-start.4 = (bf16[256,512]{1,0:T(8,128)(2,1)S(1)}, bf16[256,512]{1,0:T(8,128)(2,1)S(1)}, u32[]{:S(2)}, u32[]{:S(2)}) collective-permute-start(bf16[256,512]{1,0:T(8,128)(2,1)S(1)} %get-tuple-element.21), channel_id=1, source_target_pairs={{1,13},{5,9},{9,5},{13,1},{3,15},{7,11},{11,7},{15,3},{17,29},{21,... | collective-permute-start | bytes 786440 | tf_op jit(solution)/shard_map/ppermute | solution.py:307
  20.3 11.5 %shard_map.66 = (bf16[128,512]{1,0:T(8,128)(2,1)S(1)}, bf16[128,512]{1,0:T(8,128)(2,1)S(1)}, bf16[128,512]{1,0:T(8,128)(2,1)S(1)}, bf16[128,512]{1,0:T(8,128)(2,1)S(1)}, f32[8,256,256]{2,1,0:T(8,128)S(1)}) custom-call(s32[2]{0:T(128)S(1)} %pad_add_fusion.refs_0_, bf16[512,768]{1,0:T(8,128)(2,1)S(1)} %copy-done.1, f32[4,2,256]{2,1,0:T(2,128)S(1)} %bitcast.15, ...), custom_call_target="tpu_custom_call" | custom-call | flops 2147483648 | bytes 4194304 | tf_op jit(solution)/shard_map/pallas_call | solution.py:321
  31.9 0.0 collective-permute-done.7.refs_12_
  31.9 0.0 collective-permute-done.8.refs_13_
  31.9 5.6 %shard_map.67 = (bf16[256,512]{1,0:T(8,128)(2,1)S(1)}, bf16[256,512]{1,0:T(8,128)(2,1)S(1)}, bf16[256,512]{1,0:T(8,128)(2,1)S(1)}, bf16[256,512]{1,0:T(8,128)(2,1)S(1)}) custom-call(s32[2]{0:T(128)S(1)} %pad_add_fusion.refs_0_, bf16[512,768]{1,0:T(8,128)(2,1)S(1)} %copy-done.1, f32[4,2,256]{2,1,0:T(2,128)S(1)} %bitcast.16, ...), custom_call_target="tpu_custom_call" | custom-call | flops 2147483648 | bytes 4194304 | tf_op jit(solution)/shard_map/pallas_call | solution.py:321
  37.5 3.5 %collective-permute-start.9 = (bf16[256,512]{1,0:T(8,128)(2,1)S(1)}, bf16[256,512]{1,0:T(8,128)(2,1)S(1)}, u32[]{:S(2)}, u32[]{:S(2)}) collective-permute-start(bf16[256,512]{1,0:T(8,128)(2,1)S(1)} %get-tuple-element.28), channel_id=1, source_target_pairs={{0,4},{4,0},{8,12},{12,8},{2,6},{6,2},{10,14},{14,10},{16,20},{20,... | collective-permute-start | bytes 786440 | tf_op jit(solution)/shard_map/ppermute | solution.py:307
  41.0 4.5 %collective-permute-start.10 = (bf16[256,512]{1,0:T(8,128)(2,1)S(1)}, bf16[256,512]{1,0:T(8,128)(2,1)S(1)}, u32[]{:S(2)}, u32[]{:S(2)}) collective-permute-start(bf16[256,512]{1,0:T(8,128)(2,1)S(1)} %get-tuple-element.29), channel_id=1, source_target_pairs={{0,8},{4,12},{8,0},{12,4},{2,10},{6,14},{10,2},{14,6},{16,24},{20,... | collective-permute-start | bytes 786440 | tf_op jit(solution)/shard_map/ppermute | solution.py:307
  45.5 0.0 collective-permute-done.2.refs_2_
  45.5 2.1 %collective-permute-start.11 = (bf16[256,512]{1,0:T(8,128)(2,1)S(1)}, bf16[256,512]{1,0:T(8,128)(2,1)S(1)}, u32[]{:S(2)}, u32[]{:S(2)}) collective-permute-start(bf16[256,512]{1,0:T(8,128)(2,1)S(1)} %get-tuple-element.30), channel_id=1, source_target_pairs={{0,12},{4,8},{8,4},{12,0},{2,14},{6,10},{10,6},{14,2},{16,28},{20,... | collective-permute-start | bytes 786440 | tf_op jit(solution)/shard_map/ppermute | solution.py:307
  47.6 0.0 collective-permute-done.3.refs_3_
  47.6 0.0 collective-permute-done.4.refs_4_
  47.6 3.2 %collective-permute-done.9.refs_6_ = bf16[256,512]{1,0:T(8,128)(2,1)S(1)} collective-permute-done((bf16[256,512]{1,0:T(8,128)(2,1)S(1)}, bf16[256,512]{1,0:T(8,128)(2,1)S(1)}, u32[]{:S(2)}, u32[]{:S(2)}) %collective-permute-start.9) | collective-permute-done | bytes 262176 | tf_op jit(solution)/shard_map/ppermute | solution.py:307
  50.8 9.6 %collective-permute-done.10.refs_7_ = bf16[256,512]{1,0:T(8,128)(2,1)S(1)} collective-permute-done((bf16[256,512]{1,0:T(8,128)(2,1)S(1)}, bf16[256,512]{1,0:T(8,128)(2,1)S(1)}, u32[]{:S(2)}, u32[]{:S(2)}) %collective-permute-start.10) | collective-permute-done | bytes 262176 | tf_op jit(solution)/shard_map/ppermute | solution.py:307
  60.4 0.0 collective-permute-done.11.refs_8_
  60.4 1.6 %shard_map.68 = bf16[16,64,512]{2,1,0:T(8,128)(2,1)} custom-call(s32[2]{0:T(128)S(1)} %pad_add_fusion.refs_0_, bf16[256,512]{1,0:T(8,128)(2,1)S(1)} %get-tuple-element.18.refs_11_.refs_1_, bf16[256,512]{1,0:T(8,128)(2,1)S(1)} %collective-permute-done.2.refs_2_, bf16[256,512]{1,0:T(8,128)(2,1)S(1)} %collective-permute-done.3.refs_3_, ...), custom_call_target="tpu_custom_call" | custom-call | bytes 3145728 | tf_op jit(solution)/shard_map/pallas_call | solution.py:386
Async XLA Ops:
  0.0 16.1 %collective-permute-start.1 = (bf16[512,4,2,256]{3,2,1,0:T(2,128)(2,1)}, bf16[512,4,2,256]{3,2,1,0:T(2,128)(2,1)S(1)}, u32[]{:S(2)}, u32[]{:S(2)}) collective-permute-start(bf16[512,4,2,256]{3,2,1,0:T(2,128)(2,1)} %bitcast.10), channel_id=1, source_target_pairs={{0,1},{1,0},{2,3},{3,2},{4,5},{5,4},{6,7},{7,6},{8,9},{9,8},{10,11... | collective-permute-start | bytes 6291464 | tf_op jit(solution)/shard_map/ppermute | solution.py:301
  2.7 16.3 %collective-permute-start.5 = (bf16[128,4,2,256]{3,2,1,0:T(2,128)(2,1)}, bf16[128,4,2,256]{3,2,1,0:T(2,128)(2,1)S(1)}, u32[]{:S(2)}, u32[]{:S(2)}) collective-permute-start(bf16[128,4,2,256]{3,2,1,0:T(2,128)(2,1)} %slice_bitcast_fusion), channel_id=1, source_target_pairs={{0,2},{4,6},{8,10},{12,14},{16,18},{20,22},{24,26},{28,30}} | collective-permute-start | bytes 1572872 | tf_op jit(solution)/shard_map/ppermute | solution.py:298
  7.1 12.5 %collective-permute-start.6 = (bf16[128,4,2,256]{3,2,1,0:T(2,128)(2,1)}, bf16[128,4,2,256]{3,2,1,0:T(2,128)(2,1)S(1)}, u32[]{:S(2)}, u32[]{:S(2)}) collective-permute-start(bf16[128,4,2,256]{3,2,1,0:T(2,128)(2,1)} %slice_bitcast_fusion), channel_id=1, source_target_pairs={{1,2},{5,6},{9,10},{13,14},{17,18},{21,22},{25,26},{29,30}} | collective-permute-start | bytes 1572872 | tf_op jit(solution)/shard_map/ppermute | solution.py:298
  7.8 7.6 %collective-permute-start = (f32[4,2,256]{2,1,0:T(2,128)}, f32[4,2,256]{2,1,0:T(2,128)S(1)}, u32[]{:S(2)}, u32[]{:S(2)}) collective-permute-start(f32[4,2,256]{2,1,0:T(2,128)} %bitcast.13), channel_id=1, source_target_pairs={{0,1},{1,0},{2,3},{3,2},{4,5},{5,4},{6,7},{7,6},{8,9},{9,8},{10,11... | collective-permute-start | bytes 24584 | tf_op jit(solution)/shard_map/ppermute | solution.py:301
  10.7 21.2 %collective-permute-start.7 = (bf16[112,4,2,256]{3,2,1,0:T(2,128)(2,1)}, bf16[112,4,2,256]{3,2,1,0:T(2,128)(2,1)}, u32[]{:S(2)}, u32[]{:S(2)}) collective-permute-start(bf16[112,4,2,256]{3,2,1,0:T(2,128)(2,1)} %slice_bitcast_fusion.1), channel_id=1, source_target_pairs={{0,2},{4,6},{8,10},{12,14},{16,18},{20,22},{24,26},{28,30}} | collective-permute-start | bytes 1376264 | tf_op jit(solution)/shard_map/ppermute | solution.py:298
  12.8 0.7 %copy-start.5 = (s32[64]{0:T(128)S(1)}, s32[64]{0:T(128)}, u32[]{:S(2)}) copy-start(s32[64]{0:T(128)} %param.8) | copy-start | bytes 772
  13.5 2.6 %copy-start = (bf16[1,1,512,4,2,256]{5,4,3,2,1,0:T(2,128)(2,1)S(1)}, bf16[1,1,512,4,2,256]{5,4,3,2,1,0:T(2,128)(2,1)}, u32[]{:S(2)}) copy-start(bf16[1,1,512,4,2,256]{5,4,3,2,1,0:T(2,128)(2,1)} %param.6) | copy-start | bytes 6291460
  13.5 2.6 %copy-start.1 = (bf16[512,768]{1,0:T(8,128)(2,1)S(1)}, bf16[512,768]{1,0:T(8,128)(2,1)}, u32[]{:S(2)}) copy-start(bf16[512,768]{1,0:T(8,128)(2,1)} %constant.13.clone.refs_1_) | copy-start | bytes 2359300
  13.5 2.6 %copy-start.2 = (bf16[512,512]{1,0:T(8,128)(2,1)S(1)}, bf16[512,512]{1,0:T(8,128)(2,1)}, u32[]{:S(2)}) copy-start(bf16[512,512]{1,0:T(8,128)(2,1)} %constant.14.clone.refs_4_) | copy-start | bytes 1572868
  13.5 2.6 %copy-start.3 = (f32[1,1,4,2,256]{4,3,2,1,0:T(2,128)S(1)}, f32[1,1,4,2,256]{4,3,2,1,0:T(2,128)}, u32[]{:S(2)}) copy-start(f32[1,1,4,2,256]{4,3,2,1,0:T(2,128)} %param.7) | copy-start | bytes 24580
  13.5 2.6 %copy-start.4 = (s32[1024]{0:T(1024)S(1)}, s32[1024]{0:T(1024)}, u32[]{:S(2)}) copy-start(s32[1024]{0:T(1024)} %param.9) | copy-start | bytes 12292
  15.4 16.5 %collective-permute-start.8 = (bf16[112,4,2,256]{3,2,1,0:T(2,128)(2,1)}, bf16[112,4,2,256]{3,2,1,0:T(2,128)(2,1)S(1)}, u32[]{:S(2)}, u32[]{:S(2)}) collective-permute-start(bf16[112,4,2,256]{3,2,1,0:T(2,128)(2,1)} %slice_bitcast_fusion.1), channel_id=1, source_target_pairs={{1,2},{5,6},{9,10},{13,14},{17,18},{21,22},{25,26},{29,30}} | collective-permute-start | bytes 1376264 | tf_op jit(solution)/shard_map/ppermute | solution.py:298
  16.8 28.7 %collective-permute-start.2 = (bf16[256,512]{1,0:T(8,128)(2,1)S(1)}, bf16[256,512]{1,0:T(8,128)(2,1)S(1)}, u32[]{:S(2)}, u32[]{:S(2)}) collective-permute-start(bf16[256,512]{1,0:T(8,128)(2,1)S(1)} %get-tuple-element.19), channel_id=1, source_target_pairs={{1,5},{5,1},{9,13},{13,9},{3,7},{7,3},{11,15},{15,11},{17,21},{21,... | collective-permute-start | bytes 786440 | tf_op jit(solution)/shard_map/ppermute | solution.py:307
  19.0 28.7 %collective-permute-start.3 = (bf16[256,512]{1,0:T(8,128)(2,1)S(1)}, bf16[256,512]{1,0:T(8,128)(2,1)S(1)}, u32[]{:S(2)}, u32[]{:S(2)}) collective-permute-start(bf16[256,512]{1,0:T(8,128)(2,1)S(1)} %get-tuple-element.20), channel_id=1, source_target_pairs={{1,9},{5,13},{9,1},{13,5},{3,11},{7,15},{11,3},{15,7},{17,25},{21,... | collective-permute-start | bytes 786440 | tf_op jit(solution)/shard_map/ppermute | solution.py:307
  19.6 28.0 %collective-permute-start.4 = (bf16[256,512]{1,0:T(8,128)(2,1)S(1)}, bf16[256,512]{1,0:T(8,128)(2,1)S(1)}, u32[]{:S(2)}, u32[]{:S(2)}) collective-permute-start(bf16[256,512]{1,0:T(8,128)(2,1)S(1)} %get-tuple-element.21), channel_id=1, source_target_pairs={{1,13},{5,9},{9,5},{13,1},{3,15},{7,11},{11,7},{15,3},{17,29},{21,... | collective-permute-start | bytes 786440 | tf_op jit(solution)/shard_map/ppermute | solution.py:307
  37.5 13.3 %collective-permute-start.9 = (bf16[256,512]{1,0:T(8,128)(2,1)S(1)}, bf16[256,512]{1,0:T(8,128)(2,1)S(1)}, u32[]{:S(2)}, u32[]{:S(2)}) collective-permute-start(bf16[256,512]{1,0:T(8,128)(2,1)S(1)} %get-tuple-element.28), channel_id=1, source_target_pairs={{0,4},{4,0},{8,12},{12,8},{2,6},{6,2},{10,14},{14,10},{16,20},{20,... | collective-permute-start | bytes 786440 | tf_op jit(solution)/shard_map/ppermute | solution.py:307
  41.0 19.5 %collective-permute-start.10 = (bf16[256,512]{1,0:T(8,128)(2,1)S(1)}, bf16[256,512]{1,0:T(8,128)(2,1)S(1)}, u32[]{:S(2)}, u32[]{:S(2)}) collective-permute-start(bf16[256,512]{1,0:T(8,128)(2,1)S(1)} %get-tuple-element.29), channel_id=1, source_target_pairs={{0,8},{4,12},{8,0},{12,4},{2,10},{6,14},{10,2},{14,6},{16,24},{20,... | collective-permute-start | bytes 786440 | tf_op jit(solution)/shard_map/ppermute | solution.py:307
  45.5 14.9 %collective-permute-start.11 = (bf16[256,512]{1,0:T(8,128)(2,1)S(1)}, bf16[256,512]{1,0:T(8,128)(2,1)S(1)}, u32[]{:S(2)}, u32[]{:S(2)}) collective-permute-start(bf16[256,512]{1,0:T(8,128)(2,1)S(1)} %get-tuple-element.30), channel_id=1, source_target_pairs={{0,12},{4,8},{8,4},{12,0},{2,14},{6,10},{10,6},{14,2},{16,28},{20,... | collective-permute-start | bytes 786440 | tf_op jit(solution)/shard_map/ppermute | solution.py:307

commit v5 on v3

v5 whole, which is shorter than its diff:
```python
import functools

import jax
import jax.numpy as jnp
import numpy as np
from jax import lax
from jax.experimental import pallas as pl
from jax.experimental.pallas import tpu as pltpu
from jax.sharding import PartitionSpec as P


NS = 256
CYL = 4
UPCH = 16
TAPS = 16
SET_BEAMS = 16
BLOCK = 8
LANES = 128
ROWS = 2 * UPCH


def window_taps():
    span = TAPS * UPCH
    steps = np.arange(span, dtype=np.float64)
    weights = np.sinc((steps - (span - 1) / 2.0) / UPCH) * np.sin(np.pi * (steps + 0.5) / span) ** 2
    return weights / np.sqrt(np.sum(weights * weights))


def filter_matrix():
    weights = window_taps()
    fine = np.arange(UPCH)
    sample = np.arange(TAPS * UPCH)
    phase = 2.0 * np.pi * ((fine[:, None] * sample[None, :]) % UPCH) / UPCH
    cosine = np.cos(phase) * weights
    sine = np.sin(phase) * weights
    table = np.zeros((2, BLOCK, UPCH, TAPS + BLOCK, UPCH, 2))
    for frame in range(BLOCK):
        taps = slice(frame + 1, frame + 1 + TAPS)
        cos_part = cosine.reshape(UPCH, TAPS, UPCH)
        sin_part = sine.reshape(UPCH, TAPS, UPCH)
        table[0, frame, :, taps, :, 0] = cos_part
        table[0, frame, :, taps, :, 1] = sin_part
        table[1, frame, :, taps, :, 0] = -sin_part
        table[1, frame, :, taps, :, 1] = cos_part
    table = table.reshape(2 * BLOCK * UPCH, (TAPS + BLOCK) * ROWS).astype(np.float32)
    high = table.astype(jnp.bfloat16)
    low = (table - high.astype(np.float32)).astype(jnp.bfloat16)
    return np.concatenate([high, low], axis=0)


def beam_matrix():
    rows = np.arange(NS)
    angle = 2.0 * np.pi * (rows[:, None] * rows[None, :] % NS) / NS
    scale = 1.0 / np.sqrt(NS)
    cosine = (np.cos(angle) * scale).astype(np.float32)
    sine = (np.sin(angle) * scale).astype(np.float32)
    upper = np.concatenate([cosine, -sine], axis=1)
    lower = np.concatenate([sine, cosine], axis=1)
    table = np.concatenate([upper, lower], axis=0).astype(jnp.bfloat16)
    table = table.reshape(2 * NS, 2, NS // LANES, LANES).transpose(0, 2, 1, 3).reshape(2 * NS, 2 * NS)
    return (table.astype(np.float32) * 0.5).astype(jnp.bfloat16)


def columns(cyl):
    return slice(cyl * NS, (cyl + 1) * NS)


def form_powers(spectra, gain_ref, beam_ref, cal_ref, emit):
    half = BLOCK * UPCH
    for cyl in range(CYL):
        spec = spectra(cyl)
        real, imag = spec[:half], spec[half:]
        gain_real = gain_ref[cyl, 0:1, :]
        gain_imag = gain_ref[cyl, 1:2, :]
        rows = slice(cyl * half, (cyl + 1) * half)
        cal_ref[rows, :NS] = (real * gain_real - imag * gain_imag).astype(jnp.bfloat16)
        cal_ref[rows, NS:] = (real * gain_imag + imag * gain_real).astype(jnp.bfloat16)
    for strip in range(NS // LANES):
        beam = jnp.dot(
            cal_ref[...],
            beam_ref[:, strip * 2 * LANES : (strip + 1) * 2 * LANES],
            preferred_element_type=jnp.float32,
        )
        beams = [beam[cyl * half : (cyl + 1) * half] for cyl in range(CYL)]
        (r0, i0), (r1, i1), (r2, i2), (r3, i3) = [(b[:, :LANES], b[:, LANES:]) for b in beams]
        pr, pi, mr, mi = r0 + r2, i0 + i2, r0 - r2, i0 - i2
        sr, si, dr, di = r1 + r3, i1 + i3, r1 - r3, i1 - i3
        formed = [(pr + sr, pi + si), (mr + di, mi - dr), (pr - sr, pi - si), (mr - di, mi + dr)]
        for element, (fr, fi) in enumerate(formed):
            emit(element * NS + strip * LANES, fr * fr + fi * fi)


def filtered(terms):
    both = None
    for table, rows in terms:
        term = jnp.dot(table, rows, preferred_element_type=jnp.float32)
        both = term if both is None else both + term
    return both[: both.shape[0] // 2] + both[both.shape[0] // 2 :]


def adder(pol, sum_ref, keep_ref):
    def first(column, power):
        sum_ref[:, column : column + LANES] = power.astype(jnp.bfloat16)

    def second(column, power):
        lanes = slice(column, column + LANES)
        total = sum_ref[:, lanes].astype(jnp.float32) + power.astype(jnp.bfloat16).astype(jnp.float32)
        sum_ref[:, lanes] = (total * keep_ref[:, lanes].astype(jnp.float32)).astype(jnp.bfloat16)

    return (first, second)[pol]


def place(sum_ref, table_ref, out_refs):
    for k, out_ref in enumerate(out_refs):
        placed = jnp.dot(sum_ref[...], table_ref[k], preferred_element_type=jnp.float32)
        out_ref[...] = placed.astype(jnp.bfloat16)


def rows_kernel(first, v_ref, out_ref, held_ref, sems):
    count = held_ref.shape[1]
    strips = NS // LANES
    copies = [
        pltpu.make_async_copy(
            v_ref.at[pl.ds(first, count), j // strips, :, pl.ds(j % strips * LANES, LANES)],
            held_ref.at[j],
            sems.at[j],
        )
        for j in range(CYL * strips)
    ]
    for copy in copies:
        copy.start()
    for j, copy in enumerate(copies):
        copy.wait()
        out_ref[:, j * LANES : (j + 1) * LANES] = held_ref[j].reshape(2 * count, LANES)


def late_kernel(block, n_owner, where_ref, filt_ref, x0, x1, g0, g1, beam_ref, keep_ref, table_ref, *refs):
    out_refs, (cal_ref, sum_ref) = refs[:n_owner], refs[n_owner:]
    rows = slice(block * BLOCK * ROWS, (block * BLOCK + TAPS + BLOCK) * ROWS)

    @pl.when(where_ref[1] == 0)
    def _():
        for pol, (x, gain) in enumerate(((x0, g0), (x1, g1))):

            def spectra(cyl, x=x):
                return filtered([(filt_ref[...], x[rows, columns(cyl)])])

            form_powers(spectra, gain, beam_ref, cal_ref, adder(pol, sum_ref, keep_ref))
        place(sum_ref, table_ref, out_refs)


def near_kernel(n_owner, where_ref, filt_ref, n0, n1, x0, x1, g0, g1, beam_ref, keep_ref, table_ref, *refs):
    out_refs, pre_ref, (cal_ref, sum_ref) = refs[:n_owner], refs[n_owner], refs[n_owner + 1 :]
    reach = BLOCK * ROWS

    @pl.when(where_ref[1] == 1)
    def _():
        for pol, (n, x, gain) in enumerate(((n0, x0, g0), (n1, x1, g1))):

            def spectra(cyl, pol=pol, n=n, x=x):
                there = n[:, columns(cyl)]
                pre_ref[pol * CYL + cyl] = filtered(
                    [(filt_ref[:, reach : 2 * reach], there), (filt_ref[:, 2 * reach :], x[:reach, columns(cyl)])]
                )
                return filtered([(filt_ref[:, :reach], there), (filt_ref[:, reach:], x[: 2 * reach, columns(cyl)])])

            form_powers(spectra, gain, beam_ref, cal_ref, adder(pol, sum_ref, keep_ref))
        place(sum_ref, table_ref, out_refs)


def far_kernel(n_owner, where_ref, edge_ref, f0, f1, g0, g1, beam_ref, keep_ref, table_ref, pre_ref, *refs):
    own_refs, out_refs, own_ref, (cal_ref, sum_ref) = refs[:3], refs[3 : 3 + n_owner], refs[3 + n_owner], refs[-2:]
    half = BLOCK * UPCH

    @pl.when(where_ref[1] == 1)
    def _():
        for pol, (f, gain) in enumerate(((f0, g0), (f1, g1))):

            def spectra(cyl, pol=pol, f=f):
                return pre_ref[pol * CYL + cyl] + filtered([(edge_ref[...], f[:, columns(cyl)])])

            form_powers(spectra, gain, beam_ref, cal_ref, adder(pol, sum_ref, keep_ref))
        place(sum_ref, table_ref, out_refs)
        own_ref[:half, :] = out_refs[0][...]
        own_ref[half:, :] = own_refs[0][...]

    @pl.when(where_ref[1] == 0)
    def _():
        own_ref[:half, :] = own_refs[1][...]
        own_ref[half:, :] = own_refs[2][...]


def place_table_kernel(most_sets, where_ref, owner_ref, out_ref):
    n_owner, beams, width = out_ref.shape
    sets = owner_ref.shape[1]
    owner = owner_ref[...].astype(jnp.float32)
    set_of = lax.broadcasted_iota(jnp.int32, (beams, sets), 0) // SET_BEAMS
    lane = lax.broadcasted_iota(jnp.int32, (beams, sets), 1)
    own = jnp.sum(jnp.where(set_of == lane, owner, 0.0), axis=1, keepdims=True)
    same = jnp.logical_and(owner == own, lane < set_of)
    rank = jnp.sum(jnp.where(same, 1.0, 0.0), axis=1, keepdims=True)
    within = lax.broadcasted_iota(jnp.int32, (beams, 1), 0) % SET_BEAMS
    column = (own * most_sets + rank).astype(jnp.int32) * SET_BEAMS + within
    lane_at = lax.broadcasted_iota(jnp.int32, (beams, width), 1)
    for k in range(n_owner):
        owner_k = where_ref[0] ^ k
        hit = (column - owner_k * width) == lane_at
        out_ref[k] = jnp.where(hit, 1.0, 0.0).astype(jnp.bfloat16)


def gather_kernel(n_owner, where_ref, *refs):
    own_ref, got, out_ref = refs[0], refs[1:-1], refs[-1]
    chunks = [got[i * (n_owner - 1) : (i + 1) * (n_owner - 1)] for i in range(4)]

    def copy(block, frame, k):
        rows = pl.ds(pl.multiple_of((where_ref[0] ^ k) * UPCH, UPCH), UPCH)
        count = block.shape[0] // UPCH
        out_ref[frame : frame + count, rows, :] = block[...].reshape(count, UPCH, block.shape[1])

    copy(own_ref, 0, 0)
    for pol in range(2):

        @pl.when(where_ref[1] == pol)
        def _(pol=pol):
            for part in range(2):
                for k in range(1, n_owner):
                    copy(chunks[2 * pol + part][k - 1], part * BLOCK, k)


VMEM = pl.BlockSpec(memory_space=pltpu.VMEM)
SMEM = pl.BlockSpec(memory_space=pltpu.SMEM)
ANY = pl.BlockSpec(memory_space=pl.ANY)


def call(body, out_shape, n_in, flops, nbytes, scalars=0, whole=0, after=0, scratch=()):
    many = isinstance(out_shape, (list, tuple))

    def kernel(*refs):
        seen = scalars + n_in + whole
        body(*refs[:seen], *refs[seen + after :])

    return pl.pallas_call(
        kernel,
        out_shape=out_shape,
        in_specs=[SMEM] * scalars + [VMEM] * n_in + [ANY] * (whole + after),
        out_specs=[VMEM] * len(out_shape) if many else VMEM,
        scratch_shapes=list(scratch),
        cost_estimate=pl.CostEstimate(flops=flops, bytes_accessed=nbytes, transcendentals=0),
        compiler_params=pltpu.CompilerParams(vmem_limit_bytes=40 << 20),
    )


def per_device(voltages, feed_gains, owner_table, keep_flags):
    samples = voltages[0, 0]
    gain = feed_gains[0, 0]
    frame_count = samples.shape[0] // UPCH
    kept = frame_count // 2
    n_owner = lax.axis_size("freq")
    assert voltages.shape[1] == 1 and kept == 2 * BLOCK and kept >= TAPS
    assert n_owner & (n_owner - 1) == 0
    n_tm = lax.axis_size("tm")
    me = lax.axis_index("freq")
    pol = lax.axis_index("pol")
    most_sets = 2 * owner_table.shape[0] // n_owner
    beams = keep_flags.shape[0]
    width = most_sets * SET_BEAMS
    bf16 = jnp.bfloat16
    filt = jnp.asarray(filter_matrix())
    edge = jnp.asarray(filter_matrix()[:, ROWS : BLOCK * ROWS])
    beam_table = jnp.asarray(beam_matrix())

    pairs = [(i, i + 1) for i in range(n_tm - 1)]

    def ahead(part, source):
        return lax.ppermute(part, ("tm", "pol"), [(i * 2 + source, j * 2 + 1) for i, j in pairs])

    def swap(part):
        return lax.ppermute(part, "pol", [(0, 1), (1, 0)])

    def spread(blocks, source):
        got = []
        for k in range(1, n_owner):
            route = [(i * 2 + source, (i ^ k) * 2 + 1 - source) for i in range(n_owner)]
            got.append(lax.ppermute(blocks[k], ("freq", "pol"), route))
        return got

    def form(body, *arrays, after=(), more=()):
        shape = [jax.ShapeDtypeStruct((BLOCK * UPCH, width), bf16)] * n_owner
        scratch = [pltpu.VMEM((CYL * BLOCK * UPCH, 2 * NS), bf16), pltpu.VMEM((BLOCK * UPCH, beams), bf16)]
        return call(
            body,
            shape + list(more),
            len(arrays),
            4 * 512 * 1024 * 1024,
            4 << 20,
            scalars=1,
            after=len(after),
            scratch=scratch,
        )(where, *arrays, *after)

    where = jnp.stack([me, pol]).astype(jnp.int32)
    keep = keep_flags.reshape(1, -1)
    count = BLOCK * UPCH
    near_rows = call(
        functools.partial(rows_kernel, samples.shape[0] - count),
        jax.ShapeDtypeStruct((BLOCK * ROWS, CYL * NS), bf16),
        0,
        0,
        1 << 20,
        whole=1,
        scratch=[pltpu.VMEM((CYL * NS // LANES, count, 2, LANES), bf16), pltpu.SemaphoreType.DMA((CYL * NS // LANES,))],
    )(samples)
    near0 = ahead(near_rows, 0)
    near1 = ahead(near_rows, 1)
    x = samples.transpose(0, 2, 1, 3).reshape(samples.shape[0] * 2, CYL * NS)
    x = lax.optimization_barrier(x)
    other = swap(x)
    gain_other = swap(gain)
    far_rows = x[x.shape[0] - (TAPS - 1) * ROWS : x.shape[0] - BLOCK * ROWS]
    far0 = ahead(far_rows, 0)
    far1 = ahead(far_rows, 1)
    table = call(
        functools.partial(place_table_kernel, most_sets),
        jax.ShapeDtypeStruct((n_owner, beams, width), bf16),
        1,
        1 << 24,
        4 << 20,
        scalars=1,
    )(where, owner_table.reshape(1, -1))
    common = (gain, gain_other, beam_table, keep, table)
    late = []
    got = []
    for block in range(2):
        body = functools.partial(late_kernel, block, n_owner)
        after = [late[0][0]] if block else []
        late.append(form(body, filt, x, other, *common, after=after))
        got.append(spread(late[block], 0))
    *near, pre = form(
        functools.partial(near_kernel, n_owner),
        filt,
        near1,
        near0,
        x,
        other,
        *common,
        after=late[1][:1],
        more=[jax.ShapeDtypeStruct((2 * CYL, BLOCK * ROWS, NS), jnp.float32)],
    )
    near_got = spread(near, 1)
    *far, own = form(
        functools.partial(far_kernel, n_owner),
        edge,
        far1,
        far0,
        *common,
        pre,
        near[0],
        late[0][0],
        late[1][0],
        more=[jax.ShapeDtypeStruct((kept * UPCH, width), bf16)],
    )
    far_got = spread(far, 1)
    own_got = swap(own)
    out_shape = jax.ShapeDtypeStruct((kept, n_owner * UPCH, width), bf16)
    arrays = [own_got, *far_got, *near_got, *got[0], *got[1]]
    return call(functools.partial(gather_kernel, n_owner), out_shape, len(arrays), 0, 3 << 20, scalars=1)(
        where, *arrays
    )


def solution(mesh):
    return jax.shard_map(
        per_device,
        mesh=mesh,
        in_specs=(
            P("pol", ("grp", "freq"), "tm", None, None, None),
            P(("grp", "freq"), "pol", None, None, None),
            P(),
            P(),
        ),
        out_specs=P(("grp", "tm", "pol"), None, "freq"),
        check_vma=False,
    )
```

time: 57.6 us -> 67.1 us (1.16)
  the two profiles are of different devices: /device:TPU:14 before, /device:TPU:1 now
where the time goes in v5:
time: 67.1 us; the launch traced here: 66.5 us
  starting transfers between devices  31.5 us (47%)
  Pallas kernels  18.9 us (28%)
  waiting for transfers between devices  10.8 us (16%)
  local copies, waits for them, and re-layouts  4.97 us (7%)
    ppermute x12, starting transfers between devices, spread(): got.append(lax.ppermute(blocks[k], ('freq', 'pol'), route))  19.2 us
    pallas_call x4, Pallas kernels, form(): call(body, shape + list(more), len(arrays), 4 * 512 * 1024 * 1024, 4 << 2...  13.9 us
    ppermute x12, waiting for transfers between devices, spread(): got.append(lax.ppermute(blocks[k], ('freq', 'pol'), route))  8.06 us
    ppermute x4, starting transfers between devices, ahead(): lax.ppermute(part, ('tm', 'pol'), [(i * 2 + source, j * 2 + 1) for i, j i...  7.41 us
    ppermute x3, starting transfers between devices, swap(): return lax.ppermute(part, 'pol', [(0, 1), (1, 0)])  4.85 us
    ppermute x4, waiting for transfers between devices, ahead(): lax.ppermute(part, ('tm', 'pol'), [(i * 2 + source, j * 2 + 1) for i, j i...  2.76 us
    transpose x1, local copies, waits for them, and re-layouts, per_device(): x = samples.transpose(0, 2, 1, 3).reshape(samples.shape[0] * 2, CYL * NS)  2.67 us
    pallas_call x1, Pallas kernels, per_device(): call(functools.partial(place_table_kernel, most_sets), jax.ShapeDtypeStru...  1.85 us
  transfers between devices with their start and end apart: 19, of which 6 were waited for; matrix products, arithmetic and copies ran while one was open for 1% of the time, Pallas kernels for 20%

profile of v5, /device:TPU:1, one launch (start us, length us, event | category | flops | bytes accessed | tf_op | source)
XLA Modules:
  0.0 66.5 jit_solution(12493818395244338323)
XLA Ops:
  0.0 2.7 %copy.8 = bf16[512,2,4,256]{3,2,1,0:T(4,128)(2,1)S(1)} copy(bf16[512,2,4,256]{3,1,2,0:T(2,128)(2,1)} %bitcast.16) | data formatting | bytes 4194304 | tf_op jit(solution)/shard_map/transpose | solution.py:315
  2.7 0.0 copy-start
  2.7 0.5 copy.9
  3.2 0.0 copy-start.4
  3.2 0.0 copy-start.6
  3.2 0.1 collective-permute-start.5
  3.3 1.0 %copy-done = bf16[1,1,512,4,2,256]{5,4,3,2,1,0:T(2,128)(2,1)S(1)} copy-done((bf16[1,1,512,4,2,256]{5,4,3,2,1,0:T(2,128)(2,1)S(1)}, bf16[1,1,512,4,2,256]{5,4,3,2,1,0:T(2,128)(2,1)}, u32[]{:S(2)}) %copy-start) | copy-done | bytes 2097176
  4.3 1.5 %shard_map.74 = bf16[256,1024]{1,0:T(8,128)(2,1)} custom-call(bf16[512,4,2,256]{3,2,1,0:T(2,128)(2,1)S(1)} %bitcast.17), custom_call_target="tpu_custom_call" | custom-call | bytes 1048576 | tf_op jit(solution)/shard_map/pallas_call | solution.py:304
  5.8 4.0 %collective-permute-start.3 = (bf16[256,1024]{1,0:T(8,128)(2,1)}, bf16[256,1024]{1,0:T(8,128)(2,1)S(1)}, u32[]{:S(2)}, u32[]{:S(2)}) collective-permute-start(bf16[256,1024]{1,0:T(8,128)(2,1)} %shard_map.74), channel_id=1, source_target_pairs={{1,3},{5,7},{9,11},{13,15},{17,19},{21,23},{25,27},{29,31}} | collective-permute-start | bytes 1572872 | tf_op jit(solution)/shard_map/ppermute | solution.py:275
  9.8 0.7 %collective-permute-start.4 = (bf16[256,1024]{1,0:T(8,128)(2,1)}, bf16[256,1024]{1,0:T(8,128)(2,1)S(1)}, u32[]{:S(2)}, u32[]{:S(2)}) collective-permute-start(bf16[256,1024]{1,0:T(8,128)(2,1)} %shard_map.74), channel_id=1, source_target_pairs={{0,3},{4,7},{8,11},{12,15},{16,19},{20,23},{24,27},{28,31}} | collective-permute-start | bytes 1572872 | tf_op jit(solution)/shard_map/ppermute | solution.py:275
  10.5 1.1 %collective-permute-start.2 = (f32[4,2,256]{2,1,0:T(2,128)S(1)}, f32[4,2,256]{2,1,0:T(2,128)S(1)}, u32[]{:S(2)}, u32[]{:S(2)}) collective-permute-start(f32[4,2,256]{2,1,0:T(2,128)S(1)} %bitcast.18), channel_id=1, source_target_pairs={{0,1},{1,0},{2,3},{3,2},{4,5},{5,4},{6,7},{7,6},{8,9},{9,8},{10,11... | collective-permute-start | bytes 24584 | tf_op jit(solution)/shard_map/ppermute | solution.py:278
  11.5 0.8 %slice.4 = bf16[224,1024]{1,0:T(8,128)(2,1)} slice(bf16[1024,1024]{1,0:T(8,128)(2,1)S(1)} %bitcast.12), slice={[544:768], [0:1024]} | slice | bytes 917504 | tf_op jit(solution)/shard_map/slice | solution.py:319
  12.3 2.1 %collective-permute-start = (bf16[224,1024]{1,0:T(8,128)(2,1)}, bf16[224,1024]{1,0:T(8,128)(2,1)}, u32[]{:S(2)}, u32[]{:S(2)}) collective-permute-start(bf16[224,1024]{1,0:T(8,128)(2,1)} %slice.4), channel_id=1, source_target_pairs={{1,3},{5,7},{9,11},{13,15},{17,19},{21,23},{25,27},{29,31}} | collective-permute-start | bytes 1376264 | tf_op jit(solution)/shard_map/ppermute | solution.py:275
  14.4 0.1 pad_add_fusion.refs_0_
  14.5 1.8 %shard_map.73.refs_8_.refs_10_ = bf16[4,1024,512]{2,1,0:T(8,128)(2,1)S(1)} custom-call(s32[2]{0:T(128)S(1)} %pad_add_fusion.refs_0_, s32[1,64]{1,0:T(1,128)S(1)} %bitcast.27), custom_call_target="tpu_custom_call" | custom-call | flops 16777216 | bytes 4194304 | tf_op jit(solution)/shard_map/pallas_call | solution.py:322
  16.4 0.0 collective-permute-done.2.refs_5_.refs_7_
  16.4 0.7 %collective-permute-start.1 = (bf16[224,1024]{1,0:T(8,128)(2,1)}, bf16[224,1024]{1,0:T(8,128)(2,1)S(1)}, u32[]{:S(2)}, u32[]{:S(2)}) collective-permute-start(bf16[224,1024]{1,0:T(8,128)(2,1)} %slice.4), channel_id=1, source_target_pairs={{0,3},{4,7},{8,11},{12,15},{16,19},{20,23},{24,27},{28,31}} | collective-permute-start | bytes 1376264 | tf_op jit(solution)/shard_map/ppermute | solution.py:275
  17.1 1.6 %shard_map.75 = (bf16[128,512]{1,0:T(8,128)(2,1)S(1)}, bf16[128,512]{1,0:T(8,128)(2,1)S(1)}, bf16[128,512]{1,0:T(8,128)(2,1)S(1)}, bf16[128,512]{1,0:T(8,128)(2,1)S(1)}) custom-call(s32[2]{0:T(128)S(1)} %pad_add_fusion.refs_0_, bf16[512,768]{1,0:T(8,128)(2,1)S(1)} %copy-done.2, bf16[1024,1024]{1,0:T(8,128)(2,1)S(1)} %bitcast.13, ...), custom_call_target="tpu_custom_call" | custom-call | flops 2147483648 | bytes 4194304 | tf_op jit(solution)/shard_map/pallas_call | solution.py:290
  18.7 1.6 %shard_map.76 = (bf16[128,512]{1,0:T(8,128)(2,1)S(1)}, bf16[128,512]{1,0:T(8,128)(2,1)S(1)}, bf16[128,512]{1,0:T(8,128)(2,1)S(1)}, bf16[128,512]{1,0:T(8,128)(2,1)S(1)}) custom-call(s32[2]{0:T(128)S(1)} %pad_add_fusion.refs_0_, bf16[512,768]{1,0:T(8,128)(2,1)S(1)} %copy-done.2, bf16[1024,1024]{1,0:T(8,128)(2,1)S(1)} %bitcast.14, ...), custom_call_target="tpu_custom_call" | custom-call | flops 2147483648 | bytes 4194304 | tf_op jit(solution)/shard_map/pallas_call | solution.py:290
  20.3 0.0 collective-permute-done.3.refs_2_
  20.4 0.0 copy-start.3
  20.4 6.6 %shard_map.77 = (bf16[128,512]{1,0:T(8,128)(2,1)S(1)}, bf16[128,512]{1,0:T(8,128)(2,1)S(1)}, bf16[128,512]{1,0:T(8,128)(2,1)S(1)}, bf16[128,512]{1,0:T(8,128)(2,1)S(1)}, f32[8,256,256]{2,1,0:T(8,128)S(1)}) custom-call(s32[2]{0:T(128)S(1)} %pad_add_fusion.refs_0_, bf16[512,768]{1,0:T(8,128)(2,1)S(1)} %copy-done.2, ...), custom_call_target="tpu_custom_call" | custom-call | flops 2147483648 | bytes 4194304 | tf_op jit(solution)/shard_map/pallas_call | solution.py:290
  27.0 2.8 %collective-permute-done.refs_2_ = bf16[224,1024]{1,0:T(8,128)(2,1)} collective-permute-done((bf16[224,1024]{1,0:T(8,128)(2,1)}, bf16[224,1024]{1,0:T(8,128)(2,1)}, u32[]{:S(2)}, u32[]{:S(2)}) %collective-permute-start) | collective-permute-done | bytes 458784 | tf_op jit(solution)/shard_map/ppermute | solution.py:275
  29.7 0.0 collective-permute-done.1.refs_3_
  29.7 4.1 %shard_map.78 = (bf16[128,512]{1,0:T(8,128)(2,1)}, bf16[128,512]{1,0:T(8,128)(2,1)S(1)}, bf16[128,512]{1,0:T(8,128)(2,1)S(1)}, bf16[128,512]{1,0:T(8,128)(2,1)S(1)}, bf16[256,512]{1,0:T(8,128)(2,1)S(1)}) custom-call(s32[2]{0:T(128)S(1)} %pad_add_fusion.refs_0_, bf16[512,224]{1,0:T(8,128)(2,1)S(1)} %copy-done.3, ...), custom_call_target="tpu_custom_call" | custom-call | flops 2147483648 | bytes 4194304 | tf_op jit(solution)/shard_map/pallas_call | solution.py:290
  33.8 3.0 %collective-permute-start.7 = (bf16[128,512]{1,0:T(8,128)(2,1)S(1)}, bf16[128,512]{1,0:T(8,128)(2,1)S(1)}, u32[]{:S(2)}, u32[]{:S(2)}) collective-permute-start(bf16[128,512]{1,0:T(8,128)(2,1)S(1)} %get-tuple-element.27), channel_id=1, source_target_pairs={{1,4},{5,0},{9,12},{13,8},{3,6},{7,2},{11,14},{15,10},{17,20},{21,... | collective-permute-start | bytes 393224 | tf_op jit(solution)/shard_map/ppermute | solution.py:284
  36.8 2.3 %collective-permute-start.8 = (bf16[128,512]{1,0:T(8,128)(2,1)S(1)}, bf16[128,512]{1,0:T(8,128)(2,1)S(1)}, u32[]{:S(2)}, u32[]{:S(2)}) collective-permute-start(bf16[128,512]{1,0:T(8,128)(2,1)S(1)} %get-tuple-element.28), channel_id=1, source_target_pairs={{1,8},{5,12},{9,0},{13,4},{3,10},{7,14},{11,2},{15,6},{17,24},{21,... | collective-permute-start | bytes 393224 | tf_op jit(solution)/shard_map/ppermute | solution.py:284
  39.1 2.3 %collective-permute-start.9 = (bf16[128,512]{1,0:T(8,128)(2,1)S(1)}, bf16[128,512]{1,0:T(8,128)(2,1)S(1)}, u32[]{:S(2)}, u32[]{:S(2)}) collective-permute-start(bf16[128,512]{1,0:T(8,128)(2,1)S(1)} %get-tuple-element.29), channel_id=1, source_target_pairs={{1,12},{5,8},{9,4},{13,0},{3,14},{7,10},{11,6},{15,2},{17,28},{21,... | collective-permute-start | bytes 393224 | tf_op jit(solution)/shard_map/ppermute | solution.py:284
  41.4 1.3 %collective-permute-start.10 = (bf16[128,512]{1,0:T(8,128)(2,1)S(1)}, bf16[128,512]{1,0:T(8,128)(2,1)S(1)}, u32[]{:S(2)}, u32[]{:S(2)}) collective-permute-start(bf16[128,512]{1,0:T(8,128)(2,1)S(1)} %get-tuple-element.30), channel_id=1, source_target_pairs={{1,4},{5,0},{9,12},{13,8},{3,6},{7,2},{11,14},{15,10},{17,20},{21,... | collective-permute-start | bytes 393224 | tf_op jit(solution)/shard_map/ppermute | solution.py:284
  42.7 1.3 %collective-permute-start.11 = (bf16[128,512]{1,0:T(8,128)(2,1)S(1)}, bf16[128,512]{1,0:T(8,128)(2,1)S(1)}, u32[]{:S(2)}, u32[]{:S(2)}) collective-permute-start(bf16[128,512]{1,0:T(8,128)(2,1)S(1)} %get-tuple-element.31), channel_id=1, source_target_pairs={{1,8},{5,12},{9,0},{13,4},{3,10},{7,14},{11,2},{15,6},{17,24},{21,... | collective-permute-start | bytes 393224 | tf_op jit(solution)/shard_map/ppermute | solution.py:284
  44.0 0.0 collective-permute-done.7.refs_2_
  44.1 1.3 %collective-permute-start.12 = (bf16[128,512]{1,0:T(8,128)(2,1)S(1)}, bf16[128,512]{1,0:T(8,128)(2,1)S(1)}, u32[]{:S(2)}, u32[]{:S(2)}) collective-permute-start(bf16[128,512]{1,0:T(8,128)(2,1)S(1)} %get-tuple-element.32), channel_id=1, source_target_pairs={{1,12},{5,8},{9,4},{13,0},{3,14},{7,10},{11,6},{15,2},{17,28},{21,... | collective-permute-start | bytes 393224 | tf_op jit(solution)/shard_map/ppermute | solution.py:284
  45.4 1.3 %collective-permute-start.16 = (bf16[128,512]{1,0:T(8,128)(2,1)S(1)}, bf16[128,512]{1,0:T(8,128)(2,1)S(1)}, u32[]{:S(2)}, u32[]{:S(2)}) collective-permute-start(bf16[128,512]{1,0:T(8,128)(2,1)S(1)} %get-tuple-element.36), channel_id=1, source_target_pairs={{0,5},{4,1},{8,13},{12,9},{2,7},{6,3},{10,15},{14,11},{16,21},{20,... | collective-permute-start | bytes 393224 | tf_op jit(solution)/shard_map/ppermute | solution.py:284
  46.7 0.0 collective-permute-done.9.refs_4_
  46.7 1.3 %collective-permute-start.17 = (bf16[128,512]{1,0:T(8,128)(2,1)S(1)}, bf16[128,512]{1,0:T(8,128)(2,1)S(1)}, u32[]{:S(2)}, u32[]{:S(2)}) collective-permute-start(bf16[128,512]{1,0:T(8,128)(2,1)S(1)} %get-tuple-element.37), channel_id=1, source_target_pairs={{0,9},{4,13},{8,1},{12,5},{2,11},{6,15},{10,3},{14,7},{16,25},{20,... | collective-permute-start | bytes 393224 | tf_op jit(solution)/shard_map/ppermute | solution.py:284
  48.0 0.0 collective-permute-done.10.refs_5_
  48.0 3.7 %collective-permute-start.6 = (bf16[256,512]{1,0:T(8,128)(2,1)S(1)}, bf16[256,512]{1,0:T(8,128)(2,1)S(1)}, u32[]{:S(2)}, u32[]{:S(2)}) collective-permute-start(bf16[256,512]{1,0:T(8,128)(2,1)S(1)} %get-tuple-element.26), channel_id=1, source_target_pairs={{0,1},{1,0},{2,3},{3,2},{4,5},{5,4},{6,7},{7,6},{8,9},{9,8},{10,11... | collective-permute-start | bytes 786440 | tf_op jit(solution)/shard_map/ppermute | solution.py:278
  51.7 1.3 %collective-permute-start.18 = (bf16[128,512]{1,0:T(8,128)(2,1)S(1)}, bf16[128,512]{1,0:T(8,128)(2,1)S(1)}, u32[]{:S(2)}, u32[]{:S(2)}) collective-permute-start(bf16[128,512]{1,0:T(8,128)(2,1)S(1)} %get-tuple-element.38), channel_id=1, source_target_pairs={{0,13},{4,9},{8,5},{12,1},{2,15},{6,11},{10,7},{14,3},{16,29},{20,... | collective-permute-start | bytes 393224 | tf_op jit(solution)/shard_map/ppermute | solution.py:284
  53.0 1.3 %collective-permute-start.13 = (bf16[128,512]{1,0:T(8,128)(2,1)S(1)}, bf16[128,512]{1,0:T(8,128)(2,1)S(1)}, u32[]{:S(2)}, u32[]{:S(2)}) collective-permute-start(bf16[128,512]{1,0:T(8,128)(2,1)S(1)} %get-tuple-element.33), channel_id=1, source_target_pairs={{0,5},{4,1},{8,13},{12,9},{2,7},{6,3},{10,15},{14,11},{16,21},{20,... | collective-permute-start | bytes 393224 | tf_op jit(solution)/shard_map/ppermute | solution.py:284
  54.3 0.0 collective-permute-done.16.refs_11_
  54.3 1.3 %collective-permute-start.14 = (bf16[128,512]{1,0:T(8,128)(2,1)S(1)}, bf16[128,512]{1,0:T(8,128)(2,1)S(1)}, u32[]{:S(2)}, u32[]{:S(2)}) collective-permute-start(bf16[128,512]{1,0:T(8,128)(2,1)S(1)} %get-tuple-element.34), channel_id=1, source_target_pairs={{0,9},{4,13},{8,1},{12,5},{2,11},{6,15},{10,3},{14,7},{16,25},{20,... | collective-permute-start | bytes 393224 | tf_op jit(solution)/shard_map/ppermute | solution.py:284
  55.6 1.2 %collective-permute-done.17.refs_12_ = bf16[128,512]{1,0:T(8,128)(2,1)S(1)} collective-permute-done((bf16[128,512]{1,0:T(8,128)(2,1)S(1)}, bf16[128,512]{1,0:T(8,128)(2,1)S(1)}, u32[]{:S(2)}, u32[]{:S(2)}) %collective-permute-start.17) | collective-permute-done | bytes 131104 | tf_op jit(solution)/shard_map/ppermute | solution.py:284
  56.8 1.3 %collective-permute-start.15 = (bf16[128,512]{1,0:T(8,128)(2,1)S(1)}, bf16[128,512]{1,0:T(8,128)(2,1)S(1)}, u32[]{:S(2)}, u32[]{:S(2)}) collective-permute-start(bf16[128,512]{1,0:T(8,128)(2,1)S(1)} %get-tuple-element.35), channel_id=1, source_target_pairs={{0,13},{4,9},{8,5},{12,1},{2,15},{6,11},{10,7},{14,3},{16,29},{20,... | collective-permute-start | bytes 393224 | tf_op jit(solution)/shard_map/ppermute | solution.py:284
  58.1 1.8 %collective-permute-done.18.refs_13_ = bf16[128,512]{1,0:T(8,128)(2,1)S(1)} collective-permute-done((bf16[128,512]{1,0:T(8,128)(2,1)S(1)}, bf16[128,512]{1,0:T(8,128)(2,1)S(1)}, u32[]{:S(2)}, u32[]{:S(2)}) %collective-permute-start.18) | collective-permute-done | bytes 131104 | tf_op jit(solution)/shard_map/ppermute | solution.py:284
  59.9 2.1 %collective-permute-done.13.refs_8_ = bf16[128,512]{1,0:T(8,128)(2,1)S(1)} collective-permute-done((bf16[128,512]{1,0:T(8,128)(2,1)S(1)}, bf16[128,512]{1,0:T(8,128)(2,1)S(1)}, u32[]{:S(2)}, u32[]{:S(2)}) %collective-permute-start.13) | collective-permute-done | bytes 131104 | tf_op jit(solution)/shard_map/ppermute | solution.py:284
  61.9 1.0 %collective-permute-done.14.refs_9_ = bf16[128,512]{1,0:T(8,128)(2,1)S(1)} collective-permute-done((bf16[128,512]{1,0:T(8,128)(2,1)S(1)}, bf16[128,512]{1,0:T(8,128)(2,1)S(1)}, u32[]{:S(2)}, u32[]{:S(2)}) %collective-permute-start.14) | collective-permute-done | bytes 131104 | tf_op jit(solution)/shard_map/ppermute | solution.py:284
  62.9 2.0 %collective-permute-done.15.refs_10_ = bf16[128,512]{1,0:T(8,128)(2,1)S(1)} collective-permute-done((bf16[128,512]{1,0:T(8,128)(2,1)S(1)}, bf16[128,512]{1,0:T(8,128)(2,1)S(1)}, u32[]{:S(2)}, u32[]{:S(2)}) %collective-permute-start.15) | collective-permute-done | bytes 131104 | tf_op jit(solution)/shard_map/ppermute | solution.py:284
  65.0 1.6 %shard_map.79 = bf16[16,64,512]{2,1,0:T(8,128)(2,1)} custom-call(s32[2]{0:T(128)S(1)} %pad_add_fusion.refs_0_, bf16[256,512]{1,0:T(8,128)(2,1)S(1)} %collective-permute-done.6.refs_1_, bf16[128,512]{1,0:T(8,128)(2,1)S(1)} %collective-permute-done.7.refs_2_, bf16[128,512]{1,0:T(8,128)(2,1)S(1)} %collective-permute-done.8.refs_3_, ...), custom_call_target="tpu_custom_call" | custom-call | bytes 3145728 | tf_op jit(solution)/shard_map/pallas_call | solution.py:366
  (15 shorter events, 0.0 us)
Async XLA Ops:
  2.7 1.6 %copy-start = (bf16[1,1,512,4,2,256]{5,4,3,2,1,0:T(2,128)(2,1)S(1)}, bf16[1,1,512,4,2,256]{5,4,3,2,1,0:T(2,128)(2,1)}, u32[]{:S(2)}) copy-start(bf16[1,1,512,4,2,256]{5,4,3,2,1,0:T(2,128)(2,1)} %param.7) | copy-start | bytes 6291460
  3.2 7.3 %copy-start.4 = (f32[1,1,4,2,256]{4,3,2,1,0:T(2,128)S(1)}, f32[1,1,4,2,256]{4,3,2,1,0:T(2,128)}, u32[]{:S(2)}) copy-start(f32[1,1,4,2,256]{4,3,2,1,0:T(2,128)} %param.8) | copy-start | bytes 24580
  3.2 11.3 %copy-start.6 = (s32[64]{0:T(128)S(1)}, s32[64]{0:T(128)}, u32[]{:S(2)}) copy-start(s32[64]{0:T(128)} %param.9) | copy-start | bytes 772
  3.2 13.9 %collective-permute-start.5 = (bf16[1024,1024]{1,0:T(8,128)(2,1)S(1)}, bf16[1024,1024]{1,0:T(8,128)(2,1)}, u32[]{:S(2)}, u32[]{:S(2)}) collective-permute-start(bf16[1024,1024]{1,0:T(8,128)(2,1)S(1)} %bitcast.11), channel_id=1, source_target_pairs={{0,1},{1,0},{2,3},{3,2},{4,5},{5,4},{6,7},{7,6},{8,9},{9,8},{10,11... | collective-permute-start | bytes 6291464 | tf_op jit(solution)/shard_map/ppermute | solution.py:278
  5.8 14.5 %collective-permute-start.3 = (bf16[256,1024]{1,0:T(8,128)(2,1)}, bf16[256,1024]{1,0:T(8,128)(2,1)S(1)}, u32[]{:S(2)}, u32[]{:S(2)}) collective-permute-start(bf16[256,1024]{1,0:T(8,128)(2,1)} %shard_map.74), channel_id=1, source_target_pairs={{1,3},{5,7},{9,11},{13,15},{17,19},{21,23},{25,27},{29,31}} | collective-permute-start | bytes 1572872 | tf_op jit(solution)/shard_map/ppermute | solution.py:275
  9.8 10.6 %collective-permute-start.4 = (bf16[256,1024]{1,0:T(8,128)(2,1)}, bf16[256,1024]{1,0:T(8,128)(2,1)S(1)}, u32[]{:S(2)}, u32[]{:S(2)}) collective-permute-start(bf16[256,1024]{1,0:T(8,128)(2,1)} %shard_map.74), channel_id=1, source_target_pairs={{0,3},{4,7},{8,11},{12,15},{16,19},{20,23},{24,27},{28,31}} | collective-permute-start | bytes 1572872 | tf_op jit(solution)/shard_map/ppermute | solution.py:275
  10.5 5.9 %collective-permute-start.2 = (f32[4,2,256]{2,1,0:T(2,128)S(1)}, f32[4,2,256]{2,1,0:T(2,128)S(1)}, u32[]{:S(2)}, u32[]{:S(2)}) collective-permute-start(f32[4,2,256]{2,1,0:T(2,128)S(1)} %bitcast.18), channel_id=1, source_target_pairs={{0,1},{1,0},{2,3},{3,2},{4,5},{5,4},{6,7},{7,6},{8,9},{9,8},{10,11... | collective-permute-start | bytes 24584 | tf_op jit(solution)/shard_map/ppermute | solution.py:278
  12.3 17.4 %collective-permute-start = (bf16[224,1024]{1,0:T(8,128)(2,1)}, bf16[224,1024]{1,0:T(8,128)(2,1)}, u32[]{:S(2)}, u32[]{:S(2)}) collective-permute-start(bf16[224,1024]{1,0:T(8,128)(2,1)} %slice.4), channel_id=1, source_target_pairs={{1,3},{5,7},{9,11},{13,15},{17,19},{21,23},{25,27},{29,31}} | collective-permute-start | bytes 1376264 | tf_op jit(solution)/shard_map/ppermute | solution.py:275
  14.5 2.6 %copy-start.1 = (bf16[512,512]{1,0:T(8,128)(2,1)S(1)}, bf16[512,512]{1,0:T(8,128)(2,1)}, u32[]{:S(2)}) copy-start(bf16[512,512]{1,0:T(8,128)(2,1)} %constant.17.clone.refs_6_.refs_8_) | copy-start | bytes 1572868
  14.5 2.6 %copy-start.2 = (bf16[512,768]{1,0:T(8,128)(2,1)S(1)}, bf16[512,768]{1,0:T(8,128)(2,1)}, u32[]{:S(2)}) copy-start(bf16[512,768]{1,0:T(8,128)(2,1)} %constant.15.clone.refs_1_) | copy-start | bytes 2359300
  14.5 2.6 %copy-start.5 = (s32[1024]{0:T(1024)S(1)}, s32[1024]{0:T(1024)}, u32[]{:S(2)}) copy-start(s32[1024]{0:T(1024)} %param.10) | copy-start | bytes 12292
  16.4 13.4 %collective-permute-start.1 = (bf16[224,1024]{1,0:T(8,128)(2,1)}, bf16[224,1024]{1,0:T(8,128)(2,1)S(1)}, u32[]{:S(2)}, u32[]{:S(2)}) collective-permute-start(bf16[224,1024]{1,0:T(8,128)(2,1)} %slice.4), channel_id=1, source_target_pairs={{0,3},{4,7},{8,11},{12,15},{16,19},{20,23},{24,27},{28,31}} | collective-permute-start | bytes 1376264 | tf_op jit(solution)/shard_map/ppermute | solution.py:275
  20.4 9.4 %copy-start.3 = (bf16[512,224]{1,0:T(8,128)(2,1)S(1)}, bf16[512,224]{1,0:T(8,128)(2,1)}, u32[]{:S(2)}) copy-start(bf16[512,224]{1,0:T(8,128)(2,1)} %constant.16.clone.refs_1_) | copy-start | bytes 688132
  33.8 10.2 %collective-permute-start.7 = (bf16[128,512]{1,0:T(8,128)(2,1)S(1)}, bf16[128,512]{1,0:T(8,128)(2,1)S(1)}, u32[]{:S(2)}, u32[]{:S(2)}) collective-permute-start(bf16[128,512]{1,0:T(8,128)(2,1)S(1)} %get-tuple-element.27), channel_id=1, source_target_pairs={{1,4},{5,0},{9,12},{13,8},{3,6},{7,2},{11,14},{15,10},{17,20},{21,... | collective-permute-start | bytes 393224 | tf_op jit(solution)/shard_map/ppermute | solution.py:284
  36.8 8.6 %collective-permute-start.8 = (bf16[128,512]{1,0:T(8,128)(2,1)S(1)}, bf16[128,512]{1,0:T(8,128)(2,1)S(1)}, u32[]{:S(2)}, u32[]{:S(2)}) collective-permute-start(bf16[128,512]{1,0:T(8,128)(2,1)S(1)} %get-tuple-element.28), channel_id=1, source_target_pairs={{1,8},{5,12},{9,0},{13,4},{3,10},{7,14},{11,2},{15,6},{17,24},{21,... | collective-permute-start | bytes 393224 | tf_op jit(solution)/shard_map/ppermute | solution.py:284
  39.1 7.6 %collective-permute-start.9 = (bf16[128,512]{1,0:T(8,128)(2,1)S(1)}, bf16[128,512]{1,0:T(8,128)(2,1)S(1)}, u32[]{:S(2)}, u32[]{:S(2)}) collective-permute-start(bf16[128,512]{1,0:T(8,128)(2,1)S(1)} %get-tuple-element.29), channel_id=1, source_target_pairs={{1,12},{5,8},{9,4},{13,0},{3,14},{7,10},{11,6},{15,2},{17,28},{21,... | collective-permute-start | bytes 393224 | tf_op jit(solution)/shard_map/ppermute | solution.py:284
  41.4 6.5 %collective-permute-start.10 = (bf16[128,512]{1,0:T(8,128)(2,1)S(1)}, bf16[128,512]{1,0:T(8,128)(2,1)S(1)}, u32[]{:S(2)}, u32[]{:S(2)}) collective-permute-start(bf16[128,512]{1,0:T(8,128)(2,1)S(1)} %get-tuple-element.30), channel_id=1, source_target_pairs={{1,4},{5,0},{9,12},{13,8},{3,6},{7,2},{11,14},{15,10},{17,20},{21,... | collective-permute-start | bytes 393224 | tf_op jit(solution)/shard_map/ppermute | solution.py:284
  42.7 9.0 %collective-permute-start.11 = (bf16[128,512]{1,0:T(8,128)(2,1)S(1)}, bf16[128,512]{1,0:T(8,128)(2,1)S(1)}, u32[]{:S(2)}, u32[]{:S(2)}) collective-permute-start(bf16[128,512]{1,0:T(8,128)(2,1)S(1)} %get-tuple-element.31), channel_id=1, source_target_pairs={{1,8},{5,12},{9,0},{13,4},{3,10},{7,14},{11,2},{15,6},{17,24},{21,... | collective-permute-start | bytes 393224 | tf_op jit(solution)/shard_map/ppermute | solution.py:284
  44.1 8.9 %collective-permute-start.12 = (bf16[128,512]{1,0:T(8,128)(2,1)S(1)}, bf16[128,512]{1,0:T(8,128)(2,1)S(1)}, u32[]{:S(2)}, u32[]{:S(2)}) collective-permute-start(bf16[128,512]{1,0:T(8,128)(2,1)S(1)} %get-tuple-element.32), channel_id=1, source_target_pairs={{1,12},{5,8},{9,4},{13,0},{3,14},{7,10},{11,6},{15,2},{17,28},{21,... | collective-permute-start | bytes 393224 | tf_op jit(solution)/shard_map/ppermute | solution.py:284
  45.4 8.9 %collective-permute-start.16 = (bf16[128,512]{1,0:T(8,128)(2,1)S(1)}, bf16[128,512]{1,0:T(8,128)(2,1)S(1)}, u32[]{:S(2)}, u32[]{:S(2)}) collective-permute-start(bf16[128,512]{1,0:T(8,128)(2,1)S(1)} %get-tuple-element.36), channel_id=1, source_target_pairs={{0,5},{4,1},{8,13},{12,9},{2,7},{6,3},{10,15},{14,11},{16,21},{20,... | collective-permute-start | bytes 393224 | tf_op jit(solution)/shard_map/ppermute | solution.py:284
  46.7 10.1 %collective-permute-start.17 = (bf16[128,512]{1,0:T(8,128)(2,1)S(1)}, bf16[128,512]{1,0:T(8,128)(2,1)S(1)}, u32[]{:S(2)}, u32[]{:S(2)}) collective-permute-start(bf16[128,512]{1,0:T(8,128)(2,1)S(1)} %get-tuple-element.37), channel_id=1, source_target_pairs={{0,9},{4,13},{8,1},{12,5},{2,11},{6,15},{10,3},{14,7},{16,25},{20,... | collective-permute-start | bytes 393224 | tf_op jit(solution)/shard_map/ppermute | solution.py:284
  48.0 17.0 %collective-permute-start.6 = (bf16[256,512]{1,0:T(8,128)(2,1)S(1)}, bf16[256,512]{1,0:T(8,128)(2,1)S(1)}, u32[]{:S(2)}, u32[]{:S(2)}) collective-permute-start(bf16[256,512]{1,0:T(8,128)(2,1)S(1)} %get-tuple-element.26), channel_id=1, source_target_pairs={{0,1},{1,0},{2,3},{3,2},{4,5},{5,4},{6,7},{7,6},{8,9},{9,8},{10,11... | collective-permute-start | bytes 786440 | tf_op jit(solution)/shard_map/ppermute | solution.py:278
  51.7 8.2 %collective-permute-start.18 = (bf16[128,512]{1,0:T(8,128)(2,1)S(1)}, bf16[128,512]{1,0:T(8,128)(2,1)S(1)}, u32[]{:S(2)}, u32[]{:S(2)}) collective-permute-start(bf16[128,512]{1,0:T(8,128)(2,1)S(1)} %get-tuple-element.38), channel_id=1, source_target_pairs={{0,13},{4,9},{8,5},{12,1},{2,15},{6,11},{10,7},{14,3},{16,29},{20,... | collective-permute-start | bytes 393224 | tf_op jit(solution)/shard_map/ppermute | solution.py:284
  53.0 8.9 %collective-permute-start.13 = (bf16[128,512]{1,0:T(8,128)(2,1)S(1)}, bf16[128,512]{1,0:T(8,128)(2,1)S(1)}, u32[]{:S(2)}, u32[]{:S(2)}) collective-permute-start(bf16[128,512]{1,0:T(8,128)(2,1)S(1)} %get-tuple-element.33), channel_id=1, source_target_pairs={{0,5},{4,1},{8,13},{12,9},{2,7},{6,3},{10,15},{14,11},{16,21},{20,... | collective-permute-start | bytes 393224 | tf_op jit(solution)/shard_map/ppermute | solution.py:284
  54.3 8.6 %collective-permute-start.14 = (bf16[128,512]{1,0:T(8,128)(2,1)S(1)}, bf16[128,512]{1,0:T(8,128)(2,1)S(1)}, u32[]{:S(2)}, u32[]{:S(2)}) collective-permute-start(bf16[128,512]{1,0:T(8,128)(2,1)S(1)} %get-tuple-element.34), channel_id=1, source_target_pairs={{0,9},{4,13},{8,1},{12,5},{2,11},{6,15},{10,3},{14,7},{16,25},{20,... | collective-permute-start | bytes 393224 | tf_op jit(solution)/shard_map/ppermute | solution.py:284
  56.8 8.2 %collective-permute-start.15 = (bf16[128,512]{1,0:T(8,128)(2,1)S(1)}, bf16[128,512]{1,0:T(8,128)(2,1)S(1)}, u32[]{:S(2)}, u32[]{:S(2)}) collective-permute-start(bf16[128,512]{1,0:T(8,128)(2,1)S(1)} %get-tuple-element.35), channel_id=1, source_target_pairs={{0,13},{4,9},{8,5},{12,1},{2,15},{6,11},{10,7},{14,3},{16,29},{20,... | collective-permute-start | bytes 393224 | tf_op jit(solution)/shard_map/ppermute | solution.py:284

commit v6 on v5

--- a/solution.py
+++ b/solution.py
@@ -116,22 +116,10 @@
         out_ref[...] = placed.astype(jnp.bfloat16)
 
 
-def rows_kernel(first, v_ref, out_ref, held_ref, sems):
-    count = held_ref.shape[1]
-    strips = NS // LANES
-    copies = [
-        pltpu.make_async_copy(
-            v_ref.at[pl.ds(first, count), j // strips, :, pl.ds(j % strips * LANES, LANES)],
-            held_ref.at[j],
-            sems.at[j],
-        )
-        for j in range(CYL * strips)
-    ]
-    for copy in copies:
-        copy.start()
-    for j, copy in enumerate(copies):
-        copy.wait()
-        out_ref[:, j * LANES : (j + 1) * LANES] = held_ref[j].reshape(2 * count, LANES)
+def halo_rows_kernel(x_ref, near_ref, far_ref):
+    near_at = x_ref.shape[0] - near_ref.shape[0]
+    near_ref[...] = x_ref[near_at:, :]
+    far_ref[...] = x_ref[near_at - far_ref.shape[0] : near_at, :]
 
 
 def late_kernel(block, n_owner, where_ref, filt_ref, x0, x1, g0, g1, beam_ref, keep_ref, table_ref, *refs):
@@ -246,7 +234,7 @@
         out_specs=[VMEM] * len(out_shape) if many else VMEM,
         scratch_shapes=list(scratch),
         cost_estimate=pl.CostEstimate(flops=flops, bytes_accessed=nbytes, transcendentals=0),
-        compiler_params=pltpu.CompilerParams(vmem_limit_bytes=40 << 20),
+        compiler_params=pltpu.CompilerParams(vmem_limit_bytes=24 << 20),
     )
 
 
@@ -300,25 +288,7 @@
 
     where = jnp.stack([me, pol]).astype(jnp.int32)
     keep = keep_flags.reshape(1, -1)
-    count = BLOCK * UPCH
-    near_rows = call(
-        functools.partial(rows_kernel, samples.shape[0] - count),
-        jax.ShapeDtypeStruct((BLOCK * ROWS, CYL * NS), bf16),
-        0,
-        0,
-        1 << 20,
-        whole=1,
-        scratch=[pltpu.VMEM((CYL * NS // LANES, count, 2, LANES), bf16), pltpu.SemaphoreType.DMA((CYL * NS // LANES,))],
-    )(samples)
-    near0 = ahead(near_rows, 0)
-    near1 = ahead(near_rows, 1)
-    x = samples.transpose(0, 2, 1, 3).reshape(samples.shape[0] * 2, CYL * NS)
-    x = lax.optimization_barrier(x)
-    other = swap(x)
-    gain_other = swap(gain)
-    far_rows = x[x.shape[0] - (TAPS - 1) * ROWS : x.shape[0] - BLOCK * ROWS]
-    far0 = ahead(far_rows, 0)
-    far1 = ahead(far_rows, 1)
+    reach, edge_rows = BLOCK * ROWS, (TAPS - 1 - BLOCK) * ROWS
     table = call(
         functools.partial(place_table_kernel, most_sets),
         jax.ShapeDtypeStruct((n_owner, beams, width), bf16),
@@ -327,6 +297,22 @@
         4 << 20,
         scalars=1,
     )(where, owner_table.reshape(1, -1))
+    samples, table = lax.optimization_barrier((samples, table))
+    x = samples.transpose(0, 2, 1, 3).reshape(samples.shape[0] * 2, CYL * NS)
+    x = lax.optimization_barrier(x)
+    near_rows, far_rows = call(
+        halo_rows_kernel,
+        [jax.ShapeDtypeStruct((rows, CYL * NS), bf16) for rows in (reach, edge_rows)],
+        1,
+        0,
+        2 << 20,
+    )(x)
+    near0 = ahead(near_rows, 0)
+    near1 = ahead(near_rows, 1)
+    other = swap(x)
+    gain_other = swap(gain)
+    far0 = ahead(far_rows, 0)
+    far1 = ahead(far_rows, 1)
     common = (gain, gain_other, beam_table, keep, table)
     late = []
     got = []
@@ -344,7 +330,7 @@
         other,
         *common,
         after=late[1][:1],
-        more=[jax.ShapeDtypeStruct((2 * CYL, BLOCK * ROWS, NS), jnp.float32)],
+        more=[jax.ShapeDtypeStruct((2 * CYL, reach, NS), jnp.float32)],
     )
     near_got = spread(near, 1)
     *far, own = form(

time: 67.1 us -> 65.4 us (0.975)
  waiting for transfers between devices: 10.8 us -> 17.3 us
  Pallas kernels: 18.9 us -> 13.6 us
  local copies, waits for them, and re-layouts: 4.97 us -> 2.25 us
    ppermute x4, waiting for transfers between devices: 2.76 us -> 9.24 us  [ahead(): lax.ppermute(part, ('tm', 'pol'), [(i * 2 + source, j * 2 + 1) for i, j i...]
    pallas_call x4, Pallas kernels: 13.9 us -> 10.1 us  [form(): call(body, shape + list(more), len(arrays), 4 * 512 * 1024 * 1024, 4 << 2...]
    transpose x1, local copies, waits for them, and re-layouts: 2.67 us -> 1.08 us  [per_device(): x = samples.transpose(0, 2, 1, 3).reshape(samples.shape[0] * 2, CYL * NS)]
    pallas_call x1, Pallas kernels: 1.52 us -> 0.06 us  [per_device(): call(halo_rows_kernel, [jax.ShapeDtypeStruct((rows, CYL * NS), bf16) for...]
    slice x1 -> x0, local copies, waits for them, and re-layouts: 0.8 us -> none  [per_device(): far_rows = x[x.shape[0] - (TAPS - 1) * ROWS:x.shape[0] - BLOCK * ROWS]]
  transfers between devices with their start and end apart: 19 -> 19, of which waited for: 6 -> 7; matrix products, arithmetic and copies ran while one was open for 1% -> 0% of each run, Pallas kernels for 20% -> 10%
where the time goes in v6:
time: 65.4 us; the launch traced here: 65 us
  starting transfers between devices  31.4 us (48%)
  waiting for transfers between devices  17.3 us (26%)
  Pallas kernels  13.6 us (21%)
  local copies, waits for them, and re-layouts  2.25 us (3%)
    ppermute x12, starting transfers between devices, spread(): got.append(lax.ppermute(blocks[k], ('freq', 'pol'), route))  19.3 us
    pallas_call x4, Pallas kernels, form(): call(body, shape + list(more), len(arrays), 4 * 512 * 1024 * 1024, 4 << 2...  10.1 us
    ppermute x4, waiting for transfers between devices, ahead(): lax.ppermute(part, ('tm', 'pol'), [(i * 2 + source, j * 2 + 1) for i, j i...  9.24 us
    ppermute x12, waiting for transfers between devices, spread(): got.append(lax.ppermute(blocks[k], ('freq', 'pol'), route))  8.06 us
    ppermute x4, starting transfers between devices, ahead(): lax.ppermute(part, ('tm', 'pol'), [(i * 2 + source, j * 2 + 1) for i, j i...  7.31 us
    ppermute x3, starting transfers between devices, swap(): return lax.ppermute(part, 'pol', [(0, 1), (1, 0)])  4.85 us
    pallas_call x1, Pallas kernels, per_device(): call(functools.partial(place_table_kernel, most_sets), jax.ShapeDtypeStru...  1.85 us
    pallas_call x1, Pallas kernels, per_device(): call(functools.partial(gather_kernel, n_owner), out_shape, len(arrays), 0...  1.59 us
  transfers between devices with their start and end apart: 19, of which 7 were waited for; matrix products, arithmetic and copies ran while one was open for 0% of the time, Pallas kernels for 10%

profile of v6, /device:TPU:1, one launch (start us, length us, event | category | flops | bytes accessed | tf_op | source)
XLA Modules:
  0.0 65.0 jit_solution(9088393709059600577)
XLA Ops:
  0.0 0.1 pad_add_fusion.refs_0_
  0.1 0.7 %copy-done.5 = s32[64]{0:T(128)S(1)} copy-done((s32[64]{0:T(128)S(1)}, s32[64]{0:T(128)}, u32[]{:S(2)}) %copy-start.5) | copy-done | bytes 280
  0.7 1.8 %shard_map.73.refs_8_.refs_10_ = bf16[4,1024,512]{2,1,0:T(8,128)(2,1)S(1)} custom-call(s32[2]{0:T(128)S(1)} %pad_add_fusion.refs_0_, s32[1,64]{1,0:T(1,128)S(1)} %bitcast.24), custom_call_target="tpu_custom_call" | custom-call | flops 16777216 | bytes 4194304 | tf_op jit(solution)/shard_map/pallas_call | solution.py:292
  2.6 1.1 %copy.8 = bf16[512,2,4,256]{3,2,1,0:T(4,128)(2,1)S(1)} copy(bf16[512,2,4,256]{3,1,2,0:T(2,128)(2,1)S(1)} %bitcast.26) | data formatting | bytes 4194304 | tf_op jit(solution)/shard_map/transpose | solution.py:301
  3.7 0.5 copy.9
  4.2 0.0 copy-start.3
  4.2 0.0 copy-start
  4.2 0.0 copy-start.1
  4.2 0.0 copy-start.4
  4.2 0.1 collective-permute-start.5
  4.3 0.1 shard_map.74
  4.4 4.6 %collective-permute-start.3 = (bf16[256,1024]{1,0:T(8,128)(2,1)S(1)}, bf16[256,1024]{1,0:T(8,128)(2,1)S(1)}, u32[]{:S(2)}, u32[]{:S(2)}) collective-permute-start(bf16[256,1024]{1,0:T(8,128)(2,1)S(1)} %get-tuple-element.29), channel_id=1, source_target_pairs={{1,3},{5,7},{9,11},{13,15},{17,19},{21,23},{25,27},{29,31}} | collective-permute-start | bytes 1572872 | tf_op jit(solution)/shard_map/ppermute | solution.py:263
  9.0 0.7 %collective-permute-start.4 = (bf16[256,1024]{1,0:T(8,128)(2,1)S(1)}, bf16[256,1024]{1,0:T(8,128)(2,1)S(1)}, u32[]{:S(2)}, u32[]{:S(2)}) collective-permute-start(bf16[256,1024]{1,0:T(8,128)(2,1)S(1)} %get-tuple-element.29), channel_id=1, source_target_pairs={{0,3},{4,7},{8,11},{12,15},{16,19},{20,23},{24,27},{28,31}} | collective-permute-start | bytes 1572872 | tf_op jit(solution)/shard_map/ppermute | solution.py:263
  9.7 1.1 %collective-permute-start.2 = (f32[4,2,256]{2,1,0:T(2,128)S(1)}, f32[4,2,256]{2,1,0:T(2,128)S(1)}, u32[]{:S(2)}, u32[]{:S(2)}) collective-permute-start(f32[4,2,256]{2,1,0:T(2,128)S(1)} %bitcast.15), channel_id=1, source_target_pairs={{0,1},{1,0},{2,3},{3,2},{4,5},{5,4},{6,7},{7,6},{8,9},{9,8},{10,11... | collective-permute-start | bytes 24584 | tf_op jit(solution)/shard_map/ppermute | solution.py:266
  10.8 1.3 %collective-permute-start = (bf16[224,1024]{1,0:T(8,128)(2,1)S(1)}, bf16[224,1024]{1,0:T(8,128)(2,1)S(1)}, u32[]{:S(2)}, u32[]{:S(2)}) collective-permute-start(bf16[224,1024]{1,0:T(8,128)(2,1)S(1)} %get-tuple-element.27), channel_id=1, source_target_pairs={{1,3},{5,7},{9,11},{13,15},{17,19},{21,23},{25,27},{29,31}} | collective-permute-start | bytes 1376264 | tf_op jit(solution)/shard_map/ppermute | solution.py:263
  12.1 0.0 collective-permute-done.2.refs_5_.refs_7_
  12.1 0.7 %collective-permute-start.1 = (bf16[224,1024]{1,0:T(8,128)(2,1)S(1)}, bf16[224,1024]{1,0:T(8,128)(2,1)S(1)}, u32[]{:S(2)}, u32[]{:S(2)}) collective-permute-start(bf16[224,1024]{1,0:T(8,128)(2,1)S(1)} %get-tuple-element.27), channel_id=1, source_target_pairs={{0,3},{4,7},{8,11},{12,15},{16,19},{20,23},{24,27},{28,31}} | collective-permute-start | bytes 1376264 | tf_op jit(solution)/shard_map/ppermute | solution.py:263
  12.8 0.0 collective-permute-done.5.refs_3_.refs_5_
  12.8 0.6 shard_map.75
  13.4 0.6 shard_map.76
  14.0 4.9 %collective-permute-done.3.refs_2_ = bf16[256,1024]{1,0:T(8,128)(2,1)S(1)} collective-permute-done((bf16[256,1024]{1,0:T(8,128)(2,1)S(1)}, bf16[256,1024]{1,0:T(8,128)(2,1)S(1)}, u32[]{:S(2)}, u32[]{:S(2)}) %collective-permute-start.3) | collective-permute-done | bytes 524320 | tf_op jit(solution)/shard_map/ppermute | solution.py:263
  18.8 5.4 %shard_map.77 = (bf16[128,512]{1,0:T(8,128)(2,1)S(1)}, bf16[128,512]{1,0:T(8,128)(2,1)S(1)}, bf16[128,512]{1,0:T(8,128)(2,1)S(1)}, bf16[128,512]{1,0:T(8,128)(2,1)S(1)}, f32[8,256,256]{2,1,0:T(8,128)S(1)}) custom-call(s32[2]{0:T(128)S(1)} %pad_add_fusion.refs_0_, bf16[512,768]{1,0:T(8,128)(2,1)S(1)} %copy-done.1, ...), custom_call_target="tpu_custom_call" | custom-call | flops 2147483648 | bytes 4194304 | tf_op jit(solution)/shard_map/pallas_call | solution.py:278
  24.3 4.4 %collective-permute-done.refs_2_ = bf16[224,1024]{1,0:T(8,128)(2,1)S(1)} collective-permute-done((bf16[224,1024]{1,0:T(8,128)(2,1)S(1)}, bf16[224,1024]{1,0:T(8,128)(2,1)S(1)}, u32[]{:S(2)}, u32[]{:S(2)}) %collective-permute-start) | collective-permute-done | bytes 458784 | tf_op jit(solution)/shard_map/ppermute | solution.py:263
  28.7 3.6 %shard_map.78 = (bf16[128,512]{1,0:T(8,128)(2,1)}, bf16[128,512]{1,0:T(8,128)(2,1)S(1)}, bf16[128,512]{1,0:T(8,128)(2,1)S(1)}, bf16[128,512]{1,0:T(8,128)(2,1)S(1)}, bf16[256,512]{1,0:T(8,128)(2,1)S(1)}) custom-call(s32[2]{0:T(128)S(1)} %pad_add_fusion.refs_0_, bf16[512,224]{1,0:T(8,128)(2,1)S(1)} %copy-done.2, ...), custom_call_target="tpu_custom_call" | custom-call | flops 2147483648 | bytes 4194304 | tf_op jit(solution)/shard_map/pallas_call | solution.py:278
  32.2 3.0 %collective-permute-start.7 = (bf16[128,512]{1,0:T(8,128)(2,1)S(1)}, bf16[128,512]{1,0:T(8,128)(2,1)S(1)}, u32[]{:S(2)}, u32[]{:S(2)}) collective-permute-start(bf16[128,512]{1,0:T(8,128)(2,1)S(1)} %get-tuple-element.35), channel_id=1, source_target_pairs={{1,4},{5,0},{9,12},{13,8},{3,6},{7,2},{11,14},{15,10},{17,20},{21,... | collective-permute-start | bytes 393224 | tf_op jit(solution)/shard_map/ppermute | solution.py:272
  35.2 2.3 %collective-permute-start.8 = (bf16[128,512]{1,0:T(8,128)(2,1)S(1)}, bf16[128,512]{1,0:T(8,128)(2,1)S(1)}, u32[]{:S(2)}, u32[]{:S(2)}) collective-permute-start(bf16[128,512]{1,0:T(8,128)(2,1)S(1)} %get-tuple-element.36), channel_id=1, source_target_pairs={{1,8},{5,12},{9,0},{13,4},{3,10},{7,14},{11,2},{15,6},{17,24},{21,... | collective-permute-start | bytes 393224 | tf_op jit(solution)/shard_map/ppermute | solution.py:272
  37.6 2.3 %collective-permute-start.9 = (bf16[128,512]{1,0:T(8,128)(2,1)S(1)}, bf16[128,512]{1,0:T(8,128)(2,1)S(1)}, u32[]{:S(2)}, u32[]{:S(2)}) collective-permute-start(bf16[128,512]{1,0:T(8,128)(2,1)S(1)} %get-tuple-element.37), channel_id=1, source_target_pairs={{1,12},{5,8},{9,4},{13,0},{3,14},{7,10},{11,6},{15,2},{17,28},{21,... | collective-permute-start | bytes 393224 | tf_op jit(solution)/shard_map/ppermute | solution.py:272
  39.9 1.3 %collective-permute-start.10 = (bf16[128,512]{1,0:T(8,128)(2,1)S(1)}, bf16[128,512]{1,0:T(8,128)(2,1)S(1)}, u32[]{:S(2)}, u32[]{:S(2)}) collective-permute-start(bf16[128,512]{1,0:T(8,128)(2,1)S(1)} %get-tuple-element.38), channel_id=1, source_target_pairs={{1,4},{5,0},{9,12},{13,8},{3,6},{7,2},{11,14},{15,10},{17,20},{21,... | collective-permute-start | bytes 393224 | tf_op jit(solution)/shard_map/ppermute | solution.py:272
  41.2 1.3 %collective-permute-start.11 = (bf16[128,512]{1,0:T(8,128)(2,1)S(1)}, bf16[128,512]{1,0:T(8,128)(2,1)S(1)}, u32[]{:S(2)}, u32[]{:S(2)}) collective-permute-start(bf16[128,512]{1,0:T(8,128)(2,1)S(1)} %get-tuple-element.39), channel_id=1, source_target_pairs={{1,8},{5,12},{9,0},{13,4},{3,10},{7,14},{11,2},{15,6},{17,24},{21,... | collective-permute-start | bytes 393224 | tf_op jit(solution)/shard_map/ppermute | solution.py:272
  42.5 0.0 collective-permute-done.7.refs_2_
  42.5 1.3 %collective-permute-start.12 = (bf16[128,512]{1,0:T(8,128)(2,1)S(1)}, bf16[128,512]{1,0:T(8,128)(2,1)S(1)}, u32[]{:S(2)}, u32[]{:S(2)}) collective-permute-start(bf16[128,512]{1,0:T(8,128)(2,1)S(1)} %get-tuple-element.40), channel_id=1, source_target_pairs={{1,12},{5,8},{9,4},{13,0},{3,14},{7,10},{11,6},{15,2},{17,28},{21,... | collective-permute-start | bytes 393224 | tf_op jit(solution)/shard_map/ppermute | solution.py:272
  43.8 1.3 %collective-permute-start.16 = (bf16[128,512]{1,0:T(8,128)(2,1)S(1)}, bf16[128,512]{1,0:T(8,128)(2,1)S(1)}, u32[]{:S(2)}, u32[]{:S(2)}) collective-permute-start(bf16[128,512]{1,0:T(8,128)(2,1)S(1)} %get-tuple-element.44), channel_id=1, source_target_pairs={{0,5},{4,1},{8,13},{12,9},{2,7},{6,3},{10,15},{14,11},{16,21},{20,... | collective-permute-start | bytes 393224 | tf_op jit(solution)/shard_map/ppermute | solution.py:272
  45.1 1.3 %collective-permute-start.17 = (bf16[128,512]{1,0:T(8,128)(2,1)S(1)}, bf16[128,512]{1,0:T(8,128)(2,1)S(1)}, u32[]{:S(2)}, u32[]{:S(2)}) collective-permute-start(bf16[128,512]{1,0:T(8,128)(2,1)S(1)} %get-tuple-element.45), channel_id=1, source_target_pairs={{0,9},{4,13},{8,1},{12,5},{2,11},{6,15},{10,3},{14,7},{16,25},{20,... | collective-permute-start | bytes 393224 | tf_op jit(solution)/shard_map/ppermute | solution.py:272
  46.4 0.0 collective-permute-done.10.refs_5_
  46.4 3.7 %collective-permute-start.6 = (bf16[256,512]{1,0:T(8,128)(2,1)S(1)}, bf16[256,512]{1,0:T(8,128)(2,1)S(1)}, u32[]{:S(2)}, u32[]{:S(2)}) collective-permute-start(bf16[256,512]{1,0:T(8,128)(2,1)S(1)} %get-tuple-element.34), channel_id=1, source_target_pairs={{0,1},{1,0},{2,3},{3,2},{4,5},{5,4},{6,7},{7,6},{8,9},{9,8},{10,11... | collective-permute-start | bytes 786440 | tf_op jit(solution)/shard_map/ppermute | solution.py:266
  50.1 0.0 collective-permute-done.11.refs_6_
  50.1 1.3 %collective-permute-start.18 = (bf16[128,512]{1,0:T(8,128)(2,1)S(1)}, bf16[128,512]{1,0:T(8,128)(2,1)S(1)}, u32[]{:S(2)}, u32[]{:S(2)}) collective-permute-start(bf16[128,512]{1,0:T(8,128)(2,1)S(1)} %get-tuple-element.46), channel_id=1, source_target_pairs={{0,13},{4,9},{8,5},{12,1},{2,15},{6,11},{10,7},{14,3},{16,29},{20,... | collective-permute-start | bytes 393224 | tf_op jit(solution)/shard_map/ppermute | solution.py:272
  51.4 1.3 %collective-permute-start.13 = (bf16[128,512]{1,0:T(8,128)(2,1)S(1)}, bf16[128,512]{1,0:T(8,128)(2,1)S(1)}, u32[]{:S(2)}, u32[]{:S(2)}) collective-permute-start(bf16[128,512]{1,0:T(8,128)(2,1)S(1)} %get-tuple-element.41), channel_id=1, source_target_pairs={{0,5},{4,1},{8,13},{12,9},{2,7},{6,3},{10,15},{14,11},{16,21},{20,... | collective-permute-start | bytes 393224 | tf_op jit(solution)/shard_map/ppermute | solution.py:272
  52.7 0.0 collective-permute-done.16.refs_11_
  52.8 1.3 %collective-permute-start.14 = (bf16[128,512]{1,0:T(8,128)(2,1)S(1)}, bf16[128,512]{1,0:T(8,128)(2,1)S(1)}, u32[]{:S(2)}, u32[]{:S(2)}) collective-permute-start(bf16[128,512]{1,0:T(8,128)(2,1)S(1)} %get-tuple-element.42), channel_id=1, source_target_pairs={{0,9},{4,13},{8,1},{12,5},{2,11},{6,15},{10,3},{14,7},{16,25},{20,... | collective-permute-start | bytes 393224 | tf_op jit(solution)/shard_map/ppermute | solution.py:272
  54.1 1.2 %collective-permute-done.17.refs_12_ = bf16[128,512]{1,0:T(8,128)(2,1)S(1)} collective-permute-done((bf16[128,512]{1,0:T(8,128)(2,1)S(1)}, bf16[128,512]{1,0:T(8,128)(2,1)S(1)}, u32[]{:S(2)}, u32[]{:S(2)}) %collective-permute-start.17) | collective-permute-done | bytes 131104 | tf_op jit(solution)/shard_map/ppermute | solution.py:272
  55.2 1.3 %collective-permute-start.15 = (bf16[128,512]{1,0:T(8,128)(2,1)S(1)}, bf16[128,512]{1,0:T(8,128)(2,1)S(1)}, u32[]{:S(2)}, u32[]{:S(2)}) collective-permute-start(bf16[128,512]{1,0:T(8,128)(2,1)S(1)} %get-tuple-element.43), channel_id=1, source_target_pairs={{0,13},{4,9},{8,5},{12,1},{2,15},{6,11},{10,7},{14,3},{16,29},{20,... | collective-permute-start | bytes 393224 | tf_op jit(solution)/shard_map/ppermute | solution.py:272
  56.5 1.8 %collective-permute-done.18.refs_13_ = bf16[128,512]{1,0:T(8,128)(2,1)S(1)} collective-permute-done((bf16[128,512]{1,0:T(8,128)(2,1)S(1)}, bf16[128,512]{1,0:T(8,128)(2,1)S(1)}, u32[]{:S(2)}, u32[]{:S(2)}) %collective-permute-start.18) | collective-permute-done | bytes 131104 | tf_op jit(solution)/shard_map/ppermute | solution.py:272
  58.3 2.1 %collective-permute-done.13.refs_8_ = bf16[128,512]{1,0:T(8,128)(2,1)S(1)} collective-permute-done((bf16[128,512]{1,0:T(8,128)(2,1)S(1)}, bf16[128,512]{1,0:T(8,128)(2,1)S(1)}, u32[]{:S(2)}, u32[]{:S(2)}) %collective-permute-start.13) | collective-permute-done | bytes 131104 | tf_op jit(solution)/shard_map/ppermute | solution.py:272
  60.4 1.0 %collective-permute-done.14.refs_9_ = bf16[128,512]{1,0:T(8,128)(2,1)S(1)} collective-permute-done((bf16[128,512]{1,0:T(8,128)(2,1)S(1)}, bf16[128,512]{1,0:T(8,128)(2,1)S(1)}, u32[]{:S(2)}, u32[]{:S(2)}) %collective-permute-start.14) | collective-permute-done | bytes 131104 | tf_op jit(solution)/shard_map/ppermute | solution.py:272
  61.3 2.0 %collective-permute-done.15.refs_10_ = bf16[128,512]{1,0:T(8,128)(2,1)S(1)} collective-permute-done((bf16[128,512]{1,0:T(8,128)(2,1)S(1)}, bf16[128,512]{1,0:T(8,128)(2,1)S(1)}, u32[]{:S(2)}, u32[]{:S(2)}) %collective-permute-start.15) | collective-permute-done | bytes 131104 | tf_op jit(solution)/shard_map/ppermute | solution.py:272
  63.4 0.0 collective-permute-done.6.refs_1_
  63.4 1.6 %shard_map.79 = bf16[16,64,512]{2,1,0:T(8,128)(2,1)} custom-call(s32[2]{0:T(128)S(1)} %pad_add_fusion.refs_0_, bf16[256,512]{1,0:T(8,128)(2,1)S(1)} %collective-permute-done.6.refs_1_, bf16[128,512]{1,0:T(8,128)(2,1)S(1)} %collective-permute-done.7.refs_2_, bf16[128,512]{1,0:T(8,128)(2,1)S(1)} %collective-permute-done.8.refs_3_, ...), custom_call_target="tpu_custom_call" | custom-call | bytes 3145728 | tf_op jit(solution)/shard_map/pallas_call | solution.py:352
  (14 shorter events, 0.0 us)
Async XLA Ops:
  0.1 0.7 %copy-start.5 = (s32[64]{0:T(128)S(1)}, s32[64]{0:T(128)}, u32[]{:S(2)}) copy-start(s32[64]{0:T(128)} %param.9) | copy-start | bytes 772
  0.7 1.9 %copy-start.6 = (bf16[1,1,512,4,2,256]{5,4,3,2,1,0:T(2,128)(2,1)S(1)}, bf16[1,1,512,4,2,256]{5,4,3,2,1,0:T(2,128)(2,1)}, u32[]{:S(2)}) copy-start(bf16[1,1,512,4,2,256]{5,4,3,2,1,0:T(2,128)(2,1)} %param.7) | copy-start | bytes 6291460
  4.2 5.5 %copy-start.3 = (f32[1,1,4,2,256]{4,3,2,1,0:T(2,128)S(1)}, f32[1,1,4,2,256]{4,3,2,1,0:T(2,128)}, u32[]{:S(2)}) copy-start(f32[1,1,4,2,256]{4,3,2,1,0:T(2,128)} %param.8) | copy-start | bytes 24580
  4.2 8.6 %copy-start = (bf16[512,512]{1,0:T(8,128)(2,1)S(1)}, bf16[512,512]{1,0:T(8,128)(2,1)}, u32[]{:S(2)}) copy-start(bf16[512,512]{1,0:T(8,128)(2,1)} %constant.17.clone.refs_6_.refs_8_) | copy-start | bytes 1572868
  4.2 8.6 %copy-start.1 = (bf16[512,768]{1,0:T(8,128)(2,1)S(1)}, bf16[512,768]{1,0:T(8,128)(2,1)}, u32[]{:S(2)}) copy-start(bf16[512,768]{1,0:T(8,128)(2,1)} %constant.15.clone.refs_1_) | copy-start | bytes 2359300
  4.2 8.6 %copy-start.4 = (s32[1024]{0:T(1024)S(1)}, s32[1024]{0:T(1024)}, u32[]{:S(2)}) copy-start(s32[1024]{0:T(1024)} %param.10) | copy-start | bytes 12292
  4.2 8.6 %collective-permute-start.5 = (bf16[1024,1024]{1,0:T(8,128)(2,1)S(1)}, bf16[1024,1024]{1,0:T(8,128)(2,1)S(1)}, u32[]{:S(2)}, u32[]{:S(2)}) collective-permute-start(bf16[1024,1024]{1,0:T(8,128)(2,1)S(1)} %bitcast.10), channel_id=1, source_target_pairs={{0,1},{1,0},{2,3},{3,2},{4,5},{5,4},{6,7},{7,6},{8,9},{9,8},{10,11... | collective-permute-start | bytes 6291464 | tf_op jit(solution)/shard_map/ppermute | solution.py:266
  4.4 14.4 %collective-permute-start.3 = (bf16[256,1024]{1,0:T(8,128)(2,1)S(1)}, bf16[256,1024]{1,0:T(8,128)(2,1)S(1)}, u32[]{:S(2)}, u32[]{:S(2)}) collective-permute-start(bf16[256,1024]{1,0:T(8,128)(2,1)S(1)} %get-tuple-element.29), channel_id=1, source_target_pairs={{1,3},{5,7},{9,11},{13,15},{17,19},{21,23},{25,27},{29,31}} | collective-permute-start | bytes 1572872 | tf_op jit(solution)/shard_map/ppermute | solution.py:263
  9.0 9.8 %collective-permute-start.4 = (bf16[256,1024]{1,0:T(8,128)(2,1)S(1)}, bf16[256,1024]{1,0:T(8,128)(2,1)S(1)}, u32[]{:S(2)}, u32[]{:S(2)}) collective-permute-start(bf16[256,1024]{1,0:T(8,128)(2,1)S(1)} %get-tuple-element.29), channel_id=1, source_target_pairs={{0,3},{4,7},{8,11},{12,15},{16,19},{20,23},{24,27},{28,31}} | collective-permute-start | bytes 1572872 | tf_op jit(solution)/shard_map/ppermute | solution.py:263
  9.7 2.4 %collective-permute-start.2 = (f32[4,2,256]{2,1,0:T(2,128)S(1)}, f32[4,2,256]{2,1,0:T(2,128)S(1)}, u32[]{:S(2)}, u32[]{:S(2)}) collective-permute-start(f32[4,2,256]{2,1,0:T(2,128)S(1)} %bitcast.15), channel_id=1, source_target_pairs={{0,1},{1,0},{2,3},{3,2},{4,5},{5,4},{6,7},{7,6},{8,9},{9,8},{10,11... | collective-permute-start | bytes 24584 | tf_op jit(solution)/shard_map/ppermute | solution.py:266
  10.8 17.9 %collective-permute-start = (bf16[224,1024]{1,0:T(8,128)(2,1)S(1)}, bf16[224,1024]{1,0:T(8,128)(2,1)S(1)}, u32[]{:S(2)}, u32[]{:S(2)}) collective-permute-start(bf16[224,1024]{1,0:T(8,128)(2,1)S(1)} %get-tuple-element.27), channel_id=1, source_target_pairs={{1,3},{5,7},{9,11},{13,15},{17,19},{21,23},{25,27},{29,31}} | collective-permute-start | bytes 1376264 | tf_op jit(solution)/shard_map/ppermute | solution.py:263
  12.1 16.6 %collective-permute-start.1 = (bf16[224,1024]{1,0:T(8,128)(2,1)S(1)}, bf16[224,1024]{1,0:T(8,128)(2,1)S(1)}, u32[]{:S(2)}, u32[]{:S(2)}) collective-permute-start(bf16[224,1024]{1,0:T(8,128)(2,1)S(1)} %get-tuple-element.27), channel_id=1, source_target_pairs={{0,3},{4,7},{8,11},{12,15},{16,19},{20,23},{24,27},{28,31}} | collective-permute-start | bytes 1376264 | tf_op jit(solution)/shard_map/ppermute | solution.py:263
  18.8 9.8 %copy-start.2 = (bf16[512,224]{1,0:T(8,128)(2,1)S(1)}, bf16[512,224]{1,0:T(8,128)(2,1)}, u32[]{:S(2)}) copy-start(bf16[512,224]{1,0:T(8,128)(2,1)} %constant.16.clone.refs_1_) | copy-start | bytes 688132
  32.2 10.3 %collective-permute-start.7 = (bf16[128,512]{1,0:T(8,128)(2,1)S(1)}, bf16[128,512]{1,0:T(8,128)(2,1)S(1)}, u32[]{:S(2)}, u32[]{:S(2)}) collective-permute-start(bf16[128,512]{1,0:T(8,128)(2,1)S(1)} %get-tuple-element.35), channel_id=1, source_target_pairs={{1,4},{5,0},{9,12},{13,8},{3,6},{7,2},{11,14},{15,10},{17,20},{21,... | collective-permute-start | bytes 393224 | tf_op jit(solution)/shard_map/ppermute | solution.py:272
  35.2 8.6 %collective-permute-start.8 = (bf16[128,512]{1,0:T(8,128)(2,1)S(1)}, bf16[128,512]{1,0:T(8,128)(2,1)S(1)}, u32[]{:S(2)}, u32[]{:S(2)}) collective-permute-start(bf16[128,512]{1,0:T(8,128)(2,1)S(1)} %get-tuple-element.36), channel_id=1, source_target_pairs={{1,8},{5,12},{9,0},{13,4},{3,10},{7,14},{11,2},{15,6},{17,24},{21,... | collective-permute-start | bytes 393224 | tf_op jit(solution)/shard_map/ppermute | solution.py:272
  37.6 7.6 %collective-permute-start.9 = (bf16[128,512]{1,0:T(8,128)(2,1)S(1)}, bf16[128,512]{1,0:T(8,128)(2,1)S(1)}, u32[]{:S(2)}, u32[]{:S(2)}) collective-permute-start(bf16[128,512]{1,0:T(8,128)(2,1)S(1)} %get-tuple-element.37), channel_id=1, source_target_pairs={{1,12},{5,8},{9,4},{13,0},{3,14},{7,10},{11,6},{15,2},{17,28},{21,... | collective-permute-start | bytes 393224 | tf_op jit(solution)/shard_map/ppermute | solution.py:272
  39.9 6.5 %collective-permute-start.10 = (bf16[128,512]{1,0:T(8,128)(2,1)S(1)}, bf16[128,512]{1,0:T(8,128)(2,1)S(1)}, u32[]{:S(2)}, u32[]{:S(2)}) collective-permute-start(bf16[128,512]{1,0:T(8,128)(2,1)S(1)} %get-tuple-element.38), channel_id=1, source_target_pairs={{1,4},{5,0},{9,12},{13,8},{3,6},{7,2},{11,14},{15,10},{17,20},{21,... | collective-permute-start | bytes 393224 | tf_op jit(solution)/shard_map/ppermute | solution.py:272
  41.2 9.0 %collective-permute-start.11 = (bf16[128,512]{1,0:T(8,128)(2,1)S(1)}, bf16[128,512]{1,0:T(8,128)(2,1)S(1)}, u32[]{:S(2)}, u32[]{:S(2)}) collective-permute-start(bf16[128,512]{1,0:T(8,128)(2,1)S(1)} %get-tuple-element.39), channel_id=1, source_target_pairs={{1,8},{5,12},{9,0},{13,4},{3,10},{7,14},{11,2},{15,6},{17,24},{21,... | collective-permute-start | bytes 393224 | tf_op jit(solution)/shard_map/ppermute | solution.py:272
  42.5 8.9 %collective-permute-start.12 = (bf16[128,512]{1,0:T(8,128)(2,1)S(1)}, bf16[128,512]{1,0:T(8,128)(2,1)S(1)}, u32[]{:S(2)}, u32[]{:S(2)}) collective-permute-start(bf16[128,512]{1,0:T(8,128)(2,1)S(1)} %get-tuple-element.40), channel_id=1, source_target_pairs={{1,12},{5,8},{9,4},{13,0},{3,14},{7,10},{11,6},{15,2},{17,28},{21,... | collective-permute-start | bytes 393224 | tf_op jit(solution)/shard_map/ppermute | solution.py:272
  43.8 8.9 %collective-permute-start.16 = (bf16[128,512]{1,0:T(8,128)(2,1)S(1)}, bf16[128,512]{1,0:T(8,128)(2,1)S(1)}, u32[]{:S(2)}, u32[]{:S(2)}) collective-permute-start(bf16[128,512]{1,0:T(8,128)(2,1)S(1)} %get-tuple-element.44), channel_id=1, source_target_pairs={{0,5},{4,1},{8,13},{12,9},{2,7},{6,3},{10,15},{14,11},{16,21},{20,... | collective-permute-start | bytes 393224 | tf_op jit(solution)/shard_map/ppermute | solution.py:272
  45.1 10.1 %collective-permute-start.17 = (bf16[128,512]{1,0:T(8,128)(2,1)S(1)}, bf16[128,512]{1,0:T(8,128)(2,1)S(1)}, u32[]{:S(2)}, u32[]{:S(2)}) collective-permute-start(bf16[128,512]{1,0:T(8,128)(2,1)S(1)} %get-tuple-element.45), channel_id=1, source_target_pairs={{0,9},{4,13},{8,1},{12,5},{2,11},{6,15},{10,3},{14,7},{16,25},{20,... | collective-permute-start | bytes 393224 | tf_op jit(solution)/shard_map/ppermute | solution.py:272
  46.4 17.0 %collective-permute-start.6 = (bf16[256,512]{1,0:T(8,128)(2,1)S(1)}, bf16[256,512]{1,0:T(8,128)(2,1)S(1)}, u32[]{:S(2)}, u32[]{:S(2)}) collective-permute-start(bf16[256,512]{1,0:T(8,128)(2,1)S(1)} %get-tuple-element.34), channel_id=1, source_target_pairs={{0,1},{1,0},{2,3},{3,2},{4,5},{5,4},{6,7},{7,6},{8,9},{9,8},{10,11... | collective-permute-start | bytes 786440 | tf_op jit(solution)/shard_map/ppermute | solution.py:266
  50.1 8.2 %collective-permute-start.18 = (bf16[128,512]{1,0:T(8,128)(2,1)S(1)}, bf16[128,512]{1,0:T(8,128)(2,1)S(1)}, u32[]{:S(2)}, u32[]{:S(2)}) collective-permute-start(bf16[128,512]{1,0:T(8,128)(2,1)S(1)} %get-tuple-element.46), channel_id=1, source_target_pairs={{0,13},{4,9},{8,5},{12,1},{2,15},{6,11},{10,7},{14,3},{16,29},{20,... | collective-permute-start | bytes 393224 | tf_op jit(solution)/shard_map/ppermute | solution.py:272
  51.4 8.9 %collective-permute-start.13 = (bf16[128,512]{1,0:T(8,128)(2,1)S(1)}, bf16[128,512]{1,0:T(8,128)(2,1)S(1)}, u32[]{:S(2)}, u32[]{:S(2)}) collective-permute-start(bf16[128,512]{1,0:T(8,128)(2,1)S(1)} %get-tuple-element.41), channel_id=1, source_target_pairs={{0,5},{4,1},{8,13},{12,9},{2,7},{6,3},{10,15},{14,11},{16,21},{20,... | collective-permute-start | bytes 393224 | tf_op jit(solution)/shard_map/ppermute | solution.py:272
  52.8 8.6 %collective-permute-start.14 = (bf16[128,512]{1,0:T(8,128)(2,1)S(1)}, bf16[128,512]{1,0:T(8,128)(2,1)S(1)}, u32[]{:S(2)}, u32[]{:S(2)}) collective-permute-start(bf16[128,512]{1,0:T(8,128)(2,1)S(1)} %get-tuple-element.42), channel_id=1, source_target_pairs={{0,9},{4,13},{8,1},{12,5},{2,11},{6,15},{10,3},{14,7},{16,25},{20,... | collective-permute-start | bytes 393224 | tf_op jit(solution)/shard_map/ppermute | solution.py:272
  55.2 8.2 %collective-permute-start.15 = (bf16[128,512]{1,0:T(8,128)(2,1)S(1)}, bf16[128,512]{1,0:T(8,128)(2,1)S(1)}, u32[]{:S(2)}, u32[]{:S(2)}) collective-permute-start(bf16[128,512]{1,0:T(8,128)(2,1)S(1)} %get-tuple-element.43), channel_id=1, source_target_pairs={{0,13},{4,9},{8,5},{12,1},{2,15},{6,11},{10,7},{14,3},{16,29},{20,... | collective-permute-start | bytes 393224 | tf_op jit(solution)/shard_map/ppermute | solution.py:272

commit v7 on v6

--- a/solution.py
+++ b/solution.py
@@ -42,10 +42,7 @@
         table[0, frame, :, taps, :, 1] = sin_part
         table[1, frame, :, taps, :, 0] = -sin_part
         table[1, frame, :, taps, :, 1] = cos_part
-    table = table.reshape(2 * BLOCK * UPCH, (TAPS + BLOCK) * ROWS).astype(np.float32)
-    high = table.astype(jnp.bfloat16)
-    low = (table - high.astype(np.float32)).astype(jnp.bfloat16)
-    return np.concatenate([high, low], axis=0)
+    return table.reshape(2 * BLOCK * UPCH, (TAPS + BLOCK) * ROWS).astype(np.float32).astype(jnp.bfloat16)
 
 
 def beam_matrix():
@@ -91,11 +88,11 @@
 
 
 def filtered(terms):
-    both = None
+    total = None
     for table, rows in terms:
         term = jnp.dot(table, rows, preferred_element_type=jnp.float32)
-        both = term if both is None else both + term
-    return both[: both.shape[0] // 2] + both[both.shape[0] // 2 :]
+        total = term if total is None else total + term
+    return total
 
 
 def adder(pol, sum_ref, keep_ref):

time: 65.4 us -> 65.6 us (level)
  Pallas kernels: 13.6 us -> 12 us
  waiting for transfers between devices: 17.3 us -> 18.8 us
    pallas_call x4, Pallas kernels: 10.1 us -> 8.54 us  [form(): call(body, shape + list(more), len(arrays), 4 * 512 * 1024 * 1024, 4 << 2...]
    ppermute x4, waiting for transfers between devices: 9.24 us -> 10.7 us  [ahead(): lax.ppermute(part, ('tm', 'pol'), [(i * 2 + source, j * 2 + 1) for i, j i...]
  transfers between devices with their start and end apart: 19 -> 19, of which waited for: 7 -> 7; matrix products, arithmetic and copies ran while one was open for 0% -> 0% of each run, Pallas kernels for 10% -> 8%
where the time goes in v7:
time: 65.6 us; the launch traced here: 65.2 us
  starting transfers between devices  31.7 us (48%)
  waiting for transfers between devices  18.8 us (29%)
  Pallas kernels  12 us (18%)
  local copies, waits for them, and re-layouts  2.25 us (3%)
    ppermute x12, starting transfers between devices, spread(): got.append(lax.ppermute(blocks[k], ('freq', 'pol'), route))  19.5 us
    ppermute x4, waiting for transfers between devices, ahead(): lax.ppermute(part, ('tm', 'pol'), [(i * 2 + source, j * 2 + 1) for i, j i...  10.7 us
    pallas_call x4, Pallas kernels, form(): call(body, shape + list(more), len(arrays), 4 * 512 * 1024 * 1024, 4 << 2...  8.54 us
    ppermute x12, waiting for transfers between devices, spread(): got.append(lax.ppermute(blocks[k], ('freq', 'pol'), route))  8.06 us
    ppermute x4, starting transfers between devices, ahead(): lax.ppermute(part, ('tm', 'pol'), [(i * 2 + source, j * 2 + 1) for i, j i...  7.31 us
    ppermute x3, starting transfers between devices, swap(): return lax.ppermute(part, 'pol', [(0, 1), (1, 0)])  4.85 us
    pallas_call x1, Pallas kernels, per_device(): call(functools.partial(place_table_kernel, most_sets), jax.ShapeDtypeStru...  1.85 us
    pallas_call x1, Pallas kernels, per_device(): call(functools.partial(gather_kernel, n_owner), out_shape, len(arrays), 0...  1.59 us
  transfers between devices with their start and end apart: 19, of which 7 were waited for; matrix products, arithmetic and copies ran while one was open for 0% of the time, Pallas kernels for 8%

profile of v7, /device:TPU:1, one launch (start us, length us, event | category | flops | bytes accessed | tf_op | source)
XLA Modules:
  0.0 65.2 jit_solution(11235892372940428112)
XLA Ops:
  0.0 0.1 pad_add_fusion.refs_0_
  0.1 0.7 %copy-done.5 = s32[64]{0:T(128)S(1)} copy-done((s32[64]{0:T(128)S(1)}, s32[64]{0:T(128)}, u32[]{:S(2)}) %copy-start.5) | copy-done | bytes 280
  0.7 1.8 %shard_map.73.refs_8_.refs_10_ = bf16[4,1024,512]{2,1,0:T(8,128)(2,1)S(1)} custom-call(s32[2]{0:T(128)S(1)} %pad_add_fusion.refs_0_, s32[1,64]{1,0:T(1,128)S(1)} %bitcast.24), custom_call_target="tpu_custom_call" | custom-call | flops 16777216 | bytes 4194304 | tf_op jit(solution)/shard_map/pallas_call | solution.py:289
  2.6 1.1 %copy.8 = bf16[512,2,4,256]{3,2,1,0:T(4,128)(2,1)S(1)} copy(bf16[512,2,4,256]{3,1,2,0:T(2,128)(2,1)S(1)} %bitcast.26) | data formatting | bytes 4194304 | tf_op jit(solution)/shard_map/transpose | solution.py:298
  3.7 0.5 copy.9
  4.2 0.0 copy-start.3
  4.2 0.0 copy-start
  4.2 0.0 copy-start.1
  4.2 0.0 copy-start.4
  4.2 0.1 collective-permute-start.5
  4.3 0.1 shard_map.74
  4.4 4.6 %collective-permute-start.3 = (bf16[256,1024]{1,0:T(8,128)(2,1)S(1)}, bf16[256,1024]{1,0:T(8,128)(2,1)S(1)}, u32[]{:S(2)}, u32[]{:S(2)}) collective-permute-start(bf16[256,1024]{1,0:T(8,128)(2,1)S(1)} %get-tuple-element.29), channel_id=1, source_target_pairs={{1,3},{5,7},{9,11},{13,15},{17,19},{21,23},{25,27},{29,31}} | collective-permute-start | bytes 1572872 | tf_op jit(solution)/shard_map/ppermute | solution.py:260
  9.0 0.7 %collective-permute-start.4 = (bf16[256,1024]{1,0:T(8,128)(2,1)S(1)}, bf16[256,1024]{1,0:T(8,128)(2,1)S(1)}, u32[]{:S(2)}, u32[]{:S(2)}) collective-permute-start(bf16[256,1024]{1,0:T(8,128)(2,1)S(1)} %get-tuple-element.29), channel_id=1, source_target_pairs={{0,3},{4,7},{8,11},{12,15},{16,19},{20,23},{24,27},{28,31}} | collective-permute-start | bytes 1572872 | tf_op jit(solution)/shard_map/ppermute | solution.py:260
  9.7 1.1 %collective-permute-start.2 = (f32[4,2,256]{2,1,0:T(2,128)S(1)}, f32[4,2,256]{2,1,0:T(2,128)S(1)}, u32[]{:S(2)}, u32[]{:S(2)}) collective-permute-start(f32[4,2,256]{2,1,0:T(2,128)S(1)} %bitcast.15), channel_id=1, source_target_pairs={{0,1},{1,0},{2,3},{3,2},{4,5},{5,4},{6,7},{7,6},{8,9},{9,8},{10,11... | collective-permute-start | bytes 24584 | tf_op jit(solution)/shard_map/ppermute | solution.py:263
  10.8 1.3 %collective-permute-start = (bf16[224,1024]{1,0:T(8,128)(2,1)S(1)}, bf16[224,1024]{1,0:T(8,128)(2,1)S(1)}, u32[]{:S(2)}, u32[]{:S(2)}) collective-permute-start(bf16[224,1024]{1,0:T(8,128)(2,1)S(1)} %get-tuple-element.27), channel_id=1, source_target_pairs={{1,3},{5,7},{9,11},{13,15},{17,19},{21,23},{25,27},{29,31}} | collective-permute-start | bytes 1376264 | tf_op jit(solution)/shard_map/ppermute | solution.py:260
  12.1 0.0 collective-permute-done.2.refs_5_.refs_7_
  12.1 0.7 %collective-permute-start.1 = (bf16[224,1024]{1,0:T(8,128)(2,1)S(1)}, bf16[224,1024]{1,0:T(8,128)(2,1)S(1)}, u32[]{:S(2)}, u32[]{:S(2)}) collective-permute-start(bf16[224,1024]{1,0:T(8,128)(2,1)S(1)} %get-tuple-element.27), channel_id=1, source_target_pairs={{0,3},{4,7},{8,11},{12,15},{16,19},{20,23},{24,27},{28,31}} | collective-permute-start | bytes 1376264 | tf_op jit(solution)/shard_map/ppermute | solution.py:260
  12.8 0.0 collective-permute-done.5.refs_3_.refs_5_
  12.8 0.6 shard_map.75
  13.4 0.6 shard_map.76
  14.0 4.9 %collective-permute-done.3.refs_2_ = bf16[256,1024]{1,0:T(8,128)(2,1)S(1)} collective-permute-done((bf16[256,1024]{1,0:T(8,128)(2,1)S(1)}, bf16[256,1024]{1,0:T(8,128)(2,1)S(1)}, u32[]{:S(2)}, u32[]{:S(2)}) %collective-permute-start.3) | collective-permute-done | bytes 524320 | tf_op jit(solution)/shard_map/ppermute | solution.py:260
  18.8 0.0 collective-permute-done.4.refs_3_
  18.8 3.9 %shard_map.77 = (bf16[128,512]{1,0:T(8,128)(2,1)S(1)}, bf16[128,512]{1,0:T(8,128)(2,1)S(1)}, bf16[128,512]{1,0:T(8,128)(2,1)S(1)}, bf16[128,512]{1,0:T(8,128)(2,1)S(1)}, f32[8,256,256]{2,1,0:T(8,128)S(1)}) custom-call(s32[2]{0:T(128)S(1)} %pad_add_fusion.refs_0_, bf16[256,768]{1,0:T(8,128)(2,1)S(1)} %copy-done.1, ...), custom_call_target="tpu_custom_call" | custom-call | flops 2147483648 | bytes 4194304 | tf_op jit(solution)/shard_map/pallas_call | solution.py:275
  22.8 5.9 %collective-permute-done.refs_2_ = bf16[224,1024]{1,0:T(8,128)(2,1)S(1)} collective-permute-done((bf16[224,1024]{1,0:T(8,128)(2,1)S(1)}, bf16[224,1024]{1,0:T(8,128)(2,1)S(1)}, u32[]{:S(2)}, u32[]{:S(2)}) %collective-permute-start) | collective-permute-done | bytes 458784 | tf_op jit(solution)/shard_map/ppermute | solution.py:260
  28.7 0.0 collective-permute-done.1.refs_3_
  28.7 3.5 %shard_map.78 = (bf16[128,512]{1,0:T(8,128)(2,1)}, bf16[128,512]{1,0:T(8,128)(2,1)S(1)}, bf16[128,512]{1,0:T(8,128)(2,1)S(1)}, bf16[128,512]{1,0:T(8,128)(2,1)S(1)}, bf16[256,512]{1,0:T(8,128)(2,1)S(1)}) custom-call(s32[2]{0:T(128)S(1)} %pad_add_fusion.refs_0_, bf16[256,224]{1,0:T(8,128)(2,1)S(1)} %copy-done.2, ...), custom_call_target="tpu_custom_call" | custom-call | flops 2147483648 | bytes 4194304 | tf_op jit(solution)/shard_map/pallas_call | solution.py:275
  32.2 3.3 %collective-permute-start.7 = (bf16[128,512]{1,0:T(8,128)(2,1)S(1)}, bf16[128,512]{1,0:T(8,128)(2,1)S(1)}, u32[]{:S(2)}, u32[]{:S(2)}) collective-permute-start(bf16[128,512]{1,0:T(8,128)(2,1)S(1)} %get-tuple-element.35), channel_id=1, source_target_pairs={{1,4},{5,0},{9,12},{13,8},{3,6},{7,2},{11,14},{15,10},{17,20},{21,... | collective-permute-start | bytes 393224 | tf_op jit(solution)/shard_map/ppermute | solution.py:269
  35.4 2.3 %collective-permute-start.8 = (bf16[128,512]{1,0:T(8,128)(2,1)S(1)}, bf16[128,512]{1,0:T(8,128)(2,1)S(1)}, u32[]{:S(2)}, u32[]{:S(2)}) collective-permute-start(bf16[128,512]{1,0:T(8,128)(2,1)S(1)} %get-tuple-element.36), channel_id=1, source_target_pairs={{1,8},{5,12},{9,0},{13,4},{3,10},{7,14},{11,2},{15,6},{17,24},{21,... | collective-permute-start | bytes 393224 | tf_op jit(solution)/shard_map/ppermute | solution.py:269
  37.7 2.3 %collective-permute-start.9 = (bf16[128,512]{1,0:T(8,128)(2,1)S(1)}, bf16[128,512]{1,0:T(8,128)(2,1)S(1)}, u32[]{:S(2)}, u32[]{:S(2)}) collective-permute-start(bf16[128,512]{1,0:T(8,128)(2,1)S(1)} %get-tuple-element.37), channel_id=1, source_target_pairs={{1,12},{5,8},{9,4},{13,0},{3,14},{7,10},{11,6},{15,2},{17,28},{21,... | collective-permute-start | bytes 393224 | tf_op jit(solution)/shard_map/ppermute | solution.py:269
  40.1 1.3 %collective-permute-start.10 = (bf16[128,512]{1,0:T(8,128)(2,1)S(1)}, bf16[128,512]{1,0:T(8,128)(2,1)S(1)}, u32[]{:S(2)}, u32[]{:S(2)}) collective-permute-start(bf16[128,512]{1,0:T(8,128)(2,1)S(1)} %get-tuple-element.38), channel_id=1, source_target_pairs={{1,4},{5,0},{9,12},{13,8},{3,6},{7,2},{11,14},{15,10},{17,20},{21,... | collective-permute-start | bytes 393224 | tf_op jit(solution)/shard_map/ppermute | solution.py:269
  41.4 1.3 %collective-permute-start.11 = (bf16[128,512]{1,0:T(8,128)(2,1)S(1)}, bf16[128,512]{1,0:T(8,128)(2,1)S(1)}, u32[]{:S(2)}, u32[]{:S(2)}) collective-permute-start(bf16[128,512]{1,0:T(8,128)(2,1)S(1)} %get-tuple-element.39), channel_id=1, source_target_pairs={{1,8},{5,12},{9,0},{13,4},{3,10},{7,14},{11,2},{15,6},{17,24},{21,... | collective-permute-start | bytes 393224 | tf_op jit(solution)/shard_map/ppermute | solution.py:269
  42.7 1.3 %collective-permute-start.12 = (bf16[128,512]{1,0:T(8,128)(2,1)S(1)}, bf16[128,512]{1,0:T(8,128)(2,1)S(1)}, u32[]{:S(2)}, u32[]{:S(2)}) collective-permute-start(bf16[128,512]{1,0:T(8,128)(2,1)S(1)} %get-tuple-element.40), channel_id=1, source_target_pairs={{1,12},{5,8},{9,4},{13,0},{3,14},{7,10},{11,6},{15,2},{17,28},{21,... | collective-permute-start | bytes 393224 | tf_op jit(solution)/shard_map/ppermute | solution.py:269
  44.0 0.0 collective-permute-done.8.refs_3_
  44.0 1.3 %collective-permute-start.16 = (bf16[128,512]{1,0:T(8,128)(2,1)S(1)}, bf16[128,512]{1,0:T(8,128)(2,1)S(1)}, u32[]{:S(2)}, u32[]{:S(2)}) collective-permute-start(bf16[128,512]{1,0:T(8,128)(2,1)S(1)} %get-tuple-element.44), channel_id=1, source_target_pairs={{0,5},{4,1},{8,13},{12,9},{2,7},{6,3},{10,15},{14,11},{16,21},{20,... | collective-permute-start | bytes 393224 | tf_op jit(solution)/shard_map/ppermute | solution.py:269
  45.3 1.3 %collective-permute-start.17 = (bf16[128,512]{1,0:T(8,128)(2,1)S(1)}, bf16[128,512]{1,0:T(8,128)(2,1)S(1)}, u32[]{:S(2)}, u32[]{:S(2)}) collective-permute-start(bf16[128,512]{1,0:T(8,128)(2,1)S(1)} %get-tuple-element.45), channel_id=1, source_target_pairs={{0,9},{4,13},{8,1},{12,5},{2,11},{6,15},{10,3},{14,7},{16,25},{20,... | collective-permute-start | bytes 393224 | tf_op jit(solution)/shard_map/ppermute | solution.py:269
  46.6 3.7 %collective-permute-start.6 = (bf16[256,512]{1,0:T(8,128)(2,1)S(1)}, bf16[256,512]{1,0:T(8,128)(2,1)S(1)}, u32[]{:S(2)}, u32[]{:S(2)}) collective-permute-start(bf16[256,512]{1,0:T(8,128)(2,1)S(1)} %get-tuple-element.34), channel_id=1, source_target_pairs={{0,1},{1,0},{2,3},{3,2},{4,5},{5,4},{6,7},{7,6},{8,9},{9,8},{10,11... | collective-permute-start | bytes 786440 | tf_op jit(solution)/shard_map/ppermute | solution.py:263
  50.3 0.0 collective-permute-done.11.refs_6_
  50.3 1.3 %collective-permute-start.18 = (bf16[128,512]{1,0:T(8,128)(2,1)S(1)}, bf16[128,512]{1,0:T(8,128)(2,1)S(1)}, u32[]{:S(2)}, u32[]{:S(2)}) collective-permute-start(bf16[128,512]{1,0:T(8,128)(2,1)S(1)} %get-tuple-element.46), channel_id=1, source_target_pairs={{0,13},{4,9},{8,5},{12,1},{2,15},{6,11},{10,7},{14,3},{16,29},{20,... | collective-permute-start | bytes 393224 | tf_op jit(solution)/shard_map/ppermute | solution.py:269
  51.6 0.0 collective-permute-done.12.refs_7_
  51.6 1.3 %collective-permute-start.13 = (bf16[128,512]{1,0:T(8,128)(2,1)S(1)}, bf16[128,512]{1,0:T(8,128)(2,1)S(1)}, u32[]{:S(2)}, u32[]{:S(2)}) collective-permute-start(bf16[128,512]{1,0:T(8,128)(2,1)S(1)} %get-tuple-element.41), channel_id=1, source_target_pairs={{0,5},{4,1},{8,13},{12,9},{2,7},{6,3},{10,15},{14,11},{16,21},{20,... | collective-permute-start | bytes 393224 | tf_op jit(solution)/shard_map/ppermute | solution.py:269
  52.9 1.3 %collective-permute-start.14 = (bf16[128,512]{1,0:T(8,128)(2,1)S(1)}, bf16[128,512]{1,0:T(8,128)(2,1)S(1)}, u32[]{:S(2)}, u32[]{:S(2)}) collective-permute-start(bf16[128,512]{1,0:T(8,128)(2,1)S(1)} %get-tuple-element.42), channel_id=1, source_target_pairs={{0,9},{4,13},{8,1},{12,5},{2,11},{6,15},{10,3},{14,7},{16,25},{20,... | collective-permute-start | bytes 393224 | tf_op jit(solution)/shard_map/ppermute | solution.py:269
  54.2 1.2 %collective-permute-done.17.refs_12_ = bf16[128,512]{1,0:T(8,128)(2,1)S(1)} collective-permute-done((bf16[128,512]{1,0:T(8,128)(2,1)S(1)}, bf16[128,512]{1,0:T(8,128)(2,1)S(1)}, u32[]{:S(2)}, u32[]{:S(2)}) %collective-permute-start.17) | collective-permute-done | bytes 131104 | tf_op jit(solution)/shard_map/ppermute | solution.py:269
  55.4 1.3 %collective-permute-start.15 = (bf16[128,512]{1,0:T(8,128)(2,1)S(1)}, bf16[128,512]{1,0:T(8,128)(2,1)S(1)}, u32[]{:S(2)}, u32[]{:S(2)}) collective-permute-start(bf16[128,512]{1,0:T(8,128)(2,1)S(1)} %get-tuple-element.43), channel_id=1, source_target_pairs={{0,13},{4,9},{8,5},{12,1},{2,15},{6,11},{10,7},{14,3},{16,29},{20,... | collective-permute-start | bytes 393224 | tf_op jit(solution)/shard_map/ppermute | solution.py:269
  56.7 1.8 %collective-permute-done.18.refs_13_ = bf16[128,512]{1,0:T(8,128)(2,1)S(1)} collective-permute-done((bf16[128,512]{1,0:T(8,128)(2,1)S(1)}, bf16[128,512]{1,0:T(8,128)(2,1)S(1)}, u32[]{:S(2)}, u32[]{:S(2)}) %collective-permute-start.18) | collective-permute-done | bytes 131104 | tf_op jit(solution)/shard_map/ppermute | solution.py:269
  58.5 2.1 %collective-permute-done.13.refs_8_ = bf16[128,512]{1,0:T(8,128)(2,1)S(1)} collective-permute-done((bf16[128,512]{1,0:T(8,128)(2,1)S(1)}, bf16[128,512]{1,0:T(8,128)(2,1)S(1)}, u32[]{:S(2)}, u32[]{:S(2)}) %collective-permute-start.13) | collective-permute-done | bytes 131104 | tf_op jit(solution)/shard_map/ppermute | solution.py:269
  60.6 1.0 %collective-permute-done.14.refs_9_ = bf16[128,512]{1,0:T(8,128)(2,1)S(1)} collective-permute-done((bf16[128,512]{1,0:T(8,128)(2,1)S(1)}, bf16[128,512]{1,0:T(8,128)(2,1)S(1)}, u32[]{:S(2)}, u32[]{:S(2)}) %collective-permute-start.14) | collective-permute-done | bytes 131104 | tf_op jit(solution)/shard_map/ppermute | solution.py:269
  61.5 2.0 %collective-permute-done.15.refs_10_ = bf16[128,512]{1,0:T(8,128)(2,1)S(1)} collective-permute-done((bf16[128,512]{1,0:T(8,128)(2,1)S(1)}, bf16[128,512]{1,0:T(8,128)(2,1)S(1)}, u32[]{:S(2)}, u32[]{:S(2)}) %collective-permute-start.15) | collective-permute-done | bytes 131104 | tf_op jit(solution)/shard_map/ppermute | solution.py:269
  63.6 1.6 %shard_map.79 = bf16[16,64,512]{2,1,0:T(8,128)(2,1)} custom-call(s32[2]{0:T(128)S(1)} %pad_add_fusion.refs_0_, bf16[256,512]{1,0:T(8,128)(2,1)S(1)} %collective-permute-done.6.refs_1_, bf16[128,512]{1,0:T(8,128)(2,1)S(1)} %collective-permute-done.7.refs_2_, bf16[128,512]{1,0:T(8,128)(2,1)S(1)} %collective-permute-done.8.refs_3_, ...), custom_call_target="tpu_custom_call" | custom-call | bytes 3145728 | tf_op jit(solution)/shard_map/pallas_call | solution.py:349
  (14 shorter events, 0.0 us)
Async XLA Ops:
  0.1 0.7 %copy-start.5 = (s32[64]{0:T(128)S(1)}, s32[64]{0:T(128)}, u32[]{:S(2)}) copy-start(s32[64]{0:T(128)} %param.9) | copy-start | bytes 772
  0.7 1.9 %copy-start.6 = (bf16[1,1,512,4,2,256]{5,4,3,2,1,0:T(2,128)(2,1)S(1)}, bf16[1,1,512,4,2,256]{5,4,3,2,1,0:T(2,128)(2,1)}, u32[]{:S(2)}) copy-start(bf16[1,1,512,4,2,256]{5,4,3,2,1,0:T(2,128)(2,1)} %param.7) | copy-start | bytes 6291460
  4.2 5.5 %copy-start.3 = (f32[1,1,4,2,256]{4,3,2,1,0:T(2,128)S(1)}, f32[1,1,4,2,256]{4,3,2,1,0:T(2,128)}, u32[]{:S(2)}) copy-start(f32[1,1,4,2,256]{4,3,2,1,0:T(2,128)} %param.8) | copy-start | bytes 24580
  4.2 8.6 %copy-start = (bf16[512,512]{1,0:T(8,128)(2,1)S(1)}, bf16[512,512]{1,0:T(8,128)(2,1)}, u32[]{:S(2)}) copy-start(bf16[512,512]{1,0:T(8,128)(2,1)} %constant.17.clone.refs_6_.refs_8_) | copy-start | bytes 1572868
  4.2 8.6 %copy-start.1 = (bf16[256,768]{1,0:T(8,128)(2,1)S(1)}, bf16[256,768]{1,0:T(8,128)(2,1)}, u32[]{:S(2)}) copy-start(bf16[256,768]{1,0:T(8,128)(2,1)} %constant.15.clone.refs_1_) | copy-start | bytes 1179652
  4.2 8.6 %copy-start.4 = (s32[1024]{0:T(1024)S(1)}, s32[1024]{0:T(1024)}, u32[]{:S(2)}) copy-start(s32[1024]{0:T(1024)} %param.10) | copy-start | bytes 12292
  4.2 8.6 %collective-permute-start.5 = (bf16[1024,1024]{1,0:T(8,128)(2,1)S(1)}, bf16[1024,1024]{1,0:T(8,128)(2,1)S(1)}, u32[]{:S(2)}, u32[]{:S(2)}) collective-permute-start(bf16[1024,1024]{1,0:T(8,128)(2,1)S(1)} %bitcast.10), channel_id=1, source_target_pairs={{0,1},{1,0},{2,3},{3,2},{4,5},{5,4},{6,7},{7,6},{8,9},{9,8},{10,11... | collective-permute-start | bytes 6291464 | tf_op jit(solution)/shard_map/ppermute | solution.py:263
  4.4 14.4 %collective-permute-start.3 = (bf16[256,1024]{1,0:T(8,128)(2,1)S(1)}, bf16[256,1024]{1,0:T(8,128)(2,1)S(1)}, u32[]{:S(2)}, u32[]{:S(2)}) collective-permute-start(bf16[256,1024]{1,0:T(8,128)(2,1)S(1)} %get-tuple-element.29), channel_id=1, source_target_pairs={{1,3},{5,7},{9,11},{13,15},{17,19},{21,23},{25,27},{29,31}} | collective-permute-start | bytes 1572872 | tf_op jit(solution)/shard_map/ppermute | solution.py:260
  9.0 9.8 %collective-permute-start.4 = (bf16[256,1024]{1,0:T(8,128)(2,1)S(1)}, bf16[256,1024]{1,0:T(8,128)(2,1)S(1)}, u32[]{:S(2)}, u32[]{:S(2)}) collective-permute-start(bf16[256,1024]{1,0:T(8,128)(2,1)S(1)} %get-tuple-element.29), channel_id=1, source_target_pairs={{0,3},{4,7},{8,11},{12,15},{16,19},{20,23},{24,27},{28,31}} | collective-permute-start | bytes 1572872 | tf_op jit(solution)/shard_map/ppermute | solution.py:260
  9.7 2.4 %collective-permute-start.2 = (f32[4,2,256]{2,1,0:T(2,128)S(1)}, f32[4,2,256]{2,1,0:T(2,128)S(1)}, u32[]{:S(2)}, u32[]{:S(2)}) collective-permute-start(f32[4,2,256]{2,1,0:T(2,128)S(1)} %bitcast.15), channel_id=1, source_target_pairs={{0,1},{1,0},{2,3},{3,2},{4,5},{5,4},{6,7},{7,6},{8,9},{9,8},{10,11... | collective-permute-start | bytes 24584 | tf_op jit(solution)/shard_map/ppermute | solution.py:263
  10.8 17.9 %collective-permute-start = (bf16[224,1024]{1,0:T(8,128)(2,1)S(1)}, bf16[224,1024]{1,0:T(8,128)(2,1)S(1)}, u32[]{:S(2)}, u32[]{:S(2)}) collective-permute-start(bf16[224,1024]{1,0:T(8,128)(2,1)S(1)} %get-tuple-element.27), channel_id=1, source_target_pairs={{1,3},{5,7},{9,11},{13,15},{17,19},{21,23},{25,27},{29,31}} | collective-permute-start | bytes 1376264 | tf_op jit(solution)/shard_map/ppermute | solution.py:260
  12.1 16.6 %collective-permute-start.1 = (bf16[224,1024]{1,0:T(8,128)(2,1)S(1)}, bf16[224,1024]{1,0:T(8,128)(2,1)S(1)}, u32[]{:S(2)}, u32[]{:S(2)}) collective-permute-start(bf16[224,1024]{1,0:T(8,128)(2,1)S(1)} %get-tuple-element.27), channel_id=1, source_target_pairs={{0,3},{4,7},{8,11},{12,15},{16,19},{20,23},{24,27},{28,31}} | collective-permute-start | bytes 1376264 | tf_op jit(solution)/shard_map/ppermute | solution.py:260
  18.8 9.8 %copy-start.2 = (bf16[256,224]{1,0:T(8,128)(2,1)S(1)}, bf16[256,224]{1,0:T(8,128)(2,1)}, u32[]{:S(2)}) copy-start(bf16[256,224]{1,0:T(8,128)(2,1)} %constant.16.clone.refs_1_) | copy-start | bytes 344068
  32.2 10.5 %collective-permute-start.7 = (bf16[128,512]{1,0:T(8,128)(2,1)S(1)}, bf16[128,512]{1,0:T(8,128)(2,1)S(1)}, u32[]{:S(2)}, u32[]{:S(2)}) collective-permute-start(bf16[128,512]{1,0:T(8,128)(2,1)S(1)} %get-tuple-element.35), channel_id=1, source_target_pairs={{1,4},{5,0},{9,12},{13,8},{3,6},{7,2},{11,14},{15,10},{17,20},{21,... | collective-permute-start | bytes 393224 | tf_op jit(solution)/shard_map/ppermute | solution.py:269
  35.4 8.6 %collective-permute-start.8 = (bf16[128,512]{1,0:T(8,128)(2,1)S(1)}, bf16[128,512]{1,0:T(8,128)(2,1)S(1)}, u32[]{:S(2)}, u32[]{:S(2)}) collective-permute-start(bf16[128,512]{1,0:T(8,128)(2,1)S(1)} %get-tuple-element.36), channel_id=1, source_target_pairs={{1,8},{5,12},{9,0},{13,4},{3,10},{7,14},{11,2},{15,6},{17,24},{21,... | collective-permute-start | bytes 393224 | tf_op jit(solution)/shard_map/ppermute | solution.py:269
  37.7 7.6 %collective-permute-start.9 = (bf16[128,512]{1,0:T(8,128)(2,1)S(1)}, bf16[128,512]{1,0:T(8,128)(2,1)S(1)}, u32[]{:S(2)}, u32[]{:S(2)}) collective-permute-start(bf16[128,512]{1,0:T(8,128)(2,1)S(1)} %get-tuple-element.37), channel_id=1, source_target_pairs={{1,12},{5,8},{9,4},{13,0},{3,14},{7,10},{11,6},{15,2},{17,28},{21,... | collective-permute-start | bytes 393224 | tf_op jit(solution)/shard_map/ppermute | solution.py:269
  40.1 6.5 %collective-permute-start.10 = (bf16[128,512]{1,0:T(8,128)(2,1)S(1)}, bf16[128,512]{1,0:T(8,128)(2,1)S(1)}, u32[]{:S(2)}, u32[]{:S(2)}) collective-permute-start(bf16[128,512]{1,0:T(8,128)(2,1)S(1)} %get-tuple-element.38), channel_id=1, source_target_pairs={{1,4},{5,0},{9,12},{13,8},{3,6},{7,2},{11,14},{15,10},{17,20},{21,... | collective-permute-start | bytes 393224 | tf_op jit(solution)/shard_map/ppermute | solution.py:269
  41.4 9.0 %collective-permute-start.11 = (bf16[128,512]{1,0:T(8,128)(2,1)S(1)}, bf16[128,512]{1,0:T(8,128)(2,1)S(1)}, u32[]{:S(2)}, u32[]{:S(2)}) collective-permute-start(bf16[128,512]{1,0:T(8,128)(2,1)S(1)} %get-tuple-element.39), channel_id=1, source_target_pairs={{1,8},{5,12},{9,0},{13,4},{3,10},{7,14},{11,2},{15,6},{17,24},{21,... | collective-permute-start | bytes 393224 | tf_op jit(solution)/shard_map/ppermute | solution.py:269
  42.7 8.9 %collective-permute-start.12 = (bf16[128,512]{1,0:T(8,128)(2,1)S(1)}, bf16[128,512]{1,0:T(8,128)(2,1)S(1)}, u32[]{:S(2)}, u32[]{:S(2)}) collective-permute-start(bf16[128,512]{1,0:T(8,128)(2,1)S(1)} %get-tuple-element.40), channel_id=1, source_target_pairs={{1,12},{5,8},{9,4},{13,0},{3,14},{7,10},{11,6},{15,2},{17,28},{21,... | collective-permute-start | bytes 393224 | tf_op jit(solution)/shard_map/ppermute | solution.py:269
  44.0 8.9 %collective-permute-start.16 = (bf16[128,512]{1,0:T(8,128)(2,1)S(1)}, bf16[128,512]{1,0:T(8,128)(2,1)S(1)}, u32[]{:S(2)}, u32[]{:S(2)}) collective-permute-start(bf16[128,512]{1,0:T(8,128)(2,1)S(1)} %get-tuple-element.44), channel_id=1, source_target_pairs={{0,5},{4,1},{8,13},{12,9},{2,7},{6,3},{10,15},{14,11},{16,21},{20,... | collective-permute-start | bytes 393224 | tf_op jit(solution)/shard_map/ppermute | solution.py:269
  45.3 10.1 %collective-permute-start.17 = (bf16[128,512]{1,0:T(8,128)(2,1)S(1)}, bf16[128,512]{1,0:T(8,128)(2,1)S(1)}, u32[]{:S(2)}, u32[]{:S(2)}) collective-permute-start(bf16[128,512]{1,0:T(8,128)(2,1)S(1)} %get-tuple-element.45), channel_id=1, source_target_pairs={{0,9},{4,13},{8,1},{12,5},{2,11},{6,15},{10,3},{14,7},{16,25},{20,... | collective-permute-start | bytes 393224 | tf_op jit(solution)/shard_map/ppermute | solution.py:269
  46.6 17.0 %collective-permute-start.6 = (bf16[256,512]{1,0:T(8,128)(2,1)S(1)}, bf16[256,512]{1,0:T(8,128)(2,1)S(1)}, u32[]{:S(2)}, u32[]{:S(2)}) collective-permute-start(bf16[256,512]{1,0:T(8,128)(2,1)S(1)} %get-tuple-element.34), channel_id=1, source_target_pairs={{0,1},{1,0},{2,3},{3,2},{4,5},{5,4},{6,7},{7,6},{8,9},{9,8},{10,11... | collective-permute-start | bytes 786440 | tf_op jit(solution)/shard_map/ppermute | solution.py:263
  50.3 8.2 %collective-permute-start.18 = (bf16[128,512]{1,0:T(8,128)(2,1)S(1)}, bf16[128,512]{1,0:T(8,128)(2,1)S(1)}, u32[]{:S(2)}, u32[]{:S(2)}) collective-permute-start(bf16[128,512]{1,0:T(8,128)(2,1)S(1)} %get-tuple-element.46), channel_id=1, source_target_pairs={{0,13},{4,9},{8,5},{12,1},{2,15},{6,11},{10,7},{14,3},{16,29},{20,... | collective-permute-start | bytes 393224 | tf_op jit(solution)/shard_map/ppermute | solution.py:269
  51.6 8.9 %collective-permute-start.13 = (bf16[128,512]{1,0:T(8,128)(2,1)S(1)}, bf16[128,512]{1,0:T(8,128)(2,1)S(1)}, u32[]{:S(2)}, u32[]{:S(2)}) collective-permute-start(bf16[128,512]{1,0:T(8,128)(2,1)S(1)} %get-tuple-element.41), channel_id=1, source_target_pairs={{0,5},{4,1},{8,13},{12,9},{2,7},{6,3},{10,15},{14,11},{16,21},{20,... | collective-permute-start | bytes 393224 | tf_op jit(solution)/shard_map/ppermute | solution.py:269
  52.9 8.6 %collective-permute-start.14 = (bf16[128,512]{1,0:T(8,128)(2,1)S(1)}, bf16[128,512]{1,0:T(8,128)(2,1)S(1)}, u32[]{:S(2)}, u32[]{:S(2)}) collective-permute-start(bf16[128,512]{1,0:T(8,128)(2,1)S(1)} %get-tuple-element.42), channel_id=1, source_target_pairs={{0,9},{4,13},{8,1},{12,5},{2,11},{6,15},{10,3},{14,7},{16,25},{20,... | collective-permute-start | bytes 393224 | tf_op jit(solution)/shard_map/ppermute | solution.py:269
  55.4 8.2 %collective-permute-start.15 = (bf16[128,512]{1,0:T(8,128)(2,1)S(1)}, bf16[128,512]{1,0:T(8,128)(2,1)S(1)}, u32[]{:S(2)}, u32[]{:S(2)}) collective-permute-start(bf16[128,512]{1,0:T(8,128)(2,1)S(1)} %get-tuple-element.43), channel_id=1, source_target_pairs={{0,13},{4,9},{8,5},{12,1},{2,15},{6,11},{10,7},{14,3},{16,29},{20,... | collective-permute-start | bytes 393224 | tf_op jit(solution)/shard_map/ppermute | solution.py:269

commit v8 on v7

--- a/solution.py
+++ b/solution.py
@@ -95,16 +95,24 @@
     return total
 
 
-def adder(pol, sum_ref, keep_ref):
-    def first(column, power):
-        sum_ref[:, column : column + LANES] = power.astype(jnp.bfloat16)
-
-    def second(column, power):
+def keeper(power_ref, at=0):
+    rows = pl.ds(at, BLOCK * UPCH)
+
+    def emit(column, power):
+        power_ref[rows, column : column + LANES] = power.astype(jnp.bfloat16)
+
+    return emit
+
+
+def adder(power_ref, keep_ref, sum_ref, at=0):
+    rows = pl.ds(at, BLOCK * UPCH)
+
+    def emit(column, power):
         lanes = slice(column, column + LANES)
-        total = sum_ref[:, lanes].astype(jnp.float32) + power.astype(jnp.bfloat16).astype(jnp.float32)
-        sum_ref[:, lanes] = (total * keep_ref[:, lanes].astype(jnp.float32)).astype(jnp.bfloat16)
-
-    return (first, second)[pol]
+        total = power_ref[rows, lanes].astype(jnp.float32) + power.astype(jnp.bfloat16).astype(jnp.float32)
+        sum_ref[rows, lanes] = (total * keep_ref[:, lanes].astype(jnp.float32)).astype(jnp.bfloat16)
+
+    return emit
 
 
 def place(sum_ref, table_ref, out_refs):
@@ -119,18 +127,38 @@
     far_ref[...] = x_ref[near_at - far_ref.shape[0] : near_at, :]
 
 
-def late_kernel(block, n_owner, where_ref, filt_ref, x0, x1, g0, g1, beam_ref, keep_ref, table_ref, *refs):
-    out_refs, (cal_ref, sum_ref) = refs[:n_owner], refs[n_owner:]
-    rows = slice(block * BLOCK * ROWS, (block * BLOCK + TAPS + BLOCK) * ROWS)
-
+def each_late_block(blocks, filt_ref, x_ref, gain_ref, beam_ref, cal_ref, emitter):
+    def step(block, carry):
+        first = pl.multiple_of(block * BLOCK * ROWS, BLOCK * ROWS)
+        rows = pl.ds(first, (TAPS + BLOCK) * ROWS)
+
+        def spectra(cyl):
+            return filtered([(filt_ref[...], x_ref[rows, columns(cyl)])])
+
+        at = pl.multiple_of(block * BLOCK * UPCH, BLOCK * UPCH)
+        form_powers(spectra, gain_ref, beam_ref, cal_ref, emitter(at))
+        return carry
+
+    lax.fori_loop(0, blocks, step, 0)
+
+
+def late_own_kernel(blocks, where_ref, filt_ref, x_ref, gain_ref, beam_ref, out_ref, cal_ref):
     @pl.when(where_ref[1] == 0)
     def _():
-        for pol, (x, gain) in enumerate(((x0, g0), (x1, g1))):
-
-            def spectra(cyl, x=x):
-                return filtered([(filt_ref[...], x[rows, columns(cyl)])])
-
-            form_powers(spectra, gain, beam_ref, cal_ref, adder(pol, sum_ref, keep_ref))
+        each_late_block(blocks, filt_ref, x_ref, gain_ref, beam_ref, cal_ref, lambda at: keeper(out_ref, at))
+
+
+def late_kernel(
+    blocks, where_ref, filt_ref, x_ref, gain_ref, beam_ref, keep_ref, table_ref, power_ref, *refs
+):
+    out_refs, (cal_ref, sum_ref) = refs[:-2], refs[-2:]
+
+    @pl.when(where_ref[1] == 0)
+    def _():
+        def emitter(at):
+            return adder(power_ref, keep_ref, sum_ref, at)
+
+        each_late_block(blocks, filt_ref, x_ref, gain_ref, beam_ref, cal_ref, emitter)
         place(sum_ref, table_ref, out_refs)
 
 
@@ -149,12 +177,13 @@
                 )
                 return filtered([(filt_ref[:, :reach], there), (filt_ref[:, reach:], x[: 2 * reach, columns(cyl)])])
 
-            form_powers(spectra, gain, beam_ref, cal_ref, adder(pol, sum_ref, keep_ref))
+            emit = adder(sum_ref, keep_ref, sum_ref) if pol else keeper(sum_ref)
+            form_powers(spectra, gain, beam_ref, cal_ref, emit)
         place(sum_ref, table_ref, out_refs)
 
 
 def far_kernel(n_owner, where_ref, edge_ref, f0, f1, g0, g1, beam_ref, keep_ref, table_ref, pre_ref, *refs):
-    own_refs, out_refs, own_ref, (cal_ref, sum_ref) = refs[:3], refs[3 : 3 + n_owner], refs[3 + n_owner], refs[-2:]
+    own_refs, out_refs, own_ref, (cal_ref, sum_ref) = refs[:2], refs[2 : 2 + n_owner], refs[2 + n_owner], refs[-2:]
     half = BLOCK * UPCH
 
     @pl.when(where_ref[1] == 1)
@@ -164,15 +193,15 @@
             def spectra(cyl, pol=pol, f=f):
                 return pre_ref[pol * CYL + cyl] + filtered([(edge_ref[...], f[:, columns(cyl)])])
 
-            form_powers(spectra, gain, beam_ref, cal_ref, adder(pol, sum_ref, keep_ref))
+            emit = adder(sum_ref, keep_ref, sum_ref) if pol else keeper(sum_ref)
+            form_powers(spectra, gain, beam_ref, cal_ref, emit)
         place(sum_ref, table_ref, out_refs)
         own_ref[:half, :] = out_refs[0][...]
         own_ref[half:, :] = own_refs[0][...]
 
     @pl.when(where_ref[1] == 0)
     def _():
-        own_ref[:half, :] = own_refs[1][...]
-        own_ref[half:, :] = own_refs[2][...]
+        own_ref[...] = own_refs[1][...]
 
 
 def place_table_kernel(most_sets, where_ref, owner_ref, out_ref):
@@ -195,7 +224,7 @@
 
 def gather_kernel(n_owner, where_ref, *refs):
     own_ref, got, out_ref = refs[0], refs[1:-1], refs[-1]
-    chunks = [got[i * (n_owner - 1) : (i + 1) * (n_owner - 1)] for i in range(4)]
+    far, near, late = (got[i * (n_owner - 1) : (i + 1) * (n_owner - 1)] for i in range(3))
 
     def copy(block, frame, k):
         rows = pl.ds(pl.multiple_of((where_ref[0] ^ k) * UPCH, UPCH), UPCH)
@@ -203,13 +232,17 @@
         out_ref[frame : frame + count, rows, :] = block[...].reshape(count, UPCH, block.shape[1])
 
     copy(own_ref, 0, 0)
-    for pol in range(2):
-
-        @pl.when(where_ref[1] == pol)
-        def _(pol=pol):
-            for part in range(2):
-                for k in range(1, n_owner):
-                    copy(chunks[2 * pol + part][k - 1], part * BLOCK, k)
+
+    @pl.when(where_ref[1] == 0)
+    def _():
+        for k in range(1, n_owner):
+            copy(far[k - 1], 0, k)
+            copy(near[k - 1], BLOCK, k)
+
+    @pl.when(where_ref[1] == 1)
+    def _():
+        for k in range(1, n_owner):
+            copy(late[k - 1], 0, k)
 
 
 VMEM = pl.BlockSpec(memory_space=pltpu.VMEM)
@@ -269,9 +302,9 @@
             got.append(lax.ppermute(blocks[k], ("freq", "pol"), route))
         return got
 
-    def form(body, *arrays, after=(), more=()):
-        shape = [jax.ShapeDtypeStruct((BLOCK * UPCH, width), bf16)] * n_owner
-        scratch = [pltpu.VMEM((CYL * BLOCK * UPCH, 2 * NS), bf16), pltpu.VMEM((BLOCK * UPCH, beams), bf16)]
+    def form(body, rows, *arrays, after=(), more=()):
+        shape = [jax.ShapeDtypeStruct((rows, width), bf16)] * n_owner
+        scratch = [pltpu.VMEM((CYL * BLOCK * UPCH, 2 * NS), bf16), pltpu.VMEM((rows, beams), bf16)]
         return call(
             body,
             shape + list(more),
@@ -311,41 +344,49 @@
     far0 = ahead(far_rows, 0)
     far1 = ahead(far_rows, 1)
     common = (gain, gain_other, beam_table, keep, table)
-    late = []
-    got = []
-    for block in range(2):
-        body = functools.partial(late_kernel, block, n_owner)
-        after = [late[0][0]] if block else []
-        late.append(form(body, filt, x, other, *common, after=after))
-        got.append(spread(late[block], 0))
+    blocks = kept // BLOCK
+    late_own = call(
+        functools.partial(late_own_kernel, blocks),
+        jax.ShapeDtypeStruct((kept * UPCH, beams), bf16),
+        4,
+        4 * 512 * 1024 * 1024,
+        4 << 20,
+        scalars=1,
+        scratch=[pltpu.VMEM((CYL * BLOCK * UPCH, 2 * NS), bf16)],
+    )(where, filt, x, gain, beam_table)
+    body = functools.partial(late_kernel, blocks)
+    rows = kept * UPCH
+    late = form(body, rows, filt, other, gain_other, beam_table, keep, table, late_own)
+    late_got = spread(late, 0)
     *near, pre = form(
         functools.partial(near_kernel, n_owner),
+        BLOCK * UPCH,
         filt,
         near1,
         near0,
         x,
         other,
         *common,
-        after=late[1][:1],
+        after=late[:1],
         more=[jax.ShapeDtypeStruct((2 * CYL, reach, NS), jnp.float32)],
     )
     near_got = spread(near, 1)
     *far, own = form(
         functools.partial(far_kernel, n_owner),
+        BLOCK * UPCH,
         edge,
         far1,
         far0,
         *common,
         pre,
         near[0],
-        late[0][0],
-        late[1][0],
+        late[0],
         more=[jax.ShapeDtypeStruct((kept * UPCH, width), bf16)],
     )
     far_got = spread(far, 1)
     own_got = swap(own)
     out_shape = jax.ShapeDtypeStruct((kept, n_owner * UPCH, width), bf16)
-    arrays = [own_got, *far_got, *near_got, *got[0], *got[1]]
+    arrays = [own_got, *far_got, *near_got, *late_got]
     return call(functools.partial(gather_kernel, n_owner), out_shape, len(arrays), 0, 3 << 20, scalars=1)(
         where, *arrays
     )

time: 65.6 us -> 65.8 us (level)
  the two profiles are of different devices: /device:TPU:1 before, /device:TPU:11 now
where the time goes in v8:
time: 65.8 us; the launch traced here: 65.4 us
  waiting for transfers between devices  26.9 us (41%)
  starting transfers between devices  24 us (36%)
  Pallas kernels  11.9 us (18%)
  local copies, waits for them, and re-layouts  2.26 us (3%)
    ppermute x9, starting transfers between devices, spread(): got.append(lax.ppermute(blocks[k], ('freq', 'pol'), route))  17.9 us
    ppermute x4, waiting for transfers between devices, ahead(): lax.ppermute(part, ('tm', 'pol'), [(i * 2 + source, j * 2 + 1) for i, j i...  14.9 us
    ppermute x9, waiting for transfers between devices, spread(): got.append(lax.ppermute(blocks[k], ('freq', 'pol'), route))  11.9 us
    pallas_call x3, Pallas kernels, form(): call(body, shape + list(more), len(arrays), 4 * 512 * 1024 * 1024, 4 << 2...  7.85 us
    ppermute x4, starting transfers between devices, ahead(): lax.ppermute(part, ('tm', 'pol'), [(i * 2 + source, j * 2 + 1) for i, j i...  5.17 us
    pallas_call x1, Pallas kernels, per_device(): call(functools.partial(place_table_kernel, most_sets), jax.ShapeDtypeStru...  1.85 us
    pallas_call x1, Pallas kernels, per_device(): call(functools.partial(gather_kernel, n_owner), out_shape, len(arrays), 0...  1.59 us
  transfers between devices with their start and end apart: 16, of which 6 were waited for; matrix products, arithmetic and copies ran while one was open for 0% of the time, Pallas kernels for 8%

profile of v8, /device:TPU:11, one launch (start us, length us, event | category | flops | bytes accessed | tf_op | source)
XLA Modules:
  0.0 65.4 jit_solution(14764233748755467237)
XLA Ops:
  0.0 0.1 pad_add_fusion.refs_0_
  0.1 0.7 copy-done.5
  0.7 1.8 %shard_map.73.refs_6_.refs_10_.refs_8_ = bf16[4,1024,512]{2,1,0:T(8,128)(2,1)S(1)} custom-call(s32[2]{0:T(128)S(1)} %pad_add_fusion.refs_0_, s32[1,64]{1,0:T(1,128)S(1)} %bitcast.21), custom_call_target="tpu_custom_call" | custom-call | flops 16777216 | bytes 4194304 | tf_op jit(solution)/shard_map/pallas_call | solution.py:322
  2.6 1.1 %copy.8 = bf16[512,2,4,256]{3,2,1,0:T(4,128)(2,1)S(1)} copy(bf16[512,2,4,256]{3,1,2,0:T(2,128)(2,1)S(1)} %bitcast.23) | data formatting | bytes 4194304 | tf_op jit(solution)/shard_map/transpose | solution.py:331
  3.7 0.5 copy.9
  4.2 0.0 copy-start.3
  4.2 0.0 copy-start
  4.2 0.0 copy-start.1
  4.2 0.7 %collective-permute-start.5 = (bf16[1024,1024]{1,0:T(8,128)(2,1)S(1)}, bf16[1024,1024]{1,0:T(8,128)(2,1)S(1)}, u32[]{:S(2)}, u32[]{:S(2)}) collective-permute-start(bf16[1024,1024]{1,0:T(8,128)(2,1)S(1)} %bitcast.10), channel_id=1, source_target_pairs={{0,1},{1,0},{2,3},{3,2},{4,5},{5,4},{6,7},{7,6},{8,9},{9,8},{10,11... | collective-permute-start | bytes 6291464 | tf_op jit(solution)/shard_map/ppermute | solution.py:296
  5.0 0.1 shard_map.74
  5.0 1.3 %collective-permute-start.3 = (bf16[256,1024]{1,0:T(8,128)(2,1)S(1)}, bf16[256,1024]{1,0:T(8,128)(2,1)S(1)}, u32[]{:S(2)}, u32[]{:S(2)}) collective-permute-start(bf16[256,1024]{1,0:T(8,128)(2,1)S(1)} %get-tuple-element.25), channel_id=1, source_target_pairs={{1,3},{5,7},{9,11},{13,15},{17,19},{21,23},{25,27},{29,31}} | collective-permute-start | bytes 1572872 | tf_op jit(solution)/shard_map/ppermute | solution.py:293
  6.3 1.3 %collective-permute-start.4 = (bf16[256,1024]{1,0:T(8,128)(2,1)S(1)}, bf16[256,1024]{1,0:T(8,128)(2,1)S(1)}, u32[]{:S(2)}, u32[]{:S(2)}) collective-permute-start(bf16[256,1024]{1,0:T(8,128)(2,1)S(1)} %get-tuple-element.25), channel_id=1, source_target_pairs={{0,3},{4,7},{8,11},{12,15},{16,19},{20,23},{24,27},{28,31}} | collective-permute-start | bytes 1572872 | tf_op jit(solution)/shard_map/ppermute | solution.py:293
  7.6 0.1 collective-permute-start.2
  7.7 0.0 copy-start.4
  7.7 1.3 %collective-permute-start = (bf16[224,1024]{1,0:T(8,128)(2,1)S(1)}, bf16[224,1024]{1,0:T(8,128)(2,1)S(1)}, u32[]{:S(2)}, u32[]{:S(2)}) collective-permute-start(bf16[224,1024]{1,0:T(8,128)(2,1)S(1)} %get-tuple-element.23), channel_id=1, source_target_pairs={{1,3},{5,7},{9,11},{13,15},{17,19},{21,23},{25,27},{29,31}} | collective-permute-start | bytes 1376264 | tf_op jit(solution)/shard_map/ppermute | solution.py:293
  9.0 0.0 collective-permute-done.2.refs_3_.refs_7_.refs_5_
  9.0 1.3 %collective-permute-start.1 = (bf16[224,1024]{1,0:T(8,128)(2,1)S(1)}, bf16[224,1024]{1,0:T(8,128)(2,1)S(1)}, u32[]{:S(2)}, u32[]{:S(2)}) collective-permute-start(bf16[224,1024]{1,0:T(8,128)(2,1)S(1)} %get-tuple-element.23), channel_id=1, source_target_pairs={{0,3},{4,7},{8,11},{12,15},{16,19},{20,23},{24,27},{28,31}} | collective-permute-start | bytes 1376264 | tf_op jit(solution)/shard_map/ppermute | solution.py:293
  10.4 0.6 shard_map.75.refs_7_
  10.9 0.0 collective-permute-done.5.refs_2_.refs_5_
  10.9 0.6 shard_map.76
  11.5 7.2 %collective-permute-done.3.refs_2_ = bf16[256,1024]{1,0:T(8,128)(2,1)S(1)} collective-permute-done((bf16[256,1024]{1,0:T(8,128)(2,1)S(1)}, bf16[256,1024]{1,0:T(8,128)(2,1)S(1)}, u32[]{:S(2)}, u32[]{:S(2)}) %collective-permute-start.3) | collective-permute-done | bytes 524320 | tf_op jit(solution)/shard_map/ppermute | solution.py:293
  18.7 3.7 %collective-permute-done.4.refs_3_ = bf16[256,1024]{1,0:T(8,128)(2,1)S(1)} collective-permute-done((bf16[256,1024]{1,0:T(8,128)(2,1)S(1)}, bf16[256,1024]{1,0:T(8,128)(2,1)S(1)}, u32[]{:S(2)}, u32[]{:S(2)}) %collective-permute-start.4) | collective-permute-done | bytes 524320 | tf_op jit(solution)/shard_map/ppermute | solution.py:293
  22.4 4.0 %shard_map.77 = (bf16[128,512]{1,0:T(8,128)(2,1)S(1)}, bf16[128,512]{1,0:T(8,128)(2,1)S(1)}, bf16[128,512]{1,0:T(8,128)(2,1)S(1)}, bf16[128,512]{1,0:T(8,128)(2,1)S(1)}, f32[8,256,256]{2,1,0:T(8,128)S(1)}) custom-call(s32[2]{0:T(128)S(1)} %pad_add_fusion.refs_0_, bf16[256,768]{1,0:T(8,128)(2,1)S(1)} %copy-done.1, ...), custom_call_target="tpu_custom_call" | custom-call | flops 2147483648 | bytes 4194304 | tf_op jit(solution)/shard_map/pallas_call | solution.py:308
  26.4 2.1 %collective-permute-done.refs_2_ = bf16[224,1024]{1,0:T(8,128)(2,1)S(1)} collective-permute-done((bf16[224,1024]{1,0:T(8,128)(2,1)S(1)}, bf16[224,1024]{1,0:T(8,128)(2,1)S(1)}, u32[]{:S(2)}, u32[]{:S(2)}) %collective-permute-start) | collective-permute-done | bytes 458784 | tf_op jit(solution)/shard_map/ppermute | solution.py:293
  28.5 1.9 %collective-permute-done.1.refs_3_ = bf16[224,1024]{1,0:T(8,128)(2,1)S(1)} collective-permute-done((bf16[224,1024]{1,0:T(8,128)(2,1)S(1)}, bf16[224,1024]{1,0:T(8,128)(2,1)S(1)}, u32[]{:S(2)}, u32[]{:S(2)}) %collective-permute-start.1) | collective-permute-done | bytes 458784 | tf_op jit(solution)/shard_map/ppermute | solution.py:293
  30.4 0.0 copy-done.2
  30.4 3.3 %shard_map.78 = (bf16[128,512]{1,0:T(8,128)(2,1)}, bf16[128,512]{1,0:T(8,128)(2,1)S(1)}, bf16[128,512]{1,0:T(8,128)(2,1)S(1)}, bf16[128,512]{1,0:T(8,128)(2,1)S(1)}, bf16[256,512]{1,0:T(8,128)(2,1)S(1)}) custom-call(s32[2]{0:T(128)S(1)} %pad_add_fusion.refs_0_, bf16[256,224]{1,0:T(8,128)(2,1)S(1)} %copy-done.2, ...), custom_call_target="tpu_custom_call" | custom-call | flops 2147483648 | bytes 4194304 | tf_op jit(solution)/shard_map/pallas_call | solution.py:308
  33.7 1.3 %collective-permute-start.7 = (bf16[128,512]{1,0:T(8,128)(2,1)S(1)}, bf16[128,512]{1,0:T(8,128)(2,1)S(1)}, u32[]{:S(2)}, u32[]{:S(2)}) collective-permute-start(bf16[128,512]{1,0:T(8,128)(2,1)S(1)} %get-tuple-element.30), channel_id=1, source_target_pairs={{1,4},{5,0},{9,12},{13,8},{3,6},{7,2},{11,14},{15,10},{17,20},{21,... | collective-permute-start | bytes 393224 | tf_op jit(solution)/shard_map/ppermute | solution.py:302
  35.0 1.3 %collective-permute-start.8 = (bf16[128,512]{1,0:T(8,128)(2,1)S(1)}, bf16[128,512]{1,0:T(8,128)(2,1)S(1)}, u32[]{:S(2)}, u32[]{:S(2)}) collective-permute-start(bf16[128,512]{1,0:T(8,128)(2,1)S(1)} %get-tuple-element.31), channel_id=1, source_target_pairs={{1,8},{5,12},{9,0},{13,4},{3,10},{7,14},{11,2},{15,6},{17,24},{21,... | collective-permute-start | bytes 393224 | tf_op jit(solution)/shard_map/ppermute | solution.py:302
  36.3 1.3 %collective-permute-start.9 = (bf16[128,512]{1,0:T(8,128)(2,1)S(1)}, bf16[128,512]{1,0:T(8,128)(2,1)S(1)}, u32[]{:S(2)}, u32[]{:S(2)}) collective-permute-start(bf16[128,512]{1,0:T(8,128)(2,1)S(1)} %get-tuple-element.32), channel_id=1, source_target_pairs={{1,12},{5,8},{9,4},{13,0},{3,14},{7,10},{11,6},{15,2},{17,28},{21,... | collective-permute-start | bytes 393224 | tf_op jit(solution)/shard_map/ppermute | solution.py:302
  37.6 1.3 %collective-permute-start.10 = (bf16[128,512]{1,0:T(8,128)(2,1)S(1)}, bf16[128,512]{1,0:T(8,128)(2,1)S(1)}, u32[]{:S(2)}, u32[]{:S(2)}) collective-permute-start(bf16[128,512]{1,0:T(8,128)(2,1)S(1)} %get-tuple-element.33), channel_id=1, source_target_pairs={{1,4},{5,0},{9,12},{13,8},{3,6},{7,2},{11,14},{15,10},{17,20},{21,... | collective-permute-start | bytes 393224 | tf_op jit(solution)/shard_map/ppermute | solution.py:302
  39.0 0.1 collective-permute-start.6
  39.0 0.0 collective-permute-done.7.refs_2_
  39.0 4.6 %collective-permute-start.11 = (bf16[128,512]{1,0:T(8,128)(2,1)S(1)}, bf16[128,512]{1,0:T(8,128)(2,1)S(1)}, u32[]{:S(2)}, u32[]{:S(2)}) collective-permute-start(bf16[128,512]{1,0:T(8,128)(2,1)S(1)} %get-tuple-element.34), channel_id=1, source_target_pairs={{1,8},{5,12},{9,0},{13,4},{3,10},{7,14},{11,2},{15,6},{17,24},{21,... | collective-permute-start | bytes 393224 | tf_op jit(solution)/shard_map/ppermute | solution.py:302
  43.6 0.0 collective-permute-done.8.refs_3_
  43.6 1.3 %collective-permute-start.13 = (bf16[256,512]{1,0:T(8,128)(2,1)S(1)}, bf16[256,512]{1,0:T(8,128)(2,1)S(1)}, u32[]{:S(2)}, u32[]{:S(2)}) collective-permute-start(bf16[256,512]{1,0:T(8,128)(2,1)S(1)} %get-tuple-element.36), channel_id=1, source_target_pairs={{0,5},{4,1},{8,13},{12,9},{2,7},{6,3},{10,15},{14,11},{16,21},{20,... | collective-permute-start | bytes 786440 | tf_op jit(solution)/shard_map/ppermute | solution.py:302
  44.9 0.0 collective-permute-done.9.refs_4_
  45.0 1.3 %collective-permute-start.14 = (bf16[256,512]{1,0:T(8,128)(2,1)S(1)}, bf16[256,512]{1,0:T(8,128)(2,1)S(1)}, u32[]{:S(2)}, u32[]{:S(2)}) collective-permute-start(bf16[256,512]{1,0:T(8,128)(2,1)S(1)} %get-tuple-element.37), channel_id=1, source_target_pairs={{0,9},{4,13},{8,1},{12,5},{2,11},{6,15},{10,3},{14,7},{16,25},{20,... | collective-permute-start | bytes 786440 | tf_op jit(solution)/shard_map/ppermute | solution.py:302
  46.3 0.0 collective-permute-done.10.refs_5_
  46.3 1.3 %collective-permute-start.15 = (bf16[256,512]{1,0:T(8,128)(2,1)S(1)}, bf16[256,512]{1,0:T(8,128)(2,1)S(1)}, u32[]{:S(2)}, u32[]{:S(2)}) collective-permute-start(bf16[256,512]{1,0:T(8,128)(2,1)S(1)} %get-tuple-element.38), channel_id=1, source_target_pairs={{0,13},{4,9},{8,5},{12,1},{2,15},{6,11},{10,7},{14,3},{16,29},{20,... | collective-permute-start | bytes 786440 | tf_op jit(solution)/shard_map/ppermute | solution.py:302
  47.6 0.0 collective-permute-done.11.refs_6_
  47.6 4.3 %collective-permute-start.12 = (bf16[128,512]{1,0:T(8,128)(2,1)S(1)}, bf16[128,512]{1,0:T(8,128)(2,1)S(1)}, u32[]{:S(2)}, u32[]{:S(2)}) collective-permute-start(bf16[128,512]{1,0:T(8,128)(2,1)S(1)} %get-tuple-element.35), channel_id=1, source_target_pairs={{1,12},{5,8},{9,4},{13,0},{3,14},{7,10},{11,6},{15,2},{17,28},{21,... | collective-permute-start | bytes 393224 | tf_op jit(solution)/shard_map/ppermute | solution.py:302
  51.9 8.7 %collective-permute-done.12.refs_7_ = bf16[128,512]{1,0:T(8,128)(2,1)S(1)} collective-permute-done((bf16[128,512]{1,0:T(8,128)(2,1)S(1)}, bf16[128,512]{1,0:T(8,128)(2,1)S(1)}, u32[]{:S(2)}, u32[]{:S(2)}) %collective-permute-start.12) | collective-permute-done | bytes 131104 | tf_op jit(solution)/shard_map/ppermute | solution.py:302
  60.5 0.0 collective-permute-done.6.refs_1_
  60.5 0.0 collective-permute-done.13.refs_8_
  60.6 0.0 collective-permute-done.14.refs_9_
  60.6 3.3 %collective-permute-done.15.refs_10_ = bf16[256,512]{1,0:T(8,128)(2,1)S(1)} collective-permute-done((bf16[256,512]{1,0:T(8,128)(2,1)S(1)}, bf16[256,512]{1,0:T(8,128)(2,1)S(1)}, u32[]{:S(2)}, u32[]{:S(2)}) %collective-permute-start.15) | collective-permute-done | bytes 262176 | tf_op jit(solution)/shard_map/ppermute | solution.py:302
  63.8 1.6 %shard_map.79 = bf16[16,64,512]{2,1,0:T(8,128)(2,1)} custom-call(s32[2]{0:T(128)S(1)} %pad_add_fusion.refs_0_, bf16[256,512]{1,0:T(8,128)(2,1)S(1)} %collective-permute-done.6.refs_1_, bf16[128,512]{1,0:T(8,128)(2,1)S(1)} %collective-permute-done.7.refs_2_, bf16[128,512]{1,0:T(8,128)(2,1)S(1)} %collective-permute-done.8.refs_3_, ...), custom_call_target="tpu_custom_call" | custom-call | bytes 3145728 | tf_op jit(solution)/shard_map/pallas_call | solution.py:390
  (8 shorter events, 0.0 us)
Async XLA Ops:
  0.1 0.7 %copy-start.5 = (s32[64]{0:T(128)S(1)}, s32[64]{0:T(128)}, u32[]{:S(2)}) copy-start(s32[64]{0:T(128)} %param.9) | copy-start | bytes 772
  0.7 1.9 %copy-start.6 = (bf16[1,1,512,4,2,256]{5,4,3,2,1,0:T(2,128)(2,1)S(1)}, bf16[1,1,512,4,2,256]{5,4,3,2,1,0:T(2,128)(2,1)}, u32[]{:S(2)}) copy-start(bf16[1,1,512,4,2,256]{5,4,3,2,1,0:T(2,128)(2,1)} %param.7) | copy-start | bytes 6291460
  4.2 3.4 %copy-start.3 = (f32[1,1,4,2,256]{4,3,2,1,0:T(2,128)S(1)}, f32[1,1,4,2,256]{4,3,2,1,0:T(2,128)}, u32[]{:S(2)}) copy-start(f32[1,1,4,2,256]{4,3,2,1,0:T(2,128)} %param.8) | copy-start | bytes 24580
  4.2 6.1 %copy-start = (bf16[512,512]{1,0:T(8,128)(2,1)S(1)}, bf16[512,512]{1,0:T(8,128)(2,1)}, u32[]{:S(2)}) copy-start(bf16[512,512]{1,0:T(8,128)(2,1)} %constant.17.clone.refs_4_.refs_8_.refs_6_) | copy-start | bytes 1572868
  4.2 6.1 %copy-start.1 = (bf16[256,768]{1,0:T(8,128)(2,1)S(1)}, bf16[256,768]{1,0:T(8,128)(2,1)}, u32[]{:S(2)}) copy-start(bf16[256,768]{1,0:T(8,128)(2,1)} %constant.15.clone.refs_1_) | copy-start | bytes 1179652
  4.2 6.7 %collective-permute-start.5 = (bf16[1024,1024]{1,0:T(8,128)(2,1)S(1)}, bf16[1024,1024]{1,0:T(8,128)(2,1)S(1)}, u32[]{:S(2)}, u32[]{:S(2)}) collective-permute-start(bf16[1024,1024]{1,0:T(8,128)(2,1)S(1)} %bitcast.10), channel_id=1, source_target_pairs={{0,1},{1,0},{2,3},{3,2},{4,5},{5,4},{6,7},{7,6},{8,9},{9,8},{10,11... | collective-permute-start | bytes 6291464 | tf_op jit(solution)/shard_map/ppermute | solution.py:296
  5.0 13.7 %collective-permute-start.3 = (bf16[256,1024]{1,0:T(8,128)(2,1)S(1)}, bf16[256,1024]{1,0:T(8,128)(2,1)S(1)}, u32[]{:S(2)}, u32[]{:S(2)}) collective-permute-start(bf16[256,1024]{1,0:T(8,128)(2,1)S(1)} %get-tuple-element.25), channel_id=1, source_target_pairs={{1,3},{5,7},{9,11},{13,15},{17,19},{21,23},{25,27},{29,31}} | collective-permute-start | bytes 1572872 | tf_op jit(solution)/shard_map/ppermute | solution.py:293
  6.3 16.1 %collective-permute-start.4 = (bf16[256,1024]{1,0:T(8,128)(2,1)S(1)}, bf16[256,1024]{1,0:T(8,128)(2,1)S(1)}, u32[]{:S(2)}, u32[]{:S(2)}) collective-permute-start(bf16[256,1024]{1,0:T(8,128)(2,1)S(1)} %get-tuple-element.25), channel_id=1, source_target_pairs={{0,3},{4,7},{8,11},{12,15},{16,19},{20,23},{24,27},{28,31}} | collective-permute-start | bytes 1572872 | tf_op jit(solution)/shard_map/ppermute | solution.py:293
  7.6 1.4 %collective-permute-start.2 = (f32[4,2,256]{2,1,0:T(2,128)S(1)}, f32[4,2,256]{2,1,0:T(2,128)S(1)}, u32[]{:S(2)}, u32[]{:S(2)}) collective-permute-start(f32[4,2,256]{2,1,0:T(2,128)S(1)} %bitcast.14), channel_id=1, source_target_pairs={{0,1},{1,0},{2,3},{3,2},{4,5},{5,4},{6,7},{7,6},{8,9},{9,8},{10,11... | collective-permute-start | bytes 24584 | tf_op jit(solution)/shard_map/ppermute | solution.py:296
  7.7 3.2 %copy-start.4 = (s32[1024]{0:T(1024)S(1)}, s32[1024]{0:T(1024)}, u32[]{:S(2)}) copy-start(s32[1024]{0:T(1024)} %param.10) | copy-start | bytes 12292
  7.7 20.8 %collective-permute-start = (bf16[224,1024]{1,0:T(8,128)(2,1)S(1)}, bf16[224,1024]{1,0:T(8,128)(2,1)S(1)}, u32[]{:S(2)}, u32[]{:S(2)}) collective-permute-start(bf16[224,1024]{1,0:T(8,128)(2,1)S(1)} %get-tuple-element.23), channel_id=1, source_target_pairs={{1,3},{5,7},{9,11},{13,15},{17,19},{21,23},{25,27},{29,31}} | collective-permute-start | bytes 1376264 | tf_op jit(solution)/shard_map/ppermute | solution.py:293
  9.0 21.4 %collective-permute-start.1 = (bf16[224,1024]{1,0:T(8,128)(2,1)S(1)}, bf16[224,1024]{1,0:T(8,128)(2,1)S(1)}, u32[]{:S(2)}, u32[]{:S(2)}) collective-permute-start(bf16[224,1024]{1,0:T(8,128)(2,1)S(1)} %get-tuple-element.23), channel_id=1, source_target_pairs={{0,3},{4,7},{8,11},{12,15},{16,19},{20,23},{24,27},{28,31}} | collective-permute-start | bytes 1376264 | tf_op jit(solution)/shard_map/ppermute | solution.py:293
  22.4 8.0 %copy-start.2 = (bf16[256,224]{1,0:T(8,128)(2,1)S(1)}, bf16[256,224]{1,0:T(8,128)(2,1)}, u32[]{:S(2)}) copy-start(bf16[256,224]{1,0:T(8,128)(2,1)} %constant.16.clone.refs_1_) | copy-start | bytes 344068
  33.7 5.3 %collective-permute-start.7 = (bf16[128,512]{1,0:T(8,128)(2,1)S(1)}, bf16[128,512]{1,0:T(8,128)(2,1)S(1)}, u32[]{:S(2)}, u32[]{:S(2)}) collective-permute-start(bf16[128,512]{1,0:T(8,128)(2,1)S(1)} %get-tuple-element.30), channel_id=1, source_target_pairs={{1,4},{5,0},{9,12},{13,8},{3,6},{7,2},{11,14},{15,10},{17,20},{21,... | collective-permute-start | bytes 393224 | tf_op jit(solution)/shard_map/ppermute | solution.py:302
  35.0 8.6 %collective-permute-start.8 = (bf16[128,512]{1,0:T(8,128)(2,1)S(1)}, bf16[128,512]{1,0:T(8,128)(2,1)S(1)}, u32[]{:S(2)}, u32[]{:S(2)}) collective-permute-start(bf16[128,512]{1,0:T(8,128)(2,1)S(1)} %get-tuple-element.31), channel_id=1, source_target_pairs={{1,8},{5,12},{9,0},{13,4},{3,10},{7,14},{11,2},{15,6},{17,24},{21,... | collective-permute-start | bytes 393224 | tf_op jit(solution)/shard_map/ppermute | solution.py:302
  36.3 8.6 %collective-permute-start.9 = (bf16[128,512]{1,0:T(8,128)(2,1)S(1)}, bf16[128,512]{1,0:T(8,128)(2,1)S(1)}, u32[]{:S(2)}, u32[]{:S(2)}) collective-permute-start(bf16[128,512]{1,0:T(8,128)(2,1)S(1)} %get-tuple-element.32), channel_id=1, source_target_pairs={{1,12},{5,8},{9,4},{13,0},{3,14},{7,10},{11,6},{15,2},{17,28},{21,... | collective-permute-start | bytes 393224 | tf_op jit(solution)/shard_map/ppermute | solution.py:302
  37.6 8.6 %collective-permute-start.10 = (bf16[128,512]{1,0:T(8,128)(2,1)S(1)}, bf16[128,512]{1,0:T(8,128)(2,1)S(1)}, u32[]{:S(2)}, u32[]{:S(2)}) collective-permute-start(bf16[128,512]{1,0:T(8,128)(2,1)S(1)} %get-tuple-element.33), channel_id=1, source_target_pairs={{1,4},{5,0},{9,12},{13,8},{3,6},{7,2},{11,14},{15,10},{17,20},{21,... | collective-permute-start | bytes 393224 | tf_op jit(solution)/shard_map/ppermute | solution.py:302
  39.0 21.6 %collective-permute-start.6 = (bf16[256,512]{1,0:T(8,128)(2,1)S(1)}, bf16[256,512]{1,0:T(8,128)(2,1)S(1)}, u32[]{:S(2)}, u32[]{:S(2)}) collective-permute-start(bf16[256,512]{1,0:T(8,128)(2,1)S(1)} %get-tuple-element.29), channel_id=1, source_target_pairs={{0,1},{1,0},{2,3},{3,2},{4,5},{5,4},{6,7},{7,6},{8,9},{9,8},{10,11... | collective-permute-start | bytes 786440 | tf_op jit(solution)/shard_map/ppermute | solution.py:296
  39.0 8.5 %collective-permute-start.11 = (bf16[128,512]{1,0:T(8,128)(2,1)S(1)}, bf16[128,512]{1,0:T(8,128)(2,1)S(1)}, u32[]{:S(2)}, u32[]{:S(2)}) collective-permute-start(bf16[128,512]{1,0:T(8,128)(2,1)S(1)} %get-tuple-element.34), channel_id=1, source_target_pairs={{1,8},{5,12},{9,0},{13,4},{3,10},{7,14},{11,2},{15,6},{17,24},{21,... | collective-permute-start | bytes 393224 | tf_op jit(solution)/shard_map/ppermute | solution.py:302
  43.6 16.9 %collective-permute-start.13 = (bf16[256,512]{1,0:T(8,128)(2,1)S(1)}, bf16[256,512]{1,0:T(8,128)(2,1)S(1)}, u32[]{:S(2)}, u32[]{:S(2)}) collective-permute-start(bf16[256,512]{1,0:T(8,128)(2,1)S(1)} %get-tuple-element.36), channel_id=1, source_target_pairs={{0,5},{4,1},{8,13},{12,9},{2,7},{6,3},{10,15},{14,11},{16,21},{20,... | collective-permute-start | bytes 786440 | tf_op jit(solution)/shard_map/ppermute | solution.py:302
  45.0 15.6 %collective-permute-start.14 = (bf16[256,512]{1,0:T(8,128)(2,1)S(1)}, bf16[256,512]{1,0:T(8,128)(2,1)S(1)}, u32[]{:S(2)}, u32[]{:S(2)}) collective-permute-start(bf16[256,512]{1,0:T(8,128)(2,1)S(1)} %get-tuple-element.37), channel_id=1, source_target_pairs={{0,9},{4,13},{8,1},{12,5},{2,11},{6,15},{10,3},{14,7},{16,25},{20,... | collective-permute-start | bytes 786440 | tf_op jit(solution)/shard_map/ppermute | solution.py:302
  46.3 17.5 %collective-permute-start.15 = (bf16[256,512]{1,0:T(8,128)(2,1)S(1)}, bf16[256,512]{1,0:T(8,128)(2,1)S(1)}, u32[]{:S(2)}, u32[]{:S(2)}) collective-permute-start(bf16[256,512]{1,0:T(8,128)(2,1)S(1)} %get-tuple-element.38), channel_id=1, source_target_pairs={{0,13},{4,9},{8,5},{12,1},{2,15},{6,11},{10,7},{14,3},{16,29},{20,... | collective-permute-start | bytes 786440 | tf_op jit(solution)/shard_map/ppermute | solution.py:302
  47.6 13.0 %collective-permute-start.12 = (bf16[128,512]{1,0:T(8,128)(2,1)S(1)}, bf16[128,512]{1,0:T(8,128)(2,1)S(1)}, u32[]{:S(2)}, u32[]{:S(2)}) collective-permute-start(bf16[128,512]{1,0:T(8,128)(2,1)S(1)} %get-tuple-element.35), channel_id=1, source_target_pairs={{1,12},{5,8},{9,4},{13,0},{3,14},{7,10},{11,6},{15,2},{17,28},{21,... | collective-permute-start | bytes 393224 | tf_op jit(solution)/shard_map/ppermute | solution.py:302

commit v9 on v8

--- a/solution.py
+++ b/solution.py
@@ -148,17 +148,17 @@
         each_late_block(blocks, filt_ref, x_ref, gain_ref, beam_ref, cal_ref, lambda at: keeper(out_ref, at))
 
 
-def late_kernel(
-    blocks, where_ref, filt_ref, x_ref, gain_ref, beam_ref, keep_ref, table_ref, power_ref, *refs
-):
+def late_kernel(block, where_ref, filt_ref, x_ref, gain_ref, beam_ref, keep_ref, table_ref, power_ref, *refs):
     out_refs, (cal_ref, sum_ref) = refs[:-2], refs[-2:]
+    rows = slice(block * BLOCK * ROWS, (block * BLOCK + TAPS + BLOCK) * ROWS)
+    mine = power_ref.at[block * BLOCK * UPCH : (block + 1) * BLOCK * UPCH]
 
     @pl.when(where_ref[1] == 0)
     def _():
-        def emitter(at):
-            return adder(power_ref, keep_ref, sum_ref, at)
-
-        each_late_block(blocks, filt_ref, x_ref, gain_ref, beam_ref, cal_ref, emitter)
+        def spectra(cyl):
+            return filtered([(filt_ref[...], x_ref[rows, columns(cyl)])])
+
+        form_powers(spectra, gain_ref, beam_ref, cal_ref.at[0], adder(mine, keep_ref, sum_ref))
         place(sum_ref, table_ref, out_refs)
 
 
@@ -178,12 +178,12 @@
                 return filtered([(filt_ref[:, :reach], there), (filt_ref[:, reach:], x[: 2 * reach, columns(cyl)])])
 
             emit = adder(sum_ref, keep_ref, sum_ref) if pol else keeper(sum_ref)
-            form_powers(spectra, gain, beam_ref, cal_ref, emit)
+            form_powers(spectra, gain, beam_ref, cal_ref.at[pol], emit)
         place(sum_ref, table_ref, out_refs)
 
 
 def far_kernel(n_owner, where_ref, edge_ref, f0, f1, g0, g1, beam_ref, keep_ref, table_ref, pre_ref, *refs):
-    own_refs, out_refs, own_ref, (cal_ref, sum_ref) = refs[:2], refs[2 : 2 + n_owner], refs[2 + n_owner], refs[-2:]
+    own_refs, out_refs, own_ref, (cal_ref, sum_ref) = refs[:3], refs[3 : 3 + n_owner], refs[3 + n_owner], refs[-2:]
     half = BLOCK * UPCH
 
     @pl.when(where_ref[1] == 1)
@@ -194,27 +194,29 @@
                 return pre_ref[pol * CYL + cyl] + filtered([(edge_ref[...], f[:, columns(cyl)])])
 
             emit = adder(sum_ref, keep_ref, sum_ref) if pol else keeper(sum_ref)
-            form_powers(spectra, gain, beam_ref, cal_ref, emit)
+            form_powers(spectra, gain, beam_ref, cal_ref.at[pol], emit)
         place(sum_ref, table_ref, out_refs)
         own_ref[:half, :] = out_refs[0][...]
         own_ref[half:, :] = own_refs[0][...]
 
     @pl.when(where_ref[1] == 0)
     def _():
-        own_ref[...] = own_refs[1][...]
+        own_ref[:half, :] = own_refs[1][...]
+        own_ref[half:, :] = own_refs[2][...]
 
 
 def place_table_kernel(most_sets, where_ref, owner_ref, out_ref):
     n_owner, beams, width = out_ref.shape
     sets = owner_ref.shape[1]
     owner = owner_ref[...].astype(jnp.float32)
-    set_of = lax.broadcasted_iota(jnp.int32, (beams, sets), 0) // SET_BEAMS
-    lane = lax.broadcasted_iota(jnp.int32, (beams, sets), 1)
+    set_of = lax.broadcasted_iota(jnp.int32, (sets, sets), 0)
+    lane = lax.broadcasted_iota(jnp.int32, (sets, sets), 1)
     own = jnp.sum(jnp.where(set_of == lane, owner, 0.0), axis=1, keepdims=True)
     same = jnp.logical_and(owner == own, lane < set_of)
     rank = jnp.sum(jnp.where(same, 1.0, 0.0), axis=1, keepdims=True)
-    within = lax.broadcasted_iota(jnp.int32, (beams, 1), 0) % SET_BEAMS
-    column = (own * most_sets + rank).astype(jnp.int32) * SET_BEAMS + within
+    first = (own * most_sets + rank).astype(jnp.int32) * SET_BEAMS
+    within = lax.broadcasted_iota(jnp.int32, (sets, SET_BEAMS, 1), 1)
+    column = (first.reshape(sets, 1, 1) + within).reshape(beams, 1)
     lane_at = lax.broadcasted_iota(jnp.int32, (beams, width), 1)
     for k in range(n_owner):
         owner_k = where_ref[0] ^ k
@@ -224,7 +226,7 @@
 
 def gather_kernel(n_owner, where_ref, *refs):
     own_ref, got, out_ref = refs[0], refs[1:-1], refs[-1]
-    far, near, late = (got[i * (n_owner - 1) : (i + 1) * (n_owner - 1)] for i in range(3))
+    chunks = [got[i * (n_owner - 1) : (i + 1) * (n_owner - 1)] for i in range(4)]
 
     def copy(block, frame, k):
         rows = pl.ds(pl.multiple_of((where_ref[0] ^ k) * UPCH, UPCH), UPCH)
@@ -232,17 +234,13 @@
         out_ref[frame : frame + count, rows, :] = block[...].reshape(count, UPCH, block.shape[1])
 
     copy(own_ref, 0, 0)
-
-    @pl.when(where_ref[1] == 0)
-    def _():
-        for k in range(1, n_owner):
-            copy(far[k - 1], 0, k)
-            copy(near[k - 1], BLOCK, k)
-
-    @pl.when(where_ref[1] == 1)
-    def _():
-        for k in range(1, n_owner):
-            copy(late[k - 1], 0, k)
+    for pol in range(2):
+
+        @pl.when(where_ref[1] == pol)
+        def _(pol=pol):
+            for part in range(2):
+                for k in range(1, n_owner):
+                    copy(chunks[2 * pol + part][k - 1], part * BLOCK, k)
 
 
 VMEM = pl.BlockSpec(memory_space=pltpu.VMEM)
@@ -304,7 +302,7 @@
 
     def form(body, rows, *arrays, after=(), more=()):
         shape = [jax.ShapeDtypeStruct((rows, width), bf16)] * n_owner
-        scratch = [pltpu.VMEM((CYL * BLOCK * UPCH, 2 * NS), bf16), pltpu.VMEM((rows, beams), bf16)]
+        scratch = [pltpu.VMEM((2, CYL * BLOCK * UPCH, 2 * NS), bf16), pltpu.VMEM((rows, beams), bf16)]
         return call(
             body,
             shape + list(more),
@@ -354,10 +352,13 @@
         scalars=1,
         scratch=[pltpu.VMEM((CYL * BLOCK * UPCH, 2 * NS), bf16)],
     )(where, filt, x, gain, beam_table)
-    body = functools.partial(late_kernel, blocks)
-    rows = kept * UPCH
-    late = form(body, rows, filt, other, gain_other, beam_table, keep, table, late_own)
-    late_got = spread(late, 0)
+    late, got = [], []
+    for block in range(blocks):
+        body = functools.partial(late_kernel, block)
+        arrays = (filt, other, gain_other, beam_table, keep, table, late_own)
+        after = [late[-1][0]] if late else []
+        late.append(form(body, BLOCK * UPCH, *arrays, after=after))
+        got += spread(late[-1], 0)
     *near, pre = form(
         functools.partial(near_kernel, n_owner),
         BLOCK * UPCH,
@@ -367,7 +368,7 @@
         x,
         other,
         *common,
-        after=late[:1],
+        after=late[1][:1],
         more=[jax.ShapeDtypeStruct((2 * CYL, reach, NS), jnp.float32)],
     )
     near_got = spread(near, 1)
@@ -380,13 +381,14 @@
         *common,
         pre,
         near[0],
-        late[0],
+        late[0][0],
+        late[1][0],
         more=[jax.ShapeDtypeStruct((kept * UPCH, width), bf16)],
     )
     far_got = spread(far, 1)
     own_got = swap(own)
     out_shape = jax.ShapeDtypeStruct((kept, n_owner * UPCH, width), bf16)
-    arrays = [own_got, *far_got, *near_got, *late_got]
+    arrays = [own_got, *far_got, *near_got, *got]
     return call(functools.partial(gather_kernel, n_owner), out_shape, len(arrays), 0, 3 << 20, scalars=1)(
         where, *arrays
     )

time: 65.8 us -> 66.1 us (level)
  the two profiles are of different devices: /device:TPU:11 before, /device:TPU:1 now
where the time goes in v9:
time: 66.1 us; the launch traced here: 65.7 us
  starting transfers between devices  31.8 us (48%)
  waiting for transfers between devices  18.1 us (27%)
  Pallas kernels  13.1 us (20%)
  local copies, waits for them, and re-layouts  2.26 us (3%)
    ppermute x12, starting transfers between devices, spread(): got.append(lax.ppermute(blocks[k], ('freq', 'pol'), route))  19.5 us
    ppermute x4, waiting for transfers between devices, ahead(): lax.ppermute(part, ('tm', 'pol'), [(i * 2 + source, j * 2 + 1) for i, j i...  10 us
    pallas_call x4, Pallas kernels, form(): call(body, shape + list(more), len(arrays), 4 * 512 * 1024 * 1024, 4 << 2...  8.59 us
    ppermute x12, waiting for transfers between devices, spread(): got.append(lax.ppermute(blocks[k], ('freq', 'pol'), route))  8.06 us
    ppermute x4, starting transfers between devices, ahead(): lax.ppermute(part, ('tm', 'pol'), [(i * 2 + source, j * 2 + 1) for i, j i...  7.44 us
    ppermute x3, starting transfers between devices, swap(): return lax.ppermute(part, 'pol', [(0, 1), (1, 0)])  4.85 us
    pallas_call x1, Pallas kernels, per_device(): call(functools.partial(place_table_kernel, most_sets), jax.ShapeDtypeStru...  2.35 us
    pallas_call x1, Pallas kernels, per_device(): call(functools.partial(gather_kernel, n_owner), out_shape, len(arrays), 0...  1.59 us
  transfers between devices with their start and end apart: 19, of which 7 were waited for; matrix products, arithmetic and copies ran while one was open for 0% of the time, Pallas kernels for 9%

profile of v9, /device:TPU:1, one launch (start us, length us, event | category | flops | bytes accessed | tf_op | source)
XLA Modules:
  0.0 65.7 jit_solution(153121335779922112)
XLA Ops:
  0.0 0.1 pad_add_fusion.refs_0_
  0.1 0.7 copy-done.5
  0.7 2.4 %shard_map.73.refs_6_.refs_10_.refs_8_ = bf16[4,1024,512]{2,1,0:T(8,128)(2,1)S(1)} custom-call(s32[2]{0:T(128)S(1)} %pad_add_fusion.refs_0_, s32[1,64]{1,0:T(1,128)S(1)} %bitcast.22), custom_call_target="tpu_custom_call" | custom-call | flops 16777216 | bytes 4194304 | tf_op jit(solution)/shard_map/pallas_call | solution.py:320
  3.1 1.1 %copy.8 = bf16[512,2,4,256]{3,2,1,0:T(4,128)(2,1)S(1)} copy(bf16[512,2,4,256]{3,1,2,0:T(2,128)(2,1)S(1)} %bitcast.24) | data formatting | bytes 4194304 | tf_op jit(solution)/shard_map/transpose | solution.py:329
  4.2 0.5 copy.9
  4.7 0.0 copy-start.3
  4.7 0.0 copy-start
  4.7 0.0 copy-start.1
  4.7 0.1 collective-permute-start.5
  4.8 0.1 shard_map.74
  4.9 4.6 %collective-permute-start.3 = (bf16[256,1024]{1,0:T(8,128)(2,1)S(1)}, bf16[256,1024]{1,0:T(8,128)(2,1)S(1)}, u32[]{:S(2)}, u32[]{:S(2)}) collective-permute-start(bf16[256,1024]{1,0:T(8,128)(2,1)S(1)} %get-tuple-element.29), channel_id=1, source_target_pairs={{1,3},{5,7},{9,11},{13,15},{17,19},{21,23},{25,27},{29,31}} | collective-permute-start | bytes 1572872 | tf_op jit(solution)/shard_map/ppermute | solution.py:291
  9.5 0.7 %collective-permute-start.4 = (bf16[256,1024]{1,0:T(8,128)(2,1)S(1)}, bf16[256,1024]{1,0:T(8,128)(2,1)S(1)}, u32[]{:S(2)}, u32[]{:S(2)}) collective-permute-start(bf16[256,1024]{1,0:T(8,128)(2,1)S(1)} %get-tuple-element.29), channel_id=1, source_target_pairs={{0,3},{4,7},{8,11},{12,15},{16,19},{20,23},{24,27},{28,31}} | collective-permute-start | bytes 1572872 | tf_op jit(solution)/shard_map/ppermute | solution.py:291
  10.2 1.1 %collective-permute-start.2 = (f32[4,2,256]{2,1,0:T(2,128)S(1)}, f32[4,2,256]{2,1,0:T(2,128)S(1)}, u32[]{:S(2)}, u32[]{:S(2)}) collective-permute-start(f32[4,2,256]{2,1,0:T(2,128)S(1)} %bitcast.14), channel_id=1, source_target_pairs={{0,1},{1,0},{2,3},{3,2},{4,5},{5,4},{6,7},{7,6},{8,9},{9,8},{10,11... | collective-permute-start | bytes 24584 | tf_op jit(solution)/shard_map/ppermute | solution.py:294
  11.3 1.4 %collective-permute-start = (bf16[224,1024]{1,0:T(8,128)(2,1)S(1)}, bf16[224,1024]{1,0:T(8,128)(2,1)S(1)}, u32[]{:S(2)}, u32[]{:S(2)}) collective-permute-start(bf16[224,1024]{1,0:T(8,128)(2,1)S(1)} %get-tuple-element.27), channel_id=1, source_target_pairs={{1,3},{5,7},{9,11},{13,15},{17,19},{21,23},{25,27},{29,31}} | collective-permute-start | bytes 1376264 | tf_op jit(solution)/shard_map/ppermute | solution.py:291
  12.7 0.6 shard_map.75.refs_7_
  13.3 0.0 collective-permute-done.2.refs_3_.refs_7_.refs_5_
  13.3 0.7 %collective-permute-start.1 = (bf16[224,1024]{1,0:T(8,128)(2,1)S(1)}, bf16[224,1024]{1,0:T(8,128)(2,1)S(1)}, u32[]{:S(2)}, u32[]{:S(2)}) collective-permute-start(bf16[224,1024]{1,0:T(8,128)(2,1)S(1)} %get-tuple-element.27), channel_id=1, source_target_pairs={{0,3},{4,7},{8,11},{12,15},{16,19},{20,23},{24,27},{28,31}} | collective-permute-start | bytes 1376264 | tf_op jit(solution)/shard_map/ppermute | solution.py:291
  14.0 0.0 collective-permute-done.5.refs_2_.refs_5_
  14.0 0.6 shard_map.76
  14.6 0.6 shard_map.77
  15.2 4.2 %collective-permute-done.3.refs_2_ = bf16[256,1024]{1,0:T(8,128)(2,1)S(1)} collective-permute-done((bf16[256,1024]{1,0:T(8,128)(2,1)S(1)}, bf16[256,1024]{1,0:T(8,128)(2,1)S(1)}, u32[]{:S(2)}, u32[]{:S(2)}) %collective-permute-start.3) | collective-permute-done | bytes 524320 | tf_op jit(solution)/shard_map/ppermute | solution.py:291
  19.3 4.0 %shard_map.78 = (bf16[128,512]{1,0:T(8,128)(2,1)S(1)}, bf16[128,512]{1,0:T(8,128)(2,1)S(1)}, bf16[128,512]{1,0:T(8,128)(2,1)S(1)}, bf16[128,512]{1,0:T(8,128)(2,1)S(1)}, f32[8,256,256]{2,1,0:T(8,128)S(1)}) custom-call(s32[2]{0:T(128)S(1)} %pad_add_fusion.refs_0_, bf16[256,768]{1,0:T(8,128)(2,1)S(1)} %copy-done.1, ...), custom_call_target="tpu_custom_call" | custom-call | flops 2147483648 | bytes 4194304 | tf_op jit(solution)/shard_map/pallas_call | solution.py:306
  23.3 5.8 %collective-permute-done.refs_2_ = bf16[224,1024]{1,0:T(8,128)(2,1)S(1)} collective-permute-done((bf16[224,1024]{1,0:T(8,128)(2,1)S(1)}, bf16[224,1024]{1,0:T(8,128)(2,1)S(1)}, u32[]{:S(2)}, u32[]{:S(2)}) %collective-permute-start) | collective-permute-done | bytes 458784 | tf_op jit(solution)/shard_map/ppermute | solution.py:291
  29.2 0.0 collective-permute-done.1.refs_3_
  29.2 3.5 %shard_map.79 = (bf16[128,512]{1,0:T(8,128)(2,1)}, bf16[128,512]{1,0:T(8,128)(2,1)S(1)}, bf16[128,512]{1,0:T(8,128)(2,1)S(1)}, bf16[128,512]{1,0:T(8,128)(2,1)S(1)}, bf16[256,512]{1,0:T(8,128)(2,1)S(1)}) custom-call(s32[2]{0:T(128)S(1)} %pad_add_fusion.refs_0_, bf16[256,224]{1,0:T(8,128)(2,1)S(1)} %copy-done.2, ...), custom_call_target="tpu_custom_call" | custom-call | flops 2147483648 | bytes 4194304 | tf_op jit(solution)/shard_map/pallas_call | solution.py:306
  32.7 3.2 %collective-permute-start.7 = (bf16[128,512]{1,0:T(8,128)(2,1)S(1)}, bf16[128,512]{1,0:T(8,128)(2,1)S(1)}, u32[]{:S(2)}, u32[]{:S(2)}) collective-permute-start(bf16[128,512]{1,0:T(8,128)(2,1)S(1)} %get-tuple-element.35), channel_id=1, source_target_pairs={{1,4},{5,0},{9,12},{13,8},{3,6},{7,2},{11,14},{15,10},{17,20},{21,... | collective-permute-start | bytes 393224 | tf_op jit(solution)/shard_map/ppermute | solution.py:300
  35.9 2.3 %collective-permute-start.8 = (bf16[128,512]{1,0:T(8,128)(2,1)S(1)}, bf16[128,512]{1,0:T(8,128)(2,1)S(1)}, u32[]{:S(2)}, u32[]{:S(2)}) collective-permute-start(bf16[128,512]{1,0:T(8,128)(2,1)S(1)} %get-tuple-element.36), channel_id=1, source_target_pairs={{1,8},{5,12},{9,0},{13,4},{3,10},{7,14},{11,2},{15,6},{17,24},{21,... | collective-permute-start | bytes 393224 | tf_op jit(solution)/shard_map/ppermute | solution.py:300
  38.2 2.3 %collective-permute-start.9 = (bf16[128,512]{1,0:T(8,128)(2,1)S(1)}, bf16[128,512]{1,0:T(8,128)(2,1)S(1)}, u32[]{:S(2)}, u32[]{:S(2)}) collective-permute-start(bf16[128,512]{1,0:T(8,128)(2,1)S(1)} %get-tuple-element.37), channel_id=1, source_target_pairs={{1,12},{5,8},{9,4},{13,0},{3,14},{7,10},{11,6},{15,2},{17,28},{21,... | collective-permute-start | bytes 393224 | tf_op jit(solution)/shard_map/ppermute | solution.py:300
  40.5 1.3 %collective-permute-start.10 = (bf16[128,512]{1,0:T(8,128)(2,1)S(1)}, bf16[128,512]{1,0:T(8,128)(2,1)S(1)}, u32[]{:S(2)}, u32[]{:S(2)}) collective-permute-start(bf16[128,512]{1,0:T(8,128)(2,1)S(1)} %get-tuple-element.38), channel_id=1, source_target_pairs={{1,4},{5,0},{9,12},{13,8},{3,6},{7,2},{11,14},{15,10},{17,20},{21,... | collective-permute-start | bytes 393224 | tf_op jit(solution)/shard_map/ppermute | solution.py:300
  41.9 1.3 %collective-permute-start.11 = (bf16[128,512]{1,0:T(8,128)(2,1)S(1)}, bf16[128,512]{1,0:T(8,128)(2,1)S(1)}, u32[]{:S(2)}, u32[]{:S(2)}) collective-permute-start(bf16[128,512]{1,0:T(8,128)(2,1)S(1)} %get-tuple-element.39), channel_id=1, source_target_pairs={{1,8},{5,12},{9,0},{13,4},{3,10},{7,14},{11,2},{15,6},{17,24},{21,... | collective-permute-start | bytes 393224 | tf_op jit(solution)/shard_map/ppermute | solution.py:300
  43.2 0.0 collective-permute-done.7.refs_2_
  43.2 1.3 %collective-permute-start.12 = (bf16[128,512]{1,0:T(8,128)(2,1)S(1)}, bf16[128,512]{1,0:T(8,128)(2,1)S(1)}, u32[]{:S(2)}, u32[]{:S(2)}) collective-permute-start(bf16[128,512]{1,0:T(8,128)(2,1)S(1)} %get-tuple-element.40), channel_id=1, source_target_pairs={{1,12},{5,8},{9,4},{13,0},{3,14},{7,10},{11,6},{15,2},{17,28},{21,... | collective-permute-start | bytes 393224 | tf_op jit(solution)/shard_map/ppermute | solution.py:300
  44.5 0.0 collective-permute-done.8.refs_3_
  44.5 1.3 %collective-permute-start.16 = (bf16[128,512]{1,0:T(8,128)(2,1)S(1)}, bf16[128,512]{1,0:T(8,128)(2,1)S(1)}, u32[]{:S(2)}, u32[]{:S(2)}) collective-permute-start(bf16[128,512]{1,0:T(8,128)(2,1)S(1)} %get-tuple-element.44), channel_id=1, source_target_pairs={{0,5},{4,1},{8,13},{12,9},{2,7},{6,3},{10,15},{14,11},{16,21},{20,... | collective-permute-start | bytes 393224 | tf_op jit(solution)/shard_map/ppermute | solution.py:300
  45.8 1.3 %collective-permute-start.17 = (bf16[128,512]{1,0:T(8,128)(2,1)S(1)}, bf16[128,512]{1,0:T(8,128)(2,1)S(1)}, u32[]{:S(2)}, u32[]{:S(2)}) collective-permute-start(bf16[128,512]{1,0:T(8,128)(2,1)S(1)} %get-tuple-element.45), channel_id=1, source_target_pairs={{0,9},{4,13},{8,1},{12,5},{2,11},{6,15},{10,3},{14,7},{16,25},{20,... | collective-permute-start | bytes 393224 | tf_op jit(solution)/shard_map/ppermute | solution.py:300
  47.1 0.0 collective-permute-done.10.refs_5_
  47.1 3.7 %collective-permute-start.6 = (bf16[256,512]{1,0:T(8,128)(2,1)S(1)}, bf16[256,512]{1,0:T(8,128)(2,1)S(1)}, u32[]{:S(2)}, u32[]{:S(2)}) collective-permute-start(bf16[256,512]{1,0:T(8,128)(2,1)S(1)} %get-tuple-element.34), channel_id=1, source_target_pairs={{0,1},{1,0},{2,3},{3,2},{4,5},{5,4},{6,7},{7,6},{8,9},{9,8},{10,11... | collective-permute-start | bytes 786440 | tf_op jit(solution)/shard_map/ppermute | solution.py:294
  50.8 0.0 collective-permute-done.11.refs_6_
  50.8 1.3 %collective-permute-start.18 = (bf16[128,512]{1,0:T(8,128)(2,1)S(1)}, bf16[128,512]{1,0:T(8,128)(2,1)S(1)}, u32[]{:S(2)}, u32[]{:S(2)}) collective-permute-start(bf16[128,512]{1,0:T(8,128)(2,1)S(1)} %get-tuple-element.46), channel_id=1, source_target_pairs={{0,13},{4,9},{8,5},{12,1},{2,15},{6,11},{10,7},{14,3},{16,29},{20,... | collective-permute-start | bytes 393224 | tf_op jit(solution)/shard_map/ppermute | solution.py:300
  52.1 1.3 %collective-permute-start.13 = (bf16[128,512]{1,0:T(8,128)(2,1)S(1)}, bf16[128,512]{1,0:T(8,128)(2,1)S(1)}, u32[]{:S(2)}, u32[]{:S(2)}) collective-permute-start(bf16[128,512]{1,0:T(8,128)(2,1)S(1)} %get-tuple-element.41), channel_id=1, source_target_pairs={{0,5},{4,1},{8,13},{12,9},{2,7},{6,3},{10,15},{14,11},{16,21},{20,... | collective-permute-start | bytes 393224 | tf_op jit(solution)/shard_map/ppermute | solution.py:300
  53.4 1.3 %collective-permute-start.14 = (bf16[128,512]{1,0:T(8,128)(2,1)S(1)}, bf16[128,512]{1,0:T(8,128)(2,1)S(1)}, u32[]{:S(2)}, u32[]{:S(2)}) collective-permute-start(bf16[128,512]{1,0:T(8,128)(2,1)S(1)} %get-tuple-element.42), channel_id=1, source_target_pairs={{0,9},{4,13},{8,1},{12,5},{2,11},{6,15},{10,3},{14,7},{16,25},{20,... | collective-permute-start | bytes 393224 | tf_op jit(solution)/shard_map/ppermute | solution.py:300
  54.7 1.2 %collective-permute-done.17.refs_12_ = bf16[128,512]{1,0:T(8,128)(2,1)S(1)} collective-permute-done((bf16[128,512]{1,0:T(8,128)(2,1)S(1)}, bf16[128,512]{1,0:T(8,128)(2,1)S(1)}, u32[]{:S(2)}, u32[]{:S(2)}) %collective-permute-start.17) | collective-permute-done | bytes 131104 | tf_op jit(solution)/shard_map/ppermute | solution.py:300
  55.9 1.3 %collective-permute-start.15 = (bf16[128,512]{1,0:T(8,128)(2,1)S(1)}, bf16[128,512]{1,0:T(8,128)(2,1)S(1)}, u32[]{:S(2)}, u32[]{:S(2)}) collective-permute-start(bf16[128,512]{1,0:T(8,128)(2,1)S(1)} %get-tuple-element.43), channel_id=1, source_target_pairs={{0,13},{4,9},{8,5},{12,1},{2,15},{6,11},{10,7},{14,3},{16,29},{20,... | collective-permute-start | bytes 393224 | tf_op jit(solution)/shard_map/ppermute | solution.py:300
  57.2 1.8 %collective-permute-done.18.refs_13_ = bf16[128,512]{1,0:T(8,128)(2,1)S(1)} collective-permute-done((bf16[128,512]{1,0:T(8,128)(2,1)S(1)}, bf16[128,512]{1,0:T(8,128)(2,1)S(1)}, u32[]{:S(2)}, u32[]{:S(2)}) %collective-permute-start.18) | collective-permute-done | bytes 131104 | tf_op jit(solution)/shard_map/ppermute | solution.py:300
  59.0 2.1 %collective-permute-done.13.refs_8_ = bf16[128,512]{1,0:T(8,128)(2,1)S(1)} collective-permute-done((bf16[128,512]{1,0:T(8,128)(2,1)S(1)}, bf16[128,512]{1,0:T(8,128)(2,1)S(1)}, u32[]{:S(2)}, u32[]{:S(2)}) %collective-permute-start.13) | collective-permute-done | bytes 131104 | tf_op jit(solution)/shard_map/ppermute | solution.py:300
  61.1 1.0 %collective-permute-done.14.refs_9_ = bf16[128,512]{1,0:T(8,128)(2,1)S(1)} collective-permute-done((bf16[128,512]{1,0:T(8,128)(2,1)S(1)}, bf16[128,512]{1,0:T(8,128)(2,1)S(1)}, u32[]{:S(2)}, u32[]{:S(2)}) %collective-permute-start.14) | collective-permute-done | bytes 131104 | tf_op jit(solution)/shard_map/ppermute | solution.py:300
  62.0 2.0 %collective-permute-done.15.refs_10_ = bf16[128,512]{1,0:T(8,128)(2,1)S(1)} collective-permute-done((bf16[128,512]{1,0:T(8,128)(2,1)S(1)}, bf16[128,512]{1,0:T(8,128)(2,1)S(1)}, u32[]{:S(2)}, u32[]{:S(2)}) %collective-permute-start.15) | collective-permute-done | bytes 131104 | tf_op jit(solution)/shard_map/ppermute | solution.py:300
  64.1 1.6 %shard_map.80 = bf16[16,64,512]{2,1,0:T(8,128)(2,1)} custom-call(s32[2]{0:T(128)S(1)} %pad_add_fusion.refs_0_, bf16[256,512]{1,0:T(8,128)(2,1)S(1)} %collective-permute-done.6.refs_1_, bf16[128,512]{1,0:T(8,128)(2,1)S(1)} %collective-permute-done.7.refs_2_, bf16[128,512]{1,0:T(8,128)(2,1)S(1)} %collective-permute-done.8.refs_3_, ...), custom_call_target="tpu_custom_call" | custom-call | bytes 3145728 | tf_op jit(solution)/shard_map/pallas_call | solution.py:392
  (15 shorter events, 0.0 us)
Async XLA Ops:
  0.1 0.7 copy-start.5
  0.7 2.4 %copy-start.6 = (bf16[1,1,512,4,2,256]{5,4,3,2,1,0:T(2,128)(2,1)S(1)}, bf16[1,1,512,4,2,256]{5,4,3,2,1,0:T(2,128)(2,1)}, u32[]{:S(2)}) copy-start(bf16[1,1,512,4,2,256]{5,4,3,2,1,0:T(2,128)(2,1)} %param.7) | copy-start | bytes 6291460
  4.7 5.5 %copy-start.3 = (f32[1,1,4,2,256]{4,3,2,1,0:T(2,128)S(1)}, f32[1,1,4,2,256]{4,3,2,1,0:T(2,128)}, u32[]{:S(2)}) copy-start(f32[1,1,4,2,256]{4,3,2,1,0:T(2,128)} %param.8) | copy-start | bytes 24580
  4.7 8.0 %copy-start = (bf16[512,512]{1,0:T(8,128)(2,1)S(1)}, bf16[512,512]{1,0:T(8,128)(2,1)}, u32[]{:S(2)}) copy-start(bf16[512,512]{1,0:T(8,128)(2,1)} %constant.17.clone.refs_4_.refs_8_.refs_6_) | copy-start | bytes 1572868
  4.7 8.0 %copy-start.1 = (bf16[256,768]{1,0:T(8,128)(2,1)S(1)}, bf16[256,768]{1,0:T(8,128)(2,1)}, u32[]{:S(2)}) copy-start(bf16[256,768]{1,0:T(8,128)(2,1)} %constant.15.clone.refs_1_) | copy-start | bytes 1179652
  4.7 9.3 %collective-permute-start.5 = (bf16[1024,1024]{1,0:T(8,128)(2,1)S(1)}, bf16[1024,1024]{1,0:T(8,128)(2,1)S(1)}, u32[]{:S(2)}, u32[]{:S(2)}) collective-permute-start(bf16[1024,1024]{1,0:T(8,128)(2,1)S(1)} %bitcast.10), channel_id=1, source_target_pairs={{0,1},{1,0},{2,3},{3,2},{4,5},{5,4},{6,7},{7,6},{8,9},{9,8},{10,11... | collective-permute-start | bytes 6291464 | tf_op jit(solution)/shard_map/ppermute | solution.py:294
  4.9 14.4 %collective-permute-start.3 = (bf16[256,1024]{1,0:T(8,128)(2,1)S(1)}, bf16[256,1024]{1,0:T(8,128)(2,1)S(1)}, u32[]{:S(2)}, u32[]{:S(2)}) collective-permute-start(bf16[256,1024]{1,0:T(8,128)(2,1)S(1)} %get-tuple-element.29), channel_id=1, source_target_pairs={{1,3},{5,7},{9,11},{13,15},{17,19},{21,23},{25,27},{29,31}} | collective-permute-start | bytes 1572872 | tf_op jit(solution)/shard_map/ppermute | solution.py:291
  9.5 9.8 %collective-permute-start.4 = (bf16[256,1024]{1,0:T(8,128)(2,1)S(1)}, bf16[256,1024]{1,0:T(8,128)(2,1)S(1)}, u32[]{:S(2)}, u32[]{:S(2)}) collective-permute-start(bf16[256,1024]{1,0:T(8,128)(2,1)S(1)} %get-tuple-element.29), channel_id=1, source_target_pairs={{0,3},{4,7},{8,11},{12,15},{16,19},{20,23},{24,27},{28,31}} | collective-permute-start | bytes 1572872 | tf_op jit(solution)/shard_map/ppermute | solution.py:291
  10.2 3.1 %collective-permute-start.2 = (f32[4,2,256]{2,1,0:T(2,128)S(1)}, f32[4,2,256]{2,1,0:T(2,128)S(1)}, u32[]{:S(2)}, u32[]{:S(2)}) collective-permute-start(f32[4,2,256]{2,1,0:T(2,128)S(1)} %bitcast.14), channel_id=1, source_target_pairs={{0,1},{1,0},{2,3},{3,2},{4,5},{5,4},{6,7},{7,6},{8,9},{9,8},{10,11... | collective-permute-start | bytes 24584 | tf_op jit(solution)/shard_map/ppermute | solution.py:294
  11.3 2.7 %copy-start.4 = (s32[1024]{0:T(1024)S(1)}, s32[1024]{0:T(1024)}, u32[]{:S(2)}) copy-start(s32[1024]{0:T(1024)} %param.10) | copy-start | bytes 12292
  11.3 17.9 %collective-permute-start = (bf16[224,1024]{1,0:T(8,128)(2,1)S(1)}, bf16[224,1024]{1,0:T(8,128)(2,1)S(1)}, u32[]{:S(2)}, u32[]{:S(2)}) collective-permute-start(bf16[224,1024]{1,0:T(8,128)(2,1)S(1)} %get-tuple-element.27), channel_id=1, source_target_pairs={{1,3},{5,7},{9,11},{13,15},{17,19},{21,23},{25,27},{29,31}} | collective-permute-start | bytes 1376264 | tf_op jit(solution)/shard_map/ppermute | solution.py:291
  13.3 15.8 %collective-permute-start.1 = (bf16[224,1024]{1,0:T(8,128)(2,1)S(1)}, bf16[224,1024]{1,0:T(8,128)(2,1)S(1)}, u32[]{:S(2)}, u32[]{:S(2)}) collective-permute-start(bf16[224,1024]{1,0:T(8,128)(2,1)S(1)} %get-tuple-element.27), channel_id=1, source_target_pairs={{0,3},{4,7},{8,11},{12,15},{16,19},{20,23},{24,27},{28,31}} | collective-permute-start | bytes 1376264 | tf_op jit(solution)/shard_map/ppermute | solution.py:291
  19.3 9.8 %copy-start.2 = (bf16[256,224]{1,0:T(8,128)(2,1)S(1)}, bf16[256,224]{1,0:T(8,128)(2,1)}, u32[]{:S(2)}) copy-start(bf16[256,224]{1,0:T(8,128)(2,1)} %constant.16.clone.refs_1_) | copy-start | bytes 344068
  32.7 10.5 %collective-permute-start.7 = (bf16[128,512]{1,0:T(8,128)(2,1)S(1)}, bf16[128,512]{1,0:T(8,128)(2,1)S(1)}, u32[]{:S(2)}, u32[]{:S(2)}) collective-permute-start(bf16[128,512]{1,0:T(8,128)(2,1)S(1)} %get-tuple-element.35), channel_id=1, source_target_pairs={{1,4},{5,0},{9,12},{13,8},{3,6},{7,2},{11,14},{15,10},{17,20},{21,... | collective-permute-start | bytes 393224 | tf_op jit(solution)/shard_map/ppermute | solution.py:300
  35.9 8.6 %collective-permute-start.8 = (bf16[128,512]{1,0:T(8,128)(2,1)S(1)}, bf16[128,512]{1,0:T(8,128)(2,1)S(1)}, u32[]{:S(2)}, u32[]{:S(2)}) collective-permute-start(bf16[128,512]{1,0:T(8,128)(2,1)S(1)} %get-tuple-element.36), channel_id=1, source_target_pairs={{1,8},{5,12},{9,0},{13,4},{3,10},{7,14},{11,2},{15,6},{17,24},{21,... | collective-permute-start | bytes 393224 | tf_op jit(solution)/shard_map/ppermute | solution.py:300
  38.2 7.6 %collective-permute-start.9 = (bf16[128,512]{1,0:T(8,128)(2,1)S(1)}, bf16[128,512]{1,0:T(8,128)(2,1)S(1)}, u32[]{:S(2)}, u32[]{:S(2)}) collective-permute-start(bf16[128,512]{1,0:T(8,128)(2,1)S(1)} %get-tuple-element.37), channel_id=1, source_target_pairs={{1,12},{5,8},{9,4},{13,0},{3,14},{7,10},{11,6},{15,2},{17,28},{21,... | collective-permute-start | bytes 393224 | tf_op jit(solution)/shard_map/ppermute | solution.py:300
  40.5 6.5 %collective-permute-start.10 = (bf16[128,512]{1,0:T(8,128)(2,1)S(1)}, bf16[128,512]{1,0:T(8,128)(2,1)S(1)}, u32[]{:S(2)}, u32[]{:S(2)}) collective-permute-start(bf16[128,512]{1,0:T(8,128)(2,1)S(1)} %get-tuple-element.38), channel_id=1, source_target_pairs={{1,4},{5,0},{9,12},{13,8},{3,6},{7,2},{11,14},{15,10},{17,20},{21,... | collective-permute-start | bytes 393224 | tf_op jit(solution)/shard_map/ppermute | solution.py:300
  41.9 9.0 %collective-permute-start.11 = (bf16[128,512]{1,0:T(8,128)(2,1)S(1)}, bf16[128,512]{1,0:T(8,128)(2,1)S(1)}, u32[]{:S(2)}, u32[]{:S(2)}) collective-permute-start(bf16[128,512]{1,0:T(8,128)(2,1)S(1)} %get-tuple-element.39), channel_id=1, source_target_pairs={{1,8},{5,12},{9,0},{13,4},{3,10},{7,14},{11,2},{15,6},{17,24},{21,... | collective-permute-start | bytes 393224 | tf_op jit(solution)/shard_map/ppermute | solution.py:300
  43.2 8.9 %collective-permute-start.12 = (bf16[128,512]{1,0:T(8,128)(2,1)S(1)}, bf16[128,512]{1,0:T(8,128)(2,1)S(1)}, u32[]{:S(2)}, u32[]{:S(2)}) collective-permute-start(bf16[128,512]{1,0:T(8,128)(2,1)S(1)} %get-tuple-element.40), channel_id=1, source_target_pairs={{1,12},{5,8},{9,4},{13,0},{3,14},{7,10},{11,6},{15,2},{17,28},{21,... | collective-permute-start | bytes 393224 | tf_op jit(solution)/shard_map/ppermute | solution.py:300
  44.5 8.9 %collective-permute-start.16 = (bf16[128,512]{1,0:T(8,128)(2,1)S(1)}, bf16[128,512]{1,0:T(8,128)(2,1)S(1)}, u32[]{:S(2)}, u32[]{:S(2)}) collective-permute-start(bf16[128,512]{1,0:T(8,128)(2,1)S(1)} %get-tuple-element.44), channel_id=1, source_target_pairs={{0,5},{4,1},{8,13},{12,9},{2,7},{6,3},{10,15},{14,11},{16,21},{20,... | collective-permute-start | bytes 393224 | tf_op jit(solution)/shard_map/ppermute | solution.py:300
  45.8 10.1 %collective-permute-start.17 = (bf16[128,512]{1,0:T(8,128)(2,1)S(1)}, bf16[128,512]{1,0:T(8,128)(2,1)S(1)}, u32[]{:S(2)}, u32[]{:S(2)}) collective-permute-start(bf16[128,512]{1,0:T(8,128)(2,1)S(1)} %get-tuple-element.45), channel_id=1, source_target_pairs={{0,9},{4,13},{8,1},{12,5},{2,11},{6,15},{10,3},{14,7},{16,25},{20,... | collective-permute-start | bytes 393224 | tf_op jit(solution)/shard_map/ppermute | solution.py:300
  47.1 17.0 %collective-permute-start.6 = (bf16[256,512]{1,0:T(8,128)(2,1)S(1)}, bf16[256,512]{1,0:T(8,128)(2,1)S(1)}, u32[]{:S(2)}, u32[]{:S(2)}) collective-permute-start(bf16[256,512]{1,0:T(8,128)(2,1)S(1)} %get-tuple-element.34), channel_id=1, source_target_pairs={{0,1},{1,0},{2,3},{3,2},{4,5},{5,4},{6,7},{7,6},{8,9},{9,8},{10,11... | collective-permute-start | bytes 786440 | tf_op jit(solution)/shard_map/ppermute | solution.py:294
  50.8 8.2 %collective-permute-start.18 = (bf16[128,512]{1,0:T(8,128)(2,1)S(1)}, bf16[128,512]{1,0:T(8,128)(2,1)S(1)}, u32[]{:S(2)}, u32[]{:S(2)}) collective-permute-start(bf16[128,512]{1,0:T(8,128)(2,1)S(1)} %get-tuple-element.46), channel_id=1, source_target_pairs={{0,13},{4,9},{8,5},{12,1},{2,15},{6,11},{10,7},{14,3},{16,29},{20,... | collective-permute-start | bytes 393224 | tf_op jit(solution)/shard_map/ppermute | solution.py:300
  52.1 8.9 %collective-permute-start.13 = (bf16[128,512]{1,0:T(8,128)(2,1)S(1)}, bf16[128,512]{1,0:T(8,128)(2,1)S(1)}, u32[]{:S(2)}, u32[]{:S(2)}) collective-permute-start(bf16[128,512]{1,0:T(8,128)(2,1)S(1)} %get-tuple-element.41), channel_id=1, source_target_pairs={{0,5},{4,1},{8,13},{12,9},{2,7},{6,3},{10,15},{14,11},{16,21},{20,... | collective-permute-start | bytes 393224 | tf_op jit(solution)/shard_map/ppermute | solution.py:300
  53.4 8.6 %collective-permute-start.14 = (bf16[128,512]{1,0:T(8,128)(2,1)S(1)}, bf16[128,512]{1,0:T(8,128)(2,1)S(1)}, u32[]{:S(2)}, u32[]{:S(2)}) collective-permute-start(bf16[128,512]{1,0:T(8,128)(2,1)S(1)} %get-tuple-element.42), channel_id=1, source_target_pairs={{0,9},{4,13},{8,1},{12,5},{2,11},{6,15},{10,3},{14,7},{16,25},{20,... | collective-permute-start | bytes 393224 | tf_op jit(solution)/shard_map/ppermute | solution.py:300
  55.9 8.2 %collective-permute-start.15 = (bf16[128,512]{1,0:T(8,128)(2,1)S(1)}, bf16[128,512]{1,0:T(8,128)(2,1)S(1)}, u32[]{:S(2)}, u32[]{:S(2)}) collective-permute-start(bf16[128,512]{1,0:T(8,128)(2,1)S(1)} %get-tuple-element.43), channel_id=1, source_target_pairs={{0,13},{4,9},{8,5},{12,1},{2,15},{6,11},{10,7},{14,3},{16,29},{20,... | collective-permute-start | bytes 393224 | tf_op jit(solution)/shard_map/ppermute | solution.py:300

commit v10 on v8

--- a/solution.py
+++ b/solution.py
@@ -118,7 +118,7 @@
 def place(sum_ref, table_ref, out_refs):
     for k, out_ref in enumerate(out_refs):
         placed = jnp.dot(sum_ref[...], table_ref[k], preferred_element_type=jnp.float32)
-        out_ref[...] = placed.astype(jnp.bfloat16)
+        out_ref[...] = placed.astype(jnp.bfloat16).reshape(out_ref.shape)
 
 
 def halo_rows_kernel(x_ref, near_ref, far_ref):
@@ -184,7 +184,7 @@
 
 def far_kernel(n_owner, where_ref, edge_ref, f0, f1, g0, g1, beam_ref, keep_ref, table_ref, pre_ref, *refs):
     own_refs, out_refs, own_ref, (cal_ref, sum_ref) = refs[:2], refs[2 : 2 + n_owner], refs[2 + n_owner], refs[-2:]
-    half = BLOCK * UPCH
+    half = BLOCK
 
     @pl.when(where_ref[1] == 1)
     def _():
@@ -196,53 +196,71 @@
             emit = adder(sum_ref, keep_ref, sum_ref) if pol else keeper(sum_ref)
             form_powers(spectra, gain, beam_ref, cal_ref, emit)
         place(sum_ref, table_ref, out_refs)
-        own_ref[:half, :] = out_refs[0][...]
-        own_ref[half:, :] = own_refs[0][...]
+        own_ref[:half] = out_refs[0][...]
+        own_ref[half:] = own_refs[0][...]
 
     @pl.when(where_ref[1] == 0)
     def _():
         own_ref[...] = own_refs[1][...]
 
 
-def place_table_kernel(most_sets, where_ref, owner_ref, out_ref):
-    n_owner, beams, width = out_ref.shape
-    sets = owner_ref.shape[1]
-    owner = owner_ref[...].astype(jnp.float32)
-    set_of = lax.broadcasted_iota(jnp.int32, (beams, sets), 0) // SET_BEAMS
-    lane = lax.broadcasted_iota(jnp.int32, (beams, sets), 1)
-    own = jnp.sum(jnp.where(set_of == lane, owner, 0.0), axis=1, keepdims=True)
-    same = jnp.logical_and(owner == own, lane < set_of)
-    rank = jnp.sum(jnp.where(same, 1.0, 0.0), axis=1, keepdims=True)
-    within = lax.broadcasted_iota(jnp.int32, (beams, 1), 0) % SET_BEAMS
-    column = (own * most_sets + rank).astype(jnp.int32) * SET_BEAMS + within
-    lane_at = lax.broadcasted_iota(jnp.int32, (beams, width), 1)
-    for k in range(n_owner):
-        owner_k = where_ref[0] ^ k
-        hit = (column - owner_k * width) == lane_at
-        out_ref[k] = jnp.where(hit, 1.0, 0.0).astype(jnp.bfloat16)
-
-
-def gather_kernel(n_owner, where_ref, *refs):
-    own_ref, got, out_ref = refs[0], refs[1:-1], refs[-1]
-    far, near, late = (got[i * (n_owner - 1) : (i + 1) * (n_owner - 1)] for i in range(3))
-
-    def copy(block, frame, k):
+def place_table_kernel(where_ref, owner_ref, out_ref, rank_ref):
+    n_owner = out_ref.shape[0]
+    for owner in range(n_owner):
+        rank_ref[owner] = 0
+    out_ref[...] = jnp.zeros_like(out_ref)
+    row = lax.broadcasted_iota(jnp.int32, (SET_BEAMS, LANES), 0)
+    lane = lax.broadcasted_iota(jnp.int32, (SET_BEAMS, LANES), 1)
+
+    def step(index, carry):
+        owner = owner_ref[index]
+        rank = rank_ref[owner]
+        rank_ref[owner] = rank + 1
+        column = rank * SET_BEAMS
+        tile = column // LANES * LANES
+        hit = lane - row == column - tile
+        rows = pl.ds(pl.multiple_of(index * SET_BEAMS, SET_BEAMS), SET_BEAMS)
+        lanes = pl.ds(pl.multiple_of(tile, LANES), LANES)
+        out_ref[where_ref[0] ^ owner, rows, lanes] = jnp.where(hit, 1.0, 0.0).astype(jnp.bfloat16)
+        return carry
+
+    lax.fori_loop(0, owner_ref.shape[0], step, 0, unroll=4)
+
+
+def put(where_ref, out_ref, sems, blocks):
+    copies = []
+    for index, (block, frame, k) in enumerate(blocks):
         rows = pl.ds(pl.multiple_of((where_ref[0] ^ k) * UPCH, UPCH), UPCH)
-        count = block.shape[0] // UPCH
-        out_ref[frame : frame + count, rows, :] = block[...].reshape(count, UPCH, block.shape[1])
-
-    copy(own_ref, 0, 0)
+        at = out_ref.at[pl.ds(frame, block.shape[0]), rows]
+        copies.append(pltpu.make_async_copy(block, at, sems.at[index]))
+    for copy in copies:
+        copy.start()
+    for copy in copies:
+        copy.wait()
+
+
+def early_gather_kernel(n_owner, where_ref, *refs):
+    near, late, out_ref, sems = refs[: n_owner - 1], refs[n_owner - 1 : -2], refs[-2], refs[-1]
 
     @pl.when(where_ref[1] == 0)
     def _():
-        for k in range(1, n_owner):
-            copy(far[k - 1], 0, k)
-            copy(near[k - 1], BLOCK, k)
+        put(where_ref, out_ref, sems, [(block, BLOCK, k + 1) for k, block in enumerate(near)])
 
     @pl.when(where_ref[1] == 1)
     def _():
-        for k in range(1, n_owner):
-            copy(late[k - 1], 0, k)
+        put(where_ref, out_ref, sems, [(block, 0, k + 1) for k, block in enumerate(late)])
+
+
+def last_gather_kernel(n_owner, where_ref, own_ref, *refs):
+    far, out_ref, sems = refs[: n_owner - 1], refs[-2], refs[-1]
+
+    @pl.when(where_ref[1] == 0)
+    def _():
+        put(where_ref, out_ref, sems, [(own_ref, 0, 0)] + [(block, 0, k + 1) for k, block in enumerate(far)])
+
+    @pl.when(where_ref[1] == 1)
+    def _():
+        put(where_ref, out_ref, sems, [(own_ref, 0, 0)])
 
 
 VMEM = pl.BlockSpec(memory_space=pltpu.VMEM)
@@ -303,7 +321,7 @@
         return got
 
     def form(body, rows, *arrays, after=(), more=()):
-        shape = [jax.ShapeDtypeStruct((rows, width), bf16)] * n_owner
+        shape = [jax.ShapeDtypeStruct((rows // UPCH, UPCH, width), bf16)] * n_owner
         scratch = [pltpu.VMEM((CYL * BLOCK * UPCH, 2 * NS), bf16), pltpu.VMEM((rows, beams), bf16)]
         return call(
             body,
@@ -320,13 +338,14 @@
     keep = keep_flags.reshape(1, -1)
     reach, edge_rows = BLOCK * ROWS, (TAPS - 1 - BLOCK) * ROWS
     table = call(
-        functools.partial(place_table_kernel, most_sets),
+        place_table_kernel,
         jax.ShapeDtypeStruct((n_owner, beams, width), bf16),
-        1,
-        1 << 24,
+        0,
+        1 << 20,
         4 << 20,
-        scalars=1,
-    )(where, owner_table.reshape(1, -1))
+        scalars=2,
+        scratch=[pltpu.SMEM((n_owner,), jnp.int32)],
+    )(where, owner_table)
     samples, table = lax.optimization_barrier((samples, table))
     x = samples.transpose(0, 2, 1, 3).reshape(samples.shape[0] * 2, CYL * NS)
     x = lax.optimization_barrier(x)
@@ -381,15 +400,26 @@
         pre,
         near[0],
         late[0],
-        more=[jax.ShapeDtypeStruct((kept * UPCH, width), bf16)],
+        more=[jax.ShapeDtypeStruct((kept, UPCH, width), bf16)],
     )
     far_got = spread(far, 1)
     own_got = swap(own)
     out_shape = jax.ShapeDtypeStruct((kept, n_owner * UPCH, width), bf16)
-    arrays = [own_got, *far_got, *near_got, *late_got]
-    return call(functools.partial(gather_kernel, n_owner), out_shape, len(arrays), 0, 3 << 20, scalars=1)(
-        where, *arrays
-    )
+
+    def gather(body, arrays, base=()):
+        return pl.pallas_call(
+            functools.partial(body, n_owner),
+            out_shape=out_shape,
+            in_specs=[SMEM] + [VMEM] * len(arrays) + [ANY] * len(base),
+            out_specs=ANY,
+            scratch_shapes=[pltpu.SemaphoreType.DMA((n_owner,))],
+            input_output_aliases={1 + len(arrays): 0} if base else {},
+            cost_estimate=pl.CostEstimate(flops=0, bytes_accessed=2 << 20, transcendentals=0),
+            compiler_params=pltpu.CompilerParams(vmem_limit_bytes=24 << 20),
+        )(where, *arrays, *base)
+
+    out = gather(early_gather_kernel, [*near_got, *late_got])
+    return gather(last_gather_kernel, [own_got, *far_got], base=[out])
 
 
 def solution(mesh):

time: 65.8 us -> 57.5 us (0.87)
  the two profiles are of different devices: /device:TPU:11 before, /device:TPU:2 now
where the time goes in v10:
time: 57.5 us; the launch traced here: 57.2 us
  starting transfers between devices  30 us (52%)
  Pallas kernels  12.8 us (22%)
  waiting for transfers between devices  11.6 us (20%)
  local copies, waits for them, and re-layouts  2.33 us (4%)
    ppermute x9, starting transfers between devices, spread(): got.append(lax.ppermute(blocks[k], ('freq', 'pol'), route))  25.3 us
    ppermute x9, waiting for transfers between devices, spread(): got.append(lax.ppermute(blocks[k], ('freq', 'pol'), route))  11.6 us
    pallas_call x3, Pallas kernels, form(): call(body, shape + list(more), len(arrays), 4 * 512 * 1024 * 1024, 4 << 2...  5.88 us
    ppermute x4, starting transfers between devices, ahead(): lax.ppermute(part, ('tm', 'pol'), [(i * 2 + source, j * 2 + 1) for i, j i...  3.02 us
    pallas_call x2, Pallas kernels, gather(): pl.pallas_call(functools.partial(body, n_owner), out_shape=out_shape, in_...  2.73 us
    pallas_call x1, Pallas kernels, per_device(): call(functools.partial(late_own_kernel, blocks), jax.ShapeDtypeStruct((ke...  2.66 us
    ppermute x3, starting transfers between devices, swap(): return lax.ppermute(part, 'pol', [(0, 1), (1, 0)])  1.69 us
    pallas_call x1, Pallas kernels, per_device(): call(place_table_kernel, jax.ShapeDtypeStruct((n_owner, beams, width), bf...  1.5 us
  transfers between devices with their start and end apart: 16, of which 4 were waited for; matrix products, arithmetic and copies ran while one was open for 0% of the time, Pallas kernels for 17%

profile of v10, /device:TPU:2, one launch (start us, length us, event | category | flops | bytes accessed | tf_op | source)
XLA Modules:
  0.0 57.2 jit_solution(8815966375102245719)
XLA Ops:
  0.0 0.1 pad_add_fusion.refs_0_.where_ref
  0.1 0.7 %copy-done.5 = s32[64]{0:T(128)S(1)} copy-done((s32[64]{0:T(128)S(1)}, s32[64]{0:T(128)}, u32[]{:S(2)}) %copy-start.5) | copy-done | bytes 280
  0.7 1.5 %shard_map.73.refs_6_.refs_10_.refs_8_ = bf16[4,1024,512]{2,1,0:T(8,128)(2,1)S(1)} custom-call(s32[2]{0:T(128)S(1)} %pad_add_fusion.refs_0_.where_ref, s32[64]{0:T(128)S(1)} %copy-done.5), custom_call_target="tpu_custom_call" | custom-call | flops 1048576 | bytes 4194304 | tf_op jit(solution)/shard_map/pallas_call | solution.py:340
  2.2 0.1 copy-done.6
  2.3 1.1 %copy.9 = bf16[512,2,4,256]{3,2,1,0:T(4,128)(2,1)S(1)} copy(bf16[512,2,4,256]{3,1,2,0:T(2,128)(2,1)S(1)} %bitcast.21) | data formatting | bytes 4194304 | tf_op jit(solution)/shard_map/transpose | solution.py:350
  3.4 0.5 copy.10
  3.9 0.0 copy-start.3
  3.9 0.0 copy-start
  3.9 0.0 copy-start.1
  3.9 0.1 collective-permute-start.5
  4.0 0.1 shard_map.74
  4.1 0.8 %collective-permute-start.3 = (bf16[256,1024]{1,0:T(8,128)(2,1)S(1)}, bf16[256,1024]{1,0:T(8,128)(2,1)S(1)}, u32[]{:S(2)}, u32[]{:S(2)}) collective-permute-start(bf16[256,1024]{1,0:T(8,128)(2,1)S(1)} %get-tuple-element.25), channel_id=1, source_target_pairs={{1,3},{5,7},{9,11},{13,15},{17,19},{21,23},{25,27},{29,31}} | collective-permute-start | bytes 1572872 | tf_op jit(solution)/shard_map/ppermute | solution.py:311
  4.9 0.7 %collective-permute-start.4 = (bf16[256,1024]{1,0:T(8,128)(2,1)S(1)}, bf16[256,1024]{1,0:T(8,128)(2,1)S(1)}, u32[]{:S(2)}, u32[]{:S(2)}) collective-permute-start(bf16[256,1024]{1,0:T(8,128)(2,1)S(1)} %get-tuple-element.25), channel_id=1, source_target_pairs={{0,3},{4,7},{8,11},{12,15},{16,19},{20,23},{24,27},{28,31}} | collective-permute-start | bytes 1572872 | tf_op jit(solution)/shard_map/ppermute | solution.py:311
  5.6 1.6 %collective-permute-start.2 = (f32[4,2,256]{2,1,0:T(2,128)S(1)}, f32[4,2,256]{2,1,0:T(2,128)S(1)}, u32[]{:S(2)}, u32[]{:S(2)}) collective-permute-start(f32[4,2,256]{2,1,0:T(2,128)S(1)} %bitcast.13), channel_id=1, source_target_pairs={{0,1},{1,0},{2,3},{3,2},{4,5},{5,4},{6,7},{7,6},{8,9},{9,8},{10,11... | collective-permute-start | bytes 24584 | tf_op jit(solution)/shard_map/ppermute | solution.py:314
  7.3 0.8 %collective-permute-start = (bf16[224,1024]{1,0:T(8,128)(2,1)S(1)}, bf16[224,1024]{1,0:T(8,128)(2,1)S(1)}, u32[]{:S(2)}, u32[]{:S(2)}) collective-permute-start(bf16[224,1024]{1,0:T(8,128)(2,1)S(1)} %get-tuple-element.23), channel_id=1, source_target_pairs={{1,3},{5,7},{9,11},{13,15},{17,19},{21,23},{25,27},{29,31}} | collective-permute-start | bytes 1376264 | tf_op jit(solution)/shard_map/ppermute | solution.py:311
  8.1 2.7 %shard_map.75.refs_7_ = bf16[256,1024]{1,0:T(8,128)(2,1)S(1)} custom-call(s32[2]{0:T(128)S(1)} %pad_add_fusion.refs_0_.where_ref, bf16[256,768]{1,0:T(8,128)(2,1)S(1)} %copy-done.1, bf16[1024,1024]{1,0:T(8,128)(2,1)S(1)} %bitcast.11, f32[4,2,256]{2,1,0:T(2,128)S(1)} %bitcast.14, bf16[512,512]{1,0:T(8,128)(2,1)S(1)} %copy-done), custom_call_target="tpu_custom_call" | custom-call | flops 2147483648 | bytes 4194304 | tf_op jit(solution)/shard_map/pallas_call | solution.py:367
  10.8 0.0 collective-permute-done.2.refs_3_.refs_7_.refs_5_
  10.8 0.7 %collective-permute-start.1 = (bf16[224,1024]{1,0:T(8,128)(2,1)S(1)}, bf16[224,1024]{1,0:T(8,128)(2,1)S(1)}, u32[]{:S(2)}, u32[]{:S(2)}) collective-permute-start(bf16[224,1024]{1,0:T(8,128)(2,1)S(1)} %get-tuple-element.23), channel_id=1, source_target_pairs={{0,3},{4,7},{8,11},{12,15},{16,19},{20,23},{24,27},{28,31}} | collective-permute-start | bytes 1376264 | tf_op jit(solution)/shard_map/ppermute | solution.py:311
  11.5 0.0 collective-permute-done.5.refs_2_.refs_5_
  11.5 4.1 %shard_map.76 = (bf16[16,16,512]{2,1,0:T(8,128)(2,1)S(1)}, bf16[16,16,512]{2,1,0:T(8,128)(2,1)S(1)}, bf16[16,16,512]{2,1,0:T(8,128)(2,1)S(1)}, bf16[16,16,512]{2,1,0:T(8,128)(2,1)S(1)}) custom-call(s32[2]{0:T(128)S(1)} %pad_add_fusion.refs_0_.where_ref, bf16[256,768]{1,0:T(8,128)(2,1)S(1)} %copy-done.1, ...), custom_call_target="tpu_custom_call" | custom-call | flops 2147483648 | bytes 4194304 | tf_op jit(solution)/shard_map/pallas_call | solution.py:326
  15.6 0.0 collective-permute-done.3.refs_2_
  15.6 0.0 collective-permute-done.4.refs_3_
  15.6 0.0 copy-start.2
  15.6 0.6 shard_map.77
  16.2 1.3 %collective-permute-start.10 = (bf16[8,16,512]{2,1,0:T(8,128)(2,1)S(1)}, bf16[8,16,512]{2,1,0:T(8,128)(2,1)S(1)}, u32[]{:S(2)}, u32[]{:S(2)}) collective-permute-start(bf16[8,16,512]{2,1,0:T(8,128)(2,1)S(1)} %get-tuple-element.33), channel_id=1, source_target_pairs={{1,4},{5,0},{9,12},{13,8},{3,6},{7,2},{11,14},{15,10},{17,20},{21,... | collective-permute-start | bytes 393224 | tf_op jit(solution)/shard_map/ppermute | solution.py:320
  17.5 1.3 %collective-permute-start.11 = (bf16[8,16,512]{2,1,0:T(8,128)(2,1)S(1)}, bf16[8,16,512]{2,1,0:T(8,128)(2,1)S(1)}, u32[]{:S(2)}, u32[]{:S(2)}) collective-permute-start(bf16[8,16,512]{2,1,0:T(8,128)(2,1)S(1)} %get-tuple-element.34), channel_id=1, source_target_pairs={{1,8},{5,12},{9,0},{13,4},{3,10},{7,14},{11,2},{15,6},{17,24},{21,... | collective-permute-start | bytes 393224 | tf_op jit(solution)/shard_map/ppermute | solution.py:320
  18.8 1.3 %collective-permute-start.12 = (bf16[8,16,512]{2,1,0:T(8,128)(2,1)S(1)}, bf16[8,16,512]{2,1,0:T(8,128)(2,1)S(1)}, u32[]{:S(2)}, u32[]{:S(2)}) collective-permute-start(bf16[8,16,512]{2,1,0:T(8,128)(2,1)S(1)} %get-tuple-element.35), channel_id=1, source_target_pairs={{1,12},{5,8},{9,4},{13,0},{3,14},{7,10},{11,6},{15,2},{17,28},{21,... | collective-permute-start | bytes 393224 | tf_op jit(solution)/shard_map/ppermute | solution.py:320
  20.1 0.0 collective-permute-done.refs_2_
  20.1 12.9 %collective-permute-start.13 = (bf16[16,16,512]{2,1,0:T(8,128)(2,1)S(1)}, bf16[16,16,512]{2,1,0:T(8,128)(2,1)S(1)}, u32[]{:S(2)}, u32[]{:S(2)}) collective-permute-start(bf16[16,16,512]{2,1,0:T(8,128)(2,1)S(1)} %get-tuple-element.36), channel_id=1, source_target_pairs={{0,5},{4,1},{8,13},{12,9},{2,7},{6,3},{10,15},{14,11},{16,21},{20,... | collective-permute-start | bytes 786440 | tf_op jit(solution)/shard_map/ppermute | solution.py:320
  33.0 0.0 collective-permute-done.1.refs_3_
  33.0 2.3 %collective-permute-start.14 = (bf16[16,16,512]{2,1,0:T(8,128)(2,1)S(1)}, bf16[16,16,512]{2,1,0:T(8,128)(2,1)S(1)}, u32[]{:S(2)}, u32[]{:S(2)}) collective-permute-start(bf16[16,16,512]{2,1,0:T(8,128)(2,1)S(1)} %get-tuple-element.37), channel_id=1, source_target_pairs={{0,9},{4,13},{8,1},{12,5},{2,11},{6,15},{10,3},{14,7},{16,25},{20,... | collective-permute-start | bytes 786440 | tf_op jit(solution)/shard_map/ppermute | solution.py:320
  35.3 0.0 collective-permute-done.10.refs_0_
  35.3 2.3 %collective-permute-start.15 = (bf16[16,16,512]{2,1,0:T(8,128)(2,1)S(1)}, bf16[16,16,512]{2,1,0:T(8,128)(2,1)S(1)}, u32[]{:S(2)}, u32[]{:S(2)}) collective-permute-start(bf16[16,16,512]{2,1,0:T(8,128)(2,1)S(1)} %get-tuple-element.38), channel_id=1, source_target_pairs={{0,13},{4,9},{8,5},{12,1},{2,15},{6,11},{10,7},{14,3},{16,29},{20,... | collective-permute-start | bytes 786440 | tf_op jit(solution)/shard_map/ppermute | solution.py:320
  37.7 1.2 %shard_map.78 = (bf16[8,16,512]{2,1,0:T(8,128)(2,1)}, bf16[8,16,512]{2,1,0:T(8,128)(2,1)S(1)}, bf16[8,16,512]{2,1,0:T(8,128)(2,1)S(1)}, bf16[8,16,512]{2,1,0:T(8,128)(2,1)S(1)}, bf16[16,16,512]{2,1,0:T(8,128)(2,1)S(1)}) custom-call(s32[2]{0:T(128)S(1)} %pad_add_fusion.refs_0_.where_ref, bf16[256,224]{1,0:T(8,128)(2,1)S(1)} %copy-done.2, ...), custom_call_target="tpu_custom_call" | custom-call | flops 2147483648 | bytes 4194304 | tf_op jit(solution)/shard_map/pallas_call | solution.py:326
  38.9 0.0 collective-permute-done.11.refs_1_
  38.9 0.0 collective-permute-start.6
  38.9 0.0 collective-permute-done.12.refs_2_
  38.9 1.3 %collective-permute-start.7 = (bf16[8,16,512]{2,1,0:T(8,128)(2,1)S(1)}, bf16[8,16,512]{2,1,0:T(8,128)(2,1)S(1)}, u32[]{:S(2)}, u32[]{:S(2)}) collective-permute-start(bf16[8,16,512]{2,1,0:T(8,128)(2,1)S(1)} %get-tuple-element.30), channel_id=1, source_target_pairs={{1,4},{5,0},{9,12},{13,8},{3,6},{7,2},{11,14},{15,10},{17,20},{21,... | collective-permute-start | bytes 393224 | tf_op jit(solution)/shard_map/ppermute | solution.py:320
  40.2 0.0 collective-permute-done.13.refs_3_
  40.2 1.3 %collective-permute-start.8 = (bf16[8,16,512]{2,1,0:T(8,128)(2,1)S(1)}, bf16[8,16,512]{2,1,0:T(8,128)(2,1)S(1)}, u32[]{:S(2)}, u32[]{:S(2)}) collective-permute-start(bf16[8,16,512]{2,1,0:T(8,128)(2,1)S(1)} %get-tuple-element.31), channel_id=1, source_target_pairs={{1,8},{5,12},{9,0},{13,4},{3,10},{7,14},{11,2},{15,6},{17,24},{21,... | collective-permute-start | bytes 393224 | tf_op jit(solution)/shard_map/ppermute | solution.py:320
  41.5 0.0 collective-permute-done.14.refs_4_
  41.5 1.3 %collective-permute-start.9 = (bf16[8,16,512]{2,1,0:T(8,128)(2,1)S(1)}, bf16[8,16,512]{2,1,0:T(8,128)(2,1)S(1)}, u32[]{:S(2)}, u32[]{:S(2)}) collective-permute-start(bf16[8,16,512]{2,1,0:T(8,128)(2,1)S(1)} %get-tuple-element.32), channel_id=1, source_target_pairs={{1,12},{5,8},{9,4},{13,0},{3,14},{7,10},{11,6},{15,2},{17,28},{21,... | collective-permute-start | bytes 393224 | tf_op jit(solution)/shard_map/ppermute | solution.py:320
  42.8 0.3 collective-permute-done.15.refs_5_
  43.2 1.3 %shard_map.79.refs_3_ = bf16[16,64,512]{2,1,0:T(8,128)(2,1)} custom-call(s32[2]{0:T(128)S(1)} %pad_add_fusion.refs_0_.where_ref, bf16[8,16,512]{2,1,0:T(8,128)(2,1)S(1)} %collective-permute-done.10.refs_0_, bf16[8,16,512]{2,1,0:T(8,128)(2,1)S(1)} %collective-permute-done.11.refs_1_, bf16[8,16,512]{2,1,0:T(8,128)(2,1)S(1)} %collective-permute-done.12.refs_2_, ...), custom_call_target="tpu_custom_call" | custom-call | bytes 2097152 | tf_op jit(solution)/shard_map/pallas_call | solution.py:410
  44.5 3.7 %collective-permute-done.7.refs_0_ = bf16[8,16,512]{2,1,0:T(8,128)(2,1)S(1)} collective-permute-done((bf16[8,16,512]{2,1,0:T(8,128)(2,1)S(1)}, bf16[8,16,512]{2,1,0:T(8,128)(2,1)S(1)}, u32[]{:S(2)}, u32[]{:S(2)}) %collective-permute-start.7) | collective-permute-done | bytes 131104 | tf_op jit(solution)/shard_map/ppermute | solution.py:320
  48.2 2.4 %collective-permute-done.8.refs_1_ = bf16[8,16,512]{2,1,0:T(8,128)(2,1)S(1)} collective-permute-done((bf16[8,16,512]{2,1,0:T(8,128)(2,1)S(1)}, bf16[8,16,512]{2,1,0:T(8,128)(2,1)S(1)}, u32[]{:S(2)}, u32[]{:S(2)}) %collective-permute-start.8) | collective-permute-done | bytes 131104 | tf_op jit(solution)/shard_map/ppermute | solution.py:320
  50.6 5.1 %collective-permute-done.9.refs_2_ = bf16[8,16,512]{2,1,0:T(8,128)(2,1)S(1)} collective-permute-done((bf16[8,16,512]{2,1,0:T(8,128)(2,1)S(1)}, bf16[8,16,512]{2,1,0:T(8,128)(2,1)S(1)}, u32[]{:S(2)}, u32[]{:S(2)}) %collective-permute-start.9) | collective-permute-done | bytes 131104 | tf_op jit(solution)/shard_map/ppermute | solution.py:320
  55.7 1.4 %shard_map.80 = bf16[16,64,512]{2,1,0:T(8,128)(2,1)} custom-call(s32[2]{0:T(128)S(1)} %pad_add_fusion.refs_0_.where_ref, bf16[16,16,512]{2,1,0:T(8,128)(2,1)S(1)} %collective-permute-done.6.own_ref, bf16[8,16,512]{2,1,0:T(8,128)(2,1)S(1)} %collective-permute-done.7.refs_0_, ...), custom_call_target="tpu_custom_call", output_to_operand_aliasing={{}: (5, {})} | custom-call | bytes 2097152 | tf_op jit(solution)/shard_map/pallas_call | solution.py:410
  (9 shorter events, 0.0 us)
Async XLA Ops:
  0.1 0.7 %copy-start.5 = (s32[64]{0:T(128)S(1)}, s32[64]{0:T(128)}, u32[]{:S(2)}) copy-start(s32[64]{0:T(128)} %refs_1_.5) | copy-start | bytes 772
  0.7 1.6 %copy-start.6 = (bf16[1,1,512,4,2,256]{5,4,3,2,1,0:T(2,128)(2,1)S(1)}, bf16[1,1,512,4,2,256]{5,4,3,2,1,0:T(2,128)(2,1)}, u32[]{:S(2)}) copy-start(bf16[1,1,512,4,2,256]{5,4,3,2,1,0:T(2,128)(2,1)} %param.7) | copy-start | bytes 6291460
  3.9 1.7 %copy-start.3 = (f32[1,1,4,2,256]{4,3,2,1,0:T(2,128)S(1)}, f32[1,1,4,2,256]{4,3,2,1,0:T(2,128)}, u32[]{:S(2)}) copy-start(f32[1,1,4,2,256]{4,3,2,1,0:T(2,128)} %param.8) | copy-start | bytes 24580
  3.9 4.2 %copy-start = (bf16[512,512]{1,0:T(8,128)(2,1)S(1)}, bf16[512,512]{1,0:T(8,128)(2,1)}, u32[]{:S(2)}) copy-start(bf16[512,512]{1,0:T(8,128)(2,1)} %constant.17.clone.refs_4_.refs_8_.refs_6_) | copy-start | bytes 1572868
  3.9 4.2 %copy-start.1 = (bf16[256,768]{1,0:T(8,128)(2,1)S(1)}, bf16[256,768]{1,0:T(8,128)(2,1)}, u32[]{:S(2)}) copy-start(bf16[256,768]{1,0:T(8,128)(2,1)} %constant.15.clone.refs_1_) | copy-start | bytes 1179652
  3.9 7.5 %collective-permute-start.5 = (bf16[1024,1024]{1,0:T(8,128)(2,1)S(1)}, bf16[1024,1024]{1,0:T(8,128)(2,1)S(1)}, u32[]{:S(2)}, u32[]{:S(2)}) collective-permute-start(bf16[1024,1024]{1,0:T(8,128)(2,1)S(1)} %bitcast.9), channel_id=1, source_target_pairs={{0,1},{1,0},{2,3},{3,2},{4,5},{5,4},{6,7},{7,6},{8,9},{9,8},{10,11... | collective-permute-start | bytes 6291464 | tf_op jit(solution)/shard_map/ppermute | solution.py:314
  4.1 11.5 %collective-permute-start.3 = (bf16[256,1024]{1,0:T(8,128)(2,1)S(1)}, bf16[256,1024]{1,0:T(8,128)(2,1)S(1)}, u32[]{:S(2)}, u32[]{:S(2)}) collective-permute-start(bf16[256,1024]{1,0:T(8,128)(2,1)S(1)} %get-tuple-element.25), channel_id=1, source_target_pairs={{1,3},{5,7},{9,11},{13,15},{17,19},{21,23},{25,27},{29,31}} | collective-permute-start | bytes 1572872 | tf_op jit(solution)/shard_map/ppermute | solution.py:311
  4.9 10.7 %collective-permute-start.4 = (bf16[256,1024]{1,0:T(8,128)(2,1)S(1)}, bf16[256,1024]{1,0:T(8,128)(2,1)S(1)}, u32[]{:S(2)}, u32[]{:S(2)}) collective-permute-start(bf16[256,1024]{1,0:T(8,128)(2,1)S(1)} %get-tuple-element.25), channel_id=1, source_target_pairs={{0,3},{4,7},{8,11},{12,15},{16,19},{20,23},{24,27},{28,31}} | collective-permute-start | bytes 1572872 | tf_op jit(solution)/shard_map/ppermute | solution.py:311
  5.6 5.1 %collective-permute-start.2 = (f32[4,2,256]{2,1,0:T(2,128)S(1)}, f32[4,2,256]{2,1,0:T(2,128)S(1)}, u32[]{:S(2)}, u32[]{:S(2)}) collective-permute-start(f32[4,2,256]{2,1,0:T(2,128)S(1)} %bitcast.13), channel_id=1, source_target_pairs={{0,1},{1,0},{2,3},{3,2},{4,5},{5,4},{6,7},{7,6},{8,9},{9,8},{10,11... | collective-permute-start | bytes 24584 | tf_op jit(solution)/shard_map/ppermute | solution.py:314
  7.3 4.2 %copy-start.4 = (s32[1024]{0:T(1024)S(1)}, s32[1024]{0:T(1024)}, u32[]{:S(2)}) copy-start(s32[1024]{0:T(1024)} %param.10) | copy-start | bytes 12292
  7.3 12.8 %collective-permute-start = (bf16[224,1024]{1,0:T(8,128)(2,1)S(1)}, bf16[224,1024]{1,0:T(8,128)(2,1)S(1)}, u32[]{:S(2)}, u32[]{:S(2)}) collective-permute-start(bf16[224,1024]{1,0:T(8,128)(2,1)S(1)} %get-tuple-element.23), channel_id=1, source_target_pairs={{1,3},{5,7},{9,11},{13,15},{17,19},{21,23},{25,27},{29,31}} | collective-permute-start | bytes 1376264 | tf_op jit(solution)/shard_map/ppermute | solution.py:311
  10.8 22.2 %collective-permute-start.1 = (bf16[224,1024]{1,0:T(8,128)(2,1)S(1)}, bf16[224,1024]{1,0:T(8,128)(2,1)S(1)}, u32[]{:S(2)}, u32[]{:S(2)}) collective-permute-start(bf16[224,1024]{1,0:T(8,128)(2,1)S(1)} %get-tuple-element.23), channel_id=1, source_target_pairs={{0,3},{4,7},{8,11},{12,15},{16,19},{20,23},{24,27},{28,31}} | collective-permute-start | bytes 1376264 | tf_op jit(solution)/shard_map/ppermute | solution.py:311
  15.6 22.0 %copy-start.2 = (bf16[256,224]{1,0:T(8,128)(2,1)S(1)}, bf16[256,224]{1,0:T(8,128)(2,1)}, u32[]{:S(2)}) copy-start(bf16[256,224]{1,0:T(8,128)(2,1)} %constant.16.clone.refs_1_) | copy-start | bytes 344068
  16.2 19.1 %collective-permute-start.10 = (bf16[8,16,512]{2,1,0:T(8,128)(2,1)S(1)}, bf16[8,16,512]{2,1,0:T(8,128)(2,1)S(1)}, u32[]{:S(2)}, u32[]{:S(2)}) collective-permute-start(bf16[8,16,512]{2,1,0:T(8,128)(2,1)S(1)} %get-tuple-element.33), channel_id=1, source_target_pairs={{1,4},{5,0},{9,12},{13,8},{3,6},{7,2},{11,14},{15,10},{17,20},{21,... | collective-permute-start | bytes 393224 | tf_op jit(solution)/shard_map/ppermute | solution.py:320
  17.5 21.4 %collective-permute-start.11 = (bf16[8,16,512]{2,1,0:T(8,128)(2,1)S(1)}, bf16[8,16,512]{2,1,0:T(8,128)(2,1)S(1)}, u32[]{:S(2)}, u32[]{:S(2)}) collective-permute-start(bf16[8,16,512]{2,1,0:T(8,128)(2,1)S(1)} %get-tuple-element.34), channel_id=1, source_target_pairs={{1,8},{5,12},{9,0},{13,4},{3,10},{7,14},{11,2},{15,6},{17,24},{21,... | collective-permute-start | bytes 393224 | tf_op jit(solution)/shard_map/ppermute | solution.py:320
  18.8 20.1 %collective-permute-start.12 = (bf16[8,16,512]{2,1,0:T(8,128)(2,1)S(1)}, bf16[8,16,512]{2,1,0:T(8,128)(2,1)S(1)}, u32[]{:S(2)}, u32[]{:S(2)}) collective-permute-start(bf16[8,16,512]{2,1,0:T(8,128)(2,1)S(1)} %get-tuple-element.35), channel_id=1, source_target_pairs={{1,12},{5,8},{9,4},{13,0},{3,14},{7,10},{11,6},{15,2},{17,28},{21,... | collective-permute-start | bytes 393224 | tf_op jit(solution)/shard_map/ppermute | solution.py:320
  20.1 20.1 %collective-permute-start.13 = (bf16[16,16,512]{2,1,0:T(8,128)(2,1)S(1)}, bf16[16,16,512]{2,1,0:T(8,128)(2,1)S(1)}, u32[]{:S(2)}, u32[]{:S(2)}) collective-permute-start(bf16[16,16,512]{2,1,0:T(8,128)(2,1)S(1)} %get-tuple-element.36), channel_id=1, source_target_pairs={{0,5},{4,1},{8,13},{12,9},{2,7},{6,3},{10,15},{14,11},{16,21},{20,... | collective-permute-start | bytes 786440 | tf_op jit(solution)/shard_map/ppermute | solution.py:320
  33.0 8.5 %collective-permute-start.14 = (bf16[16,16,512]{2,1,0:T(8,128)(2,1)S(1)}, bf16[16,16,512]{2,1,0:T(8,128)(2,1)S(1)}, u32[]{:S(2)}, u32[]{:S(2)}) collective-permute-start(bf16[16,16,512]{2,1,0:T(8,128)(2,1)S(1)} %get-tuple-element.37), channel_id=1, source_target_pairs={{0,9},{4,13},{8,1},{12,5},{2,11},{6,15},{10,3},{14,7},{16,25},{20,... | collective-permute-start | bytes 786440 | tf_op jit(solution)/shard_map/ppermute | solution.py:320
  35.3 7.8 %collective-permute-start.15 = (bf16[16,16,512]{2,1,0:T(8,128)(2,1)S(1)}, bf16[16,16,512]{2,1,0:T(8,128)(2,1)S(1)}, u32[]{:S(2)}, u32[]{:S(2)}) collective-permute-start(bf16[16,16,512]{2,1,0:T(8,128)(2,1)S(1)} %get-tuple-element.38), channel_id=1, source_target_pairs={{0,13},{4,9},{8,5},{12,1},{2,15},{6,11},{10,7},{14,3},{16,29},{20,... | collective-permute-start | bytes 786440 | tf_op jit(solution)/shard_map/ppermute | solution.py:320
  38.9 16.9 %collective-permute-start.6 = (bf16[16,16,512]{2,1,0:T(8,128)(2,1)S(1)}, bf16[16,16,512]{2,1,0:T(8,128)(2,1)S(1)}, u32[]{:S(2)}, u32[]{:S(2)}) collective-permute-start(bf16[16,16,512]{2,1,0:T(8,128)(2,1)S(1)} %get-tuple-element.29), channel_id=1, source_target_pairs={{0,1},{1,0},{2,3},{3,2},{4,5},{5,4},{6,7},{7,6},{8,9},{9,8},{10,11... | collective-permute-start | bytes 786440 | tf_op jit(solution)/shard_map/ppermute | solution.py:314
  38.9 9.3 %collective-permute-start.7 = (bf16[8,16,512]{2,1,0:T(8,128)(2,1)S(1)}, bf16[8,16,512]{2,1,0:T(8,128)(2,1)S(1)}, u32[]{:S(2)}, u32[]{:S(2)}) collective-permute-start(bf16[8,16,512]{2,1,0:T(8,128)(2,1)S(1)} %get-tuple-element.30), channel_id=1, source_target_pairs={{1,4},{5,0},{9,12},{13,8},{3,6},{7,2},{11,14},{15,10},{17,20},{21,... | collective-permute-start | bytes 393224 | tf_op jit(solution)/shard_map/ppermute | solution.py:320
  40.2 10.4 %collective-permute-start.8 = (bf16[8,16,512]{2,1,0:T(8,128)(2,1)S(1)}, bf16[8,16,512]{2,1,0:T(8,128)(2,1)S(1)}, u32[]{:S(2)}, u32[]{:S(2)}) collective-permute-start(bf16[8,16,512]{2,1,0:T(8,128)(2,1)S(1)} %get-tuple-element.31), channel_id=1, source_target_pairs={{1,8},{5,12},{9,0},{13,4},{3,10},{7,14},{11,2},{15,6},{17,24},{21,... | collective-permute-start | bytes 393224 | tf_op jit(solution)/shard_map/ppermute | solution.py:320
  41.5 14.2 %collective-permute-start.9 = (bf16[8,16,512]{2,1,0:T(8,128)(2,1)S(1)}, bf16[8,16,512]{2,1,0:T(8,128)(2,1)S(1)}, u32[]{:S(2)}, u32[]{:S(2)}) collective-permute-start(bf16[8,16,512]{2,1,0:T(8,128)(2,1)S(1)} %get-tuple-element.32), channel_id=1, source_target_pairs={{1,12},{5,8},{9,4},{13,0},{3,14},{7,10},{11,6},{15,2},{17,28},{21,... | collective-permute-start | bytes 393224 | tf_op jit(solution)/shard_map/ppermute | solution.py:320

commit v11 on v10

--- a/solution.py
+++ b/solution.py
@@ -115,16 +115,30 @@
     return emit
 
 
-def place(sum_ref, table_ref, out_refs):
-    for k, out_ref in enumerate(out_refs):
-        placed = jnp.dot(sum_ref[...], table_ref[k], preferred_element_type=jnp.float32)
-        out_ref[...] = placed.astype(jnp.bfloat16).reshape(out_ref.shape)
-
-
-def halo_rows_kernel(x_ref, near_ref, far_ref):
-    near_at = x_ref.shape[0] - near_ref.shape[0]
-    near_ref[...] = x_ref[near_at:, :]
-    far_ref[...] = x_ref[near_at - far_ref.shape[0] : near_at, :]
+def place(sum_ref, table, out_ref):
+    placed = jnp.dot(sum_ref[...], table, preferred_element_type=jnp.float32)
+    out_ref[...] = placed.astype(jnp.bfloat16).reshape(out_ref.shape)
+
+
+def place_kernel(pol, where_ref, sum_ref, table_ref, *out_refs):
+    @pl.when(where_ref[1] == pol)
+    def _():
+        for k, out_ref in enumerate(out_refs):
+            place(sum_ref, table_ref[k], out_ref)
+
+
+def near_rows_kernel(x_ref, out_ref):
+    out_ref[...] = x_ref[x_ref.shape[0] - out_ref.shape[0] :, :]
+
+
+def far_rows_kernel(reach, where_ref, x_ref, other_ref, out_ref):
+    count = out_ref.shape[0] // 2
+    at = x_ref.shape[0] - reach - count
+
+    @pl.when(where_ref[1] == 1)
+    def _():
+        out_ref[:count, :] = x_ref[at : at + count, :]
+        out_ref[count:, :] = other_ref[at : at + count, :]
 
 
 def each_late_block(blocks, filt_ref, x_ref, gain_ref, beam_ref, cal_ref, emitter):
@@ -149,21 +163,20 @@
 
 
 def late_kernel(
-    blocks, where_ref, filt_ref, x_ref, gain_ref, beam_ref, keep_ref, table_ref, power_ref, *refs
+    blocks, where_ref, filt_ref, x_ref, gain_ref, beam_ref, keep_ref, table_ref, power_ref, sum_ref, out_ref, cal_ref
 ):
-    out_refs, (cal_ref, sum_ref) = refs[:-2], refs[-2:]
-
     @pl.when(where_ref[1] == 0)
     def _():
         def emitter(at):
             return adder(power_ref, keep_ref, sum_ref, at)
 
         each_late_block(blocks, filt_ref, x_ref, gain_ref, beam_ref, cal_ref, emitter)
-        place(sum_ref, table_ref, out_refs)
-
-
-def near_kernel(n_owner, where_ref, filt_ref, n0, n1, x0, x1, g0, g1, beam_ref, keep_ref, table_ref, *refs):
-    out_refs, pre_ref, (cal_ref, sum_ref) = refs[:n_owner], refs[n_owner], refs[n_owner + 1 :]
+        place(sum_ref, table_ref[table_ref.shape[0] - 1], out_ref)
+
+
+def near_kernel(
+    where_ref, filt_ref, n0, n1, x0, x1, g0, g1, beam_ref, keep_ref, table_ref, sum_ref, out_ref, pre_ref, cal_ref
+):
     reach = BLOCK * ROWS
 
     @pl.when(where_ref[1] == 1)
@@ -179,29 +192,38 @@
 
             emit = adder(sum_ref, keep_ref, sum_ref) if pol else keeper(sum_ref)
             form_powers(spectra, gain, beam_ref, cal_ref, emit)
-        place(sum_ref, table_ref, out_refs)
-
-
-def far_kernel(n_owner, where_ref, edge_ref, f0, f1, g0, g1, beam_ref, keep_ref, table_ref, pre_ref, *refs):
-    own_refs, out_refs, own_ref, (cal_ref, sum_ref) = refs[:2], refs[2 : 2 + n_owner], refs[2 + n_owner], refs[-2:]
-    half = BLOCK
-
-    @pl.when(where_ref[1] == 1)
-    def _():
-        for pol, (f, gain) in enumerate(((f0, g0), (f1, g1))):
-
-            def spectra(cyl, pol=pol, f=f):
-                return pre_ref[pol * CYL + cyl] + filtered([(edge_ref[...], f[:, columns(cyl)])])
+        place(sum_ref, table_ref[table_ref.shape[0] - 1], out_ref)
+
+
+def far_kernel(
+    where_ref, edge_ref, far_ref, g0, g1, beam_ref, keep_ref, table_ref, pre_ref, sum_ref, out_ref, cal_ref
+):
+    count = far_ref.shape[0] // 2
+
+    @pl.when(where_ref[1] == 1)
+    def _():
+        for pol, gain in enumerate((g0, g1)):
+
+            def spectra(cyl, pol=pol):
+                rows = far_ref[pol * count : (pol + 1) * count, columns(cyl)]
+                return pre_ref[pol * CYL + cyl] + filtered([(edge_ref[...], rows)])
 
             emit = adder(sum_ref, keep_ref, sum_ref) if pol else keeper(sum_ref)
             form_powers(spectra, gain, beam_ref, cal_ref, emit)
-        place(sum_ref, table_ref, out_refs)
-        own_ref[:half] = out_refs[0][...]
-        own_ref[half:] = own_refs[0][...]
+        place(sum_ref, table_ref[table_ref.shape[0] - 1], out_ref)
+
+
+def far_place_kernel(where_ref, sum_ref, table_ref, near_ref, late_ref, own_ref, *out_refs):
+    @pl.when(where_ref[1] == 1)
+    def _():
+        for k, out_ref in enumerate(out_refs, 1):
+            place(sum_ref, table_ref[k], out_ref)
+        place(sum_ref, table_ref[0], own_ref.at[:BLOCK])
+        own_ref[BLOCK:] = near_ref[...]
 
     @pl.when(where_ref[1] == 0)
     def _():
-        own_ref[...] = own_refs[1][...]
+        own_ref[...] = late_ref[...]
 
 
 def place_table_kernel(where_ref, owner_ref, out_ref, rank_ref):
@@ -320,50 +342,28 @@
             got.append(lax.ppermute(blocks[k], ("freq", "pol"), route))
         return got
 
-    def form(body, rows, *arrays, after=(), more=()):
-        shape = [jax.ShapeDtypeStruct((rows // UPCH, UPCH, width), bf16)] * n_owner
-        scratch = [pltpu.VMEM((CYL * BLOCK * UPCH, 2 * NS), bf16), pltpu.VMEM((rows, beams), bf16)]
+    def form(body, frames, *arrays, more=()):
+        shape = [jax.ShapeDtypeStruct((frames * UPCH, beams), bf16), jax.ShapeDtypeStruct((frames, UPCH, width), bf16)]
+        scratch = [pltpu.VMEM((CYL * BLOCK * UPCH, 2 * NS), bf16)]
         return call(
-            body,
-            shape + list(more),
-            len(arrays),
-            4 * 512 * 1024 * 1024,
-            4 << 20,
-            scalars=1,
-            after=len(after),
-            scratch=scratch,
-        )(where, *arrays, *after)
+            body, shape + list(more), len(arrays), 4 * 512 * 1024 * 1024, 4 << 20, scalars=1, scratch=scratch
+        )(where, *arrays)
+
+    def rest(body, frames, *arrays, more=(), count=n_owner - 1):
+        shape = [jax.ShapeDtypeStruct((frames, UPCH, width), bf16)] * count
+        return call(body, list(more) + shape, len(arrays), 1 << 29, 4 << 20, scalars=1)(where, *arrays)
 
     where = jnp.stack([me, pol]).astype(jnp.int32)
     keep = keep_flags.reshape(1, -1)
     reach, edge_rows = BLOCK * ROWS, (TAPS - 1 - BLOCK) * ROWS
-    table = call(
-        place_table_kernel,
-        jax.ShapeDtypeStruct((n_owner, beams, width), bf16),
-        0,
-        1 << 20,
-        4 << 20,
-        scalars=2,
-        scratch=[pltpu.SMEM((n_owner,), jnp.int32)],
-    )(where, owner_table)
-    samples, table = lax.optimization_barrier((samples, table))
+    blocks = kept // BLOCK
     x = samples.transpose(0, 2, 1, 3).reshape(samples.shape[0] * 2, CYL * NS)
     x = lax.optimization_barrier(x)
-    near_rows, far_rows = call(
-        halo_rows_kernel,
-        [jax.ShapeDtypeStruct((rows, CYL * NS), bf16) for rows in (reach, edge_rows)],
-        1,
-        0,
-        2 << 20,
-    )(x)
+    near_rows = call(near_rows_kernel, jax.ShapeDtypeStruct((reach, CYL * NS), bf16), 1, 0, 1 << 20)(x)
     near0 = ahead(near_rows, 0)
     near1 = ahead(near_rows, 1)
     other = swap(x)
     gain_other = swap(gain)
-    far0 = ahead(far_rows, 0)
-    far1 = ahead(far_rows, 1)
-    common = (gain, gain_other, beam_table, keep, table)
-    blocks = kept // BLOCK
     late_own = call(
         functools.partial(late_own_kernel, blocks),
         jax.ShapeDtypeStruct((kept * UPCH, beams), bf16),
@@ -373,35 +373,56 @@
         scalars=1,
         scratch=[pltpu.VMEM((CYL * BLOCK * UPCH, 2 * NS), bf16)],
     )(where, filt, x, gain, beam_table)
-    body = functools.partial(late_kernel, blocks)
-    rows = kept * UPCH
-    late = form(body, rows, filt, other, gain_other, beam_table, keep, table, late_own)
+    table = call(
+        place_table_kernel,
+        jax.ShapeDtypeStruct((n_owner, beams, width), bf16),
+        0,
+        1 << 20,
+        4 << 20,
+        scalars=2,
+        after=1,
+        scratch=[pltpu.SMEM((n_owner,), jnp.int32)],
+    )(where, owner_table, late_own)
+    late_sum, late_last = form(
+        functools.partial(late_kernel, blocks), kept, filt, other, gain_other, beam_table, keep, table, late_own
+    )
+    far_rows = call(
+        functools.partial(far_rows_kernel, reach),
+        jax.ShapeDtypeStruct((2 * edge_rows, CYL * NS), bf16),
+        2,
+        0,
+        2 << 20,
+        scalars=1,
+    )(where, x, other)
+    far_halo = ahead(far_rows, 1)
+    late = [*rest(functools.partial(place_kernel, 0), kept, late_sum, table), late_last]
     late_got = spread(late, 0)
-    *near, pre = form(
-        functools.partial(near_kernel, n_owner),
-        BLOCK * UPCH,
+    common = (gain, gain_other, beam_table, keep, table)
+    near_sum, near_last, pre = form(
+        near_kernel,
+        BLOCK,
         filt,
         near1,
         near0,
         x,
         other,
         *common,
-        after=late[:1],
         more=[jax.ShapeDtypeStruct((2 * CYL, reach, NS), jnp.float32)],
     )
+    near = [*rest(functools.partial(place_kernel, 1), BLOCK, near_sum, table), near_last]
     near_got = spread(near, 1)
-    *far, own = form(
-        functools.partial(far_kernel, n_owner),
-        BLOCK * UPCH,
-        edge,
-        far1,
-        far0,
-        *common,
-        pre,
+    far_sum, far_last = form(far_kernel, BLOCK, edge, far_halo, *common, pre)
+    own, *far = rest(
+        far_place_kernel,
+        BLOCK,
+        far_sum,
+        table,
         near[0],
         late[0],
         more=[jax.ShapeDtypeStruct((kept, UPCH, width), bf16)],
+        count=n_owner - 2,
     )
+    far = [own, *far, far_last]
     far_got = spread(far, 1)
     own_got = swap(own)
     out_shape = jax.ShapeDtypeStruct((kept, n_owner * UPCH, width), bf16)

time: 57.5 us -> 71.1 us (1.24)
  the two profiles are of different devices: /device:TPU:2 before, /device:TPU:0 now
where the time goes in v11:
time: 71.1 us; the launch traced here: 70.6 us
  starting transfers between devices  35 us (49%)
  Pallas kernels  17.6 us (25%)
  waiting for transfers between devices  14.4 us (20%)
  local copies, waits for them, and re-layouts  3.2 us (5%)
    ppermute x9, starting transfers between devices, spread(): got.append(lax.ppermute(blocks[k], ('freq', 'pol'), route))  25.2 us
    ppermute x9, waiting for transfers between devices, spread(): got.append(lax.ppermute(blocks[k], ('freq', 'pol'), route))  10.5 us
    ppermute x3, starting transfers between devices, ahead(): lax.ppermute(part, ('tm', 'pol'), [(i * 2 + source, j * 2 + 1) for i, j i...  7.3 us
    pallas_call x3, Pallas kernels, form(): call(body, shape + list(more), len(arrays), 4 * 512 * 1024 * 1024, 4 << 2...  6.47 us
    ppermute x3, waiting for transfers between devices, swap(): return lax.ppermute(part, 'pol', [(0, 1), (1, 0)])  3.85 us
    pallas_call x2, Pallas kernels, gather(): pl.pallas_call(functools.partial(body, n_owner), out_shape=out_shape, in_...  2.73 us
    transpose x1, local copies, waits for them, and re-layouts, per_device(): x = samples.transpose(0, 2, 1, 3).reshape(samples.shape[0] * 2, CYL * NS)  2.67 us
    pallas_call x1, Pallas kernels, per_device(): call(functools.partial(late_own_kernel, blocks), jax.ShapeDtypeStruct((ke...  2.64 us
  transfers between devices with their start and end apart: 15, of which 4 were waited for; matrix products, arithmetic and copies ran while one was open for 0% of the time, Pallas kernels for 21%

profile of v11, /device:TPU:0, one launch (start us, length us, event | category | flops | bytes accessed | tf_op | source)
XLA Modules:
  0.0 70.6 jit_solution(403437587526329255)
XLA Ops:
  0.0 2.7 %copy.9 = bf16[512,2,4,256]{3,2,1,0:T(4,128)(2,1)S(1)} copy(bf16[512,2,4,256]{3,1,2,0:T(2,128)(2,1)} %bitcast.23) | data formatting | bytes 4194304 | tf_op jit(solution)/shard_map/transpose | solution.py:360
  2.7 0.5 copy.10
  3.2 0.6 collective-permute-start
  3.7 0.1 pad_add_fusion.refs_0_.where_ref
  3.8 3.8 %collective-permute-done.refs_2_.refs_5_ = bf16[1024,1024]{1,0:T(8,128)(2,1)} collective-permute-done((bf16[1024,1024]{1,0:T(8,128)(2,1)S(1)}, bf16[1024,1024]{1,0:T(8,128)(2,1)}, u32[]{:S(2)}, u32[]{:S(2)}) %collective-permute-start) | collective-permute-done | bytes 2097184 | tf_op jit(solution)/shard_map/ppermute | solution.py:336
  7.6 1.6 %shard_map.73 = bf16[448,1024]{1,0:T(8,128)(2,1)S(1)} custom-call(s32[2]{0:T(128)S(1)} %pad_add_fusion.refs_0_.where_ref, bf16[1024,1024]{1,0:T(8,128)(2,1)S(1)} %bitcast.11, bf16[1024,1024]{1,0:T(8,128)(2,1)} %collective-permute-done.refs_2_.refs_5_), custom_call_target="tpu_custom_call" | custom-call | bytes 2097152 | tf_op jit(solution)/shard_map/pallas_call | solution.py:389
  9.3 0.0 copy-start.2
  9.3 0.0 copy-start
  9.3 0.0 copy-start.1
  9.3 0.9 %collective-permute-start.1 = (bf16[448,1024]{1,0:T(8,128)(2,1)S(1)}, bf16[448,1024]{1,0:T(8,128)(2,1)S(1)}, u32[]{:S(2)}, u32[]{:S(2)}) collective-permute-start(bf16[448,1024]{1,0:T(8,128)(2,1)S(1)} %shard_map.73), channel_id=1, source_target_pairs={{1,3},{5,7},{9,11},{13,15},{17,19},{21,23},{25,27},{29,31}} | collective-permute-start | bytes 2752520 | tf_op jit(solution)/shard_map/ppermute | solution.py:333
  10.2 0.7 collective-permute-start.3
  10.9 5.8 %collective-permute-start.4 = (bf16[256,1024]{1,0:T(8,128)(2,1)S(1)}, bf16[256,1024]{1,0:T(8,128)(2,1)S(1)}, u32[]{:S(2)}, u32[]{:S(2)}) collective-permute-start(bf16[256,1024]{1,0:T(8,128)(2,1)S(1)} %shard_map.76), channel_id=1, source_target_pairs={{0,3},{4,7},{8,11},{12,15},{16,19},{20,23},{24,27},{28,31}} | collective-permute-start | bytes 1572872 | tf_op jit(solution)/shard_map/ppermute | solution.py:333
  16.7 0.0 copy-start.4
  16.7 0.1 collective-permute-start.2
  16.8 2.6 %shard_map.74.refs_2_.refs_7_ = bf16[256,1024]{1,0:T(8,128)(2,1)S(1)} custom-call(s32[2]{0:T(128)S(1)} %pad_add_fusion.refs_0_.where_ref, bf16[256,768]{1,0:T(8,128)(2,1)S(1)} %copy-done.1, bf16[1024,1024]{1,0:T(8,128)(2,1)S(1)} %bitcast.13, f32[4,2,256]{2,1,0:T(2,128)S(1)} %bitcast.16, bf16[512,512]{1,0:T(8,128)(2,1)S(1)} %copy-done), custom_call_target="tpu_custom_call" | custom-call | flops 2147483648 | bytes 4194304 | tf_op jit(solution)/shard_map/pallas_call | solution.py:367
  19.4 0.0 copy-start.3
  19.5 1.5 %shard_map.75.refs_10_.refs_7_.refs_2_.refs_6_ = bf16[4,1024,512]{2,1,0:T(8,128)(2,1)S(1)} custom-call(s32[2]{0:T(128)S(1)} %pad_add_fusion.refs_0_.where_ref, s32[64]{0:T(128)S(1)} %copy-done.4, bf16[256,1024]{1,0:T(8,128)(2,1)S(1)} %shard_map.74.refs_2_.refs_7_), custom_call_target="tpu_custom_call" | custom-call | flops 1048576 | bytes 4194304 | tf_op jit(solution)/shard_map/pallas_call | solution.py:376
  21.0 0.0 collective-permute-done.2.refs_7_.refs_4_.refs_3_
  21.0 4.3 %shard_map.80 = (bf16[256,1024]{1,0:T(8,128)(2,1)S(1)}, bf16[16,16,512]{2,1,0:T(8,128)(2,1)S(1)}) custom-call(s32[2]{0:T(128)S(1)} %pad_add_fusion.refs_0_.where_ref, bf16[256,768]{1,0:T(8,128)(2,1)S(1)} %copy-done.1, bf16[1024,1024]{1,0:T(8,128)(2,1)} %collective-permute-done.refs_2_.refs_5_, ...), custom_call_target="tpu_custom_call" | custom-call | flops 2147483648 | bytes 4194304 | tf_op jit(solution)/shard_map/pallas_call | solution.py:348
  25.3 1.5 %shard_map.81 = (bf16[16,16,512]{2,1,0:T(8,128)(2,1)S(1)}, bf16[16,16,512]{2,1,0:T(8,128)(2,1)S(1)}, bf16[16,16,512]{2,1,0:T(8,128)(2,1)S(1)}) custom-call(s32[2]{0:T(128)S(1)} %pad_add_fusion.refs_0_.where_ref, bf16[256,1024]{1,0:T(8,128)(2,1)S(1)} %get-tuple-element.25.refs_1_, bf16[4,1024,512]{2,1,0:T(8,128)(2,1)S(1)} %shard_map.75.refs_10_.refs_7_.refs_2_.refs_6_), custom_call_target="tpu_custom_call" | custom-call | flops 536870912 | bytes 4194304 | tf_op jit(solution)/shard_map/pallas_call | solution.py:354
  26.8 1.3 %collective-permute-start.12 = (bf16[16,16,512]{2,1,0:T(8,128)(2,1)S(1)}, bf16[16,16,512]{2,1,0:T(8,128)(2,1)S(1)}, u32[]{:S(2)}, u32[]{:S(2)}) collective-permute-start(bf16[16,16,512]{2,1,0:T(8,128)(2,1)S(1)} %get-tuple-element.34), channel_id=1, source_target_pairs={{0,5},{4,1},{8,13},{12,9},{2,7},{6,3},{10,15},{14,11},{16,21},{20,... | collective-permute-start | bytes 786440 | tf_op jit(solution)/shard_map/ppermute | solution.py:342
  28.1 1.3 %collective-permute-start.13 = (bf16[16,16,512]{2,1,0:T(8,128)(2,1)S(1)}, bf16[16,16,512]{2,1,0:T(8,128)(2,1)S(1)}, u32[]{:S(2)}, u32[]{:S(2)}) collective-permute-start(bf16[16,16,512]{2,1,0:T(8,128)(2,1)S(1)} %get-tuple-element.35), channel_id=1, source_target_pairs={{0,9},{4,13},{8,1},{12,5},{2,11},{6,15},{10,3},{14,7},{16,25},{20,... | collective-permute-start | bytes 786440 | tf_op jit(solution)/shard_map/ppermute | solution.py:342
  29.5 0.0 collective-permute-done.3.refs_2_
  29.5 0.0 collective-permute-done.4.refs_3_
  29.5 1.6 %shard_map.77 = (bf16[128,1024]{1,0:T(8,128)(2,1)S(1)}, bf16[8,16,512]{2,1,0:T(8,128)(2,1)S(1)}, f32[8,256,256]{2,1,0:T(8,128)S(1)}) custom-call(s32[2]{0:T(128)S(1)} %pad_add_fusion.refs_0_.where_ref, bf16[256,768]{1,0:T(8,128)(2,1)S(1)} %copy-done.1, bf16[256,1024]{1,0:T(8,128)(2,1)S(1)} %collective-permute-done.3.refs_2_, ...), custom_call_target="tpu_custom_call" | custom-call | flops 2147483648 | bytes 4194304 | tf_op jit(solution)/shard_map/pallas_call | solution.py:348
  31.1 0.0 copy-start.5
  31.1 0.6 shard_map.79
  31.7 1.3 %collective-permute-start.10 = (bf16[8,16,512]{2,1,0:T(8,128)(2,1)S(1)}, bf16[8,16,512]{2,1,0:T(8,128)(2,1)S(1)}, u32[]{:S(2)}, u32[]{:S(2)}) collective-permute-start(bf16[8,16,512]{2,1,0:T(8,128)(2,1)S(1)} %get-tuple-element.32), channel_id=1, source_target_pairs={{1,8},{5,12},{9,0},{13,4},{3,10},{7,14},{11,2},{15,6},{17,24},{21,... | collective-permute-start | bytes 393224 | tf_op jit(solution)/shard_map/ppermute | solution.py:342
  33.0 1.3 %collective-permute-start.9 = (bf16[8,16,512]{2,1,0:T(8,128)(2,1)S(1)}, bf16[8,16,512]{2,1,0:T(8,128)(2,1)S(1)}, u32[]{:S(2)}, u32[]{:S(2)}) collective-permute-start(bf16[8,16,512]{2,1,0:T(8,128)(2,1)S(1)} %get-tuple-element.31), channel_id=1, source_target_pairs={{1,4},{5,0},{9,12},{13,8},{3,6},{7,2},{11,14},{15,10},{17,20},{21,... | collective-permute-start | bytes 393224 | tf_op jit(solution)/shard_map/ppermute | solution.py:342
  34.3 0.0 collective-permute-done.1.refs_2_
  34.3 14.9 %collective-permute-start.14 = (bf16[16,16,512]{2,1,0:T(8,128)(2,1)S(1)}, bf16[16,16,512]{2,1,0:T(8,128)(2,1)S(1)}, u32[]{:S(2)}, u32[]{:S(2)}) collective-permute-start(bf16[16,16,512]{2,1,0:T(8,128)(2,1)S(1)} %get-tuple-element.36), channel_id=1, source_target_pairs={{0,13},{4,9},{8,5},{12,1},{2,15},{6,11},{10,7},{14,3},{16,29},{20,... | collective-permute-start | bytes 786440 | tf_op jit(solution)/shard_map/ppermute | solution.py:342
  49.2 0.6 shard_map.78
  49.7 0.0 collective-permute-done.10.refs_1_
  49.7 1.3 %collective-permute-start.11 = (bf16[8,16,512]{2,1,0:T(8,128)(2,1)S(1)}, bf16[8,16,512]{2,1,0:T(8,128)(2,1)S(1)}, u32[]{:S(2)}, u32[]{:S(2)}) collective-permute-start(bf16[8,16,512]{2,1,0:T(8,128)(2,1)S(1)} %get-tuple-element.33), channel_id=1, source_target_pairs={{1,12},{5,8},{9,4},{13,0},{3,14},{7,10},{11,6},{15,2},{17,28},{21,... | collective-permute-start | bytes 393224 | tf_op jit(solution)/shard_map/ppermute | solution.py:342
  51.0 0.6 shard_map.82
  51.6 0.0 collective-permute-done.9.refs_0_
  51.6 1.9 %collective-permute-start.5 = (bf16[16,16,512]{2,1,0:T(8,128)(2,1)S(1)}, bf16[16,16,512]{2,1,0:T(8,128)(2,1)S(1)}, u32[]{:S(2)}, u32[]{:S(2)}) collective-permute-start(bf16[16,16,512]{2,1,0:T(8,128)(2,1)S(1)} %get-tuple-element.27), channel_id=1, source_target_pairs={{0,1},{1,0},{2,3},{3,2},{4,5},{5,4},{6,7},{7,6},{8,9},{9,8},{10,11... | collective-permute-start | bytes 786440 | tf_op jit(solution)/shard_map/ppermute | solution.py:336
  53.5 4.4 %collective-permute-done.11.refs_2_ = bf16[8,16,512]{2,1,0:T(8,128)(2,1)S(1)} collective-permute-done((bf16[8,16,512]{2,1,0:T(8,128)(2,1)S(1)}, bf16[8,16,512]{2,1,0:T(8,128)(2,1)S(1)}, u32[]{:S(2)}, u32[]{:S(2)}) %collective-permute-start.11) | collective-permute-done | bytes 131104 | tf_op jit(solution)/shard_map/ppermute | solution.py:342
  57.9 1.3 %collective-permute-start.6 = (bf16[8,16,512]{2,1,0:T(8,128)(2,1)S(1)}, bf16[8,16,512]{2,1,0:T(8,128)(2,1)S(1)}, u32[]{:S(2)}, u32[]{:S(2)}) collective-permute-start(bf16[8,16,512]{2,1,0:T(8,128)(2,1)S(1)} %get-tuple-element.28), channel_id=1, source_target_pairs={{1,4},{5,0},{9,12},{13,8},{3,6},{7,2},{11,14},{15,10},{17,20},{21,... | collective-permute-start | bytes 393224 | tf_op jit(solution)/shard_map/ppermute | solution.py:342
  59.2 1.3 %collective-permute-start.7 = (bf16[8,16,512]{2,1,0:T(8,128)(2,1)S(1)}, bf16[8,16,512]{2,1,0:T(8,128)(2,1)S(1)}, u32[]{:S(2)}, u32[]{:S(2)}) collective-permute-start(bf16[8,16,512]{2,1,0:T(8,128)(2,1)S(1)} %get-tuple-element.29), channel_id=1, source_target_pairs={{1,8},{5,12},{9,0},{13,4},{3,10},{7,14},{11,2},{15,6},{17,24},{21,... | collective-permute-start | bytes 393224 | tf_op jit(solution)/shard_map/ppermute | solution.py:342
  60.5 0.0 collective-permute-done.13.refs_4_
  60.5 1.3 %collective-permute-start.8 = (bf16[8,16,512]{2,1,0:T(8,128)(2,1)S(1)}, bf16[8,16,512]{2,1,0:T(8,128)(2,1)S(1)}, u32[]{:S(2)}, u32[]{:S(2)}) collective-permute-start(bf16[8,16,512]{2,1,0:T(8,128)(2,1)S(1)} %get-tuple-element.30), channel_id=1, source_target_pairs={{1,12},{5,8},{9,4},{13,0},{3,14},{7,10},{11,6},{15,2},{17,28},{21,... | collective-permute-start | bytes 393224 | tf_op jit(solution)/shard_map/ppermute | solution.py:342
  61.8 1.3 %shard_map.83.refs_3_ = bf16[16,64,512]{2,1,0:T(8,128)(2,1)} custom-call(s32[2]{0:T(128)S(1)} %pad_add_fusion.refs_0_.where_ref, bf16[8,16,512]{2,1,0:T(8,128)(2,1)S(1)} %collective-permute-done.9.refs_0_, bf16[8,16,512]{2,1,0:T(8,128)(2,1)S(1)} %collective-permute-done.10.refs_1_, bf16[8,16,512]{2,1,0:T(8,128)(2,1)S(1)} %collective-permute-done.11.refs_2_, ...), custom_call_target="tpu_custom_call" | custom-call | bytes 2097152 | tf_op jit(solution)/shard_map/pallas_call | solution.py:431
  63.2 1.0 %collective-permute-done.6.refs_0_ = bf16[8,16,512]{2,1,0:T(8,128)(2,1)S(1)} collective-permute-done((bf16[8,16,512]{2,1,0:T(8,128)(2,1)S(1)}, bf16[8,16,512]{2,1,0:T(8,128)(2,1)S(1)}, u32[]{:S(2)}, u32[]{:S(2)}) %collective-permute-start.6) | collective-permute-done | bytes 131104 | tf_op jit(solution)/shard_map/ppermute | solution.py:342
  64.2 5.0 %collective-permute-done.7.refs_1_ = bf16[8,16,512]{2,1,0:T(8,128)(2,1)S(1)} collective-permute-done((bf16[8,16,512]{2,1,0:T(8,128)(2,1)S(1)}, bf16[8,16,512]{2,1,0:T(8,128)(2,1)S(1)}, u32[]{:S(2)}, u32[]{:S(2)}) %collective-permute-start.7) | collective-permute-done | bytes 131104 | tf_op jit(solution)/shard_map/ppermute | solution.py:342
  69.2 0.0 collective-permute-done.8.refs_2_
  69.2 0.0 collective-permute-done.5.own_ref
  69.2 1.4 %shard_map.84 = bf16[16,64,512]{2,1,0:T(8,128)(2,1)} custom-call(s32[2]{0:T(128)S(1)} %pad_add_fusion.refs_0_.where_ref, bf16[16,16,512]{2,1,0:T(8,128)(2,1)S(1)} %collective-permute-done.5.own_ref, bf16[8,16,512]{2,1,0:T(8,128)(2,1)S(1)} %collective-permute-done.6.refs_0_, ...), custom_call_target="tpu_custom_call", output_to_operand_aliasing={{}: (5, {})} | custom-call | bytes 2097152 | tf_op jit(solution)/shard_map/pallas_call | solution.py:431
  (9 shorter events, 0.1 us)
Async XLA Ops:
  3.2 4.5 %collective-permute-start = (bf16[1024,1024]{1,0:T(8,128)(2,1)S(1)}, bf16[1024,1024]{1,0:T(8,128)(2,1)}, u32[]{:S(2)}, u32[]{:S(2)}) collective-permute-start(bf16[1024,1024]{1,0:T(8,128)(2,1)S(1)} %bitcast.10), channel_id=1, source_target_pairs={{0,1},{1,0},{2,3},{3,2},{4,5},{5,4},{6,7},{7,6},{8,9},{9,8},{10,11... | collective-permute-start | bytes 6291464 | tf_op jit(solution)/shard_map/ppermute | solution.py:336
  9.3 7.4 %copy-start.2 = (f32[1,1,4,2,256]{4,3,2,1,0:T(2,128)S(1)}, f32[1,1,4,2,256]{4,3,2,1,0:T(2,128)}, u32[]{:S(2)}) copy-start(f32[1,1,4,2,256]{4,3,2,1,0:T(2,128)} %param.8) | copy-start | bytes 24580
  9.3 7.5 %copy-start = (bf16[512,512]{1,0:T(8,128)(2,1)S(1)}, bf16[512,512]{1,0:T(8,128)(2,1)}, u32[]{:S(2)}) copy-start(bf16[512,512]{1,0:T(8,128)(2,1)} %constant.17.clone.refs_4_.refs_8_.refs_5_) | copy-start | bytes 1572868
  9.3 7.5 %copy-start.1 = (bf16[256,768]{1,0:T(8,128)(2,1)S(1)}, bf16[256,768]{1,0:T(8,128)(2,1)}, u32[]{:S(2)}) copy-start(bf16[256,768]{1,0:T(8,128)(2,1)} %constant.15.clone.refs_1_) | copy-start | bytes 1179652
  9.3 25.0 %collective-permute-start.1 = (bf16[448,1024]{1,0:T(8,128)(2,1)S(1)}, bf16[448,1024]{1,0:T(8,128)(2,1)S(1)}, u32[]{:S(2)}, u32[]{:S(2)}) collective-permute-start(bf16[448,1024]{1,0:T(8,128)(2,1)S(1)} %shard_map.73), channel_id=1, source_target_pairs={{1,3},{5,7},{9,11},{13,15},{17,19},{21,23},{25,27},{29,31}} | collective-permute-start | bytes 2752520 | tf_op jit(solution)/shard_map/ppermute | solution.py:333
  10.2 19.3 %collective-permute-start.3 = (bf16[256,1024]{1,0:T(8,128)(2,1)S(1)}, bf16[256,1024]{1,0:T(8,128)(2,1)S(1)}, u32[]{:S(2)}, u32[]{:S(2)}) collective-permute-start(bf16[256,1024]{1,0:T(8,128)(2,1)S(1)} %shard_map.76), channel_id=1, source_target_pairs={{1,3},{5,7},{9,11},{13,15},{17,19},{21,23},{25,27},{29,31}} | collective-permute-start | bytes 1572872 | tf_op jit(solution)/shard_map/ppermute | solution.py:333
  10.9 18.6 %collective-permute-start.4 = (bf16[256,1024]{1,0:T(8,128)(2,1)S(1)}, bf16[256,1024]{1,0:T(8,128)(2,1)S(1)}, u32[]{:S(2)}, u32[]{:S(2)}) collective-permute-start(bf16[256,1024]{1,0:T(8,128)(2,1)S(1)} %shard_map.76), channel_id=1, source_target_pairs={{0,3},{4,7},{8,11},{12,15},{16,19},{20,23},{24,27},{28,31}} | collective-permute-start | bytes 1572872 | tf_op jit(solution)/shard_map/ppermute | solution.py:333
  16.7 2.8 %copy-start.4 = (s32[64]{0:T(128)S(1)}, s32[64]{0:T(128)}, u32[]{:S(2)}) copy-start(s32[64]{0:T(128)} %refs_1_.5) | copy-start | bytes 772
  16.7 4.3 %collective-permute-start.2 = (f32[4,2,256]{2,1,0:T(2,128)S(1)}, f32[4,2,256]{2,1,0:T(2,128)S(1)}, u32[]{:S(2)}, u32[]{:S(2)}) collective-permute-start(f32[4,2,256]{2,1,0:T(2,128)S(1)} %bitcast.15), channel_id=1, source_target_pairs={{0,1},{1,0},{2,3},{3,2},{4,5},{5,4},{6,7},{7,6},{8,9},{9,8},{10,11... | collective-permute-start | bytes 24584 | tf_op jit(solution)/shard_map/ppermute | solution.py:336
  19.4 1.5 %copy-start.3 = (s32[1024]{0:T(1024)S(1)}, s32[1024]{0:T(1024)}, u32[]{:S(2)}) copy-start(s32[1024]{0:T(1024)} %param.10) | copy-start | bytes 12292
  26.8 32.4 %collective-permute-start.12 = (bf16[16,16,512]{2,1,0:T(8,128)(2,1)S(1)}, bf16[16,16,512]{2,1,0:T(8,128)(2,1)S(1)}, u32[]{:S(2)}, u32[]{:S(2)}) collective-permute-start(bf16[16,16,512]{2,1,0:T(8,128)(2,1)S(1)} %get-tuple-element.34), channel_id=1, source_target_pairs={{0,5},{4,1},{8,13},{12,9},{2,7},{6,3},{10,15},{14,11},{16,21},{20,... | collective-permute-start | bytes 786440 | tf_op jit(solution)/shard_map/ppermute | solution.py:342
  28.1 32.4 %collective-permute-start.13 = (bf16[16,16,512]{2,1,0:T(8,128)(2,1)S(1)}, bf16[16,16,512]{2,1,0:T(8,128)(2,1)S(1)}, u32[]{:S(2)}, u32[]{:S(2)}) collective-permute-start(bf16[16,16,512]{2,1,0:T(8,128)(2,1)S(1)} %get-tuple-element.35), channel_id=1, source_target_pairs={{0,9},{4,13},{8,1},{12,5},{2,11},{6,15},{10,3},{14,7},{16,25},{20,... | collective-permute-start | bytes 786440 | tf_op jit(solution)/shard_map/ppermute | solution.py:342
  31.1 18.1 %copy-start.5 = (bf16[256,224]{1,0:T(8,128)(2,1)S(1)}, bf16[256,224]{1,0:T(8,128)(2,1)}, u32[]{:S(2)}) copy-start(bf16[256,224]{1,0:T(8,128)(2,1)} %constant.16.clone.refs_1_) | copy-start | bytes 344068
  31.7 18.1 %collective-permute-start.10 = (bf16[8,16,512]{2,1,0:T(8,128)(2,1)S(1)}, bf16[8,16,512]{2,1,0:T(8,128)(2,1)S(1)}, u32[]{:S(2)}, u32[]{:S(2)}) collective-permute-start(bf16[8,16,512]{2,1,0:T(8,128)(2,1)S(1)} %get-tuple-element.32), channel_id=1, source_target_pairs={{1,8},{5,12},{9,0},{13,4},{3,10},{7,14},{11,2},{15,6},{17,24},{21,... | collective-permute-start | bytes 393224 | tf_op jit(solution)/shard_map/ppermute | solution.py:342
  33.0 18.6 %collective-permute-start.9 = (bf16[8,16,512]{2,1,0:T(8,128)(2,1)S(1)}, bf16[8,16,512]{2,1,0:T(8,128)(2,1)S(1)}, u32[]{:S(2)}, u32[]{:S(2)}) collective-permute-start(bf16[8,16,512]{2,1,0:T(8,128)(2,1)S(1)} %get-tuple-element.31), channel_id=1, source_target_pairs={{1,4},{5,0},{9,12},{13,8},{3,6},{7,2},{11,14},{15,10},{17,20},{21,... | collective-permute-start | bytes 393224 | tf_op jit(solution)/shard_map/ppermute | solution.py:342
  34.3 27.6 %collective-permute-start.14 = (bf16[16,16,512]{2,1,0:T(8,128)(2,1)S(1)}, bf16[16,16,512]{2,1,0:T(8,128)(2,1)S(1)}, u32[]{:S(2)}, u32[]{:S(2)}) collective-permute-start(bf16[16,16,512]{2,1,0:T(8,128)(2,1)S(1)} %get-tuple-element.36), channel_id=1, source_target_pairs={{0,13},{4,9},{8,5},{12,1},{2,15},{6,11},{10,7},{14,3},{16,29},{20,... | collective-permute-start | bytes 786440 | tf_op jit(solution)/shard_map/ppermute | solution.py:342
  49.7 8.2 %collective-permute-start.11 = (bf16[8,16,512]{2,1,0:T(8,128)(2,1)S(1)}, bf16[8,16,512]{2,1,0:T(8,128)(2,1)S(1)}, u32[]{:S(2)}, u32[]{:S(2)}) collective-permute-start(bf16[8,16,512]{2,1,0:T(8,128)(2,1)S(1)} %get-tuple-element.33), channel_id=1, source_target_pairs={{1,12},{5,8},{9,4},{13,0},{3,14},{7,10},{11,6},{15,2},{17,28},{21,... | collective-permute-start | bytes 393224 | tf_op jit(solution)/shard_map/ppermute | solution.py:342
  51.6 17.6 %collective-permute-start.5 = (bf16[16,16,512]{2,1,0:T(8,128)(2,1)S(1)}, bf16[16,16,512]{2,1,0:T(8,128)(2,1)S(1)}, u32[]{:S(2)}, u32[]{:S(2)}) collective-permute-start(bf16[16,16,512]{2,1,0:T(8,128)(2,1)S(1)} %get-tuple-element.27), channel_id=1, source_target_pairs={{0,1},{1,0},{2,3},{3,2},{4,5},{5,4},{6,7},{7,6},{8,9},{9,8},{10,11... | collective-permute-start | bytes 786440 | tf_op jit(solution)/shard_map/ppermute | solution.py:336
  57.9 6.3 %collective-permute-start.6 = (bf16[8,16,512]{2,1,0:T(8,128)(2,1)S(1)}, bf16[8,16,512]{2,1,0:T(8,128)(2,1)S(1)}, u32[]{:S(2)}, u32[]{:S(2)}) collective-permute-start(bf16[8,16,512]{2,1,0:T(8,128)(2,1)S(1)} %get-tuple-element.28), channel_id=1, source_target_pairs={{1,4},{5,0},{9,12},{13,8},{3,6},{7,2},{11,14},{15,10},{17,20},{21,... | collective-permute-start | bytes 393224 | tf_op jit(solution)/shard_map/ppermute | solution.py:342
  59.2 10.0 %collective-permute-start.7 = (bf16[8,16,512]{2,1,0:T(8,128)(2,1)S(1)}, bf16[8,16,512]{2,1,0:T(8,128)(2,1)S(1)}, u32[]{:S(2)}, u32[]{:S(2)}) collective-permute-start(bf16[8,16,512]{2,1,0:T(8,128)(2,1)S(1)} %get-tuple-element.29), channel_id=1, source_target_pairs={{1,8},{5,12},{9,0},{13,4},{3,10},{7,14},{11,2},{15,6},{17,24},{21,... | collective-permute-start | bytes 393224 | tf_op jit(solution)/shard_map/ppermute | solution.py:342
  60.5 8.7 %collective-permute-start.8 = (bf16[8,16,512]{2,1,0:T(8,128)(2,1)S(1)}, bf16[8,16,512]{2,1,0:T(8,128)(2,1)S(1)}, u32[]{:S(2)}, u32[]{:S(2)}) collective-permute-start(bf16[8,16,512]{2,1,0:T(8,128)(2,1)S(1)} %get-tuple-element.30), channel_id=1, source_target_pairs={{1,12},{5,8},{9,4},{13,0},{3,14},{7,10},{11,6},{15,2},{17,28},{21,... | collective-permute-start | bytes 393224 | tf_op jit(solution)/shard_map/ppermute | solution.py:342

commit v12 on v11

--- a/solution.py
+++ b/solution.py
@@ -127,18 +127,10 @@
             place(sum_ref, table_ref[k], out_ref)
 
 
-def near_rows_kernel(x_ref, out_ref):
-    out_ref[...] = x_ref[x_ref.shape[0] - out_ref.shape[0] :, :]
-
-
-def far_rows_kernel(reach, where_ref, x_ref, other_ref, out_ref):
-    count = out_ref.shape[0] // 2
-    at = x_ref.shape[0] - reach - count
-
-    @pl.when(where_ref[1] == 1)
-    def _():
-        out_ref[:count, :] = x_ref[at : at + count, :]
-        out_ref[count:, :] = other_ref[at : at + count, :]
+def halo_rows_kernel(x_ref, near_ref, far_ref):
+    near_at = x_ref.shape[0] - near_ref.shape[0]
+    near_ref[...] = x_ref[near_at:, :]
+    far_ref[...] = x_ref[near_at - far_ref.shape[0] : near_at, :]
 
 
 def each_late_block(blocks, filt_ref, x_ref, gain_ref, beam_ref, cal_ref, emitter):
@@ -196,17 +188,14 @@
 
 
 def far_kernel(
-    where_ref, edge_ref, far_ref, g0, g1, beam_ref, keep_ref, table_ref, pre_ref, sum_ref, out_ref, cal_ref
+    where_ref, edge_ref, f0, f1, g0, g1, beam_ref, keep_ref, table_ref, pre_ref, sum_ref, out_ref, cal_ref
 ):
-    count = far_ref.shape[0] // 2
-
     @pl.when(where_ref[1] == 1)
     def _():
-        for pol, gain in enumerate((g0, g1)):
-
-            def spectra(cyl, pol=pol):
-                rows = far_ref[pol * count : (pol + 1) * count, columns(cyl)]
-                return pre_ref[pol * CYL + cyl] + filtered([(edge_ref[...], rows)])
+        for pol, (far_ref, gain) in enumerate(((f0, g0), (f1, g1))):
+
+            def spectra(cyl, pol=pol, far_ref=far_ref):
+                return pre_ref[pol * CYL + cyl] + filtered([(edge_ref[...], far_ref[:, columns(cyl)])])
 
             emit = adder(sum_ref, keep_ref, sum_ref) if pol else keeper(sum_ref)
             form_powers(spectra, gain, beam_ref, cal_ref, emit)
@@ -357,13 +346,31 @@
     keep = keep_flags.reshape(1, -1)
     reach, edge_rows = BLOCK * ROWS, (TAPS - 1 - BLOCK) * ROWS
     blocks = kept // BLOCK
+    table = call(
+        place_table_kernel,
+        jax.ShapeDtypeStruct((n_owner, beams, width), bf16),
+        0,
+        1 << 20,
+        4 << 20,
+        scalars=2,
+        scratch=[pltpu.SMEM((n_owner,), jnp.int32)],
+    )(where, owner_table)
+    samples, table = lax.optimization_barrier((samples, table))
     x = samples.transpose(0, 2, 1, 3).reshape(samples.shape[0] * 2, CYL * NS)
     x = lax.optimization_barrier(x)
-    near_rows = call(near_rows_kernel, jax.ShapeDtypeStruct((reach, CYL * NS), bf16), 1, 0, 1 << 20)(x)
+    near_rows, far_rows = call(
+        halo_rows_kernel,
+        [jax.ShapeDtypeStruct((rows, CYL * NS), bf16) for rows in (reach, edge_rows)],
+        1,
+        0,
+        2 << 20,
+    )(x)
     near0 = ahead(near_rows, 0)
     near1 = ahead(near_rows, 1)
     other = swap(x)
     gain_other = swap(gain)
+    far0 = ahead(far_rows, 0)
+    far1 = ahead(far_rows, 1)
     late_own = call(
         functools.partial(late_own_kernel, blocks),
         jax.ShapeDtypeStruct((kept * UPCH, beams), bf16),
@@ -373,28 +380,9 @@
         scalars=1,
         scratch=[pltpu.VMEM((CYL * BLOCK * UPCH, 2 * NS), bf16)],
     )(where, filt, x, gain, beam_table)
-    table = call(
-        place_table_kernel,
-        jax.ShapeDtypeStruct((n_owner, beams, width), bf16),
-        0,
-        1 << 20,
-        4 << 20,
-        scalars=2,
-        after=1,
-        scratch=[pltpu.SMEM((n_owner,), jnp.int32)],
-    )(where, owner_table, late_own)
     late_sum, late_last = form(
         functools.partial(late_kernel, blocks), kept, filt, other, gain_other, beam_table, keep, table, late_own
     )
-    far_rows = call(
-        functools.partial(far_rows_kernel, reach),
-        jax.ShapeDtypeStruct((2 * edge_rows, CYL * NS), bf16),
-        2,
-        0,
-        2 << 20,
-        scalars=1,
-    )(where, x, other)
-    far_halo = ahead(far_rows, 1)
     late = [*rest(functools.partial(place_kernel, 0), kept, late_sum, table), late_last]
     late_got = spread(late, 0)
     common = (gain, gain_other, beam_table, keep, table)
@@ -411,7 +399,7 @@
     )
     near = [*rest(functools.partial(place_kernel, 1), BLOCK, near_sum, table), near_last]
     near_got = spread(near, 1)
-    far_sum, far_last = form(far_kernel, BLOCK, edge, far_halo, *common, pre)
+    far_sum, far_last = form(far_kernel, BLOCK, edge, far1, far0, *common, pre)
     own, *far = rest(
         far_place_kernel,
         BLOCK,

time: 71.1 us -> 59.6 us (0.84)
  the two profiles are of different devices: /device:TPU:0 before, /device:TPU:15 now
where the time goes in v12:
time: 59.6 us; the launch traced here: 59.2 us
  starting transfers between devices  23.9 us (40%)
  waiting for transfers between devices  18.5 us (31%)
  Pallas kernels  14 us (23%)
  local copies, waits for them, and re-layouts  2.35 us (4%)
    ppermute x9, starting transfers between devices, spread(): got.append(lax.ppermute(blocks[k], ('freq', 'pol'), route))  16.1 us
    ppermute x4, waiting for transfers between devices, ahead(): lax.ppermute(part, ('tm', 'pol'), [(i * 2 + source, j * 2 + 1) for i, j i...  11 us
    ppermute x9, waiting for transfers between devices, spread(): got.append(lax.ppermute(blocks[k], ('freq', 'pol'), route))  6.95 us
    pallas_call x3, Pallas kernels, form(): call(body, shape + list(more), len(arrays), 4 * 512 * 1024 * 1024, 4 << 2...  6.34 us
    ppermute x4, starting transfers between devices, ahead(): lax.ppermute(part, ('tm', 'pol'), [(i * 2 + source, j * 2 + 1) for i, j i...  5.16 us
    pallas_call x3, Pallas kernels, rest(): call(body, list(more) + shape, len(arrays), 1 << 29, 4 << 20, scalars=1)  2.81 us
    pallas_call x2, Pallas kernels, gather(): pl.pallas_call(functools.partial(body, n_owner), out_shape=out_shape, in_...  2.77 us
    ppermute x3, starting transfers between devices, swap(): return lax.ppermute(part, 'pol', [(0, 1), (1, 0)])  2.64 us
  transfers between devices with their start and end apart: 16, of which 4 were waited for; matrix products, arithmetic and copies ran while one was open for 0% of the time, Pallas kernels for 19%

profile of v12, /device:TPU:15, one launch (start us, length us, event | category | flops | bytes accessed | tf_op | source)
XLA Modules:
  0.0 59.2 jit_solution(327672955260734691)
XLA Ops:
  0.0 0.1 pad_add_fusion.refs_0_.where_ref
  0.1 0.7 %copy-done.4 = s32[64]{0:T(128)S(1)} copy-done((s32[64]{0:T(128)S(1)}, s32[64]{0:T(128)}, u32[]{:S(2)}) %copy-start.4) | copy-done | bytes 280
  0.7 1.5 %shard_map.73.refs_10_.refs_8_.refs_2_.refs_6_ = bf16[4,1024,512]{2,1,0:T(8,128)(2,1)S(1)} custom-call(s32[2]{0:T(128)S(1)} %pad_add_fusion.refs_0_.where_ref, s32[64]{0:T(128)S(1)} %copy-done.4), custom_call_target="tpu_custom_call" | custom-call | flops 1048576 | bytes 4194304 | tf_op jit(solution)/shard_map/pallas_call | solution.py:349
  2.2 0.1 copy-done.6
  2.3 1.1 %copy.9 = bf16[512,2,4,256]{3,2,1,0:T(4,128)(2,1)S(1)} copy(bf16[512,2,4,256]{3,1,2,0:T(2,128)(2,1)S(1)} %bitcast.21) | data formatting | bytes 4194304 | tf_op jit(solution)/shard_map/transpose | solution.py:359
  3.4 0.5 copy.10
  3.9 0.0 copy-start.2
  3.9 0.0 copy-start
  3.9 0.0 copy-start.1
  4.0 0.7 %collective-permute-start.5 = (bf16[1024,1024]{1,0:T(8,128)(2,1)S(1)}, bf16[1024,1024]{1,0:T(8,128)(2,1)S(1)}, u32[]{:S(2)}, u32[]{:S(2)}) collective-permute-start(bf16[1024,1024]{1,0:T(8,128)(2,1)S(1)} %bitcast.9), channel_id=1, source_target_pairs={{0,1},{1,0},{2,3},{3,2},{4,5},{5,4},{6,7},{7,6},{8,9},{9,8},{10,11... | collective-permute-start | bytes 6291464 | tf_op jit(solution)/shard_map/ppermute | solution.py:325
  4.7 0.1 shard_map.74
  4.8 1.3 %collective-permute-start.3 = (bf16[256,1024]{1,0:T(8,128)(2,1)S(1)}, bf16[256,1024]{1,0:T(8,128)(2,1)S(1)}, u32[]{:S(2)}, u32[]{:S(2)}) collective-permute-start(bf16[256,1024]{1,0:T(8,128)(2,1)S(1)} %get-tuple-element.28), channel_id=1, source_target_pairs={{1,3},{5,7},{9,11},{13,15},{17,19},{21,23},{25,27},{29,31}} | collective-permute-start | bytes 1572872 | tf_op jit(solution)/shard_map/ppermute | solution.py:322
  6.1 1.3 %collective-permute-start.4 = (bf16[256,1024]{1,0:T(8,128)(2,1)S(1)}, bf16[256,1024]{1,0:T(8,128)(2,1)S(1)}, u32[]{:S(2)}, u32[]{:S(2)}) collective-permute-start(bf16[256,1024]{1,0:T(8,128)(2,1)S(1)} %get-tuple-element.28), channel_id=1, source_target_pairs={{0,3},{4,7},{8,11},{12,15},{16,19},{20,23},{24,27},{28,31}} | collective-permute-start | bytes 1572872 | tf_op jit(solution)/shard_map/ppermute | solution.py:322
  7.4 1.3 %collective-permute-start = (bf16[224,1024]{1,0:T(8,128)(2,1)S(1)}, bf16[224,1024]{1,0:T(8,128)(2,1)S(1)}, u32[]{:S(2)}, u32[]{:S(2)}) collective-permute-start(bf16[224,1024]{1,0:T(8,128)(2,1)S(1)} %get-tuple-element.26), channel_id=1, source_target_pairs={{1,3},{5,7},{9,11},{13,15},{17,19},{21,23},{25,27},{29,31}} | collective-permute-start | bytes 1376264 | tf_op jit(solution)/shard_map/ppermute | solution.py:322
  8.7 0.0 copy-start.3
  8.7 0.1 collective-permute-start.2
  8.8 0.6 shard_map.78.refs_7_
  9.3 0.6 collective-permute-done.2.refs_7_.refs_5_.refs_3_
  9.9 1.3 %collective-permute-start.1 = (bf16[224,1024]{1,0:T(8,128)(2,1)S(1)}, bf16[224,1024]{1,0:T(8,128)(2,1)S(1)}, u32[]{:S(2)}, u32[]{:S(2)}) collective-permute-start(bf16[224,1024]{1,0:T(8,128)(2,1)S(1)} %get-tuple-element.26), channel_id=1, source_target_pairs={{0,3},{4,7},{8,11},{12,15},{16,19},{20,23},{24,27},{28,31}} | collective-permute-start | bytes 1376264 | tf_op jit(solution)/shard_map/ppermute | solution.py:322
  11.2 7.2 %collective-permute-done.3.refs_2_ = bf16[256,1024]{1,0:T(8,128)(2,1)S(1)} collective-permute-done((bf16[256,1024]{1,0:T(8,128)(2,1)S(1)}, bf16[256,1024]{1,0:T(8,128)(2,1)S(1)}, u32[]{:S(2)}, u32[]{:S(2)}) %collective-permute-start.3) | collective-permute-done | bytes 524320 | tf_op jit(solution)/shard_map/ppermute | solution.py:322
  18.4 3.7 %collective-permute-done.4.refs_3_ = bf16[256,1024]{1,0:T(8,128)(2,1)S(1)} collective-permute-done((bf16[256,1024]{1,0:T(8,128)(2,1)S(1)}, bf16[256,1024]{1,0:T(8,128)(2,1)S(1)}, u32[]{:S(2)}, u32[]{:S(2)}) %collective-permute-start.4) | collective-permute-done | bytes 524320 | tf_op jit(solution)/shard_map/ppermute | solution.py:322
  22.2 3.5 %shard_map.75 = (bf16[128,1024]{1,0:T(8,128)(2,1)S(1)}, bf16[8,16,512]{2,1,0:T(8,128)(2,1)S(1)}, f32[8,256,256]{2,1,0:T(8,128)S(1)}) custom-call(s32[2]{0:T(128)S(1)} %pad_add_fusion.refs_0_.where_ref, bf16[256,768]{1,0:T(8,128)(2,1)S(1)} %copy-done.1, bf16[256,1024]{1,0:T(8,128)(2,1)S(1)} %collective-permute-done.3.refs_2_, ...), custom_call_target="tpu_custom_call" | custom-call | flops 2147483648 | bytes 4194304 | tf_op jit(solution)/shard_map/pallas_call | solution.py:337
  25.7 1.1 %shard_map.77 = (bf16[8,16,512]{2,1,0:T(8,128)(2,1)S(1)}, bf16[8,16,512]{2,1,0:T(8,128)(2,1)S(1)}, bf16[8,16,512]{2,1,0:T(8,128)(2,1)S(1)}) custom-call(s32[2]{0:T(128)S(1)} %pad_add_fusion.refs_0_.where_ref, bf16[128,1024]{1,0:T(8,128)(2,1)S(1)} %get-tuple-element.31.refs_1_, bf16[4,1024,512]{2,1,0:T(8,128)(2,1)S(1)} %shard_map.73.refs_10_.refs_8_.refs_2_.refs_6_), custom_call_target="tpu_custom_call" | custom-call | flops 536870912 | bytes 4194304 | tf_op jit(solution)/shard_map/pallas_call | solution.py:343
  26.8 1.3 %collective-permute-start.10 = (bf16[8,16,512]{2,1,0:T(8,128)(2,1)S(1)}, bf16[8,16,512]{2,1,0:T(8,128)(2,1)S(1)}, u32[]{:S(2)}, u32[]{:S(2)}) collective-permute-start(bf16[8,16,512]{2,1,0:T(8,128)(2,1)S(1)} %get-tuple-element.39), channel_id=1, source_target_pairs={{1,4},{5,0},{9,12},{13,8},{3,6},{7,2},{11,14},{15,10},{17,20},{21,... | collective-permute-start | bytes 393224 | tf_op jit(solution)/shard_map/ppermute | solution.py:331
  28.1 1.3 %collective-permute-start.11 = (bf16[8,16,512]{2,1,0:T(8,128)(2,1)S(1)}, bf16[8,16,512]{2,1,0:T(8,128)(2,1)S(1)}, u32[]{:S(2)}, u32[]{:S(2)}) collective-permute-start(bf16[8,16,512]{2,1,0:T(8,128)(2,1)S(1)} %get-tuple-element.40), channel_id=1, source_target_pairs={{1,8},{5,12},{9,0},{13,4},{3,10},{7,14},{11,2},{15,6},{17,24},{21,... | collective-permute-start | bytes 393224 | tf_op jit(solution)/shard_map/ppermute | solution.py:331
  29.5 1.3 %collective-permute-start.12 = (bf16[8,16,512]{2,1,0:T(8,128)(2,1)S(1)}, bf16[8,16,512]{2,1,0:T(8,128)(2,1)S(1)}, u32[]{:S(2)}, u32[]{:S(2)}) collective-permute-start(bf16[8,16,512]{2,1,0:T(8,128)(2,1)S(1)} %get-tuple-element.41), channel_id=1, source_target_pairs={{1,12},{5,8},{9,4},{13,0},{3,14},{7,10},{11,6},{15,2},{17,28},{21,... | collective-permute-start | bytes 393224 | tf_op jit(solution)/shard_map/ppermute | solution.py:331
  30.8 0.6 shard_map.79
  31.3 0.0 copy-start.5
  31.3 0.6 shard_map.80
  31.9 1.3 %collective-permute-start.13 = (bf16[16,16,512]{2,1,0:T(8,128)(2,1)S(1)}, bf16[16,16,512]{2,1,0:T(8,128)(2,1)S(1)}, u32[]{:S(2)}, u32[]{:S(2)}) collective-permute-start(bf16[16,16,512]{2,1,0:T(8,128)(2,1)S(1)} %get-tuple-element.42), channel_id=1, source_target_pairs={{0,5},{4,1},{8,13},{12,9},{2,7},{6,3},{10,15},{14,11},{16,21},{20,... | collective-permute-start | bytes 786440 | tf_op jit(solution)/shard_map/ppermute | solution.py:331
  33.2 0.0 collective-permute-done.1.refs_3_
  33.2 1.3 %collective-permute-start.14 = (bf16[16,16,512]{2,1,0:T(8,128)(2,1)S(1)}, bf16[16,16,512]{2,1,0:T(8,128)(2,1)S(1)}, u32[]{:S(2)}, u32[]{:S(2)}) collective-permute-start(bf16[16,16,512]{2,1,0:T(8,128)(2,1)S(1)} %get-tuple-element.43), channel_id=1, source_target_pairs={{0,9},{4,13},{8,1},{12,5},{2,11},{6,15},{10,3},{14,7},{16,25},{20,... | collective-permute-start | bytes 786440 | tf_op jit(solution)/shard_map/ppermute | solution.py:331
  34.5 2.3 %shard_map.76 = (bf16[128,1024]{1,0:T(8,128)(2,1)S(1)}, bf16[8,16,512]{2,1,0:T(8,128)(2,1)S(1)}) custom-call(s32[2]{0:T(128)S(1)} %pad_add_fusion.refs_0_.where_ref, bf16[256,224]{1,0:T(8,128)(2,1)S(1)} %copy-done.5, bf16[224,1024]{1,0:T(8,128)(2,1)S(1)} %collective-permute-done.refs_2_, bf16[224,1024]{1,0:T(8,128)(2,1)S(1)} %collective-permute-done.1.refs_3_, ...), custom_call_target="tpu_custom_call" | custom-call | flops 2147483648 | bytes 4194304 | tf_op jit(solution)/shard_map/pallas_call | solution.py:337
  36.8 0.0 collective-permute-done.10.refs_0_
  36.8 1.3 %collective-permute-start.15 = (bf16[16,16,512]{2,1,0:T(8,128)(2,1)S(1)}, bf16[16,16,512]{2,1,0:T(8,128)(2,1)S(1)}, u32[]{:S(2)}, u32[]{:S(2)}) collective-permute-start(bf16[16,16,512]{2,1,0:T(8,128)(2,1)S(1)} %get-tuple-element.44), channel_id=1, source_target_pairs={{0,13},{4,9},{8,5},{12,1},{2,15},{6,11},{10,7},{14,3},{16,29},{20,... | collective-permute-start | bytes 786440 | tf_op jit(solution)/shard_map/ppermute | solution.py:331
  38.1 1.1 %shard_map.81 = (bf16[16,16,512]{2,1,0:T(8,128)(2,1)S(1)}, bf16[8,16,512]{2,1,0:T(8,128)(2,1)S(1)}, bf16[8,16,512]{2,1,0:T(8,128)(2,1)S(1)}) custom-call(s32[2]{0:T(128)S(1)} %pad_add_fusion.refs_0_.where_ref, bf16[128,1024]{1,0:T(8,128)(2,1)S(1)} %get-tuple-element.30.refs_1_, bf16[4,1024,512]{2,1,0:T(8,128)(2,1)S(1)} %shard_map.73.refs_10_.refs_8_.refs_2_.refs_6_, ...), custom_call_target="tpu_custom_call" | custom-call | flops 536870912 | bytes 4194304 | tf_op jit(solution)/shard_map/pallas_call | solution.py:343
  39.2 0.0 collective-permute-done.11.refs_1_
  39.3 1.8 %collective-permute-start.6 = (bf16[16,16,512]{2,1,0:T(8,128)(2,1)S(1)}, bf16[16,16,512]{2,1,0:T(8,128)(2,1)S(1)}, u32[]{:S(2)}, u32[]{:S(2)}) collective-permute-start(bf16[16,16,512]{2,1,0:T(8,128)(2,1)S(1)} %get-tuple-element.35), channel_id=1, source_target_pairs={{0,1},{1,0},{2,3},{3,2},{4,5},{5,4},{6,7},{7,6},{8,9},{9,8},{10,11... | collective-permute-start | bytes 786440 | tf_op jit(solution)/shard_map/ppermute | solution.py:325
  41.1 4.0 %collective-permute-start.7 = (bf16[8,16,512]{2,1,0:T(8,128)(2,1)S(1)}, bf16[8,16,512]{2,1,0:T(8,128)(2,1)S(1)}, u32[]{:S(2)}, u32[]{:S(2)}) collective-permute-start(bf16[8,16,512]{2,1,0:T(8,128)(2,1)S(1)} %get-tuple-element.36), channel_id=1, source_target_pairs={{1,4},{5,0},{9,12},{13,8},{3,6},{7,2},{11,14},{15,10},{17,20},{21,... | collective-permute-start | bytes 393224 | tf_op jit(solution)/shard_map/ppermute | solution.py:331
  45.1 0.0 collective-permute-done.13.refs_3_
  45.1 1.3 %collective-permute-start.8 = (bf16[8,16,512]{2,1,0:T(8,128)(2,1)S(1)}, bf16[8,16,512]{2,1,0:T(8,128)(2,1)S(1)}, u32[]{:S(2)}, u32[]{:S(2)}) collective-permute-start(bf16[8,16,512]{2,1,0:T(8,128)(2,1)S(1)} %get-tuple-element.37), channel_id=1, source_target_pairs={{1,8},{5,12},{9,0},{13,4},{3,10},{7,14},{11,2},{15,6},{17,24},{21,... | collective-permute-start | bytes 393224 | tf_op jit(solution)/shard_map/ppermute | solution.py:331
  46.4 3.0 %collective-permute-start.9 = (bf16[8,16,512]{2,1,0:T(8,128)(2,1)S(1)}, bf16[8,16,512]{2,1,0:T(8,128)(2,1)S(1)}, u32[]{:S(2)}, u32[]{:S(2)}) collective-permute-start(bf16[8,16,512]{2,1,0:T(8,128)(2,1)S(1)} %get-tuple-element.38), channel_id=1, source_target_pairs={{1,12},{5,8},{9,4},{13,0},{3,14},{7,10},{11,6},{15,2},{17,28},{21,... | collective-permute-start | bytes 393224 | tf_op jit(solution)/shard_map/ppermute | solution.py:331
  49.4 6.9 %collective-permute-done.15.refs_5_ = bf16[16,16,512]{2,1,0:T(8,128)(2,1)S(1)} collective-permute-done((bf16[16,16,512]{2,1,0:T(8,128)(2,1)S(1)}, bf16[16,16,512]{2,1,0:T(8,128)(2,1)S(1)}, u32[]{:S(2)}, u32[]{:S(2)}) %collective-permute-start.15) | collective-permute-done | bytes 262176 | tf_op jit(solution)/shard_map/ppermute | solution.py:331
  56.4 1.5 %shard_map.82.refs_3_ = bf16[16,64,512]{2,1,0:T(8,128)(2,1)} custom-call(s32[2]{0:T(128)S(1)} %pad_add_fusion.refs_0_.where_ref, bf16[8,16,512]{2,1,0:T(8,128)(2,1)S(1)} %collective-permute-done.10.refs_0_, bf16[8,16,512]{2,1,0:T(8,128)(2,1)S(1)} %collective-permute-done.11.refs_1_, bf16[8,16,512]{2,1,0:T(8,128)(2,1)S(1)} %collective-permute-done.12.refs_2_, ...), custom_call_target="tpu_custom_call" | custom-call | bytes 2097152 | tf_op jit(solution)/shard_map/pallas_call | solution.py:419
  57.8 0.0 collective-permute-done.7.refs_0_
  57.9 0.0 collective-permute-done.8.refs_1_
  57.9 0.0 collective-permute-done.6.own_ref
  57.9 1.3 %shard_map.83 = bf16[16,64,512]{2,1,0:T(8,128)(2,1)} custom-call(s32[2]{0:T(128)S(1)} %pad_add_fusion.refs_0_.where_ref, bf16[16,16,512]{2,1,0:T(8,128)(2,1)S(1)} %collective-permute-done.6.own_ref, bf16[8,16,512]{2,1,0:T(8,128)(2,1)S(1)} %collective-permute-done.7.refs_0_, ...), custom_call_target="tpu_custom_call", output_to_operand_aliasing={{}: (5, {})} | custom-call | bytes 2097152 | tf_op jit(solution)/shard_map/pallas_call | solution.py:419
  (12 shorter events, 0.0 us)
Async XLA Ops:
  0.1 0.7 %copy-start.4 = (s32[64]{0:T(128)S(1)}, s32[64]{0:T(128)}, u32[]{:S(2)}) copy-start(s32[64]{0:T(128)} %refs_1_.5) | copy-start | bytes 772
  0.7 1.6 %copy-start.6 = (bf16[1,1,512,4,2,256]{5,4,3,2,1,0:T(2,128)(2,1)S(1)}, bf16[1,1,512,4,2,256]{5,4,3,2,1,0:T(2,128)(2,1)}, u32[]{:S(2)}) copy-start(bf16[1,1,512,4,2,256]{5,4,3,2,1,0:T(2,128)(2,1)} %param.7) | copy-start | bytes 6291460
  3.9 4.7 %copy-start.2 = (f32[1,1,4,2,256]{4,3,2,1,0:T(2,128)S(1)}, f32[1,1,4,2,256]{4,3,2,1,0:T(2,128)}, u32[]{:S(2)}) copy-start(f32[1,1,4,2,256]{4,3,2,1,0:T(2,128)} %param.8) | copy-start | bytes 24580
  3.9 4.8 %copy-start = (bf16[512,512]{1,0:T(8,128)(2,1)S(1)}, bf16[512,512]{1,0:T(8,128)(2,1)}, u32[]{:S(2)}) copy-start(bf16[512,512]{1,0:T(8,128)(2,1)} %constant.17.clone.refs_8_.refs_6_.refs_4_) | copy-start | bytes 1572868
  3.9 4.8 %copy-start.1 = (bf16[256,768]{1,0:T(8,128)(2,1)S(1)}, bf16[256,768]{1,0:T(8,128)(2,1)}, u32[]{:S(2)}) copy-start(bf16[256,768]{1,0:T(8,128)(2,1)} %constant.15.clone.refs_1_) | copy-start | bytes 1179652
  4.0 18.2 %collective-permute-start.5 = (bf16[1024,1024]{1,0:T(8,128)(2,1)S(1)}, bf16[1024,1024]{1,0:T(8,128)(2,1)S(1)}, u32[]{:S(2)}, u32[]{:S(2)}) collective-permute-start(bf16[1024,1024]{1,0:T(8,128)(2,1)S(1)} %bitcast.9), channel_id=1, source_target_pairs={{0,1},{1,0},{2,3},{3,2},{4,5},{5,4},{6,7},{7,6},{8,9},{9,8},{10,11... | collective-permute-start | bytes 6291464 | tf_op jit(solution)/shard_map/ppermute | solution.py:325
  4.8 13.7 %collective-permute-start.3 = (bf16[256,1024]{1,0:T(8,128)(2,1)S(1)}, bf16[256,1024]{1,0:T(8,128)(2,1)S(1)}, u32[]{:S(2)}, u32[]{:S(2)}) collective-permute-start(bf16[256,1024]{1,0:T(8,128)(2,1)S(1)} %get-tuple-element.28), channel_id=1, source_target_pairs={{1,3},{5,7},{9,11},{13,15},{17,19},{21,23},{25,27},{29,31}} | collective-permute-start | bytes 1572872 | tf_op jit(solution)/shard_map/ppermute | solution.py:322
  6.1 16.1 %collective-permute-start.4 = (bf16[256,1024]{1,0:T(8,128)(2,1)S(1)}, bf16[256,1024]{1,0:T(8,128)(2,1)S(1)}, u32[]{:S(2)}, u32[]{:S(2)}) collective-permute-start(bf16[256,1024]{1,0:T(8,128)(2,1)S(1)} %get-tuple-element.28), channel_id=1, source_target_pairs={{0,3},{4,7},{8,11},{12,15},{16,19},{20,23},{24,27},{28,31}} | collective-permute-start | bytes 1572872 | tf_op jit(solution)/shard_map/ppermute | solution.py:322
  7.4 24.5 %collective-permute-start = (bf16[224,1024]{1,0:T(8,128)(2,1)S(1)}, bf16[224,1024]{1,0:T(8,128)(2,1)S(1)}, u32[]{:S(2)}, u32[]{:S(2)}) collective-permute-start(bf16[224,1024]{1,0:T(8,128)(2,1)S(1)} %get-tuple-element.26), channel_id=1, source_target_pairs={{1,3},{5,7},{9,11},{13,15},{17,19},{21,23},{25,27},{29,31}} | collective-permute-start | bytes 1376264 | tf_op jit(solution)/shard_map/ppermute | solution.py:322
  8.7 13.5 %copy-start.3 = (s32[1024]{0:T(1024)S(1)}, s32[1024]{0:T(1024)}, u32[]{:S(2)}) copy-start(s32[1024]{0:T(1024)} %param.10) | copy-start | bytes 12292
  8.7 1.2 %collective-permute-start.2 = (f32[4,2,256]{2,1,0:T(2,128)S(1)}, f32[4,2,256]{2,1,0:T(2,128)S(1)}, u32[]{:S(2)}, u32[]{:S(2)}) collective-permute-start(f32[4,2,256]{2,1,0:T(2,128)S(1)} %bitcast.13), channel_id=1, source_target_pairs={{0,1},{1,0},{2,3},{3,2},{4,5},{5,4},{6,7},{7,6},{8,9},{9,8},{10,11... | collective-permute-start | bytes 24584 | tf_op jit(solution)/shard_map/ppermute | solution.py:325
  9.9 23.3 %collective-permute-start.1 = (bf16[224,1024]{1,0:T(8,128)(2,1)S(1)}, bf16[224,1024]{1,0:T(8,128)(2,1)S(1)}, u32[]{:S(2)}, u32[]{:S(2)}) collective-permute-start(bf16[224,1024]{1,0:T(8,128)(2,1)S(1)} %get-tuple-element.26), channel_id=1, source_target_pairs={{0,3},{4,7},{8,11},{12,15},{16,19},{20,23},{24,27},{28,31}} | collective-permute-start | bytes 1376264 | tf_op jit(solution)/shard_map/ppermute | solution.py:322
  26.8 10.0 %collective-permute-start.10 = (bf16[8,16,512]{2,1,0:T(8,128)(2,1)S(1)}, bf16[8,16,512]{2,1,0:T(8,128)(2,1)S(1)}, u32[]{:S(2)}, u32[]{:S(2)}) collective-permute-start(bf16[8,16,512]{2,1,0:T(8,128)(2,1)S(1)} %get-tuple-element.39), channel_id=1, source_target_pairs={{1,4},{5,0},{9,12},{13,8},{3,6},{7,2},{11,14},{15,10},{17,20},{21,... | collective-permute-start | bytes 393224 | tf_op jit(solution)/shard_map/ppermute | solution.py:331
  28.1 11.1 %collective-permute-start.11 = (bf16[8,16,512]{2,1,0:T(8,128)(2,1)S(1)}, bf16[8,16,512]{2,1,0:T(8,128)(2,1)S(1)}, u32[]{:S(2)}, u32[]{:S(2)}) collective-permute-start(bf16[8,16,512]{2,1,0:T(8,128)(2,1)S(1)} %get-tuple-element.40), channel_id=1, source_target_pairs={{1,8},{5,12},{9,0},{13,4},{3,10},{7,14},{11,2},{15,6},{17,24},{21,... | collective-permute-start | bytes 393224 | tf_op jit(solution)/shard_map/ppermute | solution.py:331
  29.5 11.6 %collective-permute-start.12 = (bf16[8,16,512]{2,1,0:T(8,128)(2,1)S(1)}, bf16[8,16,512]{2,1,0:T(8,128)(2,1)S(1)}, u32[]{:S(2)}, u32[]{:S(2)}) collective-permute-start(bf16[8,16,512]{2,1,0:T(8,128)(2,1)S(1)} %get-tuple-element.41), channel_id=1, source_target_pairs={{1,12},{5,8},{9,4},{13,0},{3,14},{7,10},{11,6},{15,2},{17,28},{21,... | collective-permute-start | bytes 393224 | tf_op jit(solution)/shard_map/ppermute | solution.py:331
  31.3 3.2 %copy-start.5 = (bf16[256,224]{1,0:T(8,128)(2,1)S(1)}, bf16[256,224]{1,0:T(8,128)(2,1)}, u32[]{:S(2)}) copy-start(bf16[256,224]{1,0:T(8,128)(2,1)} %constant.16.clone.refs_1_) | copy-start | bytes 344068
  31.9 13.2 %collective-permute-start.13 = (bf16[16,16,512]{2,1,0:T(8,128)(2,1)S(1)}, bf16[16,16,512]{2,1,0:T(8,128)(2,1)S(1)}, u32[]{:S(2)}, u32[]{:S(2)}) collective-permute-start(bf16[16,16,512]{2,1,0:T(8,128)(2,1)S(1)} %get-tuple-element.42), channel_id=1, source_target_pairs={{0,5},{4,1},{8,13},{12,9},{2,7},{6,3},{10,15},{14,11},{16,21},{20,... | collective-permute-start | bytes 786440 | tf_op jit(solution)/shard_map/ppermute | solution.py:331
  33.2 13.2 %collective-permute-start.14 = (bf16[16,16,512]{2,1,0:T(8,128)(2,1)S(1)}, bf16[16,16,512]{2,1,0:T(8,128)(2,1)S(1)}, u32[]{:S(2)}, u32[]{:S(2)}) collective-permute-start(bf16[16,16,512]{2,1,0:T(8,128)(2,1)S(1)} %get-tuple-element.43), channel_id=1, source_target_pairs={{0,9},{4,13},{8,1},{12,5},{2,11},{6,15},{10,3},{14,7},{16,25},{20,... | collective-permute-start | bytes 786440 | tf_op jit(solution)/shard_map/ppermute | solution.py:331
  36.8 19.6 %collective-permute-start.15 = (bf16[16,16,512]{2,1,0:T(8,128)(2,1)S(1)}, bf16[16,16,512]{2,1,0:T(8,128)(2,1)S(1)}, u32[]{:S(2)}, u32[]{:S(2)}) collective-permute-start(bf16[16,16,512]{2,1,0:T(8,128)(2,1)S(1)} %get-tuple-element.44), channel_id=1, source_target_pairs={{0,13},{4,9},{8,5},{12,1},{2,15},{6,11},{10,7},{14,3},{16,29},{20,... | collective-permute-start | bytes 786440 | tf_op jit(solution)/shard_map/ppermute | solution.py:331
  39.3 18.6 %collective-permute-start.6 = (bf16[16,16,512]{2,1,0:T(8,128)(2,1)S(1)}, bf16[16,16,512]{2,1,0:T(8,128)(2,1)S(1)}, u32[]{:S(2)}, u32[]{:S(2)}) collective-permute-start(bf16[16,16,512]{2,1,0:T(8,128)(2,1)S(1)} %get-tuple-element.35), channel_id=1, source_target_pairs={{0,1},{1,0},{2,3},{3,2},{4,5},{5,4},{6,7},{7,6},{8,9},{9,8},{10,11... | collective-permute-start | bytes 786440 | tf_op jit(solution)/shard_map/ppermute | solution.py:325
  41.1 16.8 %collective-permute-start.7 = (bf16[8,16,512]{2,1,0:T(8,128)(2,1)S(1)}, bf16[8,16,512]{2,1,0:T(8,128)(2,1)S(1)}, u32[]{:S(2)}, u32[]{:S(2)}) collective-permute-start(bf16[8,16,512]{2,1,0:T(8,128)(2,1)S(1)} %get-tuple-element.36), channel_id=1, source_target_pairs={{1,4},{5,0},{9,12},{13,8},{3,6},{7,2},{11,14},{15,10},{17,20},{21,... | collective-permute-start | bytes 393224 | tf_op jit(solution)/shard_map/ppermute | solution.py:331
  45.1 12.7 %collective-permute-start.8 = (bf16[8,16,512]{2,1,0:T(8,128)(2,1)S(1)}, bf16[8,16,512]{2,1,0:T(8,128)(2,1)S(1)}, u32[]{:S(2)}, u32[]{:S(2)}) collective-permute-start(bf16[8,16,512]{2,1,0:T(8,128)(2,1)S(1)} %get-tuple-element.37), channel_id=1, source_target_pairs={{1,8},{5,12},{9,0},{13,4},{3,10},{7,14},{11,2},{15,6},{17,24},{21,... | collective-permute-start | bytes 393224 | tf_op jit(solution)/shard_map/ppermute | solution.py:331
  46.4 11.4 %collective-permute-start.9 = (bf16[8,16,512]{2,1,0:T(8,128)(2,1)S(1)}, bf16[8,16,512]{2,1,0:T(8,128)(2,1)S(1)}, u32[]{:S(2)}, u32[]{:S(2)}) collective-permute-start(bf16[8,16,512]{2,1,0:T(8,128)(2,1)S(1)} %get-tuple-element.38), channel_id=1, source_target_pairs={{1,12},{5,8},{9,4},{13,0},{3,14},{7,10},{11,6},{15,2},{17,28},{21,... | collective-permute-start | bytes 393224 | tf_op jit(solution)/shard_map/ppermute | solution.py:331

commit v13 on v12

--- a/solution.py
+++ b/solution.py
@@ -120,8 +120,8 @@
     out_ref[...] = placed.astype(jnp.bfloat16).reshape(out_ref.shape)
 
 
-def place_kernel(pol, where_ref, sum_ref, table_ref, *out_refs):
-    @pl.when(where_ref[1] == pol)
+def place_kernel(pol, sum_ref, table_ref, *out_refs):
+    @pl.when(lax.axis_index("pol") == pol)
     def _():
         for k, out_ref in enumerate(out_refs):
             place(sum_ref, table_ref[k], out_ref)
@@ -148,16 +148,16 @@
     lax.fori_loop(0, blocks, step, 0)
 
 
-def late_own_kernel(blocks, where_ref, filt_ref, x_ref, gain_ref, beam_ref, out_ref, cal_ref):
-    @pl.when(where_ref[1] == 0)
+def late_own_kernel(blocks, filt_ref, x_ref, gain_ref, beam_ref, out_ref, cal_ref):
+    @pl.when(lax.axis_index("pol") == 0)
     def _():
         each_late_block(blocks, filt_ref, x_ref, gain_ref, beam_ref, cal_ref, lambda at: keeper(out_ref, at))
 
 
 def late_kernel(
-    blocks, where_ref, filt_ref, x_ref, gain_ref, beam_ref, keep_ref, table_ref, power_ref, sum_ref, out_ref, cal_ref
+    blocks, filt_ref, x_ref, gain_ref, beam_ref, keep_ref, table_ref, power_ref, sum_ref, out_ref, cal_ref
 ):
-    @pl.when(where_ref[1] == 0)
+    @pl.when(lax.axis_index("pol") == 0)
     def _():
         def emitter(at):
             return adder(power_ref, keep_ref, sum_ref, at)
@@ -167,11 +167,11 @@
 
 
 def near_kernel(
-    where_ref, filt_ref, n0, n1, x0, x1, g0, g1, beam_ref, keep_ref, table_ref, sum_ref, out_ref, pre_ref, cal_ref
+    filt_ref, n0, n1, x0, x1, g0, g1, beam_ref, keep_ref, table_ref, sum_ref, out_ref, pre_ref, cal_ref
 ):
     reach = BLOCK * ROWS
 
-    @pl.when(where_ref[1] == 1)
+    @pl.when(lax.axis_index("pol") == 1)
     def _():
         for pol, (n, x, gain) in enumerate(((n0, x0, g0), (n1, x1, g1))):
 
@@ -188,9 +188,9 @@
 
 
 def far_kernel(
-    where_ref, edge_ref, f0, f1, g0, g1, beam_ref, keep_ref, table_ref, pre_ref, sum_ref, out_ref, cal_ref
+    edge_ref, f0, f1, g0, g1, beam_ref, keep_ref, table_ref, pre_ref, sum_ref, out_ref, next_ref, cal_ref
 ):
-    @pl.when(where_ref[1] == 1)
+    @pl.when(lax.axis_index("pol") == 1)
     def _():
         for pol, (far_ref, gain) in enumerate(((f0, g0), (f1, g1))):
 
@@ -200,22 +200,23 @@
             emit = adder(sum_ref, keep_ref, sum_ref) if pol else keeper(sum_ref)
             form_powers(spectra, gain, beam_ref, cal_ref, emit)
         place(sum_ref, table_ref[table_ref.shape[0] - 1], out_ref)
-
-
-def far_place_kernel(where_ref, sum_ref, table_ref, near_ref, late_ref, own_ref, *out_refs):
-    @pl.when(where_ref[1] == 1)
+        place(sum_ref, table_ref[table_ref.shape[0] - 2], next_ref)
+
+
+def far_place_kernel(sum_ref, table_ref, near_ref, late_ref, own_ref, *out_refs):
+    @pl.when(lax.axis_index("pol") == 1)
     def _():
         for k, out_ref in enumerate(out_refs, 1):
             place(sum_ref, table_ref[k], out_ref)
         place(sum_ref, table_ref[0], own_ref.at[:BLOCK])
         own_ref[BLOCK:] = near_ref[...]
 
-    @pl.when(where_ref[1] == 0)
+    @pl.when(lax.axis_index("pol") == 0)
     def _():
         own_ref[...] = late_ref[...]
 
 
-def place_table_kernel(where_ref, owner_ref, out_ref, rank_ref):
+def place_table_kernel(owner_ref, out_ref, rank_ref):
     n_owner = out_ref.shape[0]
     for owner in range(n_owner):
         rank_ref[owner] = 0
@@ -232,16 +233,16 @@
         hit = lane - row == column - tile
         rows = pl.ds(pl.multiple_of(index * SET_BEAMS, SET_BEAMS), SET_BEAMS)
         lanes = pl.ds(pl.multiple_of(tile, LANES), LANES)
-        out_ref[where_ref[0] ^ owner, rows, lanes] = jnp.where(hit, 1.0, 0.0).astype(jnp.bfloat16)
+        out_ref[lax.axis_index("freq") ^ owner, rows, lanes] = jnp.where(hit, 1.0, 0.0).astype(jnp.bfloat16)
         return carry
 
     lax.fori_loop(0, owner_ref.shape[0], step, 0, unroll=4)
 
 
-def put(where_ref, out_ref, sems, blocks):
+def put(out_ref, sems, blocks):
     copies = []
     for index, (block, frame, k) in enumerate(blocks):
-        rows = pl.ds(pl.multiple_of((where_ref[0] ^ k) * UPCH, UPCH), UPCH)
+        rows = pl.ds(pl.multiple_of((lax.axis_index("freq") ^ k) * UPCH, UPCH), UPCH)
         at = out_ref.at[pl.ds(frame, block.shape[0]), rows]
         copies.append(pltpu.make_async_copy(block, at, sems.at[index]))
     for copy in copies:
@@ -250,28 +251,25 @@
         copy.wait()
 
 
-def early_gather_kernel(n_owner, where_ref, *refs):
+def early_gather_kernel(n_owner, own_ref, *refs):
     near, late, out_ref, sems = refs[: n_owner - 1], refs[n_owner - 1 : -2], refs[-2], refs[-1]
-
-    @pl.when(where_ref[1] == 0)
-    def _():
-        put(where_ref, out_ref, sems, [(block, BLOCK, k + 1) for k, block in enumerate(near)])
-
-    @pl.when(where_ref[1] == 1)
-    def _():
-        put(where_ref, out_ref, sems, [(block, 0, k + 1) for k, block in enumerate(late)])
-
-
-def last_gather_kernel(n_owner, where_ref, own_ref, *refs):
+    own = [(own_ref, 0, 0)]
+
+    @pl.when(lax.axis_index("pol") == 0)
+    def _():
+        put(out_ref, sems, own + [(block, BLOCK, k + 1) for k, block in enumerate(near)])
+
+    @pl.when(lax.axis_index("pol") == 1)
+    def _():
+        put(out_ref, sems, own + [(block, 0, k + 1) for k, block in enumerate(late)])
+
+
+def last_gather_kernel(n_owner, *refs):
     far, out_ref, sems = refs[: n_owner - 1], refs[-2], refs[-1]
 
-    @pl.when(where_ref[1] == 0)
-    def _():
-        put(where_ref, out_ref, sems, [(own_ref, 0, 0)] + [(block, 0, k + 1) for k, block in enumerate(far)])
-
-    @pl.when(where_ref[1] == 1)
-    def _():
-        put(where_ref, out_ref, sems, [(own_ref, 0, 0)])
+    @pl.when(lax.axis_index("pol") == 0)
+    def _():
+        put(out_ref, sems, [(block, 0, k + 1) for k, block in enumerate(far)])
 
 
 VMEM = pl.BlockSpec(memory_space=pltpu.VMEM)
@@ -306,8 +304,6 @@
     assert voltages.shape[1] == 1 and kept == 2 * BLOCK and kept >= TAPS
     assert n_owner & (n_owner - 1) == 0
     n_tm = lax.axis_size("tm")
-    me = lax.axis_index("freq")
-    pol = lax.axis_index("pol")
     most_sets = 2 * owner_table.shape[0] // n_owner
     beams = keep_flags.shape[0]
     width = most_sets * SET_BEAMS
@@ -335,14 +331,13 @@
         shape = [jax.ShapeDtypeStruct((frames * UPCH, beams), bf16), jax.ShapeDtypeStruct((frames, UPCH, width), bf16)]
         scratch = [pltpu.VMEM((CYL * BLOCK * UPCH, 2 * NS), bf16)]
         return call(
-            body, shape + list(more), len(arrays), 4 * 512 * 1024 * 1024, 4 << 20, scalars=1, scratch=scratch
-        )(where, *arrays)
+            body, shape + list(more), len(arrays), 4 * 512 * 1024 * 1024, 4 << 20, scratch=scratch
+        )(*arrays)
 
     def rest(body, frames, *arrays, more=(), count=n_owner - 1):
         shape = [jax.ShapeDtypeStruct((frames, UPCH, width), bf16)] * count
-        return call(body, list(more) + shape, len(arrays), 1 << 29, 4 << 20, scalars=1)(where, *arrays)
-
-    where = jnp.stack([me, pol]).astype(jnp.int32)
+        return call(body, list(more) + shape, len(arrays), 1 << 29, 4 << 20)(*arrays)
+
     keep = keep_flags.reshape(1, -1)
     reach, edge_rows = BLOCK * ROWS, (TAPS - 1 - BLOCK) * ROWS
     blocks = kept // BLOCK
@@ -352,9 +347,9 @@
         0,
         1 << 20,
         4 << 20,
-        scalars=2,
+        scalars=1,
         scratch=[pltpu.SMEM((n_owner,), jnp.int32)],
-    )(where, owner_table)
+    )(owner_table)
     samples, table = lax.optimization_barrier((samples, table))
     x = samples.transpose(0, 2, 1, 3).reshape(samples.shape[0] * 2, CYL * NS)
     x = lax.optimization_barrier(x)
@@ -377,9 +372,8 @@
         4,
         4 * 512 * 1024 * 1024,
         4 << 20,
-        scalars=1,
         scratch=[pltpu.VMEM((CYL * BLOCK * UPCH, 2 * NS), bf16)],
-    )(where, filt, x, gain, beam_table)
+    )(filt, x, gain, beam_table)
     late_sum, late_last = form(
         functools.partial(late_kernel, blocks), kept, filt, other, gain_other, beam_table, keep, table, late_own
     )
@@ -399,7 +393,8 @@
     )
     near = [*rest(functools.partial(place_kernel, 1), BLOCK, near_sum, table), near_last]
     near_got = spread(near, 1)
-    far_sum, far_last = form(far_kernel, BLOCK, edge, far1, far0, *common, pre)
+    block_shape = jax.ShapeDtypeStruct((BLOCK, UPCH, width), bf16)
+    far_sum, far_last, far_next = form(far_kernel, BLOCK, edge, far1, far0, *common, pre, more=[block_shape])
     own, *far = rest(
         far_place_kernel,
         BLOCK,
@@ -408,9 +403,9 @@
         near[0],
         late[0],
         more=[jax.ShapeDtypeStruct((kept, UPCH, width), bf16)],
-        count=n_owner - 2,
+        count=n_owner - 3,
     )
-    far = [own, *far, far_last]
+    far = [own, *far, far_next, far_last]
     far_got = spread(far, 1)
     own_got = swap(own)
     out_shape = jax.ShapeDtypeStruct((kept, n_owner * UPCH, width), bf16)
@@ -419,16 +414,16 @@
         return pl.pallas_call(
             functools.partial(body, n_owner),
             out_shape=out_shape,
-            in_specs=[SMEM] + [VMEM] * len(arrays) + [ANY] * len(base),
+            in_specs=[VMEM] * len(arrays) + [ANY] * len(base),
             out_specs=ANY,
             scratch_shapes=[pltpu.SemaphoreType.DMA((n_owner,))],
-            input_output_aliases={1 + len(arrays): 0} if base else {},
+            input_output_aliases={len(arrays): 0} if base else {},
             cost_estimate=pl.CostEstimate(flops=0, bytes_accessed=2 << 20, transcendentals=0),
             compiler_params=pltpu.CompilerParams(vmem_limit_bytes=24 << 20),
-        )(where, *arrays, *base)
-
-    out = gather(early_gather_kernel, [*near_got, *late_got])
-    return gather(last_gather_kernel, [own_got, *far_got], base=[out])
+        )(*arrays, *base)
+
+    out = gather(early_gather_kernel, [own_got, *near_got, *late_got])
+    return gather(last_gather_kernel, far_got, base=[out])
 
 
 def solution(mesh):

time: 59.6 us -> 63.6 us (1.067)
  the two profiles are of different devices: /device:TPU:15 before, /device:TPU:11 now
where the time goes in v13:
time: 63.6 us; the launch traced here: 63.2 us
  waiting for transfers between devices  26.2 us (41%)
  starting transfers between devices  25.7 us (40%)
  Pallas kernels  8.64 us (14%)
  local copies, waits for them, and re-layouts  2.31 us (4%)
    ppermute x9, starting transfers between devices, spread(): got.append(lax.ppermute(blocks[k], ('freq', 'pol'), route))  19.6 us
    ppermute x4, waiting for transfers between devices, ahead(): lax.ppermute(part, ('tm', 'pol'), [(i * 2 + source, j * 2 + 1) for i, j i...  13.8 us
    ppermute x9, waiting for transfers between devices, spread(): got.append(lax.ppermute(blocks[k], ('freq', 'pol'), route))  12.5 us
    ppermute x4, starting transfers between devices, ahead(): lax.ppermute(part, ('tm', 'pol'), [(i * 2 + source, j * 2 + 1) for i, j i...  5.17 us
    pallas_call x3, Pallas kernels, form(): call(body, shape + list(more), len(arrays), 4 * 512 * 1024 * 1024, 4 << 2...  4.91 us
    pallas_call x1, Pallas kernels, per_device(): call(place_table_kernel, jax.ShapeDtypeStruct((n_owner, beams, width), bf...  1.53 us
  transfers between devices with their start and end apart: 16, of which 6 were waited for; matrix products, arithmetic and copies ran while one was open for 0% of the time, Pallas kernels for 11%

profile of v13, /device:TPU:11, one launch (start us, length us, event | category | flops | bytes accessed | tf_op | source)
XLA Modules:
  0.0 63.2 jit_solution(223398855801805866)
XLA Ops:
  0.0 0.7 %copy-done.4 = s32[64]{0:T(128)S(1)} copy-done((s32[64]{0:T(128)S(1)}, s32[64]{0:T(128)}, u32[]{:S(2)}) %copy-start.4) | copy-done | bytes 280
  0.7 1.5 %shard_map.73.refs_9_.refs_7_.refs_1_.refs_5_ = bf16[4,1024,512]{2,1,0:T(8,128)(2,1)S(1)} custom-call(s32[64]{0:T(128)S(1)} %copy-done.4), custom_call_target="tpu_custom_call" | custom-call | flops 1048576 | bytes 4194304 | tf_op jit(solution)/shard_map/pallas_call | solution.py:344
  2.2 0.0 copy-done.6
  2.2 1.1 %copy.9 = bf16[512,2,4,256]{3,2,1,0:T(4,128)(2,1)S(1)} copy(bf16[512,2,4,256]{3,1,2,0:T(2,128)(2,1)S(1)} %bitcast.19) | data formatting | bytes 4194304 | tf_op jit(solution)/shard_map/transpose | solution.py:354
  3.3 0.5 copy.10
  3.8 0.0 copy-start.2
  3.8 0.0 copy-start
  3.9 0.0 copy-start.1
  3.9 0.7 %collective-permute-start.5 = (bf16[1024,1024]{1,0:T(8,128)(2,1)S(1)}, bf16[1024,1024]{1,0:T(8,128)(2,1)S(1)}, u32[]{:S(2)}, u32[]{:S(2)}) collective-permute-start(bf16[1024,1024]{1,0:T(8,128)(2,1)S(1)} %bitcast.7), channel_id=1, source_target_pairs={{0,1},{1,0},{2,3},{3,2},{4,5},{5,4},{6,7},{7,6},{8,9},{9,8},{10,11... | collective-permute-start | bytes 6291464 | tf_op jit(solution)/shard_map/ppermute | solution.py:321
  4.6 0.1 shard_map.74
  4.7 1.3 %collective-permute-start.3 = (bf16[256,1024]{1,0:T(8,128)(2,1)S(1)}, bf16[256,1024]{1,0:T(8,128)(2,1)S(1)}, u32[]{:S(2)}, u32[]{:S(2)}) collective-permute-start(bf16[256,1024]{1,0:T(8,128)(2,1)S(1)} %get-tuple-element.28), channel_id=1, source_target_pairs={{1,3},{5,7},{9,11},{13,15},{17,19},{21,23},{25,27},{29,31}} | collective-permute-start | bytes 1572872 | tf_op jit(solution)/shard_map/ppermute | solution.py:318
  6.0 1.3 %collective-permute-start.4 = (bf16[256,1024]{1,0:T(8,128)(2,1)S(1)}, bf16[256,1024]{1,0:T(8,128)(2,1)S(1)}, u32[]{:S(2)}, u32[]{:S(2)}) collective-permute-start(bf16[256,1024]{1,0:T(8,128)(2,1)S(1)} %get-tuple-element.28), channel_id=1, source_target_pairs={{0,3},{4,7},{8,11},{12,15},{16,19},{20,23},{24,27},{28,31}} | collective-permute-start | bytes 1572872 | tf_op jit(solution)/shard_map/ppermute | solution.py:318
  7.3 0.1 collective-permute-start.2
  7.4 0.0 copy-start.3
  7.4 1.3 %collective-permute-start = (bf16[224,1024]{1,0:T(8,128)(2,1)S(1)}, bf16[224,1024]{1,0:T(8,128)(2,1)S(1)}, u32[]{:S(2)}, u32[]{:S(2)}) collective-permute-start(bf16[224,1024]{1,0:T(8,128)(2,1)S(1)} %get-tuple-element.26), channel_id=1, source_target_pairs={{1,3},{5,7},{9,11},{13,15},{17,19},{21,23},{25,27},{29,31}} | collective-permute-start | bytes 1376264 | tf_op jit(solution)/shard_map/ppermute | solution.py:318
  8.7 0.0 collective-permute-done.2.refs_6_.refs_4_.refs_2_
  8.7 1.3 %collective-permute-start.1 = (bf16[224,1024]{1,0:T(8,128)(2,1)S(1)}, bf16[224,1024]{1,0:T(8,128)(2,1)S(1)}, u32[]{:S(2)}, u32[]{:S(2)}) collective-permute-start(bf16[224,1024]{1,0:T(8,128)(2,1)S(1)} %get-tuple-element.26), channel_id=1, source_target_pairs={{0,3},{4,7},{8,11},{12,15},{16,19},{20,23},{24,27},{28,31}} | collective-permute-start | bytes 1376264 | tf_op jit(solution)/shard_map/ppermute | solution.py:318
  10.0 8.3 %collective-permute-done.3.refs_1_ = bf16[256,1024]{1,0:T(8,128)(2,1)S(1)} collective-permute-done((bf16[256,1024]{1,0:T(8,128)(2,1)S(1)}, bf16[256,1024]{1,0:T(8,128)(2,1)S(1)}, u32[]{:S(2)}, u32[]{:S(2)}) %collective-permute-start.3) | collective-permute-done | bytes 524320 | tf_op jit(solution)/shard_map/ppermute | solution.py:318
  18.3 3.7 %collective-permute-done.4.refs_2_ = bf16[256,1024]{1,0:T(8,128)(2,1)S(1)} collective-permute-done((bf16[256,1024]{1,0:T(8,128)(2,1)S(1)}, bf16[256,1024]{1,0:T(8,128)(2,1)S(1)}, u32[]{:S(2)}, u32[]{:S(2)}) %collective-permute-start.4) | collective-permute-done | bytes 524320 | tf_op jit(solution)/shard_map/ppermute | solution.py:318
  22.1 0.0 collective-permute-done.5.refs_4_.refs_1_
  22.1 3.0 %shard_map.75 = (bf16[128,1024]{1,0:T(8,128)(2,1)S(1)}, bf16[8,16,512]{2,1,0:T(8,128)(2,1)S(1)}, f32[8,256,256]{2,1,0:T(8,128)S(1)}) custom-call(bf16[256,768]{1,0:T(8,128)(2,1)S(1)} %copy-done.1, bf16[256,1024]{1,0:T(8,128)(2,1)S(1)} %collective-permute-done.3.refs_1_, bf16[256,1024]{1,0:T(8,128)(2,1)S(1)} %collective-permute-done.4.refs_2_, ...), custom_call_target="tpu_custom_call" | custom-call | flops 2147483648 | bytes 4194304 | tf_op jit(solution)/shard_map/pallas_call | solution.py:333
  25.1 0.6 shard_map.77
  25.7 1.3 %collective-permute-start.10 = (bf16[8,16,512]{2,1,0:T(8,128)(2,1)S(1)}, bf16[8,16,512]{2,1,0:T(8,128)(2,1)S(1)}, u32[]{:S(2)}, u32[]{:S(2)}) collective-permute-start(bf16[8,16,512]{2,1,0:T(8,128)(2,1)S(1)} %get-tuple-element.39), channel_id=1, source_target_pairs={{1,4},{5,0},{9,12},{13,8},{3,6},{7,2},{11,14},{15,10},{17,20},{21,... | collective-permute-start | bytes 393224 | tf_op jit(solution)/shard_map/ppermute | solution.py:327
  27.0 1.3 %collective-permute-start.11 = (bf16[8,16,512]{2,1,0:T(8,128)(2,1)S(1)}, bf16[8,16,512]{2,1,0:T(8,128)(2,1)S(1)}, u32[]{:S(2)}, u32[]{:S(2)}) collective-permute-start(bf16[8,16,512]{2,1,0:T(8,128)(2,1)S(1)} %get-tuple-element.40), channel_id=1, source_target_pairs={{1,8},{5,12},{9,0},{13,4},{3,10},{7,14},{11,2},{15,6},{17,24},{21,... | collective-permute-start | bytes 393224 | tf_op jit(solution)/shard_map/ppermute | solution.py:327
  28.3 0.0 copy-start.5
  28.4 0.1 collective-permute-done.refs_1_
  28.5 1.6 %collective-permute-done.1.refs_2_ = bf16[224,1024]{1,0:T(8,128)(2,1)S(1)} collective-permute-done((bf16[224,1024]{1,0:T(8,128)(2,1)S(1)}, bf16[224,1024]{1,0:T(8,128)(2,1)S(1)}, u32[]{:S(2)}, u32[]{:S(2)}) %collective-permute-start.1) | collective-permute-done | bytes 458784 | tf_op jit(solution)/shard_map/ppermute | solution.py:318
  30.1 1.9 %shard_map.76 = (bf16[128,1024]{1,0:T(8,128)(2,1)S(1)}, bf16[8,16,512]{2,1,0:T(8,128)(2,1)S(1)}, bf16[8,16,512]{2,1,0:T(8,128)(2,1)S(1)}) custom-call(bf16[256,224]{1,0:T(8,128)(2,1)S(1)} %copy-done.5, bf16[224,1024]{1,0:T(8,128)(2,1)S(1)} %collective-permute-done.refs_1_, bf16[224,1024]{1,0:T(8,128)(2,1)S(1)} %collective-permute-done.1.refs_2_, ...), custom_call_target="tpu_custom_call" | custom-call | flops 2147483648 | bytes 4194304 | tf_op jit(solution)/shard_map/pallas_call | solution.py:333
  32.0 0.5 shard_map.81
  32.4 0.1 collective-permute-start.9
  32.5 1.3 %collective-permute-start.13 = (bf16[16,16,512]{2,1,0:T(8,128)(2,1)S(1)}, bf16[16,16,512]{2,1,0:T(8,128)(2,1)S(1)}, u32[]{:S(2)}, u32[]{:S(2)}) collective-permute-start(bf16[16,16,512]{2,1,0:T(8,128)(2,1)S(1)} %get-tuple-element.42), channel_id=1, source_target_pairs={{0,5},{4,1},{8,13},{12,9},{2,7},{6,3},{10,15},{14,11},{16,21},{20,... | collective-permute-start | bytes 786440 | tf_op jit(solution)/shard_map/ppermute | solution.py:327
  33.8 5.7 %collective-permute-start.12 = (bf16[8,16,512]{2,1,0:T(8,128)(2,1)S(1)}, bf16[8,16,512]{2,1,0:T(8,128)(2,1)S(1)}, u32[]{:S(2)}, u32[]{:S(2)}) collective-permute-start(bf16[8,16,512]{2,1,0:T(8,128)(2,1)S(1)} %get-tuple-element.41), channel_id=1, source_target_pairs={{1,12},{5,8},{9,4},{13,0},{3,14},{7,10},{11,6},{15,2},{17,28},{21,... | collective-permute-start | bytes 393224 | tf_op jit(solution)/shard_map/ppermute | solution.py:327
  39.5 0.0 collective-permute-done.10.refs_0_
  39.6 1.3 %collective-permute-start.14 = (bf16[16,16,512]{2,1,0:T(8,128)(2,1)S(1)}, bf16[16,16,512]{2,1,0:T(8,128)(2,1)S(1)}, u32[]{:S(2)}, u32[]{:S(2)}) collective-permute-start(bf16[16,16,512]{2,1,0:T(8,128)(2,1)S(1)} %get-tuple-element.43), channel_id=1, source_target_pairs={{0,9},{4,13},{8,1},{12,5},{2,11},{6,15},{10,3},{14,7},{16,25},{20,... | collective-permute-start | bytes 786440 | tf_op jit(solution)/shard_map/ppermute | solution.py:327
  40.9 0.0 collective-permute-done.11.refs_1_
  40.9 1.3 %collective-permute-start.15 = (bf16[16,16,512]{2,1,0:T(8,128)(2,1)S(1)}, bf16[16,16,512]{2,1,0:T(8,128)(2,1)S(1)}, u32[]{:S(2)}, u32[]{:S(2)}) collective-permute-start(bf16[16,16,512]{2,1,0:T(8,128)(2,1)S(1)} %get-tuple-element.44), channel_id=1, source_target_pairs={{0,13},{4,9},{8,5},{12,1},{2,15},{6,11},{10,7},{14,3},{16,29},{20,... | collective-permute-start | bytes 786440 | tf_op jit(solution)/shard_map/ppermute | solution.py:327
  42.2 5.9 %collective-permute-done.12.refs_2_ = bf16[8,16,512]{2,1,0:T(8,128)(2,1)S(1)} collective-permute-done((bf16[8,16,512]{2,1,0:T(8,128)(2,1)S(1)}, bf16[8,16,512]{2,1,0:T(8,128)(2,1)S(1)}, u32[]{:S(2)}, u32[]{:S(2)}) %collective-permute-start.12) | collective-permute-done | bytes 131104 | tf_op jit(solution)/shard_map/ppermute | solution.py:327
  48.1 1.3 %collective-permute-start.6 = (bf16[8,16,512]{2,1,0:T(8,128)(2,1)S(1)}, bf16[8,16,512]{2,1,0:T(8,128)(2,1)S(1)}, u32[]{:S(2)}, u32[]{:S(2)}) collective-permute-start(bf16[8,16,512]{2,1,0:T(8,128)(2,1)S(1)} %get-tuple-element.35), channel_id=1, source_target_pairs={{1,4},{5,0},{9,12},{13,8},{3,6},{7,2},{11,14},{15,10},{17,20},{21,... | collective-permute-start | bytes 393224 | tf_op jit(solution)/shard_map/ppermute | solution.py:327
  49.3 0.0 collective-permute-done.9.own_ref
  49.4 1.3 %collective-permute-start.7 = (bf16[8,16,512]{2,1,0:T(8,128)(2,1)S(1)}, bf16[8,16,512]{2,1,0:T(8,128)(2,1)S(1)}, u32[]{:S(2)}, u32[]{:S(2)}) collective-permute-start(bf16[8,16,512]{2,1,0:T(8,128)(2,1)S(1)} %get-tuple-element.36), channel_id=1, source_target_pairs={{1,8},{5,12},{9,0},{13,4},{3,10},{7,14},{11,2},{15,6},{17,24},{21,... | collective-permute-start | bytes 393224 | tf_op jit(solution)/shard_map/ppermute | solution.py:327
  50.7 0.0 collective-permute-done.13.refs_3_
  50.7 4.9 %collective-permute-start.8 = (bf16[8,16,512]{2,1,0:T(8,128)(2,1)S(1)}, bf16[8,16,512]{2,1,0:T(8,128)(2,1)S(1)}, u32[]{:S(2)}, u32[]{:S(2)}) collective-permute-start(bf16[8,16,512]{2,1,0:T(8,128)(2,1)S(1)} %get-tuple-element.37), channel_id=1, source_target_pairs={{1,12},{5,8},{9,4},{13,0},{3,14},{7,10},{11,6},{15,2},{17,28},{21,... | collective-permute-start | bytes 393224 | tf_op jit(solution)/shard_map/ppermute | solution.py:327
  55.6 0.0 collective-permute-done.14.refs_4_
  55.6 6.5 %collective-permute-done.15.refs_5_ = bf16[16,16,512]{2,1,0:T(8,128)(2,1)S(1)} collective-permute-done((bf16[16,16,512]{2,1,0:T(8,128)(2,1)S(1)}, bf16[16,16,512]{2,1,0:T(8,128)(2,1)S(1)}, u32[]{:S(2)}, u32[]{:S(2)}) %collective-permute-start.15) | collective-permute-done | bytes 262176 | tf_op jit(solution)/shard_map/ppermute | solution.py:327
  62.1 1.0 %shard_map.82.refs_3_ = bf16[16,64,512]{2,1,0:T(8,128)(2,1)} custom-call(bf16[16,16,512]{2,1,0:T(8,128)(2,1)S(1)} %collective-permute-done.9.own_ref, bf16[8,16,512]{2,1,0:T(8,128)(2,1)S(1)} %collective-permute-done.10.refs_0_, bf16[8,16,512]{2,1,0:T(8,128)(2,1)S(1)} %collective-permute-done.11.refs_1_, ...), custom_call_target="tpu_custom_call" | custom-call | bytes 2097152 | tf_op jit(solution)/shard_map/pallas_call | solution.py:414
  63.1 0.0 collective-permute-done.7.refs_1_
  63.1 0.0 collective-permute-done.8.refs_2_
  63.2 0.1 shard_map.83
  (11 shorter events, 0.1 us)
Async XLA Ops:
  0.0 0.7 %copy-start.4 = (s32[64]{0:T(128)S(1)}, s32[64]{0:T(128)}, u32[]{:S(2)}) copy-start(s32[64]{0:T(128)} %refs_0_.5) | copy-start | bytes 772
  0.7 1.6 %copy-start.6 = (bf16[1,1,512,4,2,256]{5,4,3,2,1,0:T(2,128)(2,1)S(1)}, bf16[1,1,512,4,2,256]{5,4,3,2,1,0:T(2,128)(2,1)}, u32[]{:S(2)}) copy-start(bf16[1,1,512,4,2,256]{5,4,3,2,1,0:T(2,128)(2,1)} %param.7) | copy-start | bytes 6291460
  3.8 3.4 %copy-start.2 = (f32[1,1,4,2,256]{4,3,2,1,0:T(2,128)S(1)}, f32[1,1,4,2,256]{4,3,2,1,0:T(2,128)}, u32[]{:S(2)}) copy-start(f32[1,1,4,2,256]{4,3,2,1,0:T(2,128)} %param.8) | copy-start | bytes 24580
  3.8 4.8 %copy-start = (bf16[512,512]{1,0:T(8,128)(2,1)S(1)}, bf16[512,512]{1,0:T(8,128)(2,1)}, u32[]{:S(2)}) copy-start(bf16[512,512]{1,0:T(8,128)(2,1)} %constant.8.clone.refs_7_.refs_5_.refs_3_) | copy-start | bytes 1572868
  3.9 4.8 %copy-start.1 = (bf16[256,768]{1,0:T(8,128)(2,1)S(1)}, bf16[256,768]{1,0:T(8,128)(2,1)}, u32[]{:S(2)}) copy-start(bf16[256,768]{1,0:T(8,128)(2,1)} %constant.6.clone.refs_0_) | copy-start | bytes 1179652
  3.9 18.2 %collective-permute-start.5 = (bf16[1024,1024]{1,0:T(8,128)(2,1)S(1)}, bf16[1024,1024]{1,0:T(8,128)(2,1)S(1)}, u32[]{:S(2)}, u32[]{:S(2)}) collective-permute-start(bf16[1024,1024]{1,0:T(8,128)(2,1)S(1)} %bitcast.7), channel_id=1, source_target_pairs={{0,1},{1,0},{2,3},{3,2},{4,5},{5,4},{6,7},{7,6},{8,9},{9,8},{10,11... | collective-permute-start | bytes 6291464 | tf_op jit(solution)/shard_map/ppermute | solution.py:321
  4.7 13.7 %collective-permute-start.3 = (bf16[256,1024]{1,0:T(8,128)(2,1)S(1)}, bf16[256,1024]{1,0:T(8,128)(2,1)S(1)}, u32[]{:S(2)}, u32[]{:S(2)}) collective-permute-start(bf16[256,1024]{1,0:T(8,128)(2,1)S(1)} %get-tuple-element.28), channel_id=1, source_target_pairs={{1,3},{5,7},{9,11},{13,15},{17,19},{21,23},{25,27},{29,31}} | collective-permute-start | bytes 1572872 | tf_op jit(solution)/shard_map/ppermute | solution.py:318
  6.0 16.1 %collective-permute-start.4 = (bf16[256,1024]{1,0:T(8,128)(2,1)S(1)}, bf16[256,1024]{1,0:T(8,128)(2,1)S(1)}, u32[]{:S(2)}, u32[]{:S(2)}) collective-permute-start(bf16[256,1024]{1,0:T(8,128)(2,1)S(1)} %get-tuple-element.28), channel_id=1, source_target_pairs={{0,3},{4,7},{8,11},{12,15},{16,19},{20,23},{24,27},{28,31}} | collective-permute-start | bytes 1572872 | tf_op jit(solution)/shard_map/ppermute | solution.py:318
  7.3 1.4 %collective-permute-start.2 = (f32[4,2,256]{2,1,0:T(2,128)S(1)}, f32[4,2,256]{2,1,0:T(2,128)S(1)}, u32[]{:S(2)}, u32[]{:S(2)}) collective-permute-start(f32[4,2,256]{2,1,0:T(2,128)S(1)} %bitcast.11), channel_id=1, source_target_pairs={{0,1},{1,0},{2,3},{3,2},{4,5},{5,4},{6,7},{7,6},{8,9},{9,8},{10,11... | collective-permute-start | bytes 24584 | tf_op jit(solution)/shard_map/ppermute | solution.py:321
  7.4 14.7 %copy-start.3 = (s32[1024]{0:T(1024)S(1)}, s32[1024]{0:T(1024)}, u32[]{:S(2)}) copy-start(s32[1024]{0:T(1024)} %param.10) | copy-start | bytes 12292
  7.4 21.1 %collective-permute-start = (bf16[224,1024]{1,0:T(8,128)(2,1)S(1)}, bf16[224,1024]{1,0:T(8,128)(2,1)S(1)}, u32[]{:S(2)}, u32[]{:S(2)}) collective-permute-start(bf16[224,1024]{1,0:T(8,128)(2,1)S(1)} %get-tuple-element.26), channel_id=1, source_target_pairs={{1,3},{5,7},{9,11},{13,15},{17,19},{21,23},{25,27},{29,31}} | collective-permute-start | bytes 1376264 | tf_op jit(solution)/shard_map/ppermute | solution.py:318
  8.7 21.3 %collective-permute-start.1 = (bf16[224,1024]{1,0:T(8,128)(2,1)S(1)}, bf16[224,1024]{1,0:T(8,128)(2,1)S(1)}, u32[]{:S(2)}, u32[]{:S(2)}) collective-permute-start(bf16[224,1024]{1,0:T(8,128)(2,1)S(1)} %get-tuple-element.26), channel_id=1, source_target_pairs={{0,3},{4,7},{8,11},{12,15},{16,19},{20,23},{24,27},{28,31}} | collective-permute-start | bytes 1376264 | tf_op jit(solution)/shard_map/ppermute | solution.py:318
  25.7 13.9 %collective-permute-start.10 = (bf16[8,16,512]{2,1,0:T(8,128)(2,1)S(1)}, bf16[8,16,512]{2,1,0:T(8,128)(2,1)S(1)}, u32[]{:S(2)}, u32[]{:S(2)}) collective-permute-start(bf16[8,16,512]{2,1,0:T(8,128)(2,1)S(1)} %get-tuple-element.39), channel_id=1, source_target_pairs={{1,4},{5,0},{9,12},{13,8},{3,6},{7,2},{11,14},{15,10},{17,20},{21,... | collective-permute-start | bytes 393224 | tf_op jit(solution)/shard_map/ppermute | solution.py:327
  27.0 13.9 %collective-permute-start.11 = (bf16[8,16,512]{2,1,0:T(8,128)(2,1)S(1)}, bf16[8,16,512]{2,1,0:T(8,128)(2,1)S(1)}, u32[]{:S(2)}, u32[]{:S(2)}) collective-permute-start(bf16[8,16,512]{2,1,0:T(8,128)(2,1)S(1)} %get-tuple-element.40), channel_id=1, source_target_pairs={{1,8},{5,12},{9,0},{13,4},{3,10},{7,14},{11,2},{15,6},{17,24},{21,... | collective-permute-start | bytes 393224 | tf_op jit(solution)/shard_map/ppermute | solution.py:327
  28.3 1.7 %copy-start.5 = (bf16[256,224]{1,0:T(8,128)(2,1)S(1)}, bf16[256,224]{1,0:T(8,128)(2,1)}, u32[]{:S(2)}) copy-start(bf16[256,224]{1,0:T(8,128)(2,1)} %constant.7.clone.refs_0_) | copy-start | bytes 344068
  32.4 16.9 %collective-permute-start.9 = (bf16[16,16,512]{2,1,0:T(8,128)(2,1)S(1)}, bf16[16,16,512]{2,1,0:T(8,128)(2,1)S(1)}, u32[]{:S(2)}, u32[]{:S(2)}) collective-permute-start(bf16[16,16,512]{2,1,0:T(8,128)(2,1)S(1)} %get-tuple-element.38), channel_id=1, source_target_pairs={{0,1},{1,0},{2,3},{3,2},{4,5},{5,4},{6,7},{7,6},{8,9},{9,8},{10,11... | collective-permute-start | bytes 786440 | tf_op jit(solution)/shard_map/ppermute | solution.py:321
  32.5 18.1 %collective-permute-start.13 = (bf16[16,16,512]{2,1,0:T(8,128)(2,1)S(1)}, bf16[16,16,512]{2,1,0:T(8,128)(2,1)S(1)}, u32[]{:S(2)}, u32[]{:S(2)}) collective-permute-start(bf16[16,16,512]{2,1,0:T(8,128)(2,1)S(1)} %get-tuple-element.42), channel_id=1, source_target_pairs={{0,5},{4,1},{8,13},{12,9},{2,7},{6,3},{10,15},{14,11},{16,21},{20,... | collective-permute-start | bytes 786440 | tf_op jit(solution)/shard_map/ppermute | solution.py:327
  33.8 14.2 %collective-permute-start.12 = (bf16[8,16,512]{2,1,0:T(8,128)(2,1)S(1)}, bf16[8,16,512]{2,1,0:T(8,128)(2,1)S(1)}, u32[]{:S(2)}, u32[]{:S(2)}) collective-permute-start(bf16[8,16,512]{2,1,0:T(8,128)(2,1)S(1)} %get-tuple-element.41), channel_id=1, source_target_pairs={{1,12},{5,8},{9,4},{13,0},{3,14},{7,10},{11,6},{15,2},{17,28},{21,... | collective-permute-start | bytes 393224 | tf_op jit(solution)/shard_map/ppermute | solution.py:327
  39.6 16.0 %collective-permute-start.14 = (bf16[16,16,512]{2,1,0:T(8,128)(2,1)S(1)}, bf16[16,16,512]{2,1,0:T(8,128)(2,1)S(1)}, u32[]{:S(2)}, u32[]{:S(2)}) collective-permute-start(bf16[16,16,512]{2,1,0:T(8,128)(2,1)S(1)} %get-tuple-element.43), channel_id=1, source_target_pairs={{0,9},{4,13},{8,1},{12,5},{2,11},{6,15},{10,3},{14,7},{16,25},{20,... | collective-permute-start | bytes 786440 | tf_op jit(solution)/shard_map/ppermute | solution.py:327
  40.9 21.3 %collective-permute-start.15 = (bf16[16,16,512]{2,1,0:T(8,128)(2,1)S(1)}, bf16[16,16,512]{2,1,0:T(8,128)(2,1)S(1)}, u32[]{:S(2)}, u32[]{:S(2)}) collective-permute-start(bf16[16,16,512]{2,1,0:T(8,128)(2,1)S(1)} %get-tuple-element.44), channel_id=1, source_target_pairs={{0,13},{4,9},{8,5},{12,1},{2,15},{6,11},{10,7},{14,3},{16,29},{20,... | collective-permute-start | bytes 786440 | tf_op jit(solution)/shard_map/ppermute | solution.py:327
  48.1 15.1 %collective-permute-start.6 = (bf16[8,16,512]{2,1,0:T(8,128)(2,1)S(1)}, bf16[8,16,512]{2,1,0:T(8,128)(2,1)S(1)}, u32[]{:S(2)}, u32[]{:S(2)}) collective-permute-start(bf16[8,16,512]{2,1,0:T(8,128)(2,1)S(1)} %get-tuple-element.35), channel_id=1, source_target_pairs={{1,4},{5,0},{9,12},{13,8},{3,6},{7,2},{11,14},{15,10},{17,20},{21,... | collective-permute-start | bytes 393224 | tf_op jit(solution)/shard_map/ppermute | solution.py:327
  49.4 13.8 %collective-permute-start.7 = (bf16[8,16,512]{2,1,0:T(8,128)(2,1)S(1)}, bf16[8,16,512]{2,1,0:T(8,128)(2,1)S(1)}, u32[]{:S(2)}, u32[]{:S(2)}) collective-permute-start(bf16[8,16,512]{2,1,0:T(8,128)(2,1)S(1)} %get-tuple-element.36), channel_id=1, source_target_pairs={{1,8},{5,12},{9,0},{13,4},{3,10},{7,14},{11,2},{15,6},{17,24},{21,... | collective-permute-start | bytes 393224 | tf_op jit(solution)/shard_map/ppermute | solution.py:327
  50.7 12.5 %collective-permute-start.8 = (bf16[8,16,512]{2,1,0:T(8,128)(2,1)S(1)}, bf16[8,16,512]{2,1,0:T(8,128)(2,1)S(1)}, u32[]{:S(2)}, u32[]{:S(2)}) collective-permute-start(bf16[8,16,512]{2,1,0:T(8,128)(2,1)S(1)} %get-tuple-element.37), channel_id=1, source_target_pairs={{1,12},{5,8},{9,4},{13,0},{3,14},{7,10},{11,6},{15,2},{17,28},{21,... | collective-permute-start | bytes 393224 | tf_op jit(solution)/shard_map/ppermute | solution.py:327

commit v14 on v13

--- a/solution.py
+++ b/solution.py
@@ -167,7 +167,7 @@
 
 
 def near_kernel(
-    filt_ref, n0, n1, x0, x1, g0, g1, beam_ref, keep_ref, table_ref, sum_ref, out_ref, pre_ref, cal_ref
+    filt_ref, n0, n1, x0, x1, g0, g1, beam_ref, keep_ref, table_ref, sum_ref, out_ref, cal_ref
 ):
     reach = BLOCK * ROWS
 
@@ -175,16 +175,25 @@
     def _():
         for pol, (n, x, gain) in enumerate(((n0, x0, g0), (n1, x1, g1))):
 
-            def spectra(cyl, pol=pol, n=n, x=x):
-                there = n[:, columns(cyl)]
-                pre_ref[pol * CYL + cyl] = filtered(
-                    [(filt_ref[:, reach : 2 * reach], there), (filt_ref[:, 2 * reach :], x[:reach, columns(cyl)])]
-                )
-                return filtered([(filt_ref[:, :reach], there), (filt_ref[:, reach:], x[: 2 * reach, columns(cyl)])])
+            def spectra(cyl, n=n, x=x):
+                there, here = n[:, columns(cyl)], x[: 2 * reach, columns(cyl)]
+                return filtered([(filt_ref[:, :reach], there), (filt_ref[:, reach:], here)])
 
             emit = adder(sum_ref, keep_ref, sum_ref) if pol else keeper(sum_ref)
             form_powers(spectra, gain, beam_ref, cal_ref, emit)
         place(sum_ref, table_ref[table_ref.shape[0] - 1], out_ref)
+
+
+def ahead_kernel(filt_ref, n0, n1, x0, x1, pre_ref):
+    reach = BLOCK * ROWS
+
+    @pl.when(lax.axis_index("pol") == 1)
+    def _():
+        for pol, (n, x) in enumerate(((n0, x0), (n1, x1))):
+            for cyl in range(CYL):
+                there, here = n[:, columns(cyl)], x[:reach, columns(cyl)]
+                terms = [(filt_ref[:, reach : 2 * reach], there), (filt_ref[:, 2 * reach :], here)]
+                pre_ref[pol * CYL + cyl] = filtered(terms)
 
 
 def far_kernel(
@@ -341,16 +350,6 @@
     keep = keep_flags.reshape(1, -1)
     reach, edge_rows = BLOCK * ROWS, (TAPS - 1 - BLOCK) * ROWS
     blocks = kept // BLOCK
-    table = call(
-        place_table_kernel,
-        jax.ShapeDtypeStruct((n_owner, beams, width), bf16),
-        0,
-        1 << 20,
-        4 << 20,
-        scalars=1,
-        scratch=[pltpu.SMEM((n_owner,), jnp.int32)],
-    )(owner_table)
-    samples, table = lax.optimization_barrier((samples, table))
     x = samples.transpose(0, 2, 1, 3).reshape(samples.shape[0] * 2, CYL * NS)
     x = lax.optimization_barrier(x)
     near_rows, far_rows = call(
@@ -374,25 +373,33 @@
         4 << 20,
         scratch=[pltpu.VMEM((CYL * BLOCK * UPCH, 2 * NS), bf16)],
     )(filt, x, gain, beam_table)
+    table = call(
+        place_table_kernel,
+        jax.ShapeDtypeStruct((n_owner, beams, width), bf16),
+        0,
+        1 << 20,
+        4 << 20,
+        scalars=1,
+        after=1,
+        scratch=[pltpu.SMEM((n_owner,), jnp.int32)],
+    )(owner_table, late_own)
     late_sum, late_last = form(
         functools.partial(late_kernel, blocks), kept, filt, other, gain_other, beam_table, keep, table, late_own
     )
     late = [*rest(functools.partial(place_kernel, 0), kept, late_sum, table), late_last]
     late_got = spread(late, 0)
     common = (gain, gain_other, beam_table, keep, table)
-    near_sum, near_last, pre = form(
-        near_kernel,
-        BLOCK,
-        filt,
-        near1,
-        near0,
-        x,
-        other,
-        *common,
-        more=[jax.ShapeDtypeStruct((2 * CYL, reach, NS), jnp.float32)],
-    )
+    near_sum, near_last = form(near_kernel, BLOCK, filt, near1, near0, x, other, *common)
     near = [*rest(functools.partial(place_kernel, 1), BLOCK, near_sum, table), near_last]
     near_got = spread(near, 1)
+    pre = call(
+        ahead_kernel,
+        jax.ShapeDtypeStruct((2 * CYL, reach, NS), jnp.float32),
+        5,
+        2 * 512 * 1024 * 1024,
+        4 << 20,
+        after=1,
+    )(filt, near1, near0, x, other, near[0])
     block_shape = jax.ShapeDtypeStruct((BLOCK, UPCH, width), bf16)
     far_sum, far_last, far_next = form(far_kernel, BLOCK, edge, far1, far0, *common, pre, more=[block_shape])
     own, *far = rest(

time: 63.6 us -> 62.9 us (0.989)
  waiting for transfers between devices: 26.2 us -> 24.6 us
  local copies, waits for them, and re-layouts: 2.31 us -> 3.2 us
    transpose x1, local copies, waits for them, and re-layouts: 1.08 us -> 2.67 us  [per_device(): x = samples.transpose(0, 2, 1, 3).reshape(samples.shape[0] * 2, CYL * NS)]
    ppermute x4, waiting for transfers between devices: 13.8 us -> 12.2 us  [ahead(): lax.ppermute(part, ('tm', 'pol'), [(i * 2 + source, j * 2 + 1) for i, j i...]
    pallas_call x3, Pallas kernels: 4.91 us -> 4.17 us  [form(): call(body, shape + list(more), len(arrays), 4 * 512 * 1024 * 1024, 4 << 2...]
    pallas_call x0 -> x1, Pallas kernels: none -> 0.72 us  [per_device(): call(ahead_kernel, jax.ShapeDtypeStruct((2 * CYL, reach, NS), jnp.float32...]
    unnamed x15 -> x13, local copies, waits for them, and re-layouts: 1.23 us -> 0.53 us
  transfers between devices with their start and end apart: 16 -> 16, of which waited for: 6 -> 6; matrix products, arithmetic and copies ran while one was open for 0% -> 0% of each run, Pallas kernels for 11% -> 14%
where the time goes in v14:
time: 62.9 us; the launch traced here: 62.6 us
  starting transfers between devices  25.7 us (41%)
  waiting for transfers between devices  24.6 us (39%)
  Pallas kernels  8.65 us (14%)
  local copies, waits for them, and re-layouts  3.2 us (5%)
    ppermute x9, starting transfers between devices, spread(): got.append(lax.ppermute(blocks[k], ('freq', 'pol'), route))  19.6 us
    ppermute x9, waiting for transfers between devices, spread(): got.append(lax.ppermute(blocks[k], ('freq', 'pol'), route))  12.5 us
    ppermute x4, waiting for transfers between devices, ahead(): lax.ppermute(part, ('tm', 'pol'), [(i * 2 + source, j * 2 + 1) for i, j i...  12.2 us
    ppermute x4, starting transfers between devices, ahead(): lax.ppermute(part, ('tm', 'pol'), [(i * 2 + source, j * 2 + 1) for i, j i...  5.17 us
    pallas_call x3, Pallas kernels, form(): call(body, shape + list(more), len(arrays), 4 * 512 * 1024 * 1024, 4 << 2...  4.17 us
    transpose x1, local copies, waits for them, and re-layouts, per_device(): x = samples.transpose(0, 2, 1, 3).reshape(samples.shape[0] * 2, CYL * NS)  2.67 us
    pallas_call x1, Pallas kernels, per_device(): call(place_table_kernel, jax.ShapeDtypeStruct((n_owner, beams, width), bf...  1.54 us
  transfers between devices with their start and end apart: 16, of which 6 were waited for; matrix products, arithmetic and copies ran while one was open for 0% of the time, Pallas kernels for 14%

profile of v14, /device:TPU:11, one launch (start us, length us, event | category | flops | bytes accessed | tf_op | source)
XLA Modules:
  0.0 62.6 jit_solution(9406309069867083665)
XLA Ops:
  0.0 2.7 %copy.9 = bf16[512,2,4,256]{3,2,1,0:T(4,128)(2,1)S(1)} copy(bf16[512,2,4,256]{3,1,2,0:T(2,128)(2,1)} %bitcast.21) | data formatting | bytes 4194304 | tf_op jit(solution)/shard_map/transpose | solution.py:353
  2.7 0.5 copy.10
  3.2 0.0 copy-start.2
  3.2 0.0 copy-start
  3.2 0.0 copy-start.1
  3.2 0.7 %collective-permute-start.5 = (bf16[1024,1024]{1,0:T(8,128)(2,1)S(1)}, bf16[1024,1024]{1,0:T(8,128)(2,1)S(1)}, u32[]{:S(2)}, u32[]{:S(2)}) collective-permute-start(bf16[1024,1024]{1,0:T(8,128)(2,1)S(1)} %bitcast.8), channel_id=1, source_target_pairs={{0,1},{1,0},{2,3},{3,2},{4,5},{5,4},{6,7},{7,6},{8,9},{9,8},{10,11... | collective-permute-start | bytes 6291464 | tf_op jit(solution)/shard_map/ppermute | solution.py:330
  3.9 0.1 shard_map.73
  4.0 1.3 %collective-permute-start.3 = (bf16[256,1024]{1,0:T(8,128)(2,1)S(1)}, bf16[256,1024]{1,0:T(8,128)(2,1)S(1)}, u32[]{:S(2)}, u32[]{:S(2)}) collective-permute-start(bf16[256,1024]{1,0:T(8,128)(2,1)S(1)} %get-tuple-element.23), channel_id=1, source_target_pairs={{1,3},{5,7},{9,11},{13,15},{17,19},{21,23},{25,27},{29,31}} | collective-permute-start | bytes 1572872 | tf_op jit(solution)/shard_map/ppermute | solution.py:327
  5.3 1.3 %collective-permute-start.4 = (bf16[256,1024]{1,0:T(8,128)(2,1)S(1)}, bf16[256,1024]{1,0:T(8,128)(2,1)S(1)}, u32[]{:S(2)}, u32[]{:S(2)}) collective-permute-start(bf16[256,1024]{1,0:T(8,128)(2,1)S(1)} %get-tuple-element.23), channel_id=1, source_target_pairs={{0,3},{4,7},{8,11},{12,15},{16,19},{20,23},{24,27},{28,31}} | collective-permute-start | bytes 1572872 | tf_op jit(solution)/shard_map/ppermute | solution.py:327
  6.6 0.1 collective-permute-start.2
  6.7 0.0 copy-start.4
  6.7 1.3 %collective-permute-start = (bf16[224,1024]{1,0:T(8,128)(2,1)S(1)}, bf16[224,1024]{1,0:T(8,128)(2,1)S(1)}, u32[]{:S(2)}, u32[]{:S(2)}) collective-permute-start(bf16[224,1024]{1,0:T(8,128)(2,1)S(1)} %get-tuple-element.22), channel_id=1, source_target_pairs={{1,3},{5,7},{9,11},{13,15},{17,19},{21,23},{25,27},{29,31}} | collective-permute-start | bytes 1376264 | tf_op jit(solution)/shard_map/ppermute | solution.py:327
  8.1 0.0 copy-start.3
  8.1 1.5 %shard_map.75.refs_9_.refs_1_.refs_7_.refs_5_ = bf16[4,1024,512]{2,1,0:T(8,128)(2,1)S(1)} custom-call(s32[64]{0:T(128)S(1)} %copy-done.4, bf16[256,1024]{1,0:T(8,128)(2,1)S(1)} %shard_map.74.refs_1_.refs_6_), custom_call_target="tpu_custom_call" | custom-call | flops 1048576 | bytes 4194304 | tf_op jit(solution)/shard_map/pallas_call | solution.py:376
  9.6 0.0 collective-permute-done.2.refs_6_.refs_4_.refs_2_
  9.6 1.3 %collective-permute-start.1 = (bf16[224,1024]{1,0:T(8,128)(2,1)S(1)}, bf16[224,1024]{1,0:T(8,128)(2,1)S(1)}, u32[]{:S(2)}, u32[]{:S(2)}) collective-permute-start(bf16[224,1024]{1,0:T(8,128)(2,1)S(1)} %get-tuple-element.22), channel_id=1, source_target_pairs={{0,3},{4,7},{8,11},{12,15},{16,19},{20,23},{24,27},{28,31}} | collective-permute-start | bytes 1376264 | tf_op jit(solution)/shard_map/ppermute | solution.py:327
  10.9 6.7 %collective-permute-done.3.refs_1_ = bf16[256,1024]{1,0:T(8,128)(2,1)S(1)} collective-permute-done((bf16[256,1024]{1,0:T(8,128)(2,1)S(1)}, bf16[256,1024]{1,0:T(8,128)(2,1)S(1)}, u32[]{:S(2)}, u32[]{:S(2)}) %collective-permute-start.3) | collective-permute-done | bytes 524320 | tf_op jit(solution)/shard_map/ppermute | solution.py:327
  17.7 3.7 %collective-permute-done.4.refs_2_ = bf16[256,1024]{1,0:T(8,128)(2,1)S(1)} collective-permute-done((bf16[256,1024]{1,0:T(8,128)(2,1)S(1)}, bf16[256,1024]{1,0:T(8,128)(2,1)S(1)}, u32[]{:S(2)}, u32[]{:S(2)}) %collective-permute-start.4) | collective-permute-done | bytes 524320 | tf_op jit(solution)/shard_map/ppermute | solution.py:327
  21.4 0.0 collective-permute-done.5.refs_4_.refs_1_
  21.4 2.3 %shard_map.76 = (bf16[128,1024]{1,0:T(8,128)(2,1)S(1)}, bf16[8,16,512]{2,1,0:T(8,128)(2,1)S(1)}) custom-call(bf16[256,768]{1,0:T(8,128)(2,1)S(1)} %copy-done, bf16[256,1024]{1,0:T(8,128)(2,1)S(1)} %collective-permute-done.3.refs_1_, bf16[256,1024]{1,0:T(8,128)(2,1)S(1)} %collective-permute-done.4.refs_2_, bf16[1024,1024]{1,0:T(8,128)(2,1)S(1)} %bitcast.11, ...), custom_call_target="tpu_custom_call" | custom-call | flops 2147483648 | bytes 4194304 | tf_op jit(solution)/shard_map/pallas_call | solution.py:342
  23.7 0.6 shard_map.77
  24.3 1.3 %collective-permute-start.10 = (bf16[8,16,512]{2,1,0:T(8,128)(2,1)S(1)}, bf16[8,16,512]{2,1,0:T(8,128)(2,1)S(1)}, u32[]{:S(2)}, u32[]{:S(2)}) collective-permute-start(bf16[8,16,512]{2,1,0:T(8,128)(2,1)S(1)} %get-tuple-element.33), channel_id=1, source_target_pairs={{1,4},{5,0},{9,12},{13,8},{3,6},{7,2},{11,14},{15,10},{17,20},{21,... | collective-permute-start | bytes 393224 | tf_op jit(solution)/shard_map/ppermute | solution.py:336
  25.6 1.3 %collective-permute-start.11 = (bf16[8,16,512]{2,1,0:T(8,128)(2,1)S(1)}, bf16[8,16,512]{2,1,0:T(8,128)(2,1)S(1)}, u32[]{:S(2)}, u32[]{:S(2)}) collective-permute-start(bf16[8,16,512]{2,1,0:T(8,128)(2,1)S(1)} %get-tuple-element.34), channel_id=1, source_target_pairs={{1,8},{5,12},{9,0},{13,4},{3,10},{7,14},{11,2},{15,6},{17,24},{21,... | collective-permute-start | bytes 393224 | tf_op jit(solution)/shard_map/ppermute | solution.py:336
  27.0 0.0 copy-start.5
  27.0 0.7 %shard_map.78.refs_8_ = f32[8,256,256]{2,1,0:T(8,128)S(1)} custom-call(bf16[256,768]{1,0:T(8,128)(2,1)S(1)} %copy-done, bf16[256,1024]{1,0:T(8,128)(2,1)S(1)} %collective-permute-done.3.refs_1_, bf16[256,1024]{1,0:T(8,128)(2,1)S(1)} %collective-permute-done.4.refs_2_, bf16[1024,1024]{1,0:T(8,128)(2,1)S(1)} %bitcast.12, ...), custom_call_target="tpu_custom_call" | custom-call | flops 1073741824 | bytes 4194304 | tf_op jit(solution)/shard_map/pallas_call | solution.py:395
  27.7 0.1 collective-permute-done.refs_1_
  27.8 1.6 %collective-permute-done.1.refs_2_ = bf16[224,1024]{1,0:T(8,128)(2,1)S(1)} collective-permute-done((bf16[224,1024]{1,0:T(8,128)(2,1)S(1)}, bf16[224,1024]{1,0:T(8,128)(2,1)S(1)}, u32[]{:S(2)}, u32[]{:S(2)}) %collective-permute-start.1) | collective-permute-done | bytes 458784 | tf_op jit(solution)/shard_map/ppermute | solution.py:327
  29.4 1.9 %shard_map.79 = (bf16[128,1024]{1,0:T(8,128)(2,1)S(1)}, bf16[8,16,512]{2,1,0:T(8,128)(2,1)S(1)}, bf16[8,16,512]{2,1,0:T(8,128)(2,1)S(1)}) custom-call(bf16[256,224]{1,0:T(8,128)(2,1)S(1)} %copy-done.5, bf16[224,1024]{1,0:T(8,128)(2,1)S(1)} %collective-permute-done.refs_1_, bf16[224,1024]{1,0:T(8,128)(2,1)S(1)} %collective-permute-done.1.refs_2_, ...), custom_call_target="tpu_custom_call" | custom-call | flops 2147483648 | bytes 4194304 | tf_op jit(solution)/shard_map/pallas_call | solution.py:342
  31.3 0.5 shard_map.82
  31.8 0.1 collective-permute-start.9
  31.9 1.3 %collective-permute-start.13 = (bf16[16,16,512]{2,1,0:T(8,128)(2,1)S(1)}, bf16[16,16,512]{2,1,0:T(8,128)(2,1)S(1)}, u32[]{:S(2)}, u32[]{:S(2)}) collective-permute-start(bf16[16,16,512]{2,1,0:T(8,128)(2,1)S(1)} %get-tuple-element.36), channel_id=1, source_target_pairs={{0,5},{4,1},{8,13},{12,9},{2,7},{6,3},{10,15},{14,11},{16,21},{20,... | collective-permute-start | bytes 786440 | tf_op jit(solution)/shard_map/ppermute | solution.py:336
  33.2 5.7 %collective-permute-start.12 = (bf16[8,16,512]{2,1,0:T(8,128)(2,1)S(1)}, bf16[8,16,512]{2,1,0:T(8,128)(2,1)S(1)}, u32[]{:S(2)}, u32[]{:S(2)}) collective-permute-start(bf16[8,16,512]{2,1,0:T(8,128)(2,1)S(1)} %get-tuple-element.35), channel_id=1, source_target_pairs={{1,12},{5,8},{9,4},{13,0},{3,14},{7,10},{11,6},{15,2},{17,28},{21,... | collective-permute-start | bytes 393224 | tf_op jit(solution)/shard_map/ppermute | solution.py:336
  38.9 0.0 collective-permute-done.10.refs_0_
  38.9 1.3 %collective-permute-start.14 = (bf16[16,16,512]{2,1,0:T(8,128)(2,1)S(1)}, bf16[16,16,512]{2,1,0:T(8,128)(2,1)S(1)}, u32[]{:S(2)}, u32[]{:S(2)}) collective-permute-start(bf16[16,16,512]{2,1,0:T(8,128)(2,1)S(1)} %get-tuple-element.37), channel_id=1, source_target_pairs={{0,9},{4,13},{8,1},{12,5},{2,11},{6,15},{10,3},{14,7},{16,25},{20,... | collective-permute-start | bytes 786440 | tf_op jit(solution)/shard_map/ppermute | solution.py:336
  40.2 0.0 collective-permute-done.11.refs_1_
  40.2 1.3 %collective-permute-start.15 = (bf16[16,16,512]{2,1,0:T(8,128)(2,1)S(1)}, bf16[16,16,512]{2,1,0:T(8,128)(2,1)S(1)}, u32[]{:S(2)}, u32[]{:S(2)}) collective-permute-start(bf16[16,16,512]{2,1,0:T(8,128)(2,1)S(1)} %get-tuple-element.38), channel_id=1, source_target_pairs={{0,13},{4,9},{8,5},{12,1},{2,15},{6,11},{10,7},{14,3},{16,29},{20,... | collective-permute-start | bytes 786440 | tf_op jit(solution)/shard_map/ppermute | solution.py:336
  41.5 6.2 %collective-permute-done.12.refs_2_ = bf16[8,16,512]{2,1,0:T(8,128)(2,1)S(1)} collective-permute-done((bf16[8,16,512]{2,1,0:T(8,128)(2,1)S(1)}, bf16[8,16,512]{2,1,0:T(8,128)(2,1)S(1)}, u32[]{:S(2)}, u32[]{:S(2)}) %collective-permute-start.12) | collective-permute-done | bytes 131104 | tf_op jit(solution)/shard_map/ppermute | solution.py:336
  47.7 1.3 %collective-permute-start.6 = (bf16[8,16,512]{2,1,0:T(8,128)(2,1)S(1)}, bf16[8,16,512]{2,1,0:T(8,128)(2,1)S(1)}, u32[]{:S(2)}, u32[]{:S(2)}) collective-permute-start(bf16[8,16,512]{2,1,0:T(8,128)(2,1)S(1)} %get-tuple-element.29), channel_id=1, source_target_pairs={{1,4},{5,0},{9,12},{13,8},{3,6},{7,2},{11,14},{15,10},{17,20},{21,... | collective-permute-start | bytes 393224 | tf_op jit(solution)/shard_map/ppermute | solution.py:336
  49.0 0.0 collective-permute-done.9.own_ref
  49.0 1.3 %collective-permute-start.7 = (bf16[8,16,512]{2,1,0:T(8,128)(2,1)S(1)}, bf16[8,16,512]{2,1,0:T(8,128)(2,1)S(1)}, u32[]{:S(2)}, u32[]{:S(2)}) collective-permute-start(bf16[8,16,512]{2,1,0:T(8,128)(2,1)S(1)} %get-tuple-element.30), channel_id=1, source_target_pairs={{1,8},{5,12},{9,0},{13,4},{3,10},{7,14},{11,2},{15,6},{17,24},{21,... | collective-permute-start | bytes 393224 | tf_op jit(solution)/shard_map/ppermute | solution.py:336
  50.3 0.0 collective-permute-done.13.refs_3_
  50.3 4.9 %collective-permute-start.8 = (bf16[8,16,512]{2,1,0:T(8,128)(2,1)S(1)}, bf16[8,16,512]{2,1,0:T(8,128)(2,1)S(1)}, u32[]{:S(2)}, u32[]{:S(2)}) collective-permute-start(bf16[8,16,512]{2,1,0:T(8,128)(2,1)S(1)} %get-tuple-element.31), channel_id=1, source_target_pairs={{1,12},{5,8},{9,4},{13,0},{3,14},{7,10},{11,6},{15,2},{17,28},{21,... | collective-permute-start | bytes 393224 | tf_op jit(solution)/shard_map/ppermute | solution.py:336
  55.2 0.0 collective-permute-done.14.refs_4_
  55.2 6.2 %collective-permute-done.15.refs_5_ = bf16[16,16,512]{2,1,0:T(8,128)(2,1)S(1)} collective-permute-done((bf16[16,16,512]{2,1,0:T(8,128)(2,1)S(1)}, bf16[16,16,512]{2,1,0:T(8,128)(2,1)S(1)}, u32[]{:S(2)}, u32[]{:S(2)}) %collective-permute-start.15) | collective-permute-done | bytes 262176 | tf_op jit(solution)/shard_map/ppermute | solution.py:336
  61.5 1.0 %shard_map.83.refs_3_ = bf16[16,64,512]{2,1,0:T(8,128)(2,1)} custom-call(bf16[16,16,512]{2,1,0:T(8,128)(2,1)S(1)} %collective-permute-done.9.own_ref, bf16[8,16,512]{2,1,0:T(8,128)(2,1)S(1)} %collective-permute-done.10.refs_0_, bf16[8,16,512]{2,1,0:T(8,128)(2,1)S(1)} %collective-permute-done.11.refs_1_, ...), custom_call_target="tpu_custom_call" | custom-call | bytes 2097152 | tf_op jit(solution)/shard_map/pallas_call | solution.py:421
  62.5 0.0 collective-permute-done.6.refs_0_
  62.5 0.0 collective-permute-done.8.refs_2_
  62.5 0.1 shard_map.84
  (10 shorter events, 0.1 us)
Async XLA Ops:
  3.2 3.4 %copy-start.2 = (f32[1,1,4,2,256]{4,3,2,1,0:T(2,128)S(1)}, f32[1,1,4,2,256]{4,3,2,1,0:T(2,128)}, u32[]{:S(2)}) copy-start(f32[1,1,4,2,256]{4,3,2,1,0:T(2,128)} %param.8) | copy-start | bytes 24580
  3.2 4.8 %copy-start = (bf16[256,768]{1,0:T(8,128)(2,1)S(1)}, bf16[256,768]{1,0:T(8,128)(2,1)}, u32[]{:S(2)}) copy-start(bf16[256,768]{1,0:T(8,128)(2,1)} %constant.6.clone.refs_0_) | copy-start | bytes 1179652
  3.2 4.8 %copy-start.1 = (bf16[512,512]{1,0:T(8,128)(2,1)S(1)}, bf16[512,512]{1,0:T(8,128)(2,1)}, u32[]{:S(2)}) copy-start(bf16[512,512]{1,0:T(8,128)(2,1)} %constant.8.clone.refs_3_.refs_7_.refs_5_) | copy-start | bytes 1572868
  3.2 18.2 %collective-permute-start.5 = (bf16[1024,1024]{1,0:T(8,128)(2,1)S(1)}, bf16[1024,1024]{1,0:T(8,128)(2,1)S(1)}, u32[]{:S(2)}, u32[]{:S(2)}) collective-permute-start(bf16[1024,1024]{1,0:T(8,128)(2,1)S(1)} %bitcast.8), channel_id=1, source_target_pairs={{0,1},{1,0},{2,3},{3,2},{4,5},{5,4},{6,7},{7,6},{8,9},{9,8},{10,11... | collective-permute-start | bytes 6291464 | tf_op jit(solution)/shard_map/ppermute | solution.py:330
  4.0 13.7 %collective-permute-start.3 = (bf16[256,1024]{1,0:T(8,128)(2,1)S(1)}, bf16[256,1024]{1,0:T(8,128)(2,1)S(1)}, u32[]{:S(2)}, u32[]{:S(2)}) collective-permute-start(bf16[256,1024]{1,0:T(8,128)(2,1)S(1)} %get-tuple-element.23), channel_id=1, source_target_pairs={{1,3},{5,7},{9,11},{13,15},{17,19},{21,23},{25,27},{29,31}} | collective-permute-start | bytes 1572872 | tf_op jit(solution)/shard_map/ppermute | solution.py:327
  5.3 16.1 %collective-permute-start.4 = (bf16[256,1024]{1,0:T(8,128)(2,1)S(1)}, bf16[256,1024]{1,0:T(8,128)(2,1)S(1)}, u32[]{:S(2)}, u32[]{:S(2)}) collective-permute-start(bf16[256,1024]{1,0:T(8,128)(2,1)S(1)} %get-tuple-element.23), channel_id=1, source_target_pairs={{0,3},{4,7},{8,11},{12,15},{16,19},{20,23},{24,27},{28,31}} | collective-permute-start | bytes 1572872 | tf_op jit(solution)/shard_map/ppermute | solution.py:327
  6.6 3.0 %collective-permute-start.2 = (f32[4,2,256]{2,1,0:T(2,128)S(1)}, f32[4,2,256]{2,1,0:T(2,128)S(1)}, u32[]{:S(2)}, u32[]{:S(2)}) collective-permute-start(f32[4,2,256]{2,1,0:T(2,128)S(1)} %bitcast.13), channel_id=1, source_target_pairs={{0,1},{1,0},{2,3},{3,2},{4,5},{5,4},{6,7},{7,6},{8,9},{9,8},{10,11... | collective-permute-start | bytes 24584 | tf_op jit(solution)/shard_map/ppermute | solution.py:330
  6.7 1.4 %copy-start.4 = (s32[64]{0:T(128)S(1)}, s32[64]{0:T(128)}, u32[]{:S(2)}) copy-start(s32[64]{0:T(128)} %refs_0_.6) | copy-start | bytes 772
  6.7 21.1 %collective-permute-start = (bf16[224,1024]{1,0:T(8,128)(2,1)S(1)}, bf16[224,1024]{1,0:T(8,128)(2,1)S(1)}, u32[]{:S(2)}, u32[]{:S(2)}) collective-permute-start(bf16[224,1024]{1,0:T(8,128)(2,1)S(1)} %get-tuple-element.22), channel_id=1, source_target_pairs={{1,3},{5,7},{9,11},{13,15},{17,19},{21,23},{25,27},{29,31}} | collective-permute-start | bytes 1376264 | tf_op jit(solution)/shard_map/ppermute | solution.py:327
  8.1 13.4 %copy-start.3 = (s32[1024]{0:T(1024)S(1)}, s32[1024]{0:T(1024)}, u32[]{:S(2)}) copy-start(s32[1024]{0:T(1024)} %param.10) | copy-start | bytes 12292
  9.6 19.8 %collective-permute-start.1 = (bf16[224,1024]{1,0:T(8,128)(2,1)S(1)}, bf16[224,1024]{1,0:T(8,128)(2,1)S(1)}, u32[]{:S(2)}, u32[]{:S(2)}) collective-permute-start(bf16[224,1024]{1,0:T(8,128)(2,1)S(1)} %get-tuple-element.22), channel_id=1, source_target_pairs={{0,3},{4,7},{8,11},{12,15},{16,19},{20,23},{24,27},{28,31}} | collective-permute-start | bytes 1376264 | tf_op jit(solution)/shard_map/ppermute | solution.py:327
  24.3 14.6 %collective-permute-start.10 = (bf16[8,16,512]{2,1,0:T(8,128)(2,1)S(1)}, bf16[8,16,512]{2,1,0:T(8,128)(2,1)S(1)}, u32[]{:S(2)}, u32[]{:S(2)}) collective-permute-start(bf16[8,16,512]{2,1,0:T(8,128)(2,1)S(1)} %get-tuple-element.33), channel_id=1, source_target_pairs={{1,4},{5,0},{9,12},{13,8},{3,6},{7,2},{11,14},{15,10},{17,20},{21,... | collective-permute-start | bytes 393224 | tf_op jit(solution)/shard_map/ppermute | solution.py:336
  25.6 14.6 %collective-permute-start.11 = (bf16[8,16,512]{2,1,0:T(8,128)(2,1)S(1)}, bf16[8,16,512]{2,1,0:T(8,128)(2,1)S(1)}, u32[]{:S(2)}, u32[]{:S(2)}) collective-permute-start(bf16[8,16,512]{2,1,0:T(8,128)(2,1)S(1)} %get-tuple-element.34), channel_id=1, source_target_pairs={{1,8},{5,12},{9,0},{13,4},{3,10},{7,14},{11,2},{15,6},{17,24},{21,... | collective-permute-start | bytes 393224 | tf_op jit(solution)/shard_map/ppermute | solution.py:336
  27.0 2.4 %copy-start.5 = (bf16[256,224]{1,0:T(8,128)(2,1)S(1)}, bf16[256,224]{1,0:T(8,128)(2,1)}, u32[]{:S(2)}) copy-start(bf16[256,224]{1,0:T(8,128)(2,1)} %constant.7.clone.refs_0_) | copy-start | bytes 344068
  31.8 17.2 %collective-permute-start.9 = (bf16[16,16,512]{2,1,0:T(8,128)(2,1)S(1)}, bf16[16,16,512]{2,1,0:T(8,128)(2,1)S(1)}, u32[]{:S(2)}, u32[]{:S(2)}) collective-permute-start(bf16[16,16,512]{2,1,0:T(8,128)(2,1)S(1)} %get-tuple-element.32), channel_id=1, source_target_pairs={{0,1},{1,0},{2,3},{3,2},{4,5},{5,4},{6,7},{7,6},{8,9},{9,8},{10,11... | collective-permute-start | bytes 786440 | tf_op jit(solution)/shard_map/ppermute | solution.py:330
  31.9 18.4 %collective-permute-start.13 = (bf16[16,16,512]{2,1,0:T(8,128)(2,1)S(1)}, bf16[16,16,512]{2,1,0:T(8,128)(2,1)S(1)}, u32[]{:S(2)}, u32[]{:S(2)}) collective-permute-start(bf16[16,16,512]{2,1,0:T(8,128)(2,1)S(1)} %get-tuple-element.36), channel_id=1, source_target_pairs={{0,5},{4,1},{8,13},{12,9},{2,7},{6,3},{10,15},{14,11},{16,21},{20,... | collective-permute-start | bytes 786440 | tf_op jit(solution)/shard_map/ppermute | solution.py:336
  33.2 14.5 %collective-permute-start.12 = (bf16[8,16,512]{2,1,0:T(8,128)(2,1)S(1)}, bf16[8,16,512]{2,1,0:T(8,128)(2,1)S(1)}, u32[]{:S(2)}, u32[]{:S(2)}) collective-permute-start(bf16[8,16,512]{2,1,0:T(8,128)(2,1)S(1)} %get-tuple-element.35), channel_id=1, source_target_pairs={{1,12},{5,8},{9,4},{13,0},{3,14},{7,10},{11,6},{15,2},{17,28},{21,... | collective-permute-start | bytes 393224 | tf_op jit(solution)/shard_map/ppermute | solution.py:336
  38.9 16.3 %collective-permute-start.14 = (bf16[16,16,512]{2,1,0:T(8,128)(2,1)S(1)}, bf16[16,16,512]{2,1,0:T(8,128)(2,1)S(1)}, u32[]{:S(2)}, u32[]{:S(2)}) collective-permute-start(bf16[16,16,512]{2,1,0:T(8,128)(2,1)S(1)} %get-tuple-element.37), channel_id=1, source_target_pairs={{0,9},{4,13},{8,1},{12,5},{2,11},{6,15},{10,3},{14,7},{16,25},{20,... | collective-permute-start | bytes 786440 | tf_op jit(solution)/shard_map/ppermute | solution.py:336
  40.2 21.3 %collective-permute-start.15 = (bf16[16,16,512]{2,1,0:T(8,128)(2,1)S(1)}, bf16[16,16,512]{2,1,0:T(8,128)(2,1)S(1)}, u32[]{:S(2)}, u32[]{:S(2)}) collective-permute-start(bf16[16,16,512]{2,1,0:T(8,128)(2,1)S(1)} %get-tuple-element.38), channel_id=1, source_target_pairs={{0,13},{4,9},{8,5},{12,1},{2,15},{6,11},{10,7},{14,3},{16,29},{20,... | collective-permute-start | bytes 786440 | tf_op jit(solution)/shard_map/ppermute | solution.py:336
  47.7 14.8 %collective-permute-start.6 = (bf16[8,16,512]{2,1,0:T(8,128)(2,1)S(1)}, bf16[8,16,512]{2,1,0:T(8,128)(2,1)S(1)}, u32[]{:S(2)}, u32[]{:S(2)}) collective-permute-start(bf16[8,16,512]{2,1,0:T(8,128)(2,1)S(1)} %get-tuple-element.29), channel_id=1, source_target_pairs={{1,4},{5,0},{9,12},{13,8},{3,6},{7,2},{11,14},{15,10},{17,20},{21,... | collective-permute-start | bytes 393224 | tf_op jit(solution)/shard_map/ppermute | solution.py:336
  49.0 13.5 %collective-permute-start.7 = (bf16[8,16,512]{2,1,0:T(8,128)(2,1)S(1)}, bf16[8,16,512]{2,1,0:T(8,128)(2,1)S(1)}, u32[]{:S(2)}, u32[]{:S(2)}) collective-permute-start(bf16[8,16,512]{2,1,0:T(8,128)(2,1)S(1)} %get-tuple-element.30), channel_id=1, source_target_pairs={{1,8},{5,12},{9,0},{13,4},{3,10},{7,14},{11,2},{15,6},{17,24},{21,... | collective-permute-start | bytes 393224 | tf_op jit(solution)/shard_map/ppermute | solution.py:336
  50.3 12.2 %collective-permute-start.8 = (bf16[8,16,512]{2,1,0:T(8,128)(2,1)S(1)}, bf16[8,16,512]{2,1,0:T(8,128)(2,1)S(1)}, u32[]{:S(2)}, u32[]{:S(2)}) collective-permute-start(bf16[8,16,512]{2,1,0:T(8,128)(2,1)S(1)} %get-tuple-element.31), channel_id=1, source_target_pairs={{1,12},{5,8},{9,4},{13,0},{3,14},{7,10},{11,6},{15,2},{17,28},{21,... | collective-permute-start | bytes 393224 | tf_op jit(solution)/shard_map/ppermute | solution.py:336

commit v15 on v14

--- a/solution.py
+++ b/solution.py
@@ -127,10 +127,9 @@
             place(sum_ref, table_ref[k], out_ref)
 
 
-def halo_rows_kernel(x_ref, near_ref, far_ref):
-    near_at = x_ref.shape[0] - near_ref.shape[0]
-    near_ref[...] = x_ref[near_at:, :]
-    far_ref[...] = x_ref[near_at - far_ref.shape[0] : near_at, :]
+def far_rows_kernel(reach, x_ref, out_ref):
+    at = x_ref.shape[0] - reach - out_ref.shape[0]
+    out_ref[...] = x_ref[at : at + out_ref.shape[0], :]
 
 
 def each_late_block(blocks, filt_ref, x_ref, gain_ref, beam_ref, cal_ref, emitter):
@@ -225,11 +224,22 @@
         own_ref[...] = late_ref[...]
 
 
-def place_table_kernel(owner_ref, out_ref, rank_ref):
-    n_owner = out_ref.shape[0]
-    for owner in range(n_owner):
+def head_kernel(owner_ref, v_ref, table_ref, near_ref, held_ref, rank_ref, sems):
+    count = held_ref.shape[1]
+    strips = NS // LANES
+    copies = [
+        pltpu.make_async_copy(
+            v_ref.at[pl.ds(v_ref.shape[0] - count, count), j // strips, :, pl.ds(j % strips * LANES, LANES)],
+            held_ref.at[j],
+            sems.at[j],
+        )
+        for j in range(CYL * strips)
+    ]
+    for copy in copies:
+        copy.start()
+    for owner in range(table_ref.shape[0]):
         rank_ref[owner] = 0
-    out_ref[...] = jnp.zeros_like(out_ref)
+    table_ref[...] = jnp.zeros_like(table_ref)
     row = lax.broadcasted_iota(jnp.int32, (SET_BEAMS, LANES), 0)
     lane = lax.broadcasted_iota(jnp.int32, (SET_BEAMS, LANES), 1)
 
@@ -242,10 +252,13 @@
         hit = lane - row == column - tile
         rows = pl.ds(pl.multiple_of(index * SET_BEAMS, SET_BEAMS), SET_BEAMS)
         lanes = pl.ds(pl.multiple_of(tile, LANES), LANES)
-        out_ref[lax.axis_index("freq") ^ owner, rows, lanes] = jnp.where(hit, 1.0, 0.0).astype(jnp.bfloat16)
+        table_ref[lax.axis_index("freq") ^ owner, rows, lanes] = jnp.where(hit, 1.0, 0.0).astype(jnp.bfloat16)
         return carry
 
     lax.fori_loop(0, owner_ref.shape[0], step, 0, unroll=4)
+    for j, copy in enumerate(copies):
+        copy.wait()
+        near_ref[:, j * LANES : (j + 1) * LANES] = held_ref[j].reshape(2 * count, LANES)
 
 
 def put(out_ref, sems, blocks):
@@ -350,17 +363,28 @@
     keep = keep_flags.reshape(1, -1)
     reach, edge_rows = BLOCK * ROWS, (TAPS - 1 - BLOCK) * ROWS
     blocks = kept // BLOCK
+    strips = CYL * NS // LANES
+    table, near_rows = pl.pallas_call(
+        head_kernel,
+        out_shape=[jax.ShapeDtypeStruct((n_owner, beams, width), bf16), jax.ShapeDtypeStruct((reach, CYL * NS), bf16)],
+        in_specs=[SMEM, pl.BlockSpec(memory_space=pltpu.HBM)],
+        out_specs=[VMEM, VMEM],
+        scratch_shapes=[
+            pltpu.VMEM((strips, BLOCK * UPCH, 2, LANES), bf16),
+            pltpu.SMEM((n_owner,), jnp.int32),
+            pltpu.SemaphoreType.DMA((strips,)),
+        ],
+        cost_estimate=pl.CostEstimate(flops=1 << 20, bytes_accessed=4 << 20, transcendentals=0),
+        compiler_params=pltpu.CompilerParams(vmem_limit_bytes=24 << 20),
+    )(owner_table, pltpu.with_memory_space_constraint(samples, pltpu.HBM))
+    near0 = ahead(near_rows, 0)
+    near1 = ahead(near_rows, 1)
+    samples, table = lax.optimization_barrier((samples, table))
     x = samples.transpose(0, 2, 1, 3).reshape(samples.shape[0] * 2, CYL * NS)
     x = lax.optimization_barrier(x)
-    near_rows, far_rows = call(
-        halo_rows_kernel,
-        [jax.ShapeDtypeStruct((rows, CYL * NS), bf16) for rows in (reach, edge_rows)],
-        1,
-        0,
-        2 << 20,
+    far_rows = call(
+        functools.partial(far_rows_kernel, reach), jax.ShapeDtypeStruct((edge_rows, CYL * NS), bf16), 1, 0, 1 << 20
     )(x)
-    near0 = ahead(near_rows, 0)
-    near1 = ahead(near_rows, 1)
     other = swap(x)
     gain_other = swap(gain)
     far0 = ahead(far_rows, 0)
@@ -373,16 +397,6 @@
         4 << 20,
         scratch=[pltpu.VMEM((CYL * BLOCK * UPCH, 2 * NS), bf16)],
     )(filt, x, gain, beam_table)
-    table = call(
-        place_table_kernel,
-        jax.ShapeDtypeStruct((n_owner, beams, width), bf16),
-        0,
-        1 << 20,
-        4 << 20,
-        scalars=1,
-        after=1,
-        scratch=[pltpu.SMEM((n_owner,), jnp.int32)],
-    )(owner_table, late_own)
     late_sum, late_last = form(
         functools.partial(late_kernel, blocks), kept, filt, other, gain_other, beam_table, keep, table, late_own
     )

time: 62.9 us -> 64 us (1.017)
  waiting for transfers between devices: 24.6 us -> 26.2 us
  local copies, waits for them, and re-layouts: 3.2 us -> 2.26 us
    transpose x1, local copies, waits for them, and re-layouts: 2.67 us -> 1.08 us  [per_device(): x = samples.transpose(0, 2, 1, 3).reshape(samples.shape[0] * 2, CYL * NS)]
    ppermute x4, waiting for transfers between devices: 12.2 us -> 13.7 us  [ahead(): lax.ppermute(part, ('tm', 'pol'), [(i * 2 + source, j * 2 + 1) for i, j i...]
    unnamed x13 -> x15, local copies, waits for them, and re-layouts: 0.53 us -> 1.18 us
  transfers between devices with their start and end apart: 16 -> 16, of which waited for: 6 -> 6; matrix products, arithmetic and copies ran while one was open for 0% -> 0% of each run, Pallas kernels for 14% -> 11%
where the time goes in v15:
time: 64 us; the launch traced here: 63.6 us
  waiting for transfers between devices  26.2 us (41%)
  starting transfers between devices  25.7 us (40%)
  Pallas kernels  9.13 us (14%)
  local copies, waits for them, and re-layouts  2.26 us (4%)
    ppermute x9, starting transfers between devices, spread(): got.append(lax.ppermute(blocks[k], ('freq', 'pol'), route))  19.6 us
    ppermute x4, waiting for transfers between devices, ahead(): lax.ppermute(part, ('tm', 'pol'), [(i * 2 + source, j * 2 + 1) for i, j i...  13.7 us
    ppermute x9, waiting for transfers between devices, spread(): got.append(lax.ppermute(blocks[k], ('freq', 'pol'), route))  12.5 us
    ppermute x4, starting transfers between devices, ahead(): lax.ppermute(part, ('tm', 'pol'), [(i * 2 + source, j * 2 + 1) for i, j i...  5.16 us
    pallas_call x3, Pallas kernels, form(): call(body, shape + list(more), len(arrays), 4 * 512 * 1024 * 1024, 4 << 2...  4.2 us
    pallas_call x1, Pallas kernels, per_device(): pl.pallas_call(head_kernel, out_shape=[jax.ShapeDtypeStruct((n_owner, bea...  2.01 us
  transfers between devices with their start and end apart: 16, of which 6 were waited for; matrix products, arithmetic and copies ran while one was open for 0% of the time, Pallas kernels for 11%

profile of v15, /device:TPU:11, one launch (start us, length us, event | category | flops | bytes accessed | tf_op | source)
XLA Modules:
  0.0 63.6 jit_solution(7492531238417795795)
XLA Ops:
  0.0 0.7 %copy-done.4 = s32[64]{0:T(128)S(1)} copy-done((s32[64]{0:T(128)S(1)}, s32[64]{0:T(128)}, u32[]{:S(2)}) %copy-start.4) | copy-done | bytes 280
  0.7 2.0 %shard_map.73 = (bf16[4,1024,512]{2,1,0:T(8,128)(2,1)S(1)}, bf16[256,1024]{1,0:T(8,128)(2,1)S(1)}) custom-call(s32[64]{0:T(128)S(1)} %copy-done.4, bf16[512,4,2,256]{3,2,1,0:T(2,128)(2,1)} %bitcast.19), custom_call_target="tpu_custom_call" | custom-call | flops 1048576 | bytes 4194304 | tf_op jit(solution)/shard_map/pallas_call | solution.py:367
  2.7 1.1 %copy.9 = bf16[512,2,4,256]{3,2,1,0:T(4,128)(2,1)S(1)} copy(bf16[512,2,4,256]{3,1,2,0:T(2,128)(2,1)S(1)} %bitcast.20) | data formatting | bytes 4194304 | tf_op jit(solution)/shard_map/transpose | solution.py:383
  3.8 0.0 copy-start.2
  3.8 0.5 copy.10
  4.3 0.0 copy-start
  4.3 0.0 copy-start.1
  4.3 0.7 %collective-permute-start.5 = (bf16[1024,1024]{1,0:T(8,128)(2,1)S(1)}, bf16[1024,1024]{1,0:T(8,128)(2,1)S(1)}, u32[]{:S(2)}, u32[]{:S(2)}) collective-permute-start(bf16[1024,1024]{1,0:T(8,128)(2,1)S(1)} %bitcast.7), channel_id=1, source_target_pairs={{0,1},{1,0},{2,3},{3,2},{4,5},{5,4},{6,7},{7,6},{8,9},{9,8},{10,11... | collective-permute-start | bytes 6291464 | tf_op jit(solution)/shard_map/ppermute | solution.py:343
  5.1 1.3 %collective-permute-start.3 = (bf16[256,1024]{1,0:T(8,128)(2,1)S(1)}, bf16[256,1024]{1,0:T(8,128)(2,1)S(1)}, u32[]{:S(2)}, u32[]{:S(2)}) collective-permute-start(bf16[256,1024]{1,0:T(8,128)(2,1)S(1)} %get-tuple-element.27), channel_id=1, source_target_pairs={{1,3},{5,7},{9,11},{13,15},{17,19},{21,23},{25,27},{29,31}} | collective-permute-start | bytes 1572872 | tf_op jit(solution)/shard_map/ppermute | solution.py:340
  6.3 1.3 %collective-permute-start.4 = (bf16[256,1024]{1,0:T(8,128)(2,1)S(1)}, bf16[256,1024]{1,0:T(8,128)(2,1)S(1)}, u32[]{:S(2)}, u32[]{:S(2)}) collective-permute-start(bf16[256,1024]{1,0:T(8,128)(2,1)S(1)} %get-tuple-element.27), channel_id=1, source_target_pairs={{0,3},{4,7},{8,11},{12,15},{16,19},{20,23},{24,27},{28,31}} | collective-permute-start | bytes 1572872 | tf_op jit(solution)/shard_map/ppermute | solution.py:340
  7.7 0.1 collective-permute-start.2
  7.8 0.0 copy-start.3
  7.8 1.3 %collective-permute-start = (bf16[224,1024]{1,0:T(8,128)(2,1)S(1)}, bf16[224,1024]{1,0:T(8,128)(2,1)S(1)}, u32[]{:S(2)}, u32[]{:S(2)}) collective-permute-start(bf16[224,1024]{1,0:T(8,128)(2,1)S(1)} %shard_map.74), channel_id=1, source_target_pairs={{1,3},{5,7},{9,11},{13,15},{17,19},{21,23},{25,27},{29,31}} | collective-permute-start | bytes 1376264 | tf_op jit(solution)/shard_map/ppermute | solution.py:340
  9.1 0.0 collective-permute-done.2.refs_6_.refs_4_.refs_2_
  9.1 1.3 %collective-permute-start.1 = (bf16[224,1024]{1,0:T(8,128)(2,1)S(1)}, bf16[224,1024]{1,0:T(8,128)(2,1)S(1)}, u32[]{:S(2)}, u32[]{:S(2)}) collective-permute-start(bf16[224,1024]{1,0:T(8,128)(2,1)S(1)} %shard_map.74), channel_id=1, source_target_pairs={{0,3},{4,7},{8,11},{12,15},{16,19},{20,23},{24,27},{28,31}} | collective-permute-start | bytes 1376264 | tf_op jit(solution)/shard_map/ppermute | solution.py:340
  10.4 8.3 %collective-permute-done.3.refs_1_ = bf16[256,1024]{1,0:T(8,128)(2,1)S(1)} collective-permute-done((bf16[256,1024]{1,0:T(8,128)(2,1)S(1)}, bf16[256,1024]{1,0:T(8,128)(2,1)S(1)}, u32[]{:S(2)}, u32[]{:S(2)}) %collective-permute-start.3) | collective-permute-done | bytes 524320 | tf_op jit(solution)/shard_map/ppermute | solution.py:340
  18.7 3.7 %collective-permute-done.4.refs_2_ = bf16[256,1024]{1,0:T(8,128)(2,1)S(1)} collective-permute-done((bf16[256,1024]{1,0:T(8,128)(2,1)S(1)}, bf16[256,1024]{1,0:T(8,128)(2,1)S(1)}, u32[]{:S(2)}, u32[]{:S(2)}) %collective-permute-start.4) | collective-permute-done | bytes 524320 | tf_op jit(solution)/shard_map/ppermute | solution.py:340
  22.5 0.0 collective-permute-done.5.refs_4_.refs_1_
  22.5 2.3 %shard_map.75 = (bf16[128,1024]{1,0:T(8,128)(2,1)S(1)}, bf16[8,16,512]{2,1,0:T(8,128)(2,1)S(1)}) custom-call(bf16[256,768]{1,0:T(8,128)(2,1)S(1)} %copy-done, bf16[256,1024]{1,0:T(8,128)(2,1)S(1)} %collective-permute-done.3.refs_1_, bf16[256,1024]{1,0:T(8,128)(2,1)S(1)} %collective-permute-done.4.refs_2_, bf16[1024,1024]{1,0:T(8,128)(2,1)S(1)} %bitcast.10, ...), custom_call_target="tpu_custom_call" | custom-call | flops 2147483648 | bytes 4194304 | tf_op jit(solution)/shard_map/pallas_call | solution.py:355
  24.7 0.6 shard_map.76
  25.3 1.3 %collective-permute-start.10 = (bf16[8,16,512]{2,1,0:T(8,128)(2,1)S(1)}, bf16[8,16,512]{2,1,0:T(8,128)(2,1)S(1)}, u32[]{:S(2)}, u32[]{:S(2)}) collective-permute-start(bf16[8,16,512]{2,1,0:T(8,128)(2,1)S(1)} %get-tuple-element.37), channel_id=1, source_target_pairs={{1,4},{5,0},{9,12},{13,8},{3,6},{7,2},{11,14},{15,10},{17,20},{21,... | collective-permute-start | bytes 393224 | tf_op jit(solution)/shard_map/ppermute | solution.py:349
  26.6 1.3 %collective-permute-start.11 = (bf16[8,16,512]{2,1,0:T(8,128)(2,1)S(1)}, bf16[8,16,512]{2,1,0:T(8,128)(2,1)S(1)}, u32[]{:S(2)}, u32[]{:S(2)}) collective-permute-start(bf16[8,16,512]{2,1,0:T(8,128)(2,1)S(1)} %get-tuple-element.38), channel_id=1, source_target_pairs={{1,8},{5,12},{9,0},{13,4},{3,10},{7,14},{11,2},{15,6},{17,24},{21,... | collective-permute-start | bytes 393224 | tf_op jit(solution)/shard_map/ppermute | solution.py:349
  28.0 0.0 copy-start.5
  28.0 0.7 %shard_map.77.refs_8_ = f32[8,256,256]{2,1,0:T(8,128)S(1)} custom-call(bf16[256,768]{1,0:T(8,128)(2,1)S(1)} %copy-done, bf16[256,1024]{1,0:T(8,128)(2,1)S(1)} %collective-permute-done.3.refs_1_, bf16[256,1024]{1,0:T(8,128)(2,1)S(1)} %collective-permute-done.4.refs_2_, bf16[1024,1024]{1,0:T(8,128)(2,1)S(1)} %bitcast.11, ...), custom_call_target="tpu_custom_call" | custom-call | flops 1073741824 | bytes 4194304 | tf_op jit(solution)/shard_map/pallas_call | solution.py:409
  28.7 0.1 collective-permute-done.refs_1_
  28.8 1.6 %collective-permute-done.1.refs_2_ = bf16[224,1024]{1,0:T(8,128)(2,1)S(1)} collective-permute-done((bf16[224,1024]{1,0:T(8,128)(2,1)S(1)}, bf16[224,1024]{1,0:T(8,128)(2,1)S(1)}, u32[]{:S(2)}, u32[]{:S(2)}) %collective-permute-start.1) | collective-permute-done | bytes 458784 | tf_op jit(solution)/shard_map/ppermute | solution.py:340
  30.4 1.9 %shard_map.78 = (bf16[128,1024]{1,0:T(8,128)(2,1)S(1)}, bf16[8,16,512]{2,1,0:T(8,128)(2,1)S(1)}, bf16[8,16,512]{2,1,0:T(8,128)(2,1)S(1)}) custom-call(bf16[256,224]{1,0:T(8,128)(2,1)S(1)} %copy-done.5, bf16[224,1024]{1,0:T(8,128)(2,1)S(1)} %collective-permute-done.refs_1_, bf16[224,1024]{1,0:T(8,128)(2,1)S(1)} %collective-permute-done.1.refs_2_, ...), custom_call_target="tpu_custom_call" | custom-call | flops 2147483648 | bytes 4194304 | tf_op jit(solution)/shard_map/pallas_call | solution.py:355
  32.3 0.5 shard_map.82
  32.8 0.1 collective-permute-start.9
  32.9 1.3 %collective-permute-start.13 = (bf16[16,16,512]{2,1,0:T(8,128)(2,1)S(1)}, bf16[16,16,512]{2,1,0:T(8,128)(2,1)S(1)}, u32[]{:S(2)}, u32[]{:S(2)}) collective-permute-start(bf16[16,16,512]{2,1,0:T(8,128)(2,1)S(1)} %get-tuple-element.40), channel_id=1, source_target_pairs={{0,5},{4,1},{8,13},{12,9},{2,7},{6,3},{10,15},{14,11},{16,21},{20,... | collective-permute-start | bytes 786440 | tf_op jit(solution)/shard_map/ppermute | solution.py:349
  34.2 5.7 %collective-permute-start.12 = (bf16[8,16,512]{2,1,0:T(8,128)(2,1)S(1)}, bf16[8,16,512]{2,1,0:T(8,128)(2,1)S(1)}, u32[]{:S(2)}, u32[]{:S(2)}) collective-permute-start(bf16[8,16,512]{2,1,0:T(8,128)(2,1)S(1)} %get-tuple-element.39), channel_id=1, source_target_pairs={{1,12},{5,8},{9,4},{13,0},{3,14},{7,10},{11,6},{15,2},{17,28},{21,... | collective-permute-start | bytes 393224 | tf_op jit(solution)/shard_map/ppermute | solution.py:349
  39.9 0.0 collective-permute-done.10.refs_0_
  39.9 1.3 %collective-permute-start.14 = (bf16[16,16,512]{2,1,0:T(8,128)(2,1)S(1)}, bf16[16,16,512]{2,1,0:T(8,128)(2,1)S(1)}, u32[]{:S(2)}, u32[]{:S(2)}) collective-permute-start(bf16[16,16,512]{2,1,0:T(8,128)(2,1)S(1)} %get-tuple-element.41), channel_id=1, source_target_pairs={{0,9},{4,13},{8,1},{12,5},{2,11},{6,15},{10,3},{14,7},{16,25},{20,... | collective-permute-start | bytes 786440 | tf_op jit(solution)/shard_map/ppermute | solution.py:349
  41.2 0.0 collective-permute-done.11.refs_1_
  41.3 1.3 %collective-permute-start.15 = (bf16[16,16,512]{2,1,0:T(8,128)(2,1)S(1)}, bf16[16,16,512]{2,1,0:T(8,128)(2,1)S(1)}, u32[]{:S(2)}, u32[]{:S(2)}) collective-permute-start(bf16[16,16,512]{2,1,0:T(8,128)(2,1)S(1)} %get-tuple-element.42), channel_id=1, source_target_pairs={{0,13},{4,9},{8,5},{12,1},{2,15},{6,11},{10,7},{14,3},{16,29},{20,... | collective-permute-start | bytes 786440 | tf_op jit(solution)/shard_map/ppermute | solution.py:349
  42.6 6.2 %collective-permute-done.12.refs_2_ = bf16[8,16,512]{2,1,0:T(8,128)(2,1)S(1)} collective-permute-done((bf16[8,16,512]{2,1,0:T(8,128)(2,1)S(1)}, bf16[8,16,512]{2,1,0:T(8,128)(2,1)S(1)}, u32[]{:S(2)}, u32[]{:S(2)}) %collective-permute-start.12) | collective-permute-done | bytes 131104 | tf_op jit(solution)/shard_map/ppermute | solution.py:349
  48.7 1.3 %collective-permute-start.6 = (bf16[8,16,512]{2,1,0:T(8,128)(2,1)S(1)}, bf16[8,16,512]{2,1,0:T(8,128)(2,1)S(1)}, u32[]{:S(2)}, u32[]{:S(2)}) collective-permute-start(bf16[8,16,512]{2,1,0:T(8,128)(2,1)S(1)} %get-tuple-element.33), channel_id=1, source_target_pairs={{1,4},{5,0},{9,12},{13,8},{3,6},{7,2},{11,14},{15,10},{17,20},{21,... | collective-permute-start | bytes 393224 | tf_op jit(solution)/shard_map/ppermute | solution.py:349
  50.0 0.0 collective-permute-done.9.own_ref
  50.0 1.3 %collective-permute-start.7 = (bf16[8,16,512]{2,1,0:T(8,128)(2,1)S(1)}, bf16[8,16,512]{2,1,0:T(8,128)(2,1)S(1)}, u32[]{:S(2)}, u32[]{:S(2)}) collective-permute-start(bf16[8,16,512]{2,1,0:T(8,128)(2,1)S(1)} %get-tuple-element.34), channel_id=1, source_target_pairs={{1,8},{5,12},{9,0},{13,4},{3,10},{7,14},{11,2},{15,6},{17,24},{21,... | collective-permute-start | bytes 393224 | tf_op jit(solution)/shard_map/ppermute | solution.py:349
  51.4 0.0 collective-permute-done.13.refs_3_
  51.4 4.9 %collective-permute-start.8 = (bf16[8,16,512]{2,1,0:T(8,128)(2,1)S(1)}, bf16[8,16,512]{2,1,0:T(8,128)(2,1)S(1)}, u32[]{:S(2)}, u32[]{:S(2)}) collective-permute-start(bf16[8,16,512]{2,1,0:T(8,128)(2,1)S(1)} %get-tuple-element.35), channel_id=1, source_target_pairs={{1,12},{5,8},{9,4},{13,0},{3,14},{7,10},{11,6},{15,2},{17,28},{21,... | collective-permute-start | bytes 393224 | tf_op jit(solution)/shard_map/ppermute | solution.py:349
  56.2 0.0 collective-permute-done.14.refs_4_
  56.3 6.2 %collective-permute-done.15.refs_5_ = bf16[16,16,512]{2,1,0:T(8,128)(2,1)S(1)} collective-permute-done((bf16[16,16,512]{2,1,0:T(8,128)(2,1)S(1)}, bf16[16,16,512]{2,1,0:T(8,128)(2,1)S(1)}, u32[]{:S(2)}, u32[]{:S(2)}) %collective-permute-start.15) | collective-permute-done | bytes 262176 | tf_op jit(solution)/shard_map/ppermute | solution.py:349
  62.5 1.0 %shard_map.83.refs_3_ = bf16[16,64,512]{2,1,0:T(8,128)(2,1)} custom-call(bf16[16,16,512]{2,1,0:T(8,128)(2,1)S(1)} %collective-permute-done.9.own_ref, bf16[8,16,512]{2,1,0:T(8,128)(2,1)S(1)} %collective-permute-done.10.refs_0_, bf16[8,16,512]{2,1,0:T(8,128)(2,1)S(1)} %collective-permute-done.11.refs_1_, ...), custom_call_target="tpu_custom_call" | custom-call | bytes 2097152 | tf_op jit(solution)/shard_map/pallas_call | solution.py:435
  63.5 0.0 collective-permute-done.6.refs_0_
  63.5 0.0 collective-permute-done.7.refs_1_
  63.5 0.0 collective-permute-done.8.refs_2_
  63.5 0.1 shard_map.84
  (12 shorter events, 0.1 us)
Async XLA Ops:
  0.0 0.7 %copy-start.4 = (s32[64]{0:T(128)S(1)}, s32[64]{0:T(128)}, u32[]{:S(2)}) copy-start(s32[64]{0:T(128)} %owner_ref.1) | copy-start | bytes 772
  0.7 2.0 %copy-start.6 = (bf16[1,1,512,4,2,256]{5,4,3,2,1,0:T(2,128)(2,1)S(1)}, bf16[1,1,512,4,2,256]{5,4,3,2,1,0:T(2,128)(2,1)}, u32[]{:S(2)}) copy-start(bf16[1,1,512,4,2,256]{5,4,3,2,1,0:T(2,128)(2,1)} %param.7) | copy-start | bytes 6291460
  3.8 3.9 %copy-start.2 = (f32[1,1,4,2,256]{4,3,2,1,0:T(2,128)S(1)}, f32[1,1,4,2,256]{4,3,2,1,0:T(2,128)}, u32[]{:S(2)}) copy-start(f32[1,1,4,2,256]{4,3,2,1,0:T(2,128)} %param.8) | copy-start | bytes 24580
  4.3 4.8 %copy-start = (bf16[256,768]{1,0:T(8,128)(2,1)S(1)}, bf16[256,768]{1,0:T(8,128)(2,1)}, u32[]{:S(2)}) copy-start(bf16[256,768]{1,0:T(8,128)(2,1)} %constant.6.clone.refs_0_) | copy-start | bytes 1179652
  4.3 4.8 %copy-start.1 = (bf16[512,512]{1,0:T(8,128)(2,1)S(1)}, bf16[512,512]{1,0:T(8,128)(2,1)}, u32[]{:S(2)}) copy-start(bf16[512,512]{1,0:T(8,128)(2,1)} %constant.8.clone.refs_7_.refs_5_.refs_3_) | copy-start | bytes 1572868
  4.3 18.1 %collective-permute-start.5 = (bf16[1024,1024]{1,0:T(8,128)(2,1)S(1)}, bf16[1024,1024]{1,0:T(8,128)(2,1)S(1)}, u32[]{:S(2)}, u32[]{:S(2)}) collective-permute-start(bf16[1024,1024]{1,0:T(8,128)(2,1)S(1)} %bitcast.7), channel_id=1, source_target_pairs={{0,1},{1,0},{2,3},{3,2},{4,5},{5,4},{6,7},{7,6},{8,9},{9,8},{10,11... | collective-permute-start | bytes 6291464 | tf_op jit(solution)/shard_map/ppermute | solution.py:343
  5.1 13.7 %collective-permute-start.3 = (bf16[256,1024]{1,0:T(8,128)(2,1)S(1)}, bf16[256,1024]{1,0:T(8,128)(2,1)S(1)}, u32[]{:S(2)}, u32[]{:S(2)}) collective-permute-start(bf16[256,1024]{1,0:T(8,128)(2,1)S(1)} %get-tuple-element.27), channel_id=1, source_target_pairs={{1,3},{5,7},{9,11},{13,15},{17,19},{21,23},{25,27},{29,31}} | collective-permute-start | bytes 1572872 | tf_op jit(solution)/shard_map/ppermute | solution.py:340
  6.3 16.1 %collective-permute-start.4 = (bf16[256,1024]{1,0:T(8,128)(2,1)S(1)}, bf16[256,1024]{1,0:T(8,128)(2,1)S(1)}, u32[]{:S(2)}, u32[]{:S(2)}) collective-permute-start(bf16[256,1024]{1,0:T(8,128)(2,1)S(1)} %get-tuple-element.27), channel_id=1, source_target_pairs={{0,3},{4,7},{8,11},{12,15},{16,19},{20,23},{24,27},{28,31}} | collective-permute-start | bytes 1572872 | tf_op jit(solution)/shard_map/ppermute | solution.py:340
  7.7 1.5 %collective-permute-start.2 = (f32[4,2,256]{2,1,0:T(2,128)S(1)}, f32[4,2,256]{2,1,0:T(2,128)S(1)}, u32[]{:S(2)}, u32[]{:S(2)}) collective-permute-start(f32[4,2,256]{2,1,0:T(2,128)S(1)} %bitcast.12), channel_id=1, source_target_pairs={{0,1},{1,0},{2,3},{3,2},{4,5},{5,4},{6,7},{7,6},{8,9},{9,8},{10,11... | collective-permute-start | bytes 24584 | tf_op jit(solution)/shard_map/ppermute | solution.py:343
  7.8 14.7 %copy-start.3 = (s32[1024]{0:T(1024)S(1)}, s32[1024]{0:T(1024)}, u32[]{:S(2)}) copy-start(s32[1024]{0:T(1024)} %param.10) | copy-start | bytes 12292
  7.8 21.1 %collective-permute-start = (bf16[224,1024]{1,0:T(8,128)(2,1)S(1)}, bf16[224,1024]{1,0:T(8,128)(2,1)S(1)}, u32[]{:S(2)}, u32[]{:S(2)}) collective-permute-start(bf16[224,1024]{1,0:T(8,128)(2,1)S(1)} %shard_map.74), channel_id=1, source_target_pairs={{1,3},{5,7},{9,11},{13,15},{17,19},{21,23},{25,27},{29,31}} | collective-permute-start | bytes 1376264 | tf_op jit(solution)/shard_map/ppermute | solution.py:340
  9.1 21.3 %collective-permute-start.1 = (bf16[224,1024]{1,0:T(8,128)(2,1)S(1)}, bf16[224,1024]{1,0:T(8,128)(2,1)S(1)}, u32[]{:S(2)}, u32[]{:S(2)}) collective-permute-start(bf16[224,1024]{1,0:T(8,128)(2,1)S(1)} %shard_map.74), channel_id=1, source_target_pairs={{0,3},{4,7},{8,11},{12,15},{16,19},{20,23},{24,27},{28,31}} | collective-permute-start | bytes 1376264 | tf_op jit(solution)/shard_map/ppermute | solution.py:340
  25.3 14.6 %collective-permute-start.10 = (bf16[8,16,512]{2,1,0:T(8,128)(2,1)S(1)}, bf16[8,16,512]{2,1,0:T(8,128)(2,1)S(1)}, u32[]{:S(2)}, u32[]{:S(2)}) collective-permute-start(bf16[8,16,512]{2,1,0:T(8,128)(2,1)S(1)} %get-tuple-element.37), channel_id=1, source_target_pairs={{1,4},{5,0},{9,12},{13,8},{3,6},{7,2},{11,14},{15,10},{17,20},{21,... | collective-permute-start | bytes 393224 | tf_op jit(solution)/shard_map/ppermute | solution.py:349
  26.6 14.6 %collective-permute-start.11 = (bf16[8,16,512]{2,1,0:T(8,128)(2,1)S(1)}, bf16[8,16,512]{2,1,0:T(8,128)(2,1)S(1)}, u32[]{:S(2)}, u32[]{:S(2)}) collective-permute-start(bf16[8,16,512]{2,1,0:T(8,128)(2,1)S(1)} %get-tuple-element.38), channel_id=1, source_target_pairs={{1,8},{5,12},{9,0},{13,4},{3,10},{7,14},{11,2},{15,6},{17,24},{21,... | collective-permute-start | bytes 393224 | tf_op jit(solution)/shard_map/ppermute | solution.py:349
  28.0 2.4 %copy-start.5 = (bf16[256,224]{1,0:T(8,128)(2,1)S(1)}, bf16[256,224]{1,0:T(8,128)(2,1)}, u32[]{:S(2)}) copy-start(bf16[256,224]{1,0:T(8,128)(2,1)} %constant.7.clone.refs_0_) | copy-start | bytes 344068
  32.8 17.2 %collective-permute-start.9 = (bf16[16,16,512]{2,1,0:T(8,128)(2,1)S(1)}, bf16[16,16,512]{2,1,0:T(8,128)(2,1)S(1)}, u32[]{:S(2)}, u32[]{:S(2)}) collective-permute-start(bf16[16,16,512]{2,1,0:T(8,128)(2,1)S(1)} %get-tuple-element.36), channel_id=1, source_target_pairs={{0,1},{1,0},{2,3},{3,2},{4,5},{5,4},{6,7},{7,6},{8,9},{9,8},{10,11... | collective-permute-start | bytes 786440 | tf_op jit(solution)/shard_map/ppermute | solution.py:343
  32.9 18.4 %collective-permute-start.13 = (bf16[16,16,512]{2,1,0:T(8,128)(2,1)S(1)}, bf16[16,16,512]{2,1,0:T(8,128)(2,1)S(1)}, u32[]{:S(2)}, u32[]{:S(2)}) collective-permute-start(bf16[16,16,512]{2,1,0:T(8,128)(2,1)S(1)} %get-tuple-element.40), channel_id=1, source_target_pairs={{0,5},{4,1},{8,13},{12,9},{2,7},{6,3},{10,15},{14,11},{16,21},{20,... | collective-permute-start | bytes 786440 | tf_op jit(solution)/shard_map/ppermute | solution.py:349
  34.2 14.5 %collective-permute-start.12 = (bf16[8,16,512]{2,1,0:T(8,128)(2,1)S(1)}, bf16[8,16,512]{2,1,0:T(8,128)(2,1)S(1)}, u32[]{:S(2)}, u32[]{:S(2)}) collective-permute-start(bf16[8,16,512]{2,1,0:T(8,128)(2,1)S(1)} %get-tuple-element.39), channel_id=1, source_target_pairs={{1,12},{5,8},{9,4},{13,0},{3,14},{7,10},{11,6},{15,2},{17,28},{21,... | collective-permute-start | bytes 393224 | tf_op jit(solution)/shard_map/ppermute | solution.py:349
  39.9 16.3 %collective-permute-start.14 = (bf16[16,16,512]{2,1,0:T(8,128)(2,1)S(1)}, bf16[16,16,512]{2,1,0:T(8,128)(2,1)S(1)}, u32[]{:S(2)}, u32[]{:S(2)}) collective-permute-start(bf16[16,16,512]{2,1,0:T(8,128)(2,1)S(1)} %get-tuple-element.41), channel_id=1, source_target_pairs={{0,9},{4,13},{8,1},{12,5},{2,11},{6,15},{10,3},{14,7},{16,25},{20,... | collective-permute-start | bytes 786440 | tf_op jit(solution)/shard_map/ppermute | solution.py:349
  41.3 21.2 %collective-permute-start.15 = (bf16[16,16,512]{2,1,0:T(8,128)(2,1)S(1)}, bf16[16,16,512]{2,1,0:T(8,128)(2,1)S(1)}, u32[]{:S(2)}, u32[]{:S(2)}) collective-permute-start(bf16[16,16,512]{2,1,0:T(8,128)(2,1)S(1)} %get-tuple-element.42), channel_id=1, source_target_pairs={{0,13},{4,9},{8,5},{12,1},{2,15},{6,11},{10,7},{14,3},{16,29},{20,... | collective-permute-start | bytes 786440 | tf_op jit(solution)/shard_map/ppermute | solution.py:349
  48.7 14.8 %collective-permute-start.6 = (bf16[8,16,512]{2,1,0:T(8,128)(2,1)S(1)}, bf16[8,16,512]{2,1,0:T(8,128)(2,1)S(1)}, u32[]{:S(2)}, u32[]{:S(2)}) collective-permute-start(bf16[8,16,512]{2,1,0:T(8,128)(2,1)S(1)} %get-tuple-element.33), channel_id=1, source_target_pairs={{1,4},{5,0},{9,12},{13,8},{3,6},{7,2},{11,14},{15,10},{17,20},{21,... | collective-permute-start | bytes 393224 | tf_op jit(solution)/shard_map/ppermute | solution.py:349
  50.0 13.5 %collective-permute-start.7 = (bf16[8,16,512]{2,1,0:T(8,128)(2,1)S(1)}, bf16[8,16,512]{2,1,0:T(8,128)(2,1)S(1)}, u32[]{:S(2)}, u32[]{:S(2)}) collective-permute-start(bf16[8,16,512]{2,1,0:T(8,128)(2,1)S(1)} %get-tuple-element.34), channel_id=1, source_target_pairs={{1,8},{5,12},{9,0},{13,4},{3,10},{7,14},{11,2},{15,6},{17,24},{21,... | collective-permute-start | bytes 393224 | tf_op jit(solution)/shard_map/ppermute | solution.py:349
  51.4 12.2 %collective-permute-start.8 = (bf16[8,16,512]{2,1,0:T(8,128)(2,1)S(1)}, bf16[8,16,512]{2,1,0:T(8,128)(2,1)S(1)}, u32[]{:S(2)}, u32[]{:S(2)}) collective-permute-start(bf16[8,16,512]{2,1,0:T(8,128)(2,1)S(1)} %get-tuple-element.35), channel_id=1, source_target_pairs={{1,12},{5,8},{9,4},{13,0},{3,14},{7,10},{11,6},{15,2},{17,28},{21,... | collective-permute-start | bytes 393224 | tf_op jit(solution)/shard_map/ppermute | solution.py:349

commit v16 on v15

--- a/solution.py
+++ b/solution.py
@@ -127,9 +127,14 @@
             place(sum_ref, table_ref[k], out_ref)
 
 
-def far_rows_kernel(reach, x_ref, out_ref):
-    at = x_ref.shape[0] - reach - out_ref.shape[0]
-    out_ref[...] = x_ref[at : at + out_ref.shape[0], :]
+def far_rows_kernel(reach, x_ref, other_ref, out_ref):
+    count = out_ref.shape[0] // 2
+    at = x_ref.shape[0] - reach - count
+
+    @pl.when(lax.axis_index("pol") == 1)
+    def _():
+        out_ref[:count, :] = x_ref[at : at + count, :]
+        out_ref[count:, :] = other_ref[at : at + count, :]
 
 
 def each_late_block(blocks, filt_ref, x_ref, gain_ref, beam_ref, cal_ref, emitter):
@@ -196,14 +201,16 @@
 
 
 def far_kernel(
-    edge_ref, f0, f1, g0, g1, beam_ref, keep_ref, table_ref, pre_ref, sum_ref, out_ref, next_ref, cal_ref
+    edge_ref, far_ref, g0, g1, beam_ref, keep_ref, table_ref, pre_ref, sum_ref, out_ref, next_ref, cal_ref
 ):
     @pl.when(lax.axis_index("pol") == 1)
     def _():
-        for pol, (far_ref, gain) in enumerate(((f0, g0), (f1, g1))):
-
-            def spectra(cyl, pol=pol, far_ref=far_ref):
-                return pre_ref[pol * CYL + cyl] + filtered([(edge_ref[...], far_ref[:, columns(cyl)])])
+        count = far_ref.shape[0] // 2
+        for pol, gain in enumerate((g0, g1)):
+
+            def spectra(cyl, pol=pol):
+                rows = far_ref[pol * count : (pol + 1) * count, columns(cyl)]
+                return pre_ref[pol * CYL + cyl] + filtered([(edge_ref[...], rows)])
 
             emit = adder(sum_ref, keep_ref, sum_ref) if pol else keeper(sum_ref)
             form_powers(spectra, gain, beam_ref, cal_ref, emit)
@@ -224,7 +231,7 @@
         own_ref[...] = late_ref[...]
 
 
-def head_kernel(owner_ref, v_ref, table_ref, near_ref, held_ref, rank_ref, sems):
+def head_kernel(sets_ref, v_ref, table_ref, near_ref, held_ref, owner_ref, rank_ref, sems, sem):
     count = held_ref.shape[1]
     strips = NS // LANES
     copies = [
@@ -235,11 +242,14 @@
         )
         for j in range(CYL * strips)
     ]
+    sets_copy = pltpu.make_async_copy(sets_ref, owner_ref, sem)
+    sets_copy.start()
     for copy in copies:
         copy.start()
     for owner in range(table_ref.shape[0]):
         rank_ref[owner] = 0
     table_ref[...] = jnp.zeros_like(table_ref)
+    sets_copy.wait()
     row = lax.broadcasted_iota(jnp.int32, (SET_BEAMS, LANES), 0)
     lane = lax.broadcasted_iota(jnp.int32, (SET_BEAMS, LANES), 1)
 
@@ -367,28 +377,28 @@
     table, near_rows = pl.pallas_call(
         head_kernel,
         out_shape=[jax.ShapeDtypeStruct((n_owner, beams, width), bf16), jax.ShapeDtypeStruct((reach, CYL * NS), bf16)],
-        in_specs=[SMEM, pl.BlockSpec(memory_space=pltpu.HBM)],
+        in_specs=[pl.BlockSpec(memory_space=pltpu.HBM)] * 2,
         out_specs=[VMEM, VMEM],
         scratch_shapes=[
             pltpu.VMEM((strips, BLOCK * UPCH, 2, LANES), bf16),
+            pltpu.SMEM(owner_table.shape, jnp.int32),
             pltpu.SMEM((n_owner,), jnp.int32),
             pltpu.SemaphoreType.DMA((strips,)),
+            pltpu.SemaphoreType.DMA(()),
         ],
         cost_estimate=pl.CostEstimate(flops=1 << 20, bytes_accessed=4 << 20, transcendentals=0),
         compiler_params=pltpu.CompilerParams(vmem_limit_bytes=24 << 20),
-    )(owner_table, pltpu.with_memory_space_constraint(samples, pltpu.HBM))
+    )(*(pltpu.with_memory_space_constraint(array, pltpu.HBM) for array in (owner_table, samples)))
     near0 = ahead(near_rows, 0)
     near1 = ahead(near_rows, 1)
     samples, table = lax.optimization_barrier((samples, table))
     x = samples.transpose(0, 2, 1, 3).reshape(samples.shape[0] * 2, CYL * NS)
     x = lax.optimization_barrier(x)
-    far_rows = call(
-        functools.partial(far_rows_kernel, reach), jax.ShapeDtypeStruct((edge_rows, CYL * NS), bf16), 1, 0, 1 << 20
-    )(x)
     other = swap(x)
     gain_other = swap(gain)
-    far0 = ahead(far_rows, 0)
-    far1 = ahead(far_rows, 1)
+    shape = jax.ShapeDtypeStruct((2 * edge_rows, CYL * NS), bf16)
+    far_rows = call(functools.partial(far_rows_kernel, reach), shape, 2, 0, 2 << 20)(x, other)
+    far_halo = ahead(far_rows, 1)
     late_own = call(
         functools.partial(late_own_kernel, blocks),
         jax.ShapeDtypeStruct((kept * UPCH, beams), bf16),
@@ -415,7 +425,7 @@
         after=1,
     )(filt, near1, near0, x, other, near[0])
     block_shape = jax.ShapeDtypeStruct((BLOCK, UPCH, width), bf16)
-    far_sum, far_last, far_next = form(far_kernel, BLOCK, edge, far1, far0, *common, pre, more=[block_shape])
+    far_sum, far_last, far_next = form(far_kernel, BLOCK, edge, far_halo, *common, pre, more=[block_shape])
     own, *far = rest(
         far_place_kernel,
         BLOCK,

time: 64 us -> 55.5 us (0.87)
  the two profiles are of different devices: /device:TPU:11 before, /device:TPU:0 now
where the time goes in v16:
time: 55.5 us; the launch traced here: 55.1 us
  starting transfers between devices  29.4 us (53%)
  waiting for transfers between devices  14.2 us (26%)
  Pallas kernels  9.48 us (17%)
  local copies, waits for them, and re-layouts  1.6 us (3%)
    ppermute x9, starting transfers between devices, spread(): got.append(lax.ppermute(blocks[k], ('freq', 'pol'), route))  20.3 us
    ppermute x3, waiting for transfers between devices, ahead(): lax.ppermute(part, ('tm', 'pol'), [(i * 2 + source, j * 2 + 1) for i, j i...  7.47 us
    ppermute x9, waiting for transfers between devices, spread(): got.append(lax.ppermute(blocks[k], ('freq', 'pol'), route))  6.72 us
    ppermute x3, starting transfers between devices, ahead(): lax.ppermute(part, ('tm', 'pol'), [(i * 2 + source, j * 2 + 1) for i, j i...  6.66 us
    pallas_call x3, Pallas kernels, form(): call(body, shape + list(more), len(arrays), 4 * 512 * 1024 * 1024, 4 << 2...  2.74 us
    ppermute x3, starting transfers between devices, swap(): return lax.ppermute(part, 'pol', [(0, 1), (1, 0)])  2.5 us
    pallas_call x1, Pallas kernels, per_device(): call(functools.partial(late_own_kernel, blocks), jax.ShapeDtypeStruct((ke...  2.11 us
    pallas_call x1, Pallas kernels, per_device(): pl.pallas_call(head_kernel, out_shape=[jax.ShapeDtypeStruct((n_owner, bea...  1.9 us
  transfers between devices with their start and end apart: 15, of which 3 were waited for; matrix products, arithmetic and copies ran while one was open for 0% of the time, Pallas kernels for 12%

profile of v16, /device:TPU:0, one launch (start us, length us, event | category | flops | bytes accessed | tf_op | source)
XLA Modules:
  0.0 55.1 jit_solution(1699619407648243014)
XLA Ops:
  0.0 0.0 copy-start.5
  0.0 1.9 %shard_map.73 = (bf16[4,1024,512]{2,1,0:T(8,128)(2,1)S(1)}, bf16[256,1024]{1,0:T(8,128)(2,1)S(1)}) custom-call(s32[64]{0:T(128)} %sets_ref.1, bf16[512,4,2,256]{3,2,1,0:T(2,128)(2,1)} %bitcast.19), custom_call_target="tpu_custom_call" | custom-call | flops 1048576 | bytes 4194304 | tf_op jit(solution)/shard_map/pallas_call | solution.py:377
  1.9 0.0 copy-done.5
  1.9 1.1 %copy.9 = bf16[512,2,4,256]{3,2,1,0:T(4,128)(2,1)S(1)} copy(bf16[512,2,4,256]{3,1,2,0:T(2,128)(2,1)S(1)} %bitcast.20) | data formatting | bytes 4194304 | tf_op jit(solution)/shard_map/transpose | solution.py:395
  3.0 0.5 copy.10
  3.5 0.6 %collective-permute-start = (bf16[1024,1024]{1,0:T(8,128)(2,1)S(1)}, bf16[1024,1024]{1,0:T(8,128)(2,1)S(1)}, u32[]{:S(2)}, u32[]{:S(2)}) collective-permute-start(bf16[1024,1024]{1,0:T(8,128)(2,1)S(1)} %bitcast.7), channel_id=1, source_target_pairs={{0,1},{1,0},{2,3},{3,2},{4,5},{5,4},{6,7},{7,6},{8,9},{9,8},{10,11... | collective-permute-start | bytes 6291464 | tf_op jit(solution)/shard_map/ppermute | solution.py:353
  4.1 0.0 copy-start.2
  4.1 0.8 %collective-permute-start.3 = (bf16[256,1024]{1,0:T(8,128)(2,1)S(1)}, bf16[256,1024]{1,0:T(8,128)(2,1)S(1)}, u32[]{:S(2)}, u32[]{:S(2)}) collective-permute-start(bf16[256,1024]{1,0:T(8,128)(2,1)S(1)} %get-tuple-element.27), channel_id=1, source_target_pairs={{1,3},{5,7},{9,11},{13,15},{17,19},{21,23},{25,27},{29,31}} | collective-permute-start | bytes 1572872 | tf_op jit(solution)/shard_map/ppermute | solution.py:350
  4.9 5.1 %collective-permute-start.4 = (bf16[256,1024]{1,0:T(8,128)(2,1)S(1)}, bf16[256,1024]{1,0:T(8,128)(2,1)S(1)}, u32[]{:S(2)}, u32[]{:S(2)}) collective-permute-start(bf16[256,1024]{1,0:T(8,128)(2,1)S(1)} %get-tuple-element.27), channel_id=1, source_target_pairs={{0,3},{4,7},{8,11},{12,15},{16,19},{20,23},{24,27},{28,31}} | collective-permute-start | bytes 1572872 | tf_op jit(solution)/shard_map/ppermute | solution.py:350
  10.0 0.0 collective-permute-done.refs_1_.refs_4_
  10.1 0.7 %collective-permute-start.1 = (bf16[448,1024]{1,0:T(8,128)(2,1)S(1)}, bf16[448,1024]{1,0:T(8,128)(2,1)S(1)}, u32[]{:S(2)}, u32[]{:S(2)}) collective-permute-start(bf16[448,1024]{1,0:T(8,128)(2,1)S(1)} %shard_map.74), channel_id=1, source_target_pairs={{1,3},{5,7},{9,11},{13,15},{17,19},{21,23},{25,27},{29,31}} | collective-permute-start | bytes 2752520 | tf_op jit(solution)/shard_map/ppermute | solution.py:350
  10.8 0.0 copy-done.2
  10.8 0.0 copy-start.3
  10.8 1.9 %collective-permute-start.2 = (f32[4,2,256]{2,1,0:T(2,128)S(1)}, f32[4,2,256]{2,1,0:T(2,128)S(1)}, u32[]{:S(2)}, u32[]{:S(2)}) collective-permute-start(f32[4,2,256]{2,1,0:T(2,128)S(1)} %bitcast.12), channel_id=1, source_target_pairs={{0,1},{1,0},{2,3},{3,2},{4,5},{5,4},{6,7},{7,6},{8,9},{9,8},{10,11... | collective-permute-start | bytes 24584 | tf_op jit(solution)/shard_map/ppermute | solution.py:353
  12.7 0.0 copy-done
  12.7 0.0 copy-done.1
  12.7 2.1 %shard_map.79.refs_6_ = bf16[256,1024]{1,0:T(8,128)(2,1)S(1)} custom-call(bf16[256,768]{1,0:T(8,128)(2,1)S(1)} %copy-done, bf16[1024,1024]{1,0:T(8,128)(2,1)S(1)} %bitcast.9, f32[4,2,256]{2,1,0:T(2,128)S(1)} %bitcast.13, bf16[512,512]{1,0:T(8,128)(2,1)S(1)} %copy-done.1), custom_call_target="tpu_custom_call" | custom-call | flops 2147483648 | bytes 4194304 | tf_op jit(solution)/shard_map/pallas_call | solution.py:402
  14.8 0.0 collective-permute-done.2.refs_6_.refs_3_.refs_2_
  14.8 0.0 collective-permute-done.3.refs_1_
  14.8 7.5 %collective-permute-done.4.refs_2_ = bf16[256,1024]{1,0:T(8,128)(2,1)S(1)} collective-permute-done((bf16[256,1024]{1,0:T(8,128)(2,1)S(1)}, bf16[256,1024]{1,0:T(8,128)(2,1)S(1)}, u32[]{:S(2)}, u32[]{:S(2)}) %collective-permute-start.4) | collective-permute-done | bytes 524320 | tf_op jit(solution)/shard_map/ppermute | solution.py:350
  22.3 0.0 copy-done.3
  22.3 1.3 %collective-permute-start.10 = (bf16[8,16,512]{2,1,0:T(8,128)(2,1)S(1)}, bf16[8,16,512]{2,1,0:T(8,128)(2,1)S(1)}, u32[]{:S(2)}, u32[]{:S(2)}) collective-permute-start(bf16[8,16,512]{2,1,0:T(8,128)(2,1)S(1)} %get-tuple-element.38), channel_id=1, source_target_pairs={{1,8},{5,12},{9,0},{13,4},{3,10},{7,14},{11,2},{15,6},{17,24},{21,... | collective-permute-start | bytes 393224 | tf_op jit(solution)/shard_map/ppermute | solution.py:359
  23.6 1.3 %collective-permute-start.9 = (bf16[8,16,512]{2,1,0:T(8,128)(2,1)S(1)}, bf16[8,16,512]{2,1,0:T(8,128)(2,1)S(1)}, u32[]{:S(2)}, u32[]{:S(2)}) collective-permute-start(bf16[8,16,512]{2,1,0:T(8,128)(2,1)S(1)} %get-tuple-element.37), channel_id=1, source_target_pairs={{1,4},{5,0},{9,12},{13,8},{3,6},{7,2},{11,14},{15,10},{17,20},{21,... | collective-permute-start | bytes 393224 | tf_op jit(solution)/shard_map/ppermute | solution.py:359
  24.9 2.7 %shard_map.80 = (bf16[256,1024]{1,0:T(8,128)(2,1)S(1)}, bf16[16,16,512]{2,1,0:T(8,128)(2,1)S(1)}) custom-call(bf16[256,768]{1,0:T(8,128)(2,1)S(1)} %copy-done, bf16[1024,1024]{1,0:T(8,128)(2,1)S(1)} %collective-permute-done.refs_1_.refs_4_, f32[4,2,256]{2,1,0:T(2,128)S(1)} %collective-permute-done.2.refs_6_.refs_3_.refs_2_, bf16[512,512]{1,0:T(8,128)(2,1)S(1)} %copy-done.1, ...), custom_call_target="tpu_custom_call" | custom-call | flops 2147483648 | bytes 4194304 | tf_op jit(solution)/shard_map/pallas_call | solution.py:365
  27.6 1.0 %shard_map.81 = (bf16[16,16,512]{2,1,0:T(8,128)(2,1)S(1)}, bf16[16,16,512]{2,1,0:T(8,128)(2,1)S(1)}, bf16[16,16,512]{2,1,0:T(8,128)(2,1)S(1)}) custom-call(bf16[256,1024]{1,0:T(8,128)(2,1)S(1)} %get-tuple-element.31.refs_0_, bf16[4,1024,512]{2,1,0:T(8,128)(2,1)S(1)} %get-tuple-element.26.refs_9_.refs_1_.refs_6_.refs_5_), custom_call_target="tpu_custom_call" | custom-call | flops 536870912 | bytes 4194304 | tf_op jit(solution)/shard_map/pallas_call | solution.py:371
  28.6 2.7 %collective-permute-start.12 = (bf16[16,16,512]{2,1,0:T(8,128)(2,1)S(1)}, bf16[16,16,512]{2,1,0:T(8,128)(2,1)S(1)}, u32[]{:S(2)}, u32[]{:S(2)}) collective-permute-start(bf16[16,16,512]{2,1,0:T(8,128)(2,1)S(1)} %get-tuple-element.40), channel_id=1, source_target_pairs={{0,5},{4,1},{8,13},{12,9},{2,7},{6,3},{10,15},{14,11},{16,21},{20,... | collective-permute-start | bytes 786440 | tf_op jit(solution)/shard_map/ppermute | solution.py:359
  31.4 1.3 %collective-permute-start.13 = (bf16[16,16,512]{2,1,0:T(8,128)(2,1)S(1)}, bf16[16,16,512]{2,1,0:T(8,128)(2,1)S(1)}, u32[]{:S(2)}, u32[]{:S(2)}) collective-permute-start(bf16[16,16,512]{2,1,0:T(8,128)(2,1)S(1)} %get-tuple-element.41), channel_id=1, source_target_pairs={{0,9},{4,13},{8,1},{12,5},{2,11},{6,15},{10,3},{14,7},{16,25},{20,... | collective-permute-start | bytes 786440 | tf_op jit(solution)/shard_map/ppermute | solution.py:359
  32.7 0.0 copy-start.4
  32.7 0.0 collective-permute-done.1.refs_1_
  32.7 1.4 %collective-permute-start.11 = (bf16[8,16,512]{2,1,0:T(8,128)(2,1)S(1)}, bf16[8,16,512]{2,1,0:T(8,128)(2,1)S(1)}, u32[]{:S(2)}, u32[]{:S(2)}) collective-permute-start(bf16[8,16,512]{2,1,0:T(8,128)(2,1)S(1)} %get-tuple-element.39), channel_id=1, source_target_pairs={{1,12},{5,8},{9,4},{13,0},{3,14},{7,10},{11,6},{15,2},{17,28},{21,... | collective-permute-start | bytes 393224 | tf_op jit(solution)/shard_map/ppermute | solution.py:359
  34.2 0.0 copy-done.4
  34.2 0.0 collective-permute-done.10.refs_1_
  34.2 8.4 %collective-permute-start.14 = (bf16[16,16,512]{2,1,0:T(8,128)(2,1)S(1)}, bf16[16,16,512]{2,1,0:T(8,128)(2,1)S(1)}, u32[]{:S(2)}, u32[]{:S(2)}) collective-permute-start(bf16[16,16,512]{2,1,0:T(8,128)(2,1)S(1)} %get-tuple-element.42), channel_id=1, source_target_pairs={{0,13},{4,9},{8,5},{12,1},{2,15},{6,11},{10,7},{14,3},{16,29},{20,... | collective-permute-start | bytes 786440 | tf_op jit(solution)/shard_map/ppermute | solution.py:359
  42.6 0.0 collective-permute-done.9.refs_0_
  42.7 0.1 collective-permute-start.8
  42.7 0.0 collective-permute-done.11.refs_2_
  42.7 1.3 %collective-permute-start.5 = (bf16[8,16,512]{2,1,0:T(8,128)(2,1)S(1)}, bf16[8,16,512]{2,1,0:T(8,128)(2,1)S(1)}, u32[]{:S(2)}, u32[]{:S(2)}) collective-permute-start(bf16[8,16,512]{2,1,0:T(8,128)(2,1)S(1)} %get-tuple-element.33), channel_id=1, source_target_pairs={{1,4},{5,0},{9,12},{13,8},{3,6},{7,2},{11,14},{15,10},{17,20},{21,... | collective-permute-start | bytes 393224 | tf_op jit(solution)/shard_map/ppermute | solution.py:359
  44.0 0.0 collective-permute-done.12.refs_3_
  44.1 1.3 %collective-permute-start.6 = (bf16[8,16,512]{2,1,0:T(8,128)(2,1)S(1)}, bf16[8,16,512]{2,1,0:T(8,128)(2,1)S(1)}, u32[]{:S(2)}, u32[]{:S(2)}) collective-permute-start(bf16[8,16,512]{2,1,0:T(8,128)(2,1)S(1)} %get-tuple-element.34), channel_id=1, source_target_pairs={{1,8},{5,12},{9,0},{13,4},{3,10},{7,14},{11,2},{15,6},{17,24},{21,... | collective-permute-start | bytes 393224 | tf_op jit(solution)/shard_map/ppermute | solution.py:359
  45.4 0.0 collective-permute-done.13.refs_4_
  45.4 1.3 %collective-permute-start.7 = (bf16[8,16,512]{2,1,0:T(8,128)(2,1)S(1)}, bf16[8,16,512]{2,1,0:T(8,128)(2,1)S(1)}, u32[]{:S(2)}, u32[]{:S(2)}) collective-permute-start(bf16[8,16,512]{2,1,0:T(8,128)(2,1)S(1)} %get-tuple-element.35), channel_id=1, source_target_pairs={{1,12},{5,8},{9,4},{13,0},{3,14},{7,10},{11,6},{15,2},{17,28},{21,... | collective-permute-start | bytes 393224 | tf_op jit(solution)/shard_map/ppermute | solution.py:359
  46.7 0.0 collective-permute-done.14.refs_5_
  46.7 0.0 collective-permute-done.8.own_ref
  46.7 0.9 %shard_map.83.refs_3_ = bf16[16,64,512]{2,1,0:T(8,128)(2,1)} custom-call(bf16[16,16,512]{2,1,0:T(8,128)(2,1)S(1)} %collective-permute-done.8.own_ref, bf16[8,16,512]{2,1,0:T(8,128)(2,1)S(1)} %collective-permute-done.9.refs_0_, bf16[8,16,512]{2,1,0:T(8,128)(2,1)S(1)} %collective-permute-done.10.refs_1_, ...), custom_call_target="tpu_custom_call" | custom-call | bytes 2097152 | tf_op jit(solution)/shard_map/pallas_call | solution.py:445
  47.6 4.6 %collective-permute-done.5.refs_0_ = bf16[8,16,512]{2,1,0:T(8,128)(2,1)S(1)} collective-permute-done((bf16[8,16,512]{2,1,0:T(8,128)(2,1)S(1)}, bf16[8,16,512]{2,1,0:T(8,128)(2,1)S(1)}, u32[]{:S(2)}, u32[]{:S(2)}) %collective-permute-start.5) | collective-permute-done | bytes 131104 | tf_op jit(solution)/shard_map/ppermute | solution.py:359
  52.2 0.0 collective-permute-done.6.refs_1_
  52.2 2.1 %collective-permute-done.7.refs_2_ = bf16[8,16,512]{2,1,0:T(8,128)(2,1)S(1)} collective-permute-done((bf16[8,16,512]{2,1,0:T(8,128)(2,1)S(1)}, bf16[8,16,512]{2,1,0:T(8,128)(2,1)S(1)}, u32[]{:S(2)}, u32[]{:S(2)}) %collective-permute-start.7) | collective-permute-done | bytes 131104 | tf_op jit(solution)/shard_map/ppermute | solution.py:359
  54.3 0.8 %shard_map.84 = bf16[16,64,512]{2,1,0:T(8,128)(2,1)} custom-call(bf16[8,16,512]{2,1,0:T(8,128)(2,1)S(1)} %collective-permute-done.5.refs_0_, bf16[8,16,512]{2,1,0:T(8,128)(2,1)S(1)} %collective-permute-done.6.refs_1_, bf16[8,16,512]{2,1,0:T(8,128)(2,1)S(1)} %collective-permute-done.7.refs_2_, ...), custom_call_target="tpu_custom_call", output_to_operand_aliasing={{}: (3, {})} | custom-call | bytes 2097152 | tf_op jit(solution)/shard_map/pallas_call | solution.py:445
  (8 shorter events, 0.1 us)
Async XLA Ops:
  0.0 1.9 %copy-start.5 = (bf16[1,1,512,4,2,256]{5,4,3,2,1,0:T(2,128)(2,1)S(1)}, bf16[1,1,512,4,2,256]{5,4,3,2,1,0:T(2,128)(2,1)}, u32[]{:S(2)}) copy-start(bf16[1,1,512,4,2,256]{5,4,3,2,1,0:T(2,128)(2,1)} %param.7) | copy-start | bytes 6291460
  3.5 6.5 %collective-permute-start = (bf16[1024,1024]{1,0:T(8,128)(2,1)S(1)}, bf16[1024,1024]{1,0:T(8,128)(2,1)S(1)}, u32[]{:S(2)}, u32[]{:S(2)}) collective-permute-start(bf16[1024,1024]{1,0:T(8,128)(2,1)S(1)} %bitcast.7), channel_id=1, source_target_pairs={{0,1},{1,0},{2,3},{3,2},{4,5},{5,4},{6,7},{7,6},{8,9},{9,8},{10,11... | collective-permute-start | bytes 6291464 | tf_op jit(solution)/shard_map/ppermute | solution.py:353
  4.1 6.7 %copy-start.2 = (f32[1,1,4,2,256]{4,3,2,1,0:T(2,128)S(1)}, f32[1,1,4,2,256]{4,3,2,1,0:T(2,128)}, u32[]{:S(2)}) copy-start(f32[1,1,4,2,256]{4,3,2,1,0:T(2,128)} %param.8) | copy-start | bytes 24580
  4.1 8.6 %copy-start = (bf16[256,768]{1,0:T(8,128)(2,1)S(1)}, bf16[256,768]{1,0:T(8,128)(2,1)}, u32[]{:S(2)}) copy-start(bf16[256,768]{1,0:T(8,128)(2,1)} %constant.6.clone.refs_0_) | copy-start | bytes 1179652
  4.1 8.6 %copy-start.1 = (bf16[512,512]{1,0:T(8,128)(2,1)S(1)}, bf16[512,512]{1,0:T(8,128)(2,1)}, u32[]{:S(2)}) copy-start(bf16[512,512]{1,0:T(8,128)(2,1)} %constant.8.clone.refs_7_.refs_4_.refs_3_) | copy-start | bytes 1572868
  4.1 10.7 %collective-permute-start.3 = (bf16[256,1024]{1,0:T(8,128)(2,1)S(1)}, bf16[256,1024]{1,0:T(8,128)(2,1)S(1)}, u32[]{:S(2)}, u32[]{:S(2)}) collective-permute-start(bf16[256,1024]{1,0:T(8,128)(2,1)S(1)} %get-tuple-element.27), channel_id=1, source_target_pairs={{1,3},{5,7},{9,11},{13,15},{17,19},{21,23},{25,27},{29,31}} | collective-permute-start | bytes 1572872 | tf_op jit(solution)/shard_map/ppermute | solution.py:350
  4.9 17.4 %collective-permute-start.4 = (bf16[256,1024]{1,0:T(8,128)(2,1)S(1)}, bf16[256,1024]{1,0:T(8,128)(2,1)S(1)}, u32[]{:S(2)}, u32[]{:S(2)}) collective-permute-start(bf16[256,1024]{1,0:T(8,128)(2,1)S(1)} %get-tuple-element.27), channel_id=1, source_target_pairs={{0,3},{4,7},{8,11},{12,15},{16,19},{20,23},{24,27},{28,31}} | collective-permute-start | bytes 1572872 | tf_op jit(solution)/shard_map/ppermute | solution.py:350
  10.1 22.7 %collective-permute-start.1 = (bf16[448,1024]{1,0:T(8,128)(2,1)S(1)}, bf16[448,1024]{1,0:T(8,128)(2,1)S(1)}, u32[]{:S(2)}, u32[]{:S(2)}) collective-permute-start(bf16[448,1024]{1,0:T(8,128)(2,1)S(1)} %shard_map.74), channel_id=1, source_target_pairs={{1,3},{5,7},{9,11},{13,15},{17,19},{21,23},{25,27},{29,31}} | collective-permute-start | bytes 2752520 | tf_op jit(solution)/shard_map/ppermute | solution.py:350
  10.8 11.5 %copy-start.3 = (s32[1024]{0:T(1024)S(1)}, s32[1024]{0:T(1024)}, u32[]{:S(2)}) copy-start(s32[1024]{0:T(1024)} %param.10) | copy-start | bytes 12292
  10.8 4.0 %collective-permute-start.2 = (f32[4,2,256]{2,1,0:T(2,128)S(1)}, f32[4,2,256]{2,1,0:T(2,128)S(1)}, u32[]{:S(2)}, u32[]{:S(2)}) collective-permute-start(f32[4,2,256]{2,1,0:T(2,128)S(1)} %bitcast.12), channel_id=1, source_target_pairs={{0,1},{1,0},{2,3},{3,2},{4,5},{5,4},{6,7},{7,6},{8,9},{9,8},{10,11... | collective-permute-start | bytes 24584 | tf_op jit(solution)/shard_map/ppermute | solution.py:353
  22.3 11.9 %collective-permute-start.10 = (bf16[8,16,512]{2,1,0:T(8,128)(2,1)S(1)}, bf16[8,16,512]{2,1,0:T(8,128)(2,1)S(1)}, u32[]{:S(2)}, u32[]{:S(2)}) collective-permute-start(bf16[8,16,512]{2,1,0:T(8,128)(2,1)S(1)} %get-tuple-element.38), channel_id=1, source_target_pairs={{1,8},{5,12},{9,0},{13,4},{3,10},{7,14},{11,2},{15,6},{17,24},{21,... | collective-permute-start | bytes 393224 | tf_op jit(solution)/shard_map/ppermute | solution.py:359
  23.6 19.1 %collective-permute-start.9 = (bf16[8,16,512]{2,1,0:T(8,128)(2,1)S(1)}, bf16[8,16,512]{2,1,0:T(8,128)(2,1)S(1)}, u32[]{:S(2)}, u32[]{:S(2)}) collective-permute-start(bf16[8,16,512]{2,1,0:T(8,128)(2,1)S(1)} %get-tuple-element.37), channel_id=1, source_target_pairs={{1,4},{5,0},{9,12},{13,8},{3,6},{7,2},{11,14},{15,10},{17,20},{21,... | collective-permute-start | bytes 393224 | tf_op jit(solution)/shard_map/ppermute | solution.py:359
  28.6 15.4 %collective-permute-start.12 = (bf16[16,16,512]{2,1,0:T(8,128)(2,1)S(1)}, bf16[16,16,512]{2,1,0:T(8,128)(2,1)S(1)}, u32[]{:S(2)}, u32[]{:S(2)}) collective-permute-start(bf16[16,16,512]{2,1,0:T(8,128)(2,1)S(1)} %get-tuple-element.40), channel_id=1, source_target_pairs={{0,5},{4,1},{8,13},{12,9},{2,7},{6,3},{10,15},{14,11},{16,21},{20,... | collective-permute-start | bytes 786440 | tf_op jit(solution)/shard_map/ppermute | solution.py:359
  31.4 14.0 %collective-permute-start.13 = (bf16[16,16,512]{2,1,0:T(8,128)(2,1)S(1)}, bf16[16,16,512]{2,1,0:T(8,128)(2,1)S(1)}, u32[]{:S(2)}, u32[]{:S(2)}) collective-permute-start(bf16[16,16,512]{2,1,0:T(8,128)(2,1)S(1)} %get-tuple-element.41), channel_id=1, source_target_pairs={{0,9},{4,13},{8,1},{12,5},{2,11},{6,15},{10,3},{14,7},{16,25},{20,... | collective-permute-start | bytes 786440 | tf_op jit(solution)/shard_map/ppermute | solution.py:359
  32.7 1.5 %copy-start.4 = (bf16[256,224]{1,0:T(8,128)(2,1)S(1)}, bf16[256,224]{1,0:T(8,128)(2,1)}, u32[]{:S(2)}) copy-start(bf16[256,224]{1,0:T(8,128)(2,1)} %constant.7.clone.refs_0_) | copy-start | bytes 344068
  32.7 10.0 %collective-permute-start.11 = (bf16[8,16,512]{2,1,0:T(8,128)(2,1)S(1)}, bf16[8,16,512]{2,1,0:T(8,128)(2,1)S(1)}, u32[]{:S(2)}, u32[]{:S(2)}) collective-permute-start(bf16[8,16,512]{2,1,0:T(8,128)(2,1)S(1)} %get-tuple-element.39), channel_id=1, source_target_pairs={{1,12},{5,8},{9,4},{13,0},{3,14},{7,10},{11,6},{15,2},{17,28},{21,... | collective-permute-start | bytes 393224 | tf_op jit(solution)/shard_map/ppermute | solution.py:359
  34.2 12.4 %collective-permute-start.14 = (bf16[16,16,512]{2,1,0:T(8,128)(2,1)S(1)}, bf16[16,16,512]{2,1,0:T(8,128)(2,1)S(1)}, u32[]{:S(2)}, u32[]{:S(2)}) collective-permute-start(bf16[16,16,512]{2,1,0:T(8,128)(2,1)S(1)} %get-tuple-element.42), channel_id=1, source_target_pairs={{0,13},{4,9},{8,5},{12,1},{2,15},{6,11},{10,7},{14,3},{16,29},{20,... | collective-permute-start | bytes 786440 | tf_op jit(solution)/shard_map/ppermute | solution.py:359
  42.7 4.0 %collective-permute-start.8 = (bf16[16,16,512]{2,1,0:T(8,128)(2,1)S(1)}, bf16[16,16,512]{2,1,0:T(8,128)(2,1)S(1)}, u32[]{:S(2)}, u32[]{:S(2)}) collective-permute-start(bf16[16,16,512]{2,1,0:T(8,128)(2,1)S(1)} %get-tuple-element.36), channel_id=1, source_target_pairs={{0,1},{1,0},{2,3},{3,2},{4,5},{5,4},{6,7},{7,6},{8,9},{9,8},{10,11... | collective-permute-start | bytes 786440 | tf_op jit(solution)/shard_map/ppermute | solution.py:353
  42.7 9.5 %collective-permute-start.5 = (bf16[8,16,512]{2,1,0:T(8,128)(2,1)S(1)}, bf16[8,16,512]{2,1,0:T(8,128)(2,1)S(1)}, u32[]{:S(2)}, u32[]{:S(2)}) collective-permute-start(bf16[8,16,512]{2,1,0:T(8,128)(2,1)S(1)} %get-tuple-element.33), channel_id=1, source_target_pairs={{1,4},{5,0},{9,12},{13,8},{3,6},{7,2},{11,14},{15,10},{17,20},{21,... | collective-permute-start | bytes 393224 | tf_op jit(solution)/shard_map/ppermute | solution.py:359
  44.1 8.2 %collective-permute-start.6 = (bf16[8,16,512]{2,1,0:T(8,128)(2,1)S(1)}, bf16[8,16,512]{2,1,0:T(8,128)(2,1)S(1)}, u32[]{:S(2)}, u32[]{:S(2)}) collective-permute-start(bf16[8,16,512]{2,1,0:T(8,128)(2,1)S(1)} %get-tuple-element.34), channel_id=1, source_target_pairs={{1,8},{5,12},{9,0},{13,4},{3,10},{7,14},{11,2},{15,6},{17,24},{21,... | collective-permute-start | bytes 393224 | tf_op jit(solution)/shard_map/ppermute | solution.py:359
  45.4 8.9 %collective-permute-start.7 = (bf16[8,16,512]{2,1,0:T(8,128)(2,1)S(1)}, bf16[8,16,512]{2,1,0:T(8,128)(2,1)S(1)}, u32[]{:S(2)}, u32[]{:S(2)}) collective-permute-start(bf16[8,16,512]{2,1,0:T(8,128)(2,1)S(1)} %get-tuple-element.35), channel_id=1, source_target_pairs={{1,12},{5,8},{9,4},{13,0},{3,14},{7,10},{11,6},{15,2},{17,28},{21,... | collective-permute-start | bytes 393224 | tf_op jit(solution)/shard_map/ppermute | solution.py:359

commit v17 on v16

--- a/solution.py
+++ b/solution.py
@@ -127,46 +127,61 @@
             place(sum_ref, table_ref[k], out_ref)
 
 
-def far_rows_kernel(reach, x_ref, other_ref, out_ref):
+def first_rows_kernel(x_ref, out_ref):
+    out_ref[...] = x_ref[: out_ref.shape[0], :]
+
+
+def far_rows_kernel(x_ref, other_ref, out_ref):
     count = out_ref.shape[0] // 2
-    at = x_ref.shape[0] - reach - count
-
-    @pl.when(lax.axis_index("pol") == 1)
-    def _():
-        out_ref[:count, :] = x_ref[at : at + count, :]
-        out_ref[count:, :] = other_ref[at : at + count, :]
-
-
-def each_late_block(blocks, filt_ref, x_ref, gain_ref, beam_ref, cal_ref, emitter):
-    def step(block, carry):
-        first = pl.multiple_of(block * BLOCK * ROWS, BLOCK * ROWS)
-        rows = pl.ds(first, (TAPS + BLOCK) * ROWS)
-
-        def spectra(cyl):
-            return filtered([(filt_ref[...], x_ref[rows, columns(cyl)])])
-
-        at = pl.multiple_of(block * BLOCK * UPCH, BLOCK * UPCH)
-        form_powers(spectra, gain_ref, beam_ref, cal_ref, emitter(at))
-        return carry
-
-    lax.fori_loop(0, blocks, step, 0)
-
-
-def late_own_kernel(blocks, filt_ref, x_ref, gain_ref, beam_ref, out_ref, cal_ref):
-    @pl.when(lax.axis_index("pol") == 0)
-    def _():
-        each_late_block(blocks, filt_ref, x_ref, gain_ref, beam_ref, cal_ref, lambda at: keeper(out_ref, at))
+    at = x_ref.shape[0] - count
+
+    @pl.when(lax.axis_index("pol") == 1)
+    def _():
+        out_ref[:count, :] = x_ref[at:, :]
+        out_ref[count:, :] = other_ref[at:, :]
+
+
+def late_spectra(block, filt_ref, x_ref, near_ref):
+    first = block * BLOCK * ROWS
+    depth = (TAPS + BLOCK) * ROWS
+    here = min(depth, x_ref.shape[0] - first)
+
+    def spectra(cyl):
+        terms = [(filt_ref[:, :here], x_ref[first : first + here, columns(cyl)])]
+        if here < depth:
+            terms.append((filt_ref[:, here:], near_ref[: depth - here, columns(cyl)]))
+        return filtered(terms)
+
+    return spectra
+
+
+def late_own_kernel(filt_ref, x_ref, near_ref, gain_ref, beam_ref, out_ref, cal_ref):
+    @pl.when(lax.axis_index("pol") == 0)
+    def _():
+        for block in range(out_ref.shape[0] // (BLOCK * UPCH)):
+            spectra = late_spectra(block, filt_ref, x_ref, near_ref)
+            form_powers(spectra, gain_ref, beam_ref, cal_ref, keeper(out_ref, block * BLOCK * UPCH))
+
+
+def late_first_kernel(filt_ref, x_ref, gain_ref, beam_ref, keep_ref, power_ref, sum_ref, cal_ref):
+    @pl.when(lax.axis_index("pol") == 0)
+    def _():
+        spectra = late_spectra(0, filt_ref, x_ref, None)
+        form_powers(spectra, gain_ref, beam_ref, cal_ref, adder(power_ref, keep_ref, sum_ref))
 
 
 def late_kernel(
-    blocks, filt_ref, x_ref, gain_ref, beam_ref, keep_ref, table_ref, power_ref, sum_ref, out_ref, cal_ref
+    filt_ref, x_ref, near_ref, gain_ref, beam_ref, keep_ref, table_ref, power_ref, first_ref, sum_ref, out_ref, cal_ref
 ):
-    @pl.when(lax.axis_index("pol") == 0)
-    def _():
-        def emitter(at):
-            return adder(power_ref, keep_ref, sum_ref, at)
-
-        each_late_block(blocks, filt_ref, x_ref, gain_ref, beam_ref, cal_ref, emitter)
+    done = first_ref.shape[0]
+
+    @pl.when(lax.axis_index("pol") == 0)
+    def _():
+        sum_ref[:done, :] = first_ref[...]
+        for block in range(done // (BLOCK * UPCH), sum_ref.shape[0] // (BLOCK * UPCH)):
+            spectra = late_spectra(block, filt_ref, x_ref, near_ref)
+            emit = adder(power_ref, keep_ref, sum_ref, block * BLOCK * UPCH)
+            form_powers(spectra, gain_ref, beam_ref, cal_ref, emit)
         place(sum_ref, table_ref[table_ref.shape[0] - 1], out_ref)
 
 
@@ -372,7 +387,6 @@
 
     keep = keep_flags.reshape(1, -1)
     reach, edge_rows = BLOCK * ROWS, (TAPS - 1 - BLOCK) * ROWS
-    blocks = kept // BLOCK
     strips = CYL * NS // LANES
     table, near_rows = pl.pallas_call(
         head_kernel,
@@ -392,24 +406,36 @@
     near0 = ahead(near_rows, 0)
     near1 = ahead(near_rows, 1)
     samples, table = lax.optimization_barrier((samples, table))
-    x = samples.transpose(0, 2, 1, 3).reshape(samples.shape[0] * 2, CYL * NS)
-    x = lax.optimization_barrier(x)
+    rows = samples.transpose(0, 2, 1, 3).reshape(-1, CYL * NS)
+    rows = lax.optimization_barrier(rows)
+    shape = jax.ShapeDtypeStruct((rows.shape[0] - reach, CYL * NS), bf16)
+    x = call(first_rows_kernel, shape, 1, 0, 3 << 20)(rows)
     other = swap(x)
+    other_near = swap(near_rows)
     gain_other = swap(gain)
-    shape = jax.ShapeDtypeStruct((2 * edge_rows, CYL * NS), bf16)
-    far_rows = call(functools.partial(far_rows_kernel, reach), shape, 2, 0, 2 << 20)(x, other)
-    far_halo = ahead(far_rows, 1)
+    cal = pltpu.VMEM((CYL * BLOCK * UPCH, 2 * NS), bf16)
     late_own = call(
-        functools.partial(late_own_kernel, blocks),
+        late_own_kernel,
         jax.ShapeDtypeStruct((kept * UPCH, beams), bf16),
-        4,
+        5,
         4 * 512 * 1024 * 1024,
         4 << 20,
-        scratch=[pltpu.VMEM((CYL * BLOCK * UPCH, 2 * NS), bf16)],
-    )(filt, x, gain, beam_table)
+        scratch=[cal],
+    )(filt, x, near_rows, gain, beam_table)
+    late_first = call(
+        late_first_kernel,
+        jax.ShapeDtypeStruct((BLOCK * UPCH, beams), bf16),
+        6,
+        2 * 512 * 1024 * 1024,
+        4 << 20,
+        scratch=[cal],
+    )(filt, other, gain_other, beam_table, keep, late_own)
     late_sum, late_last = form(
-        functools.partial(late_kernel, blocks), kept, filt, other, gain_other, beam_table, keep, table, late_own
+        late_kernel, kept, filt, other, other_near, gain_other, beam_table, keep, table, late_own, late_first
     )
+    shape = jax.ShapeDtypeStruct((2 * edge_rows, CYL * NS), bf16)
+    far_rows = call(far_rows_kernel, shape, 2, 0, 2 << 20)(x, other)
+    far_halo = ahead(far_rows, 1)
     late = [*rest(functools.partial(place_kernel, 0), kept, late_sum, table), late_last]
     late_got = spread(late, 0)
     common = (gain, gain_other, beam_table, keep, table)

time: 55.5 us -> 60.6 us (1.092)
  waiting for transfers between devices: 14.2 us -> 23.5 us
  starting transfers between devices: 29.4 us -> 25.5 us
    ppermute x9, waiting for transfers between devices: 6.72 us -> 16.6 us  [spread(): got.append(lax.ppermute(blocks[k], ('freq', 'pol'), route))]
    ppermute x3, waiting for transfers between devices: 7.47 us -> 3.94 us  [ahead(): lax.ppermute(part, ('tm', 'pol'), [(i * 2 + source, j * 2 + 1) for i, j i...]
    ppermute x3 -> x4, waiting for transfers between devices: 0.01 us -> 2.97 us  [swap(): return lax.ppermute(part, 'pol', [(0, 1), (1, 0)])]
    ppermute x9, starting transfers between devices: 20.3 us -> 17.6 us  [spread(): got.append(lax.ppermute(blocks[k], ('freq', 'pol'), route))]
    ppermute x3 -> x4, starting transfers between devices: 2.5 us -> 0.78 us  [swap(): return lax.ppermute(part, 'pol', [(0, 1), (1, 0)])]
    pallas_call x3, Pallas kernels: 2.74 us -> 1.49 us  [form(): call(body, shape + list(more), len(arrays), 4 * 512 * 1024 * 1024, 4 << 2...]
    pallas_call x2 -> x4, Pallas kernels: 2.12 us -> 3.16 us  [the longest x1 1.91 us: per_device(): call(late_own_kernel, jax.ShapeDtypeStruct((kept * UPCH, beams), bf16), 5...]
  transfers between devices with their start and end apart: 15 -> 16, of which waited for: 3 -> 7; matrix products, arithmetic and copies ran while one was open for 0% -> 0% of each run, Pallas kernels for 12% -> 11%
where the time goes in v17:
time: 60.6 us; the launch traced here: 60.2 us
  starting transfers between devices  25.5 us (42%)
  waiting for transfers between devices  23.5 us (39%)
  Pallas kernels  9.21 us (15%)
  local copies, waits for them, and re-layouts  1.61 us (3%)
    ppermute x9, starting transfers between devices, spread(): got.append(lax.ppermute(blocks[k], ('freq', 'pol'), route))  17.6 us
    ppermute x9, waiting for transfers between devices, spread(): got.append(lax.ppermute(blocks[k], ('freq', 'pol'), route))  16.6 us
    ppermute x3, starting transfers between devices, ahead(): lax.ppermute(part, ('tm', 'pol'), [(i * 2 + source, j * 2 + 1) for i, j i...  7.17 us
    ppermute x3, waiting for transfers between devices, ahead(): lax.ppermute(part, ('tm', 'pol'), [(i * 2 + source, j * 2 + 1) for i, j i...  3.94 us
    ppermute x4, waiting for transfers between devices, swap(): return lax.ppermute(part, 'pol', [(0, 1), (1, 0)])  2.97 us
    pallas_call x1, Pallas kernels, per_device(): call(late_own_kernel, jax.ShapeDtypeStruct((kept * UPCH, beams), bf16), 5...  1.91 us
    pallas_call x1, Pallas kernels, per_device(): pl.pallas_call(head_kernel, out_shape=[jax.ShapeDtypeStruct((n_owner, bea...  1.9 us
    pallas_call x2, Pallas kernels, gather(): pl.pallas_call(functools.partial(body, n_owner), out_shape=out_shape, in_...  1.64 us
  transfers between devices with their start and end apart: 16, of which 7 were waited for; matrix products, arithmetic and copies ran while one was open for 0% of the time, Pallas kernels for 11%

profile of v17, /device:TPU:0, one launch (start us, length us, event | category | flops | bytes accessed | tf_op | source)
XLA Modules:
  0.0 60.2 jit_solution(11440236620550829296)
XLA Ops:
  0.0 1.9 %shard_map.73 = (bf16[4,1024,512]{2,1,0:T(8,128)(2,1)S(1)}, bf16[256,1024]{1,0:T(8,128)(2,1)S(1)}) custom-call(s32[64]{0:T(128)} %sets_ref.1, bf16[512,4,2,256]{3,2,1,0:T(2,128)(2,1)} %bitcast.16), custom_call_target="tpu_custom_call" | custom-call | flops 1048576 | bytes 4194304 | tf_op jit(solution)/shard_map/pallas_call | solution.py:391
  1.9 0.0 copy-done.5
  1.9 1.1 %copy.9 = bf16[512,2,4,256]{3,2,1,0:T(4,128)(2,1)S(1)} copy(bf16[512,2,4,256]{3,1,2,0:T(2,128)(2,1)S(1)} %bitcast.17) | data formatting | bytes 4194304 | tf_op jit(solution)/shard_map/transpose | solution.py:409
  3.0 0.5 copy.10
  3.5 0.1 shard_map.74.refs_0_.refs_3_.refs_1_
  3.6 0.0 copy-start.3
  3.6 0.0 copy-start
  3.6 0.0 copy-start.1
  3.7 0.6 collective-permute-start
  4.2 0.1 collective-permute-start.5
  4.3 3.0 %collective-permute-done.refs_1_.refs_4_ = bf16[768,1024]{1,0:T(8,128)(2,1)S(1)} collective-permute-done((bf16[768,1024]{1,0:T(8,128)(2,1)S(1)}, bf16[768,1024]{1,0:T(8,128)(2,1)S(1)}, u32[]{:S(2)}, u32[]{:S(2)}) %collective-permute-start) | collective-permute-done | bytes 1572896 | tf_op jit(solution)/shard_map/ppermute | solution.py:368
  7.3 0.7 %collective-permute-start.1 = (bf16[448,1024]{1,0:T(8,128)(2,1)S(1)}, bf16[448,1024]{1,0:T(8,128)(2,1)S(1)}, u32[]{:S(2)}, u32[]{:S(2)}) collective-permute-start(bf16[448,1024]{1,0:T(8,128)(2,1)S(1)} %shard_map.75), channel_id=1, source_target_pairs={{1,3},{5,7},{9,11},{13,15},{17,19},{21,23},{25,27},{29,31}} | collective-permute-start | bytes 2752520 | tf_op jit(solution)/shard_map/ppermute | solution.py:365
  8.0 0.7 %collective-permute-start.3 = (bf16[256,1024]{1,0:T(8,128)(2,1)S(1)}, bf16[256,1024]{1,0:T(8,128)(2,1)S(1)}, u32[]{:S(2)}, u32[]{:S(2)}) collective-permute-start(bf16[256,1024]{1,0:T(8,128)(2,1)S(1)} %get-tuple-element.27.refs_2_), channel_id=1, source_target_pairs={{1,3},{5,7},{9,11},{13,15},{17,19},{21,23},{25,27},{29,31}} | collective-permute-start | bytes 1572872 | tf_op jit(solution)/shard_map/ppermute | solution.py:365
  8.7 5.8 %collective-permute-start.4 = (bf16[256,1024]{1,0:T(8,128)(2,1)S(1)}, bf16[256,1024]{1,0:T(8,128)(2,1)S(1)}, u32[]{:S(2)}, u32[]{:S(2)}) collective-permute-start(bf16[256,1024]{1,0:T(8,128)(2,1)S(1)} %get-tuple-element.27.refs_2_), channel_id=1, source_target_pairs={{0,3},{4,7},{8,11},{12,15},{16,19},{20,23},{24,27},{28,31}} | collective-permute-start | bytes 1572872 | tf_op jit(solution)/shard_map/ppermute | solution.py:365
  14.5 0.0 copy-start.2
  14.5 0.1 collective-permute-start.2
  14.6 1.9 %shard_map.80.refs_5_.refs_7_ = bf16[256,1024]{1,0:T(8,128)(2,1)S(1)} custom-call(bf16[256,768]{1,0:T(8,128)(2,1)S(1)} %copy-done, bf16[768,1024]{1,0:T(8,128)(2,1)S(1)} %shard_map.74.refs_0_.refs_3_.refs_1_, bf16[256,1024]{1,0:T(8,128)(2,1)S(1)} %get-tuple-element.27.refs_2_, f32[4,2,256]{2,1,0:T(2,128)S(1)} %bitcast.13, bf16[512,512]{1,0:T(8,128)(2,1)S(1)} %copy-done.1), custom_call_target="tpu_custom_call" | custom-call | flops 2147483648 | bytes 4194304 | tf_op jit(solution)/shard_map/pallas_call | solution.py:417
  16.5 0.0 collective-permute-done.2.refs_6_.refs_3_.refs_2_
  16.5 1.1 %shard_map.81.refs_8_ = bf16[128,1024]{1,0:T(8,128)(2,1)S(1)} custom-call(bf16[256,768]{1,0:T(8,128)(2,1)S(1)} %copy-done, bf16[768,1024]{1,0:T(8,128)(2,1)S(1)} %collective-permute-done.refs_1_.refs_4_, f32[4,2,256]{2,1,0:T(2,128)S(1)} %collective-permute-done.2.refs_6_.refs_3_.refs_2_, bf16[512,512]{1,0:T(8,128)(2,1)S(1)} %copy-done.1, ...), custom_call_target="tpu_custom_call" | custom-call | flops 1073741824 | bytes 4194304 | tf_op jit(solution)/shard_map/pallas_call | solution.py:425
  17.7 0.0 collective-permute-done.5.refs_2_
  17.7 1.5 %shard_map.82 = (bf16[256,1024]{1,0:T(8,128)(2,1)S(1)}, bf16[16,16,512]{2,1,0:T(8,128)(2,1)S(1)}) custom-call(bf16[256,768]{1,0:T(8,128)(2,1)S(1)} %copy-done, bf16[768,1024]{1,0:T(8,128)(2,1)S(1)} %collective-permute-done.refs_1_.refs_4_, bf16[256,1024]{1,0:T(8,128)(2,1)S(1)} %collective-permute-done.5.refs_2_, ...), custom_call_target="tpu_custom_call" | custom-call | flops 2147483648 | bytes 4194304 | tf_op jit(solution)/shard_map/pallas_call | solution.py:380
  19.1 1.0 %shard_map.83 = (bf16[16,16,512]{2,1,0:T(8,128)(2,1)S(1)}, bf16[16,16,512]{2,1,0:T(8,128)(2,1)S(1)}, bf16[16,16,512]{2,1,0:T(8,128)(2,1)S(1)}) custom-call(bf16[256,1024]{1,0:T(8,128)(2,1)S(1)} %get-tuple-element.31.refs_0_, bf16[4,1024,512]{2,1,0:T(8,128)(2,1)S(1)} %get-tuple-element.26.refs_9_.refs_1_.refs_6_), custom_call_target="tpu_custom_call" | custom-call | flops 536870912 | bytes 4194304 | tf_op jit(solution)/shard_map/pallas_call | solution.py:386
  20.1 1.3 %collective-permute-start.13 = (bf16[16,16,512]{2,1,0:T(8,128)(2,1)S(1)}, bf16[16,16,512]{2,1,0:T(8,128)(2,1)S(1)}, u32[]{:S(2)}, u32[]{:S(2)}) collective-permute-start(bf16[16,16,512]{2,1,0:T(8,128)(2,1)S(1)} %get-tuple-element.40), channel_id=1, source_target_pairs={{0,5},{4,1},{8,13},{12,9},{2,7},{6,3},{10,15},{14,11},{16,21},{20,... | collective-permute-start | bytes 786440 | tf_op jit(solution)/shard_map/ppermute | solution.py:374
  21.5 1.3 %collective-permute-start.14 = (bf16[16,16,512]{2,1,0:T(8,128)(2,1)S(1)}, bf16[16,16,512]{2,1,0:T(8,128)(2,1)S(1)}, u32[]{:S(2)}, u32[]{:S(2)}) collective-permute-start(bf16[16,16,512]{2,1,0:T(8,128)(2,1)S(1)} %get-tuple-element.41), channel_id=1, source_target_pairs={{0,9},{4,13},{8,1},{12,5},{2,11},{6,15},{10,3},{14,7},{16,25},{20,... | collective-permute-start | bytes 786440 | tf_op jit(solution)/shard_map/ppermute | solution.py:374
  22.8 0.0 collective-permute-done.3.refs_1_
  22.8 3.9 %collective-permute-done.4.refs_2_ = bf16[256,1024]{1,0:T(8,128)(2,1)S(1)} collective-permute-done((bf16[256,1024]{1,0:T(8,128)(2,1)S(1)}, bf16[256,1024]{1,0:T(8,128)(2,1)S(1)}, u32[]{:S(2)}, u32[]{:S(2)}) %collective-permute-start.4) | collective-permute-done | bytes 524320 | tf_op jit(solution)/shard_map/ppermute | solution.py:365
  26.7 1.3 %collective-permute-start.10 = (bf16[8,16,512]{2,1,0:T(8,128)(2,1)S(1)}, bf16[8,16,512]{2,1,0:T(8,128)(2,1)S(1)}, u32[]{:S(2)}, u32[]{:S(2)}) collective-permute-start(bf16[8,16,512]{2,1,0:T(8,128)(2,1)S(1)} %get-tuple-element.37), channel_id=1, source_target_pairs={{1,4},{5,0},{9,12},{13,8},{3,6},{7,2},{11,14},{15,10},{17,20},{21,... | collective-permute-start | bytes 393224 | tf_op jit(solution)/shard_map/ppermute | solution.py:374
  28.0 1.3 %collective-permute-start.11 = (bf16[8,16,512]{2,1,0:T(8,128)(2,1)S(1)}, bf16[8,16,512]{2,1,0:T(8,128)(2,1)S(1)}, u32[]{:S(2)}, u32[]{:S(2)}) collective-permute-start(bf16[8,16,512]{2,1,0:T(8,128)(2,1)S(1)} %get-tuple-element.38), channel_id=1, source_target_pairs={{1,8},{5,12},{9,0},{13,4},{3,10},{7,14},{11,2},{15,6},{17,24},{21,... | collective-permute-start | bytes 393224 | tf_op jit(solution)/shard_map/ppermute | solution.py:374
  29.3 0.0 copy-start.4
  29.3 0.0 collective-permute-done.1.refs_1_
  29.3 1.4 %collective-permute-start.12 = (bf16[8,16,512]{2,1,0:T(8,128)(2,1)S(1)}, bf16[8,16,512]{2,1,0:T(8,128)(2,1)S(1)}, u32[]{:S(2)}, u32[]{:S(2)}) collective-permute-start(bf16[8,16,512]{2,1,0:T(8,128)(2,1)S(1)} %get-tuple-element.39), channel_id=1, source_target_pairs={{1,12},{5,8},{9,4},{13,0},{3,14},{7,10},{11,6},{15,2},{17,28},{21,... | collective-permute-start | bytes 393224 | tf_op jit(solution)/shard_map/ppermute | solution.py:374
  30.9 10.6 %collective-permute-done.10.refs_0_ = bf16[8,16,512]{2,1,0:T(8,128)(2,1)S(1)} collective-permute-done((bf16[8,16,512]{2,1,0:T(8,128)(2,1)S(1)}, bf16[8,16,512]{2,1,0:T(8,128)(2,1)S(1)}, u32[]{:S(2)}, u32[]{:S(2)}) %collective-permute-start.10) | collective-permute-done | bytes 131104 | tf_op jit(solution)/shard_map/ppermute | solution.py:374
  41.4 7.1 %collective-permute-start.15 = (bf16[16,16,512]{2,1,0:T(8,128)(2,1)S(1)}, bf16[16,16,512]{2,1,0:T(8,128)(2,1)S(1)}, u32[]{:S(2)}, u32[]{:S(2)}) collective-permute-start(bf16[16,16,512]{2,1,0:T(8,128)(2,1)S(1)} %get-tuple-element.42), channel_id=1, source_target_pairs={{0,13},{4,9},{8,5},{12,1},{2,15},{6,11},{10,7},{14,3},{16,29},{20,... | collective-permute-start | bytes 786440 | tf_op jit(solution)/shard_map/ppermute | solution.py:374
  48.6 0.0 collective-permute-done.11.refs_1_
  48.6 0.1 collective-permute-start.9
  48.6 0.0 collective-permute-done.12.refs_2_
  48.7 1.3 %collective-permute-start.6 = (bf16[8,16,512]{2,1,0:T(8,128)(2,1)S(1)}, bf16[8,16,512]{2,1,0:T(8,128)(2,1)S(1)}, u32[]{:S(2)}, u32[]{:S(2)}) collective-permute-start(bf16[8,16,512]{2,1,0:T(8,128)(2,1)S(1)} %get-tuple-element.33), channel_id=1, source_target_pairs={{1,4},{5,0},{9,12},{13,8},{3,6},{7,2},{11,14},{15,10},{17,20},{21,... | collective-permute-start | bytes 393224 | tf_op jit(solution)/shard_map/ppermute | solution.py:374
  50.0 0.0 collective-permute-done.13.refs_3_
  50.0 1.3 %collective-permute-start.7 = (bf16[8,16,512]{2,1,0:T(8,128)(2,1)S(1)}, bf16[8,16,512]{2,1,0:T(8,128)(2,1)S(1)}, u32[]{:S(2)}, u32[]{:S(2)}) collective-permute-start(bf16[8,16,512]{2,1,0:T(8,128)(2,1)S(1)} %get-tuple-element.34), channel_id=1, source_target_pairs={{1,8},{5,12},{9,0},{13,4},{3,10},{7,14},{11,2},{15,6},{17,24},{21,... | collective-permute-start | bytes 393224 | tf_op jit(solution)/shard_map/ppermute | solution.py:374
  51.3 0.0 collective-permute-done.14.refs_4_
  51.3 1.3 %collective-permute-start.8 = (bf16[8,16,512]{2,1,0:T(8,128)(2,1)S(1)}, bf16[8,16,512]{2,1,0:T(8,128)(2,1)S(1)}, u32[]{:S(2)}, u32[]{:S(2)}) collective-permute-start(bf16[8,16,512]{2,1,0:T(8,128)(2,1)S(1)} %get-tuple-element.35), channel_id=1, source_target_pairs={{1,12},{5,8},{9,4},{13,0},{3,14},{7,10},{11,6},{15,2},{17,28},{21,... | collective-permute-start | bytes 393224 | tf_op jit(solution)/shard_map/ppermute | solution.py:374
  52.6 1.4 %collective-permute-done.15.refs_5_ = bf16[16,16,512]{2,1,0:T(8,128)(2,1)S(1)} collective-permute-done((bf16[16,16,512]{2,1,0:T(8,128)(2,1)S(1)}, bf16[16,16,512]{2,1,0:T(8,128)(2,1)S(1)}, u32[]{:S(2)}, u32[]{:S(2)}) %collective-permute-start.15) | collective-permute-done | bytes 262176 | tf_op jit(solution)/shard_map/ppermute | solution.py:374
  54.0 0.0 collective-permute-done.9.own_ref
  54.0 0.9 %shard_map.85.refs_3_ = bf16[16,64,512]{2,1,0:T(8,128)(2,1)} custom-call(bf16[16,16,512]{2,1,0:T(8,128)(2,1)S(1)} %collective-permute-done.9.own_ref, bf16[8,16,512]{2,1,0:T(8,128)(2,1)S(1)} %collective-permute-done.10.refs_0_, bf16[8,16,512]{2,1,0:T(8,128)(2,1)S(1)} %collective-permute-done.11.refs_1_, ...), custom_call_target="tpu_custom_call" | custom-call | bytes 2097152 | tf_op jit(solution)/shard_map/pallas_call | solution.py:471
  54.9 0.1 collective-permute-done.6.refs_0_
  54.9 3.0 %collective-permute-done.7.refs_1_ = bf16[8,16,512]{2,1,0:T(8,128)(2,1)S(1)} collective-permute-done((bf16[8,16,512]{2,1,0:T(8,128)(2,1)S(1)}, bf16[8,16,512]{2,1,0:T(8,128)(2,1)S(1)}, u32[]{:S(2)}, u32[]{:S(2)}) %collective-permute-start.7) | collective-permute-done | bytes 131104 | tf_op jit(solution)/shard_map/ppermute | solution.py:374
  57.9 1.6 %collective-permute-done.8.refs_2_ = bf16[8,16,512]{2,1,0:T(8,128)(2,1)S(1)} collective-permute-done((bf16[8,16,512]{2,1,0:T(8,128)(2,1)S(1)}, bf16[8,16,512]{2,1,0:T(8,128)(2,1)S(1)}, u32[]{:S(2)}, u32[]{:S(2)}) %collective-permute-start.8) | collective-permute-done | bytes 131104 | tf_op jit(solution)/shard_map/ppermute | solution.py:374
  59.5 0.8 %shard_map.86 = bf16[16,64,512]{2,1,0:T(8,128)(2,1)} custom-call(bf16[8,16,512]{2,1,0:T(8,128)(2,1)S(1)} %collective-permute-done.6.refs_0_, bf16[8,16,512]{2,1,0:T(8,128)(2,1)S(1)} %collective-permute-done.7.refs_1_, bf16[8,16,512]{2,1,0:T(8,128)(2,1)S(1)} %collective-permute-done.8.refs_2_, ...), custom_call_target="tpu_custom_call", output_to_operand_aliasing={{}: (3, {})} | custom-call | bytes 2097152 | tf_op jit(solution)/shard_map/pallas_call | solution.py:471
  (12 shorter events, 0.1 us)
Async XLA Ops:
  0.0 1.9 %copy-start.5 = (bf16[1,1,512,4,2,256]{5,4,3,2,1,0:T(2,128)(2,1)S(1)}, bf16[1,1,512,4,2,256]{5,4,3,2,1,0:T(2,128)(2,1)}, u32[]{:S(2)}) copy-start(bf16[1,1,512,4,2,256]{5,4,3,2,1,0:T(2,128)(2,1)} %param.7) | copy-start | bytes 6291460
  3.6 10.8 %copy-start.3 = (f32[1,1,4,2,256]{4,3,2,1,0:T(2,128)S(1)}, f32[1,1,4,2,256]{4,3,2,1,0:T(2,128)}, u32[]{:S(2)}) copy-start(f32[1,1,4,2,256]{4,3,2,1,0:T(2,128)} %param.8) | copy-start | bytes 24580
  3.6 10.9 %copy-start = (bf16[256,768]{1,0:T(8,128)(2,1)S(1)}, bf16[256,768]{1,0:T(8,128)(2,1)}, u32[]{:S(2)}) copy-start(bf16[256,768]{1,0:T(8,128)(2,1)} %constant.6.clone.refs_0_) | copy-start | bytes 1179652
  3.6 10.9 %copy-start.1 = (bf16[512,512]{1,0:T(8,128)(2,1)S(1)}, bf16[512,512]{1,0:T(8,128)(2,1)}, u32[]{:S(2)}) copy-start(bf16[512,512]{1,0:T(8,128)(2,1)} %constant.8.clone.refs_7_.refs_4_.refs_3_) | copy-start | bytes 1572868
  3.7 3.6 %collective-permute-start = (bf16[768,1024]{1,0:T(8,128)(2,1)S(1)}, bf16[768,1024]{1,0:T(8,128)(2,1)S(1)}, u32[]{:S(2)}, u32[]{:S(2)}) collective-permute-start(bf16[768,1024]{1,0:T(8,128)(2,1)S(1)} %shard_map.74.refs_0_.refs_3_.refs_1_), channel_id=1, source_target_pairs={{0,1},{1,0},{2,3},{3,2},{4,5},{5,4},{6,7},{7,6},{8,9},{9,8},{10,11... | collective-permute-start | bytes 4718600 | tf_op jit(solution)/shard_map/ppermute | solution.py:368
  4.2 13.4 %collective-permute-start.5 = (bf16[256,1024]{1,0:T(8,128)(2,1)S(1)}, bf16[256,1024]{1,0:T(8,128)(2,1)S(1)}, u32[]{:S(2)}, u32[]{:S(2)}) collective-permute-start(bf16[256,1024]{1,0:T(8,128)(2,1)S(1)} %get-tuple-element.27.refs_2_), channel_id=1, source_target_pairs={{0,1},{1,0},{2,3},{3,2},{4,5},{5,4},{6,7},{7,6},{8,9},{9,8},{10,11... | collective-permute-start | bytes 1572872 | tf_op jit(solution)/shard_map/ppermute | solution.py:368
  7.3 22.1 %collective-permute-start.1 = (bf16[448,1024]{1,0:T(8,128)(2,1)S(1)}, bf16[448,1024]{1,0:T(8,128)(2,1)S(1)}, u32[]{:S(2)}, u32[]{:S(2)}) collective-permute-start(bf16[448,1024]{1,0:T(8,128)(2,1)S(1)} %shard_map.75), channel_id=1, source_target_pairs={{1,3},{5,7},{9,11},{13,15},{17,19},{21,23},{25,27},{29,31}} | collective-permute-start | bytes 2752520 | tf_op jit(solution)/shard_map/ppermute | solution.py:365
  8.0 14.8 %collective-permute-start.3 = (bf16[256,1024]{1,0:T(8,128)(2,1)S(1)}, bf16[256,1024]{1,0:T(8,128)(2,1)S(1)}, u32[]{:S(2)}, u32[]{:S(2)}) collective-permute-start(bf16[256,1024]{1,0:T(8,128)(2,1)S(1)} %get-tuple-element.27.refs_2_), channel_id=1, source_target_pairs={{1,3},{5,7},{9,11},{13,15},{17,19},{21,23},{25,27},{29,31}} | collective-permute-start | bytes 1572872 | tf_op jit(solution)/shard_map/ppermute | solution.py:365
  8.7 18.0 %collective-permute-start.4 = (bf16[256,1024]{1,0:T(8,128)(2,1)S(1)}, bf16[256,1024]{1,0:T(8,128)(2,1)S(1)}, u32[]{:S(2)}, u32[]{:S(2)}) collective-permute-start(bf16[256,1024]{1,0:T(8,128)(2,1)S(1)} %get-tuple-element.27.refs_2_), channel_id=1, source_target_pairs={{0,3},{4,7},{8,11},{12,15},{16,19},{20,23},{24,27},{28,31}} | collective-permute-start | bytes 1572872 | tf_op jit(solution)/shard_map/ppermute | solution.py:365
  14.5 2.0 %copy-start.2 = (s32[1024]{0:T(1024)S(1)}, s32[1024]{0:T(1024)}, u32[]{:S(2)}) copy-start(s32[1024]{0:T(1024)} %param.10) | copy-start | bytes 12292
  14.5 2.0 %collective-permute-start.2 = (f32[4,2,256]{2,1,0:T(2,128)S(1)}, f32[4,2,256]{2,1,0:T(2,128)S(1)}, u32[]{:S(2)}, u32[]{:S(2)}) collective-permute-start(f32[4,2,256]{2,1,0:T(2,128)S(1)} %bitcast.12), channel_id=1, source_target_pairs={{0,1},{1,0},{2,3},{3,2},{4,5},{5,4},{6,7},{7,6},{8,9},{9,8},{10,11... | collective-permute-start | bytes 24584 | tf_op jit(solution)/shard_map/ppermute | solution.py:368
  20.1 29.8 %collective-permute-start.13 = (bf16[16,16,512]{2,1,0:T(8,128)(2,1)S(1)}, bf16[16,16,512]{2,1,0:T(8,128)(2,1)S(1)}, u32[]{:S(2)}, u32[]{:S(2)}) collective-permute-start(bf16[16,16,512]{2,1,0:T(8,128)(2,1)S(1)} %get-tuple-element.40), channel_id=1, source_target_pairs={{0,5},{4,1},{8,13},{12,9},{2,7},{6,3},{10,15},{14,11},{16,21},{20,... | collective-permute-start | bytes 786440 | tf_op jit(solution)/shard_map/ppermute | solution.py:374
  21.5 29.8 %collective-permute-start.14 = (bf16[16,16,512]{2,1,0:T(8,128)(2,1)S(1)}, bf16[16,16,512]{2,1,0:T(8,128)(2,1)S(1)}, u32[]{:S(2)}, u32[]{:S(2)}) collective-permute-start(bf16[16,16,512]{2,1,0:T(8,128)(2,1)S(1)} %get-tuple-element.41), channel_id=1, source_target_pairs={{0,9},{4,13},{8,1},{12,5},{2,11},{6,15},{10,3},{14,7},{16,25},{20,... | collective-permute-start | bytes 786440 | tf_op jit(solution)/shard_map/ppermute | solution.py:374
  26.7 14.7 %collective-permute-start.10 = (bf16[8,16,512]{2,1,0:T(8,128)(2,1)S(1)}, bf16[8,16,512]{2,1,0:T(8,128)(2,1)S(1)}, u32[]{:S(2)}, u32[]{:S(2)}) collective-permute-start(bf16[8,16,512]{2,1,0:T(8,128)(2,1)S(1)} %get-tuple-element.37), channel_id=1, source_target_pairs={{1,4},{5,0},{9,12},{13,8},{3,6},{7,2},{11,14},{15,10},{17,20},{21,... | collective-permute-start | bytes 393224 | tf_op jit(solution)/shard_map/ppermute | solution.py:374
  28.0 20.6 %collective-permute-start.11 = (bf16[8,16,512]{2,1,0:T(8,128)(2,1)S(1)}, bf16[8,16,512]{2,1,0:T(8,128)(2,1)S(1)}, u32[]{:S(2)}, u32[]{:S(2)}) collective-permute-start(bf16[8,16,512]{2,1,0:T(8,128)(2,1)S(1)} %get-tuple-element.38), channel_id=1, source_target_pairs={{1,8},{5,12},{9,0},{13,4},{3,10},{7,14},{11,2},{15,6},{17,24},{21,... | collective-permute-start | bytes 393224 | tf_op jit(solution)/shard_map/ppermute | solution.py:374
  29.3 1.5 %copy-start.4 = (bf16[256,224]{1,0:T(8,128)(2,1)S(1)}, bf16[256,224]{1,0:T(8,128)(2,1)}, u32[]{:S(2)}) copy-start(bf16[256,224]{1,0:T(8,128)(2,1)} %constant.7.clone.refs_0_) | copy-start | bytes 344068
  29.3 19.3 %collective-permute-start.12 = (bf16[8,16,512]{2,1,0:T(8,128)(2,1)S(1)}, bf16[8,16,512]{2,1,0:T(8,128)(2,1)S(1)}, u32[]{:S(2)}, u32[]{:S(2)}) collective-permute-start(bf16[8,16,512]{2,1,0:T(8,128)(2,1)S(1)} %get-tuple-element.39), channel_id=1, source_target_pairs={{1,12},{5,8},{9,4},{13,0},{3,14},{7,10},{11,6},{15,2},{17,28},{21,... | collective-permute-start | bytes 393224 | tf_op jit(solution)/shard_map/ppermute | solution.py:374
  41.4 12.5 %collective-permute-start.15 = (bf16[16,16,512]{2,1,0:T(8,128)(2,1)S(1)}, bf16[16,16,512]{2,1,0:T(8,128)(2,1)S(1)}, u32[]{:S(2)}, u32[]{:S(2)}) collective-permute-start(bf16[16,16,512]{2,1,0:T(8,128)(2,1)S(1)} %get-tuple-element.42), channel_id=1, source_target_pairs={{0,13},{4,9},{8,5},{12,1},{2,15},{6,11},{10,7},{14,3},{16,29},{20,... | collective-permute-start | bytes 786440 | tf_op jit(solution)/shard_map/ppermute | solution.py:374
  48.6 5.4 %collective-permute-start.9 = (bf16[16,16,512]{2,1,0:T(8,128)(2,1)S(1)}, bf16[16,16,512]{2,1,0:T(8,128)(2,1)S(1)}, u32[]{:S(2)}, u32[]{:S(2)}) collective-permute-start(bf16[16,16,512]{2,1,0:T(8,128)(2,1)S(1)} %get-tuple-element.36), channel_id=1, source_target_pairs={{0,1},{1,0},{2,3},{3,2},{4,5},{5,4},{6,7},{7,6},{8,9},{9,8},{10,11... | collective-permute-start | bytes 786440 | tf_op jit(solution)/shard_map/ppermute | solution.py:368
  48.7 6.3 %collective-permute-start.6 = (bf16[8,16,512]{2,1,0:T(8,128)(2,1)S(1)}, bf16[8,16,512]{2,1,0:T(8,128)(2,1)S(1)}, u32[]{:S(2)}, u32[]{:S(2)}) collective-permute-start(bf16[8,16,512]{2,1,0:T(8,128)(2,1)S(1)} %get-tuple-element.33), channel_id=1, source_target_pairs={{1,4},{5,0},{9,12},{13,8},{3,6},{7,2},{11,14},{15,10},{17,20},{21,... | collective-permute-start | bytes 393224 | tf_op jit(solution)/shard_map/ppermute | solution.py:374
  50.0 7.9 %collective-permute-start.7 = (bf16[8,16,512]{2,1,0:T(8,128)(2,1)S(1)}, bf16[8,16,512]{2,1,0:T(8,128)(2,1)S(1)}, u32[]{:S(2)}, u32[]{:S(2)}) collective-permute-start(bf16[8,16,512]{2,1,0:T(8,128)(2,1)S(1)} %get-tuple-element.34), channel_id=1, source_target_pairs={{1,8},{5,12},{9,0},{13,4},{3,10},{7,14},{11,2},{15,6},{17,24},{21,... | collective-permute-start | bytes 393224 | tf_op jit(solution)/shard_map/ppermute | solution.py:374
  51.3 8.2 %collective-permute-start.8 = (bf16[8,16,512]{2,1,0:T(8,128)(2,1)S(1)}, bf16[8,16,512]{2,1,0:T(8,128)(2,1)S(1)}, u32[]{:S(2)}, u32[]{:S(2)}) collective-permute-start(bf16[8,16,512]{2,1,0:T(8,128)(2,1)S(1)} %get-tuple-element.35), channel_id=1, source_target_pairs={{1,12},{5,8},{9,4},{13,0},{3,14},{7,10},{11,6},{15,2},{17,28},{21,... | collective-permute-start | bytes 393224 | tf_op jit(solution)/shard_map/ppermute | solution.py:374

commit v18 on v17

--- a/solution.py
+++ b/solution.py
@@ -155,7 +155,9 @@
     return spectra
 
 
-def late_own_kernel(filt_ref, x_ref, near_ref, gain_ref, beam_ref, out_ref, cal_ref):
+def late_own_kernel(filt_ref, x_ref, near_ref, gain_ref, beam_ref, keep_ref, out_ref, cal_ref):
+    del keep_ref
+
     @pl.when(lax.axis_index("pol") == 0)
     def _():
         for block in range(out_ref.shape[0] // (BLOCK * UPCH)):
@@ -280,7 +282,7 @@
         table_ref[lax.axis_index("freq") ^ owner, rows, lanes] = jnp.where(hit, 1.0, 0.0).astype(jnp.bfloat16)
         return carry
 
-    lax.fori_loop(0, owner_ref.shape[0], step, 0, unroll=4)
+    lax.fori_loop(0, owner_ref.shape[0], step, 0, unroll=True)
     for j, copy in enumerate(copies):
         copy.wait()
         near_ref[:, j * LANES : (j + 1) * LANES] = held_ref[j].reshape(2 * count, LANES)
@@ -417,11 +419,11 @@
     late_own = call(
         late_own_kernel,
         jax.ShapeDtypeStruct((kept * UPCH, beams), bf16),
-        5,
+        6,
         4 * 512 * 1024 * 1024,
         4 << 20,
         scratch=[cal],
-    )(filt, x, near_rows, gain, beam_table)
+    )(filt, x, near_rows, gain, beam_table, keep)
     late_first = call(
         late_first_kernel,
         jax.ShapeDtypeStruct((BLOCK * UPCH, beams), bf16),

time: 60.6 us -> 60.5 us (level)
  no operation moved by 1% of the time
where the time goes in v18:
time: 60.5 us; the launch traced here: 60.1 us
  starting transfers between devices  25.5 us (42%)
  waiting for transfers between devices  23.5 us (39%)
  Pallas kernels  9.02 us (15%)
  local copies, waits for them, and re-layouts  1.71 us (3%)
    ppermute x9, starting transfers between devices, spread(): got.append(lax.ppermute(blocks[k], ('freq', 'pol'), route))  17.6 us
    ppermute x9, waiting for transfers between devices, spread(): got.append(lax.ppermute(blocks[k], ('freq', 'pol'), route))  16.6 us
    ppermute x3, starting transfers between devices, ahead(): lax.ppermute(part, ('tm', 'pol'), [(i * 2 + source, j * 2 + 1) for i, j i...  7.17 us
    ppermute x3, waiting for transfers between devices, ahead(): lax.ppermute(part, ('tm', 'pol'), [(i * 2 + source, j * 2 + 1) for i, j i...  3.96 us
    ppermute x4, waiting for transfers between devices, swap(): return lax.ppermute(part, 'pol', [(0, 1), (1, 0)])  2.97 us
    pallas_call x1, Pallas kernels, per_device(): call(late_own_kernel, jax.ShapeDtypeStruct((kept * UPCH, beams), bf16), 6...  1.9 us
    pallas_call x1, Pallas kernels, per_device(): pl.pallas_call(head_kernel, out_shape=[jax.ShapeDtypeStruct((n_owner, bea...  1.72 us
    pallas_call x2, Pallas kernels, gather(): pl.pallas_call(functools.partial(body, n_owner), out_shape=out_shape, in_...  1.64 us
  transfers between devices with their start and end apart: 16, of which 7 were waited for; matrix products, arithmetic and copies ran while one was open for 0% of the time, Pallas kernels for 11%

profile of v18, /device:TPU:0, one launch (start us, length us, event | category | flops | bytes accessed | tf_op | source)
XLA Modules:
  0.0 60.1 jit_solution(13304098169705079296)
XLA Ops:
  0.0 1.7 %shard_map.73 = (bf16[4,1024,512]{2,1,0:T(8,128)(2,1)S(1)}, bf16[256,1024]{1,0:T(8,128)(2,1)S(1)}) custom-call(s32[64]{0:T(128)} %sets_ref.1, bf16[512,4,2,256]{3,2,1,0:T(2,128)(2,1)} %bitcast.17), custom_call_target="tpu_custom_call" | custom-call | flops 1048576 | bytes 4194304 | tf_op jit(solution)/shard_map/pallas_call | solution.py:393
  1.7 0.1 copy-done.5
  1.8 1.1 %copy.9 = bf16[512,2,4,256]{3,2,1,0:T(4,128)(2,1)S(1)} copy(bf16[512,2,4,256]{3,1,2,0:T(2,128)(2,1)S(1)} %bitcast.18) | data formatting | bytes 4194304 | tf_op jit(solution)/shard_map/transpose | solution.py:411
  2.9 0.5 copy.10
  3.4 0.1 shard_map.74.refs_0_.refs_3_.refs_1_
  3.5 0.0 copy-start.3
  3.5 0.0 copy-start
  3.6 0.0 copy-start.1
  3.6 0.0 copy-start.2
  3.6 0.6 collective-permute-start
  4.1 0.1 collective-permute-start.5
  4.2 3.0 %collective-permute-done.refs_1_.refs_4_ = bf16[768,1024]{1,0:T(8,128)(2,1)S(1)} collective-permute-done((bf16[768,1024]{1,0:T(8,128)(2,1)S(1)}, bf16[768,1024]{1,0:T(8,128)(2,1)S(1)}, u32[]{:S(2)}, u32[]{:S(2)}) %collective-permute-start) | collective-permute-done | bytes 1572896 | tf_op jit(solution)/shard_map/ppermute | solution.py:370
  7.2 0.7 %collective-permute-start.1 = (bf16[448,1024]{1,0:T(8,128)(2,1)S(1)}, bf16[448,1024]{1,0:T(8,128)(2,1)S(1)}, u32[]{:S(2)}, u32[]{:S(2)}) collective-permute-start(bf16[448,1024]{1,0:T(8,128)(2,1)S(1)} %shard_map.75), channel_id=1, source_target_pairs={{1,3},{5,7},{9,11},{13,15},{17,19},{21,23},{25,27},{29,31}} | collective-permute-start | bytes 2752520 | tf_op jit(solution)/shard_map/ppermute | solution.py:367
  7.9 0.7 %collective-permute-start.3 = (bf16[256,1024]{1,0:T(8,128)(2,1)S(1)}, bf16[256,1024]{1,0:T(8,128)(2,1)S(1)}, u32[]{:S(2)}, u32[]{:S(2)}) collective-permute-start(bf16[256,1024]{1,0:T(8,128)(2,1)S(1)} %get-tuple-element.27.refs_2_), channel_id=1, source_target_pairs={{1,3},{5,7},{9,11},{13,15},{17,19},{21,23},{25,27},{29,31}} | collective-permute-start | bytes 1572872 | tf_op jit(solution)/shard_map/ppermute | solution.py:367
  8.6 5.8 %collective-permute-start.4 = (bf16[256,1024]{1,0:T(8,128)(2,1)S(1)}, bf16[256,1024]{1,0:T(8,128)(2,1)S(1)}, u32[]{:S(2)}, u32[]{:S(2)}) collective-permute-start(bf16[256,1024]{1,0:T(8,128)(2,1)S(1)} %get-tuple-element.27.refs_2_), channel_id=1, source_target_pairs={{0,3},{4,7},{8,11},{12,15},{16,19},{20,23},{24,27},{28,31}} | collective-permute-start | bytes 1572872 | tf_op jit(solution)/shard_map/ppermute | solution.py:367
  14.4 0.1 collective-permute-start.2
  14.5 1.9 %shard_map.80.refs_5_.refs_7_ = bf16[256,1024]{1,0:T(8,128)(2,1)S(1)} custom-call(bf16[256,768]{1,0:T(8,128)(2,1)S(1)} %copy-done, bf16[768,1024]{1,0:T(8,128)(2,1)S(1)} %shard_map.74.refs_0_.refs_3_.refs_1_, bf16[256,1024]{1,0:T(8,128)(2,1)S(1)} %get-tuple-element.27.refs_2_, f32[4,2,256]{2,1,0:T(2,128)S(1)} %bitcast.14, bf16[512,512]{1,0:T(8,128)(2,1)S(1)} %copy-done.1, ...), custom_call_target="tpu_custom_call" | custom-call | flops 2147483648 | bytes 4194304 | tf_op jit(solution)/shard_map/pallas_call | solution.py:419
  16.4 0.0 collective-permute-done.2.refs_6_.refs_3_.refs_2_
  16.4 1.1 %shard_map.81.refs_8_ = bf16[128,1024]{1,0:T(8,128)(2,1)S(1)} custom-call(bf16[256,768]{1,0:T(8,128)(2,1)S(1)} %copy-done, bf16[768,1024]{1,0:T(8,128)(2,1)S(1)} %collective-permute-done.refs_1_.refs_4_, f32[4,2,256]{2,1,0:T(2,128)S(1)} %collective-permute-done.2.refs_6_.refs_3_.refs_2_, bf16[512,512]{1,0:T(8,128)(2,1)S(1)} %copy-done.1, ...), custom_call_target="tpu_custom_call" | custom-call | flops 1073741824 | bytes 4194304 | tf_op jit(solution)/shard_map/pallas_call | solution.py:427
  17.6 0.0 collective-permute-done.5.refs_2_
  17.6 1.5 %shard_map.82 = (bf16[256,1024]{1,0:T(8,128)(2,1)S(1)}, bf16[16,16,512]{2,1,0:T(8,128)(2,1)S(1)}) custom-call(bf16[256,768]{1,0:T(8,128)(2,1)S(1)} %copy-done, bf16[768,1024]{1,0:T(8,128)(2,1)S(1)} %collective-permute-done.refs_1_.refs_4_, bf16[256,1024]{1,0:T(8,128)(2,1)S(1)} %collective-permute-done.5.refs_2_, ...), custom_call_target="tpu_custom_call" | custom-call | flops 2147483648 | bytes 4194304 | tf_op jit(solution)/shard_map/pallas_call | solution.py:382
  19.0 1.0 %shard_map.83 = (bf16[16,16,512]{2,1,0:T(8,128)(2,1)S(1)}, bf16[16,16,512]{2,1,0:T(8,128)(2,1)S(1)}, bf16[16,16,512]{2,1,0:T(8,128)(2,1)S(1)}) custom-call(bf16[256,1024]{1,0:T(8,128)(2,1)S(1)} %get-tuple-element.31.refs_0_, bf16[4,1024,512]{2,1,0:T(8,128)(2,1)S(1)} %get-tuple-element.26.refs_9_.refs_1_.refs_6_), custom_call_target="tpu_custom_call" | custom-call | flops 536870912 | bytes 4194304 | tf_op jit(solution)/shard_map/pallas_call | solution.py:388
  20.0 1.3 %collective-permute-start.13 = (bf16[16,16,512]{2,1,0:T(8,128)(2,1)S(1)}, bf16[16,16,512]{2,1,0:T(8,128)(2,1)S(1)}, u32[]{:S(2)}, u32[]{:S(2)}) collective-permute-start(bf16[16,16,512]{2,1,0:T(8,128)(2,1)S(1)} %get-tuple-element.40), channel_id=1, source_target_pairs={{0,5},{4,1},{8,13},{12,9},{2,7},{6,3},{10,15},{14,11},{16,21},{20,... | collective-permute-start | bytes 786440 | tf_op jit(solution)/shard_map/ppermute | solution.py:376
  21.4 1.3 %collective-permute-start.14 = (bf16[16,16,512]{2,1,0:T(8,128)(2,1)S(1)}, bf16[16,16,512]{2,1,0:T(8,128)(2,1)S(1)}, u32[]{:S(2)}, u32[]{:S(2)}) collective-permute-start(bf16[16,16,512]{2,1,0:T(8,128)(2,1)S(1)} %get-tuple-element.41), channel_id=1, source_target_pairs={{0,9},{4,13},{8,1},{12,5},{2,11},{6,15},{10,3},{14,7},{16,25},{20,... | collective-permute-start | bytes 786440 | tf_op jit(solution)/shard_map/ppermute | solution.py:376
  22.7 0.0 collective-permute-done.3.refs_1_
  22.7 4.0 %collective-permute-done.4.refs_2_ = bf16[256,1024]{1,0:T(8,128)(2,1)S(1)} collective-permute-done((bf16[256,1024]{1,0:T(8,128)(2,1)S(1)}, bf16[256,1024]{1,0:T(8,128)(2,1)S(1)}, u32[]{:S(2)}, u32[]{:S(2)}) %collective-permute-start.4) | collective-permute-done | bytes 524320 | tf_op jit(solution)/shard_map/ppermute | solution.py:367
  26.6 1.3 %collective-permute-start.10 = (bf16[8,16,512]{2,1,0:T(8,128)(2,1)S(1)}, bf16[8,16,512]{2,1,0:T(8,128)(2,1)S(1)}, u32[]{:S(2)}, u32[]{:S(2)}) collective-permute-start(bf16[8,16,512]{2,1,0:T(8,128)(2,1)S(1)} %get-tuple-element.37), channel_id=1, source_target_pairs={{1,4},{5,0},{9,12},{13,8},{3,6},{7,2},{11,14},{15,10},{17,20},{21,... | collective-permute-start | bytes 393224 | tf_op jit(solution)/shard_map/ppermute | solution.py:376
  27.9 1.3 %collective-permute-start.11 = (bf16[8,16,512]{2,1,0:T(8,128)(2,1)S(1)}, bf16[8,16,512]{2,1,0:T(8,128)(2,1)S(1)}, u32[]{:S(2)}, u32[]{:S(2)}) collective-permute-start(bf16[8,16,512]{2,1,0:T(8,128)(2,1)S(1)} %get-tuple-element.38), channel_id=1, source_target_pairs={{1,8},{5,12},{9,0},{13,4},{3,10},{7,14},{11,2},{15,6},{17,24},{21,... | collective-permute-start | bytes 393224 | tf_op jit(solution)/shard_map/ppermute | solution.py:376
  29.2 0.0 copy-start.4
  29.3 0.0 collective-permute-done.1.refs_1_
  29.3 1.4 %collective-permute-start.12 = (bf16[8,16,512]{2,1,0:T(8,128)(2,1)S(1)}, bf16[8,16,512]{2,1,0:T(8,128)(2,1)S(1)}, u32[]{:S(2)}, u32[]{:S(2)}) collective-permute-start(bf16[8,16,512]{2,1,0:T(8,128)(2,1)S(1)} %get-tuple-element.39), channel_id=1, source_target_pairs={{1,12},{5,8},{9,4},{13,0},{3,14},{7,10},{11,6},{15,2},{17,28},{21,... | collective-permute-start | bytes 393224 | tf_op jit(solution)/shard_map/ppermute | solution.py:376
  30.8 10.6 %collective-permute-done.10.refs_0_ = bf16[8,16,512]{2,1,0:T(8,128)(2,1)S(1)} collective-permute-done((bf16[8,16,512]{2,1,0:T(8,128)(2,1)S(1)}, bf16[8,16,512]{2,1,0:T(8,128)(2,1)S(1)}, u32[]{:S(2)}, u32[]{:S(2)}) %collective-permute-start.10) | collective-permute-done | bytes 131104 | tf_op jit(solution)/shard_map/ppermute | solution.py:376
  41.4 7.1 %collective-permute-start.15 = (bf16[16,16,512]{2,1,0:T(8,128)(2,1)S(1)}, bf16[16,16,512]{2,1,0:T(8,128)(2,1)S(1)}, u32[]{:S(2)}, u32[]{:S(2)}) collective-permute-start(bf16[16,16,512]{2,1,0:T(8,128)(2,1)S(1)} %get-tuple-element.42), channel_id=1, source_target_pairs={{0,13},{4,9},{8,5},{12,1},{2,15},{6,11},{10,7},{14,3},{16,29},{20,... | collective-permute-start | bytes 786440 | tf_op jit(solution)/shard_map/ppermute | solution.py:376
  48.5 0.0 collective-permute-done.11.refs_1_
  48.5 0.1 collective-permute-start.9
  48.5 0.0 collective-permute-done.12.refs_2_
  48.6 1.3 %collective-permute-start.6 = (bf16[8,16,512]{2,1,0:T(8,128)(2,1)S(1)}, bf16[8,16,512]{2,1,0:T(8,128)(2,1)S(1)}, u32[]{:S(2)}, u32[]{:S(2)}) collective-permute-start(bf16[8,16,512]{2,1,0:T(8,128)(2,1)S(1)} %get-tuple-element.33), channel_id=1, source_target_pairs={{1,4},{5,0},{9,12},{13,8},{3,6},{7,2},{11,14},{15,10},{17,20},{21,... | collective-permute-start | bytes 393224 | tf_op jit(solution)/shard_map/ppermute | solution.py:376
  49.9 0.0 collective-permute-done.13.refs_3_
  49.9 1.3 %collective-permute-start.7 = (bf16[8,16,512]{2,1,0:T(8,128)(2,1)S(1)}, bf16[8,16,512]{2,1,0:T(8,128)(2,1)S(1)}, u32[]{:S(2)}, u32[]{:S(2)}) collective-permute-start(bf16[8,16,512]{2,1,0:T(8,128)(2,1)S(1)} %get-tuple-element.34), channel_id=1, source_target_pairs={{1,8},{5,12},{9,0},{13,4},{3,10},{7,14},{11,2},{15,6},{17,24},{21,... | collective-permute-start | bytes 393224 | tf_op jit(solution)/shard_map/ppermute | solution.py:376
  51.2 0.0 collective-permute-done.14.refs_4_
  51.2 1.3 %collective-permute-start.8 = (bf16[8,16,512]{2,1,0:T(8,128)(2,1)S(1)}, bf16[8,16,512]{2,1,0:T(8,128)(2,1)S(1)}, u32[]{:S(2)}, u32[]{:S(2)}) collective-permute-start(bf16[8,16,512]{2,1,0:T(8,128)(2,1)S(1)} %get-tuple-element.35), channel_id=1, source_target_pairs={{1,12},{5,8},{9,4},{13,0},{3,14},{7,10},{11,6},{15,2},{17,28},{21,... | collective-permute-start | bytes 393224 | tf_op jit(solution)/shard_map/ppermute | solution.py:376
  52.5 1.4 %collective-permute-done.15.refs_5_ = bf16[16,16,512]{2,1,0:T(8,128)(2,1)S(1)} collective-permute-done((bf16[16,16,512]{2,1,0:T(8,128)(2,1)S(1)}, bf16[16,16,512]{2,1,0:T(8,128)(2,1)S(1)}, u32[]{:S(2)}, u32[]{:S(2)}) %collective-permute-start.15) | collective-permute-done | bytes 262176 | tf_op jit(solution)/shard_map/ppermute | solution.py:376
  53.9 0.0 collective-permute-done.9.own_ref
  53.9 0.9 %shard_map.85.refs_3_ = bf16[16,64,512]{2,1,0:T(8,128)(2,1)} custom-call(bf16[16,16,512]{2,1,0:T(8,128)(2,1)S(1)} %collective-permute-done.9.own_ref, bf16[8,16,512]{2,1,0:T(8,128)(2,1)S(1)} %collective-permute-done.10.refs_0_, bf16[8,16,512]{2,1,0:T(8,128)(2,1)S(1)} %collective-permute-done.11.refs_1_, ...), custom_call_target="tpu_custom_call" | custom-call | bytes 2097152 | tf_op jit(solution)/shard_map/pallas_call | solution.py:473
  54.7 0.1 collective-permute-done.6.refs_0_
  54.8 3.0 %collective-permute-done.7.refs_1_ = bf16[8,16,512]{2,1,0:T(8,128)(2,1)S(1)} collective-permute-done((bf16[8,16,512]{2,1,0:T(8,128)(2,1)S(1)}, bf16[8,16,512]{2,1,0:T(8,128)(2,1)S(1)}, u32[]{:S(2)}, u32[]{:S(2)}) %collective-permute-start.7) | collective-permute-done | bytes 131104 | tf_op jit(solution)/shard_map/ppermute | solution.py:376
  57.8 1.5 %collective-permute-done.8.refs_2_ = bf16[8,16,512]{2,1,0:T(8,128)(2,1)S(1)} collective-permute-done((bf16[8,16,512]{2,1,0:T(8,128)(2,1)S(1)}, bf16[8,16,512]{2,1,0:T(8,128)(2,1)S(1)}, u32[]{:S(2)}, u32[]{:S(2)}) %collective-permute-start.8) | collective-permute-done | bytes 131104 | tf_op jit(solution)/shard_map/ppermute | solution.py:376
  59.4 0.8 %shard_map.86 = bf16[16,64,512]{2,1,0:T(8,128)(2,1)} custom-call(bf16[8,16,512]{2,1,0:T(8,128)(2,1)S(1)} %collective-permute-done.6.refs_0_, bf16[8,16,512]{2,1,0:T(8,128)(2,1)S(1)} %collective-permute-done.7.refs_1_, bf16[8,16,512]{2,1,0:T(8,128)(2,1)S(1)} %collective-permute-done.8.refs_2_, ...), custom_call_target="tpu_custom_call", output_to_operand_aliasing={{}: (3, {})} | custom-call | bytes 2097152 | tf_op jit(solution)/shard_map/pallas_call | solution.py:473
  (12 shorter events, 0.1 us)
Async XLA Ops:
  0.0 1.8 %copy-start.5 = (bf16[1,1,512,4,2,256]{5,4,3,2,1,0:T(2,128)(2,1)S(1)}, bf16[1,1,512,4,2,256]{5,4,3,2,1,0:T(2,128)(2,1)}, u32[]{:S(2)}) copy-start(bf16[1,1,512,4,2,256]{5,4,3,2,1,0:T(2,128)(2,1)} %param.7) | copy-start | bytes 6291460
  3.5 10.8 %copy-start.3 = (f32[1,1,4,2,256]{4,3,2,1,0:T(2,128)S(1)}, f32[1,1,4,2,256]{4,3,2,1,0:T(2,128)}, u32[]{:S(2)}) copy-start(f32[1,1,4,2,256]{4,3,2,1,0:T(2,128)} %param.8) | copy-start | bytes 24580
  3.5 10.9 %copy-start = (bf16[256,768]{1,0:T(8,128)(2,1)S(1)}, bf16[256,768]{1,0:T(8,128)(2,1)}, u32[]{:S(2)}) copy-start(bf16[256,768]{1,0:T(8,128)(2,1)} %constant.6.clone.refs_0_) | copy-start | bytes 1179652
  3.6 10.9 %copy-start.1 = (bf16[512,512]{1,0:T(8,128)(2,1)S(1)}, bf16[512,512]{1,0:T(8,128)(2,1)}, u32[]{:S(2)}) copy-start(bf16[512,512]{1,0:T(8,128)(2,1)} %constant.8.clone.refs_7_.refs_4_.refs_3_) | copy-start | bytes 1572868
  3.6 10.9 %copy-start.2 = (s32[1024]{0:T(1024)S(1)}, s32[1024]{0:T(1024)}, u32[]{:S(2)}) copy-start(s32[1024]{0:T(1024)} %param.10) | copy-start | bytes 12292
  3.6 3.6 %collective-permute-start = (bf16[768,1024]{1,0:T(8,128)(2,1)S(1)}, bf16[768,1024]{1,0:T(8,128)(2,1)S(1)}, u32[]{:S(2)}, u32[]{:S(2)}) collective-permute-start(bf16[768,1024]{1,0:T(8,128)(2,1)S(1)} %shard_map.74.refs_0_.refs_3_.refs_1_), channel_id=1, source_target_pairs={{0,1},{1,0},{2,3},{3,2},{4,5},{5,4},{6,7},{7,6},{8,9},{9,8},{10,11... | collective-permute-start | bytes 4718600 | tf_op jit(solution)/shard_map/ppermute | solution.py:370
  4.1 13.4 %collective-permute-start.5 = (bf16[256,1024]{1,0:T(8,128)(2,1)S(1)}, bf16[256,1024]{1,0:T(8,128)(2,1)S(1)}, u32[]{:S(2)}, u32[]{:S(2)}) collective-permute-start(bf16[256,1024]{1,0:T(8,128)(2,1)S(1)} %get-tuple-element.27.refs_2_), channel_id=1, source_target_pairs={{0,1},{1,0},{2,3},{3,2},{4,5},{5,4},{6,7},{7,6},{8,9},{9,8},{10,11... | collective-permute-start | bytes 1572872 | tf_op jit(solution)/shard_map/ppermute | solution.py:370
  7.2 22.1 %collective-permute-start.1 = (bf16[448,1024]{1,0:T(8,128)(2,1)S(1)}, bf16[448,1024]{1,0:T(8,128)(2,1)S(1)}, u32[]{:S(2)}, u32[]{:S(2)}) collective-permute-start(bf16[448,1024]{1,0:T(8,128)(2,1)S(1)} %shard_map.75), channel_id=1, source_target_pairs={{1,3},{5,7},{9,11},{13,15},{17,19},{21,23},{25,27},{29,31}} | collective-permute-start | bytes 2752520 | tf_op jit(solution)/shard_map/ppermute | solution.py:367
  7.9 14.8 %collective-permute-start.3 = (bf16[256,1024]{1,0:T(8,128)(2,1)S(1)}, bf16[256,1024]{1,0:T(8,128)(2,1)S(1)}, u32[]{:S(2)}, u32[]{:S(2)}) collective-permute-start(bf16[256,1024]{1,0:T(8,128)(2,1)S(1)} %get-tuple-element.27.refs_2_), channel_id=1, source_target_pairs={{1,3},{5,7},{9,11},{13,15},{17,19},{21,23},{25,27},{29,31}} | collective-permute-start | bytes 1572872 | tf_op jit(solution)/shard_map/ppermute | solution.py:367
  8.6 18.0 %collective-permute-start.4 = (bf16[256,1024]{1,0:T(8,128)(2,1)S(1)}, bf16[256,1024]{1,0:T(8,128)(2,1)S(1)}, u32[]{:S(2)}, u32[]{:S(2)}) collective-permute-start(bf16[256,1024]{1,0:T(8,128)(2,1)S(1)} %get-tuple-element.27.refs_2_), channel_id=1, source_target_pairs={{0,3},{4,7},{8,11},{12,15},{16,19},{20,23},{24,27},{28,31}} | collective-permute-start | bytes 1572872 | tf_op jit(solution)/shard_map/ppermute | solution.py:367
  14.4 2.0 %collective-permute-start.2 = (f32[4,2,256]{2,1,0:T(2,128)S(1)}, f32[4,2,256]{2,1,0:T(2,128)S(1)}, u32[]{:S(2)}, u32[]{:S(2)}) collective-permute-start(f32[4,2,256]{2,1,0:T(2,128)S(1)} %bitcast.13), channel_id=1, source_target_pairs={{0,1},{1,0},{2,3},{3,2},{4,5},{5,4},{6,7},{7,6},{8,9},{9,8},{10,11... | collective-permute-start | bytes 24584 | tf_op jit(solution)/shard_map/ppermute | solution.py:370
  20.0 29.8 %collective-permute-start.13 = (bf16[16,16,512]{2,1,0:T(8,128)(2,1)S(1)}, bf16[16,16,512]{2,1,0:T(8,128)(2,1)S(1)}, u32[]{:S(2)}, u32[]{:S(2)}) collective-permute-start(bf16[16,16,512]{2,1,0:T(8,128)(2,1)S(1)} %get-tuple-element.40), channel_id=1, source_target_pairs={{0,5},{4,1},{8,13},{12,9},{2,7},{6,3},{10,15},{14,11},{16,21},{20,... | collective-permute-start | bytes 786440 | tf_op jit(solution)/shard_map/ppermute | solution.py:376
  21.4 29.8 %collective-permute-start.14 = (bf16[16,16,512]{2,1,0:T(8,128)(2,1)S(1)}, bf16[16,16,512]{2,1,0:T(8,128)(2,1)S(1)}, u32[]{:S(2)}, u32[]{:S(2)}) collective-permute-start(bf16[16,16,512]{2,1,0:T(8,128)(2,1)S(1)} %get-tuple-element.41), channel_id=1, source_target_pairs={{0,9},{4,13},{8,1},{12,5},{2,11},{6,15},{10,3},{14,7},{16,25},{20,... | collective-permute-start | bytes 786440 | tf_op jit(solution)/shard_map/ppermute | solution.py:376
  26.6 14.7 %collective-permute-start.10 = (bf16[8,16,512]{2,1,0:T(8,128)(2,1)S(1)}, bf16[8,16,512]{2,1,0:T(8,128)(2,1)S(1)}, u32[]{:S(2)}, u32[]{:S(2)}) collective-permute-start(bf16[8,16,512]{2,1,0:T(8,128)(2,1)S(1)} %get-tuple-element.37), channel_id=1, source_target_pairs={{1,4},{5,0},{9,12},{13,8},{3,6},{7,2},{11,14},{15,10},{17,20},{21,... | collective-permute-start | bytes 393224 | tf_op jit(solution)/shard_map/ppermute | solution.py:376
  27.9 20.5 %collective-permute-start.11 = (bf16[8,16,512]{2,1,0:T(8,128)(2,1)S(1)}, bf16[8,16,512]{2,1,0:T(8,128)(2,1)S(1)}, u32[]{:S(2)}, u32[]{:S(2)}) collective-permute-start(bf16[8,16,512]{2,1,0:T(8,128)(2,1)S(1)} %get-tuple-element.38), channel_id=1, source_target_pairs={{1,8},{5,12},{9,0},{13,4},{3,10},{7,14},{11,2},{15,6},{17,24},{21,... | collective-permute-start | bytes 393224 | tf_op jit(solution)/shard_map/ppermute | solution.py:376
  29.2 1.5 %copy-start.4 = (bf16[256,224]{1,0:T(8,128)(2,1)S(1)}, bf16[256,224]{1,0:T(8,128)(2,1)}, u32[]{:S(2)}) copy-start(bf16[256,224]{1,0:T(8,128)(2,1)} %constant.7.clone.refs_0_) | copy-start | bytes 344068
  29.3 19.3 %collective-permute-start.12 = (bf16[8,16,512]{2,1,0:T(8,128)(2,1)S(1)}, bf16[8,16,512]{2,1,0:T(8,128)(2,1)S(1)}, u32[]{:S(2)}, u32[]{:S(2)}) collective-permute-start(bf16[8,16,512]{2,1,0:T(8,128)(2,1)S(1)} %get-tuple-element.39), channel_id=1, source_target_pairs={{1,12},{5,8},{9,4},{13,0},{3,14},{7,10},{11,6},{15,2},{17,28},{21,... | collective-permute-start | bytes 393224 | tf_op jit(solution)/shard_map/ppermute | solution.py:376
  41.4 12.5 %collective-permute-start.15 = (bf16[16,16,512]{2,1,0:T(8,128)(2,1)S(1)}, bf16[16,16,512]{2,1,0:T(8,128)(2,1)S(1)}, u32[]{:S(2)}, u32[]{:S(2)}) collective-permute-start(bf16[16,16,512]{2,1,0:T(8,128)(2,1)S(1)} %get-tuple-element.42), channel_id=1, source_target_pairs={{0,13},{4,9},{8,5},{12,1},{2,15},{6,11},{10,7},{14,3},{16,29},{20,... | collective-permute-start | bytes 786440 | tf_op jit(solution)/shard_map/ppermute | solution.py:376
  48.5 5.4 %collective-permute-start.9 = (bf16[16,16,512]{2,1,0:T(8,128)(2,1)S(1)}, bf16[16,16,512]{2,1,0:T(8,128)(2,1)S(1)}, u32[]{:S(2)}, u32[]{:S(2)}) collective-permute-start(bf16[16,16,512]{2,1,0:T(8,128)(2,1)S(1)} %get-tuple-element.36), channel_id=1, source_target_pairs={{0,1},{1,0},{2,3},{3,2},{4,5},{5,4},{6,7},{7,6},{8,9},{9,8},{10,11... | collective-permute-start | bytes 786440 | tf_op jit(solution)/shard_map/ppermute | solution.py:370
  48.6 6.3 %collective-permute-start.6 = (bf16[8,16,512]{2,1,0:T(8,128)(2,1)S(1)}, bf16[8,16,512]{2,1,0:T(8,128)(2,1)S(1)}, u32[]{:S(2)}, u32[]{:S(2)}) collective-permute-start(bf16[8,16,512]{2,1,0:T(8,128)(2,1)S(1)} %get-tuple-element.33), channel_id=1, source_target_pairs={{1,4},{5,0},{9,12},{13,8},{3,6},{7,2},{11,14},{15,10},{17,20},{21,... | collective-permute-start | bytes 393224 | tf_op jit(solution)/shard_map/ppermute | solution.py:376
  49.9 8.0 %collective-permute-start.7 = (bf16[8,16,512]{2,1,0:T(8,128)(2,1)S(1)}, bf16[8,16,512]{2,1,0:T(8,128)(2,1)S(1)}, u32[]{:S(2)}, u32[]{:S(2)}) collective-permute-start(bf16[8,16,512]{2,1,0:T(8,128)(2,1)S(1)} %get-tuple-element.34), channel_id=1, source_target_pairs={{1,8},{5,12},{9,0},{13,4},{3,10},{7,14},{11,2},{15,6},{17,24},{21,... | collective-permute-start | bytes 393224 | tf_op jit(solution)/shard_map/ppermute | solution.py:376
  51.2 8.2 %collective-permute-start.8 = (bf16[8,16,512]{2,1,0:T(8,128)(2,1)S(1)}, bf16[8,16,512]{2,1,0:T(8,128)(2,1)S(1)}, u32[]{:S(2)}, u32[]{:S(2)}) collective-permute-start(bf16[8,16,512]{2,1,0:T(8,128)(2,1)S(1)} %get-tuple-element.35), channel_id=1, source_target_pairs={{1,12},{5,8},{9,4},{13,0},{3,14},{7,10},{11,6},{15,2},{17,28},{21,... | collective-permute-start | bytes 393224 | tf_op jit(solution)/shard_map/ppermute | solution.py:376
